TPU v7x, 128 devices: a whole 4x4x4 slice. The times are simulated.
128 devices in a mesh: region: 16 (over z, x), member: 8 (over y, core).
Axes of the slice: x: 4, y: 4, z: 4, core: 2. Of those that a mesh axis runs over, the one named last changes fastest.
Arguments:
- ensemble: bfloat16 [256, 32, 64, 512], P('region', 'member'), may hold values from -6 to 6
- increment: bfloat16 [256, 64, 512], P('region'), may hold values from -6 to 6
- coords: bfloat16 [256, 2, 512], P('region'), may hold values from -4.5 to 5.5
- sent_slots: int32 [16, 16, 1], P('region'), may hold values from 0 to 15, as said below
- pair_list: int32 [512, 2], P('region'), may hold values from 0 to 15, as said below
- pair_count: int32 [16], P('region'), may hold values from 16 to 32, as said below
Outputs:
- covariance_product: float32 [256, 64, 512], P('region', 'member')
Inputs may be any that keep to these rules, and one draw needn't show every extreme that they name: `sent_slots`: the k numbers of one home and owner are distinct. `pair_list`: the two slots of a row differ; every received slot is named by some live row of its owner. `pair_count`: some owner has exactly 32 live pairs and some has 16.
All inputs are finite; a program needn't handle non-finite values.
Results may differ from a plain program's by a relative error of at most 0.0028.
Values may be sent and summed in bfloat16 or wider, within the bound.
No kernel may reach another device: no remote copies, remote signals or barrier semaphores. Data moves between devices by JAX's collectives and lax.ppermute only.
A program may use at most 128 MiB of HBM per device.

v0:
```python
import jax
import jax.numpy as jnp
from jax import lax
from jax.sharding import PartitionSpec as P

PAIR_GROUP = 4


def gaspari_cohn(distance):
    inside_part = (
        ((-0.25 * distance + 0.5) * distance + 0.625) * distance - 5.0 / 3.0
    ) * distance * distance + 1.0
    floored = jnp.maximum(distance, 1.0)
    outside_part = (
        ((((distance / 12.0 - 0.5) * distance + 0.625) * distance + 5.0 / 3.0) * distance - 5.0)
        * distance
        + 4.0
        - 2.0 / (3.0 * floored)
    )
    return jnp.where(distance <= 1.0, inside_part, jnp.where(distance < 2.0, outside_part, 0.0))


def tile_of(left_where, right_where):
    left_float = left_where.astype(jnp.float32)
    right_float = right_where.astype(jnp.float32)
    east_gap = left_float[0][:, None] - right_float[0][None, :]
    north_gap = left_float[1][:, None] - right_float[1][None, :]
    return gaspari_cohn(jnp.sqrt(east_gap * east_gap + north_gap * north_gap)).astype(jnp.bfloat16)


def pair_terms(member_rows, places, pair_rows_all, live_total):
    slot_total, row_total, points = member_rows.shape
    start_totals = jnp.zeros((slot_total, row_total, points), jnp.float32)
    turn_count = (live_total + PAIR_GROUP - 1) // PAIR_GROUP
    tile_batch = jax.vmap(tile_of)

    def one_turn(turn_index, totals):
        pair_rows = lax.dynamic_slice_in_dim(pair_rows_all, turn_index * PAIR_GROUP, PAIR_GROUP, 0)
        first_slot = pair_rows[:, 0]
        second_slot = pair_rows[:, 1]
        live_flags = (
            turn_index * PAIR_GROUP + jnp.arange(PAIR_GROUP, dtype=jnp.int32) < live_total
        ).astype(jnp.float32)
        tiles = tile_batch(
            jnp.take(places, first_slot, axis=0), jnp.take(places, second_slot, axis=0)
        )
        rows_first = jnp.take(member_rows, first_slot, axis=0)
        rows_second = jnp.take(member_rows, second_slot, axis=0)
        to_first = jnp.einsum(
            "gjq,gpq->gjp", rows_second, tiles, preferred_element_type=jnp.float32
        )
        to_second = jnp.einsum(
            "gjp,gpq->gjq", rows_first, tiles, preferred_element_type=jnp.float32
        )
        for within in range(PAIR_GROUP):
            totals = totals.at[first_slot[within]].add(live_flags[within] * to_first[within])
            totals = totals.at[second_slot[within]].add(live_flags[within] * to_second[within])
        return totals

    return lax.fori_loop(0, turn_count, one_turn, start_totals)


def per_device(ensemble, increment, coords, sent_slots, pair_list, pair_count):
    blocks, members, levels, points = ensemble.shape
    regions = lax.axis_size("region")
    per_home = sent_slots.shape[2]
    slot_total = regions * per_home
    all_members = members * lax.axis_size("member")
    weighted = (ensemble.astype(jnp.float32) * increment[:, None].astype(jnp.float32)).astype(
        jnp.bfloat16
    )
    flat_blocks = weighted.reshape(blocks, members * levels, points)

    def diag_one(pair_entry):
        member_rows, places = pair_entry
        local_tile = tile_of(places, places)
        return lax.dot_general(
            member_rows, local_tile, (((1,), (1,)), ((), ())), preferred_element_type=jnp.float32
        )

    diagonal = lax.map(diag_one, (flat_blocks, coords))
    flat_slots = sent_slots[0].reshape(slot_total)
    places_out = jnp.take(coords, flat_slots, axis=0).reshape(regions, per_home, 2, points)
    live_total = pair_count[0]
    outgoing = jnp.take(weighted, flat_slots, axis=0).reshape(
        regions, per_home, members, levels, points
    )
    got_weighted, got_places = (
        lax.all_to_all(outgoing, "region", split_axis=0, concat_axis=0, tiled=True),
        lax.all_to_all(places_out, "region", split_axis=0, concat_axis=0, tiled=True),
    )
    member_rows = got_weighted.reshape(slot_total, members * levels, points)
    places = got_places.reshape(slot_total, 2, points)
    totals = pair_terms(member_rows, places, pair_list, live_total)
    returned = lax.all_to_all(
        totals.reshape(regions, per_home, members, levels, points),
        "region",
        split_axis=0,
        concat_axis=0,
        tiled=True,
    )
    gathered_back = (
        jnp.zeros((blocks, members, levels, points), jnp.float32)
        .at[flat_slots]
        .add(returned.reshape(slot_total, members, levels, points))
    )
    combined = diagonal.reshape(blocks, members, levels, points) + gathered_back
    member_part = jnp.sum(ensemble.astype(jnp.float32) * combined, axis=1)
    summed = lax.psum_scatter(member_part, "member", scatter_dimension=1, tiled=True)
    return summed / (all_members - 1)


def solution(mesh):
    in_specs = (
        P("region", "member", None, None),
        P("region", None, None),
        P("region", None, None),
        P("region", None, None),
        P("region", None),
        P("region"),
    )
    out_specs = P("region", "member", None)
    return jax.shard_map(
        per_device, mesh=mesh, in_specs=in_specs, out_specs=out_specs, check_vma=False
    )
```

profile of v0, /device:TPU:0, one launch (start us, length us, event | category | flops | bytes accessed | tf_op | source)
XLA Modules:
  0.0 825.1 jit_solution(8655067967581447967)
XLA Ops:
  10.0 8.0 all-to-all-start.1
  19.4 5.4 fusion.93
  24.9 5.0 gather_fusion.4
  29.9 4.6 fusion.95
  34.5 7.3 all-to-all-start
  42.4 60.8 %all-to-all-done = bf16[16,1,4,64,512]{4,3,2,1,0:T(8,128)(2,1)} async-done(((bf16[16,1,4,64,512]{4,3,2,1,0:T(8,128)(2,1)}), bf16[16,1,4,64,512]{4,3,2,1,0:T(8,128)(2,1)}, u32[]{:S(2)}, u32[]{:S(2)}) %all-to-all-start) | async-done | bytes 4194336 | tf_op jit(solution)/shard_map/all_to_all | solution.py:89
  103.2 4.3 broadcast.419.clone.1
  107.5 329.7 %while.33 = (s32[]{:T(128)}, f32[16,256,512]{2,1,0:T(8,128)}, s32[]{:T(128)}, s32[32,2]{0,1:T(2,128)S(1)}, s32[]{:T(128)}, /*index=5*/bf16[16,256,512]{2,1,0:T(8...) while((s32[]{:T(128)}, f32[16,256,512]{2,1,0:T(8,128)}, ...), condition=%wide.region_11.14_spmd, body=%wide.region_2.13_spmd.sunk | while | flops 1147160832 | bytes 40145848 | solution.py:60
  111.8 6.6 fusion.137
  134.6 6.7 fusion.140
  157.4 3.4 fusion.143
  177.9 6.6 fusion.137
  200.7 6.7 fusion.140
  243.7 6.6 fusion.137
  266.5 6.7 fusion.140
  309.6 6.6 fusion.137
  332.4 6.7 fusion.140
  375.5 6.6 fusion.137
  398.4 6.7 fusion.140
  437.3 199.7 %all-to-all-start.2 = ((f32[16,1,4,64,512]{4,3,2,1,0:T(8,128)}), f32[16,1,4,64,512]{4,3,2,1,0:T(8,128)}, u32[]{:S(2)}, u32[]{:S(2)}) async-start(f32[16,1,4,64,512]{4,3,2,1,0:T(8,128)} %bitcast.37), calls=%async_computation.2 | async-start | bytes 16777216 | tf_op jit(solution)/shard_map/all_to_all | solution.py:95
  637.2 4.3 broadcast.419.clone
  641.5 65.5 %while.32 = (s32[]{:T(128)}, f32[16,256,512]{2,1,0:T(8,128)}, bf16[16,256,512]{2,1,0:T(8,128)(2,1)}, bf16[16,2,512]{2,1,0:T(2,128)(2,1)}, s32[]{:T(128)}) while((s32[]{:T(128)}, f32[16,256,512]{2,1,0:T(8,128)}, bf16[16,256,512]{2,1,0:T(8,128)(2,1)}, bf16[16,2,512]{2,1,0:T(2,128)(2,1)}, s32[]{:T(128)}) %tuple.133), condition=%wide.region_1.2_spmd, body=%wide.region_0.1_spmd.sunk | while | flops 142869504 | bytes 810049 | solution.py:81
  650.4 3.4 fusion.128
  654.5 3.4 fusion.128
  662.6 3.4 fusion.128
  679.0 3.4 fusion.128
  687.2 3.4 fusion.128
  695.4 3.4 fusion.128
  707.0 51.0 %all-to-all-done.2 = f32[16,1,4,64,512]{4,3,2,1,0:T(8,128)} async-done(((f32[16,1,4,64,512]{4,3,2,1,0:T(8,128)}), f32[16,1,4,64,512]{4,3,2,1,0:T(8,128)}, u32[]{:S(2)}, u32[]{:S(2)}) %all-to-all-start.2) | async-done | bytes 8388640 | tf_op jit(solution)/shard_map/all_to_all | solution.py:95
  758.0 18.2 %scatter_fusion = f32[16,4,64,512]{3,2,1,0:T(8,128)} fusion(f32[16,4,64,512]{3,2,1,0:T(8,128)} %bitcast.125, s32[16]{0:T(128)S(1)} %copy-done.5, f32[16,4,64,512]{3,2,1,0:T(8,128)} %bitcast.38), kind=kCustom, calls=%fused_computation.6 | custom fusion | flops 2097152 | bytes 25165888 | tf_op jit(solution)/shard_map/scatter-add | solution.py:105
  776.2 7.6 fusion.94
  783.8 32.7 %reduce-scatter.2.cloned.1.call-done = f32[16,8,512]{2,1,0:T(8,128)} async-done(((f32[16,64,512]{2,1,0:T(8,128)}), f32[16,8,512]{2,1,0:T(8,128)}) %reduce-scatter.2.cloned.1.call-update) | async-done | bytes 262160 | tf_op jit(solution)/shard_map/reduce_scatter | solution.py:109
  (219 shorter events, 237.3 us)
Async XLA Ops:
  7.2 0.7 copy-start.4
  10.0 24.5 %all-to-all-start.1 = ((bf16[16,1,2,512]{3,2,1,0:T(2,128)(2,1)}), bf16[16,1,2,512]{3,2,1,0:T(2,128)(2,1)S(1)}, u32[]{:S(2)}, u32[]{:S(2)}) async-start(bf16[16,1,2,512]{3,2,1,0:T(2,128)(2,1)} %broadcast_select_fusion.2), calls=%async_computation.1 | async-start | bytes 65536 | tf_op jit(solution)/shard_map/all_to_all | solution.py:90
  34.5 68.8 %all-to-all-start = ((bf16[16,1,4,64,512]{4,3,2,1,0:T(8,128)(2,1)}), bf16[16,1,4,64,512]{4,3,2,1,0:T(8,128)(2,1)}, u32[]{:S(2)}, u32[]{:S(2)}) async-start(bf16[16,1,4,64,512]{4,3,2,1,0:T(8,128)(2,1)} %fusion.95), calls=%async_computation | async-start | bytes 8388608 | tf_op jit(solution)/shard_map/all_to_all | solution.py:89
  103.2 4.3 copy-start.2
  103.2 4.3 copy-start.3
  141.3 1.3 copy-start
  153.3 10.8 %copy-start.1 = (f32[4,256,512]{2,1,0:T(8,128)S(1)}, f32[4,256,512]{2,1,0:T(8,128)}, u32[]{:S(2)}) copy-start(f32[4,256,512]{2,1,0:T(8,128)} %copy-done) | copy-start | bytes 6291460 | tf_op jit(solution)/shard_map/while
  207.4 1.3 copy-start
  219.3 10.6 %copy-start.1 = (f32[4,256,512]{2,1,0:T(8,128)S(1)}, f32[4,256,512]{2,1,0:T(8,128)}, u32[]{:S(2)}) copy-start(f32[4,256,512]{2,1,0:T(8,128)} %copy-done) | copy-start | bytes 6291460 | tf_op jit(solution)/shard_map/while
  273.2 1.3 copy-start
  285.1 10.6 %copy-start.1 = (f32[4,256,512]{2,1,0:T(8,128)S(1)}, f32[4,256,512]{2,1,0:T(8,128)}, u32[]{:S(2)}) copy-start(f32[4,256,512]{2,1,0:T(8,128)} %copy-done) | copy-start | bytes 6291460 | tf_op jit(solution)/shard_map/while
  339.1 1.3 copy-start
  351.0 10.7 %copy-start.1 = (f32[4,256,512]{2,1,0:T(8,128)S(1)}, f32[4,256,512]{2,1,0:T(8,128)}, u32[]{:S(2)}) copy-start(f32[4,256,512]{2,1,0:T(8,128)} %copy-done) | copy-start | bytes 6291460 | tf_op jit(solution)/shard_map/while
  405.1 1.3 copy-start
  417.0 10.7 %copy-start.1 = (f32[4,256,512]{2,1,0:T(8,128)S(1)}, f32[4,256,512]{2,1,0:T(8,128)}, u32[]{:S(2)}) copy-start(f32[4,256,512]{2,1,0:T(8,128)} %copy-done) | copy-start | bytes 6291460 | tf_op jit(solution)/shard_map/while
  437.3 320.7 %all-to-all-start.2 = ((f32[16,1,4,64,512]{4,3,2,1,0:T(8,128)}), f32[16,1,4,64,512]{4,3,2,1,0:T(8,128)}, u32[]{:S(2)}, u32[]{:S(2)}) async-start(f32[16,1,4,64,512]{4,3,2,1,0:T(8,128)} %bitcast.37), calls=%async_computation.2 | async-start | bytes 16777216 | tf_op jit(solution)/shard_map/all_to_all | solution.py:95
  637.0 179.6 %reduce-scatter.2.cloned.1.call-start = ((), (), s32[]{:S(2)}) async-start(), calls=%async_computation.4 | async-start | bytes 2359296 | tf_op jit(solution)/shard_map/reduce_scatter | solution.py:109
  641.5 116.5 %copy-start.5 = (s32[16]{0:T(128)S(1)}, s32[16]{0:T(128)}, u32[]{:S(2)}) copy-start(s32[16]{0:T(128)} %copy-done.4) | copy-start | bytes 196
Sparse Core Ops, SparseCore 0:
  783.9 32.5 reduce-scatter.1
where the time goes:
time: 835 us; the launch traced here: 825 us
  starting transfers between devices  215 us (26%)
  other arithmetic  193 us (23%)
  waiting for transfers between devices  145 us (17%)
  matrix products  121 us (14%)
  loops' own time  74.3 us (9%)
  local copies, waits for them, and re-layouts  62.5 us (7%)
  between operations  14.1 us (2%)
    all_to_all x1, starting transfers between devices, per_device(): lax.all_to_all(totals.reshape(regions, per_home, members, levels, points)...  200 us
    another operation x1, loops' own time, pair_terms(): return lax.fori_loop(0, turn_count, one_turn, start_totals)  74.3 us
    scatter-add x20, other arithmetic, one_turn(): totals.at[second_slot[within]].add(live_flags[within] * to_second[within])  65.2 us
    scatter-add x20, other arithmetic, one_turn(): totals.at[first_slot[within]].add(live_flags[within] * to_first[within])  64.2 us
    all_to_all x1, waiting for transfers between devices, per_device(): lax.all_to_all(outgoing, 'region', split_axis=0, concat_axis=0, tiled=True)  60.8 us
    dot_general x16, matrix products, diag_one(): lax.dot_general(member_rows, local_tile, (((1,), (1,)), ((), ())), prefer...  54.4 us
    all_to_all x1, waiting for transfers between devices, per_device(): lax.all_to_all(totals.reshape(regions, per_home, members, levels, points)...  51 us
    dot_general x5, matrix products, one_turn(): jnp.einsum('gjp,gpq->gjq', rows_first, tiles, preferred_element_type=jnp....  33.4 us
  transfers between devices with their start and end apart: 4, of which 3 were waited for; matrix products, arithmetic and copies ran while one was open for 10% of the time, Pallas kernels for 0%

commit v1 on v0

v1 whole, which is shorter than its diff:
```python
import functools

import jax
import jax.numpy as jnp
from jax import lax
from jax.experimental import pallas as pl
from jax.experimental.pallas import tpu as pltpu
from jax.sharding import PartitionSpec as P

ROWS = 16
TILE_GROUP = 4
VMEM_CAP = 56 * 1024 * 1024


def pack_kernel(slots, own, ens_ref, inc_ref, coords_ref, big_ref, small_ref):
    members, levels, points = ens_ref.shape[1:]
    parts = big_ref.shape[1]
    step = levels // parts
    for part in range(parts):
        big_ref[0, part] = ens_ref[0, :, part * step : (part + 1) * step, :]
    small_ref[0, 0:step, :] = inc_ref[0]
    small_ref[0, step : step + 2, :] = coords_ref[0]
    small_ref[0, step + 2 :, :] = jnp.zeros_like(small_ref[0, step + 2 :, :])


def pack(ensemble, increment, coords, slots, own, parts):
    blocks, members, levels, points = ensemble.shape
    step = levels // parts
    total = slots.shape[0]
    return pl.pallas_call(
        pack_kernel,
        grid_spec=pltpu.PrefetchScalarGridSpec(
            num_scalar_prefetch=2,
            grid=(total,),
            in_specs=[
                pl.BlockSpec((1, members, levels, points), lambda o, s, j: (s[o], 0, 0, 0)),
                pl.BlockSpec((1, step, points), lambda o, s, j: (s[o], j[0], 0)),
                pl.BlockSpec((1, 2, points), lambda o, s, j: (s[o], 0, 0)),
            ],
            out_specs=[
                pl.BlockSpec((1, parts, members, step, points), lambda o, s, j: (o, 0, 0, 0, 0)),
                pl.BlockSpec((1, 2 * step, points), lambda o, s, j: (o, 0, 0)),
            ],
        ),
        out_shape=[
            jax.ShapeDtypeStruct((total, parts, members, step, points), ensemble.dtype),
            jax.ShapeDtypeStruct((total, 2 * step, points), increment.dtype),
        ],
        compiler_params=pltpu.CompilerParams(vmem_limit_bytes=16 * 1024 * 1024),
        name="pack",
    )(slots, own, ensemble, increment, coords)


def gaspari_cohn(east_gap, north_gap):
    squared = jnp.maximum(east_gap * east_gap + north_gap * north_gap, 2.0**-12)
    inverse = lax.rsqrt(squared)
    z = squared * inverse
    outer = jnp.maximum(2.0 - z, 0.0)
    inner = jnp.maximum(1.0 - z, 0.0)
    outer2 = outer * outer
    inner2 = inner * inner
    shifted = z + 2.0
    first = (outer2 * outer2) * (z * shifted - 0.5)
    second = (inner2 * inner2) * (inner * shifted)
    return (first + 4.0 * second) * (inverse * (1.0 / 12.0))


def write_tile(left, right, column_ref, tile_ref):
    points = left.shape[1]
    column_ref[:, 0:8] = jnp.transpose(jnp.concatenate([left, left, left, left], axis=0))
    right_east = right[0:1]
    right_north = right[1:2]

    def chunk(index, carry):
        rows = pl.ds(pl.multiple_of(index * ROWS, ROWS), ROWS)
        east = column_ref[rows, 0:1]
        north = column_ref[rows, 1:2]
        value = gaspari_cohn(east - right_east, north - right_north)
        tile_ref[rows, :] = value.astype(tile_ref.dtype)
        return carry

    lax.fori_loop(0, points // ROWS, chunk, 0, unroll=2)


def diag_kernel(ens_ref, inc_ref, coords_ref, out_ref, column_ref, tile_ref):
    members, levels, points = ens_ref.shape[1:]
    places = coords_ref[0].astype(jnp.float32)
    write_tile(places, places, column_ref, tile_ref)
    weighted = (ens_ref[0].astype(jnp.float32) * inc_ref[0].astype(jnp.float32)[None]).astype(jnp.bfloat16)
    field = jnp.dot(
        weighted.reshape(members * levels, points), tile_ref[...], preferred_element_type=jnp.float32
    ).reshape(members, levels, points)
    out_ref[0] = jnp.sum(ens_ref[0].astype(jnp.float32) * field, axis=0)


def diag(ensemble, increment, coords):
    blocks, members, levels, points = ensemble.shape
    return pl.pallas_call(
        diag_kernel,
        grid=(blocks,),
        in_specs=[
            pl.BlockSpec((1, members, levels, points), lambda b: (b, 0, 0, 0)),
            pl.BlockSpec((1, levels, points), lambda b: (b, 0, 0)),
            pl.BlockSpec((1, 2, points), lambda b: (b, 0, 0)),
        ],
        out_specs=pl.BlockSpec((1, levels, points), lambda b: (b, 0, 0)),
        out_shape=jax.ShapeDtypeStruct((blocks, levels, points), jnp.float32),
        scratch_shapes=[
            pltpu.VMEM((points, 128), jnp.float32),
            pltpu.VMEM((points, points), jnp.bfloat16),
        ],
        compiler_params=pltpu.CompilerParams(vmem_limit_bytes=16 * 1024 * 1024),
        cost_estimate=pl.CostEstimate(flops=24_000_000_000, bytes_accessed=8_000_000, transcendentals=0),
        name="diag",
    )(ensemble, increment, coords)


def tiles_kernel(pairs, count, small_ref, out_ref, column_ref):
    step = small_ref.shape[1] // 2
    group = out_ref.shape[0]
    base = pl.program_id(0) * group
    for within in range(group):

        @pl.when(base + within < count[0])
        def _():
            first = pairs[2 * (base + within)]
            second = pairs[2 * (base + within) + 1]
            left = small_ref[first, step : step + 2, :].astype(jnp.float32)
            right = small_ref[second, step : step + 2, :].astype(jnp.float32)
            write_tile(left, right, column_ref, out_ref.at[within])


def tiles(small, pairs, count):
    slot_total, rows, points = small.shape
    cap = pairs.shape[0] // 2
    return pl.pallas_call(
        tiles_kernel,
        grid_spec=pltpu.PrefetchScalarGridSpec(
            num_scalar_prefetch=2,
            grid=(cap // TILE_GROUP,),
            in_specs=[pl.BlockSpec((slot_total, rows, points), lambda i, p, c: (0, 0, 0))],
            out_specs=pl.BlockSpec((TILE_GROUP, points, points), lambda i, p, c: (i, 0, 0)),
            scratch_shapes=[pltpu.VMEM((points, 128), jnp.float32)],
        ),
        out_shape=jax.ShapeDtypeStruct((cap, points, points), jnp.bfloat16),
        compiler_params=pltpu.CompilerParams(vmem_limit_bytes=16 * 1024 * 1024),
        cost_estimate=pl.CostEstimate(flops=30_000_000_000, bytes_accessed=17_000_000, transcendentals=0),
        name="tiles",
    )(pairs, count, small)


def apply_kernel(pairs, count, ens_ref, small_ref, tiles_ref, out_ref, weighted_ref, field_ref):
    slot_total, rows, points = ens_ref.shape
    step = small_ref.shape[1] // 2
    members = rows // step
    group = tiles_ref.shape[0]
    turn = pl.program_id(0)

    @pl.when(turn == 0)
    def _():
        for slot in range(slot_total):
            gain = small_ref[slot, 0:step, :].astype(jnp.float32)
            block = ens_ref[slot].astype(jnp.float32).reshape(members, step, points)
            weighted_ref[slot] = (block * gain[None]).astype(jnp.bfloat16).reshape(rows, points)
            field_ref[slot] = jnp.zeros((rows, points), jnp.float32)

    def one(within, carry):
        first = pairs[2 * (turn * group + within)]
        second = pairs[2 * (turn * group + within) + 1]
        tile = tiles_ref[within]
        field_ref[first] += lax.dot_general(
            weighted_ref[second], tile, (((1,), (1,)), ((), ())), preferred_element_type=jnp.float32
        )
        field_ref[second] += jnp.dot(weighted_ref[first], tile, preferred_element_type=jnp.float32)
        return carry

    lax.fori_loop(0, jnp.clip(count[0] - turn * group, 0, group), one, 0)

    @pl.when(turn == pl.num_programs(0) - 1)
    def _():
        for slot in range(slot_total):
            product = ens_ref[slot].astype(jnp.float32) * field_ref[slot]
            out_ref[slot] = jnp.sum(product.reshape(members, step, points), axis=0)


def apply_pairs(ens, small, tile_stack, pairs, count):
    slot_total, rows, points = ens.shape
    cap = tile_stack.shape[0]
    step = small.shape[1] // 2
    return pl.pallas_call(
        apply_kernel,
        grid_spec=pltpu.PrefetchScalarGridSpec(
            num_scalar_prefetch=2,
            grid=(cap // TILE_GROUP,),
            in_specs=[
                pl.BlockSpec((slot_total, rows, points), lambda i, p, c: (0, 0, 0)),
                pl.BlockSpec((slot_total, 2 * step, points), lambda i, p, c: (0, 0, 0)),
                pl.BlockSpec((TILE_GROUP, points, points), lambda i, p, c: (i, 0, 0)),
            ],
            out_specs=pl.BlockSpec((slot_total, step, points), lambda i, p, c: (0, 0, 0)),
            scratch_shapes=[
                pltpu.VMEM((slot_total, rows, points), jnp.bfloat16),
                pltpu.VMEM((slot_total, rows, points), jnp.float32),
            ],
        ),
        out_shape=jax.ShapeDtypeStruct((slot_total, step, points), jnp.float32),
        compiler_params=pltpu.CompilerParams(vmem_limit_bytes=VMEM_CAP),
        cost_estimate=pl.CostEstimate(flops=9_000_000_000, bytes_accessed=22_000_000, transcendentals=0),
        name="apply",
    )(pairs, count, ens, small, tile_stack)


def finish_kernel(slots, own_ref, back_ref, out_ref, *, scale):
    out_ref[...] = own_ref[...] * scale
    for owner in range(back_ref.shape[0]):
        slot = slots[owner]
        out_ref[slot] = out_ref[slot] + back_ref[owner] * scale


def finish(own, back, slots, scale):
    return pl.pallas_call(
        functools.partial(finish_kernel, scale=scale),
        grid_spec=pltpu.PrefetchScalarGridSpec(
            num_scalar_prefetch=1,
            grid=(1,),
            in_specs=[
                pl.BlockSpec(own.shape, lambda i, s: (0, 0, 0)),
                pl.BlockSpec(back.shape, lambda i, s: (0, 0, 0)),
            ],
            out_specs=pl.BlockSpec(own.shape, lambda i, s: (0, 0, 0)),
        ),
        out_shape=jax.ShapeDtypeStruct(own.shape, jnp.float32),
        compiler_params=pltpu.CompilerParams(vmem_limit_bytes=16 * 1024 * 1024),
        name="finish",
    )(slots, own, back)


def per_device(ensemble, increment, coords, sent_slots, pair_list, pair_count):
    blocks, members, levels, points = ensemble.shape
    regions = lax.axis_size("region")
    groups = lax.axis_size("member")
    step = levels // groups
    slots = sent_slots.reshape(-1)
    pairs = pair_list.reshape(-1)
    own = lax.axis_index("member").reshape(1).astype(jnp.int32)
    big, small = pack(ensemble, increment, coords, slots, own, groups)
    got_small = lax.all_to_all(small, "region", 0, 0, tiled=True)
    got_big = lax.all_to_all(
        big.reshape(regions * groups, members * step, points), ("region", "member"), 0, 0, tiled=True
    ).reshape(regions, groups * members * step, points)
    diagonal = diag(ensemble, increment, coords)
    diagonal = lax.psum_scatter(diagonal, "member", scatter_dimension=1, tiled=True)
    tile_stack = tiles(got_small, pairs, pair_count)
    partial = apply_pairs(got_big, got_small, tile_stack, pairs, pair_count)
    back = lax.all_to_all(partial, "region", 0, 0, tiled=True)
    return finish(diagonal, back, slots, 1.0 / (members * groups - 1))


def solution(mesh):
    in_specs = (
        P("region", "member", None, None),
        P("region", None, None),
        P("region", None, None),
        P("region", None, None),
        P("region", None),
        P("region"),
    )
    out_specs = P("region", "member", None)
    return jax.shard_map(
        per_device, mesh=mesh, in_specs=in_specs, out_specs=out_specs, check_vma=False
    )
```

time: 835 us -> 209 us (0.25); the launches traced: 825 us -> 208 us
  other arithmetic: 193 us -> 0 us
  starting transfers between devices: 215 us -> 53.9 us
  waiting for transfers between devices: 145 us -> 9.01 us
  matrix products: 121 us -> 0 us
  Pallas kernels: 0 us -> 98.8 us
  loops' own time: 74.3 us -> 0 us
  local copies, waits for them, and re-layouts: 62.5 us -> 15.9 us
  blocking collectives: 0 us -> 16.4 us
    all_to_all x3 -> x2, starting transfers between devices: 215 us -> 53.8 us  [the longest x1 47 us: per_device(): back = lax.all_to_all(partial, 'region', 0, 0, tiled=True)]
    scatter-add x41 -> x0, other arithmetic: 148 us -> none  [the longest x20 65.2 us: one_turn(): totals.at[second_slot[within]].add(live_flags[within] * to_second[within])]
    dot_general x26 -> x0, matrix products: 121 us -> none  [the longest x16 54.4 us: diag_one(): lax.dot_general(member_rows, local_tile, (((1,), (1,)), ((), ())), prefer...]
    all_to_all x3 -> x2, waiting for transfers between devices: 112 us -> 8.98 us  [the longest x1 8.97 us: per_device(): back = lax.all_to_all(partial, 'region', 0, 0, tiled=True)]
    pallas_call x0 -> x5, Pallas kernels: none -> 98.8 us  [the longest x1 41.9 us: diag(): pl.pallas_call(diag_kernel, grid=(blocks,), in_specs=[pl.BlockSpec((1, me...]
    another operation x2 -> x0, loops' own time: 74.3 us -> none  [the longest x1 74.3 us: pair_terms(): return lax.fori_loop(0, turn_count, one_turn, start_totals)]
    gather x22 -> x0, local copies, waits for them, and re-layouts: 40.1 us -> none  [the longest x5 14 us: one_turn(): rows_second = jnp.take(member_rows, second_slot, axis=0)]
    reduce_scatter x1, waiting for transfers between devices: 32.7 us -> 0.02 us  [per_device(): lax.psum_scatter(diagonal, 'member', scatter_dimension=1, tiled=True)]
  transfers between devices with their start and end apart: 4 -> 3, of which waited for: 3 -> 1; matrix products, arithmetic and copies ran while one was open for 10% -> 0% of each run, Pallas kernels for 0% -> 46%
where the time goes in v1:
time: 209 us; the launch traced here: 208 us
  Pallas kernels  98.8 us (47%)
  starting transfers between devices  53.9 us (26%)
  blocking collectives  16.4 us (8%)
  local copies, waits for them, and re-layouts  15.9 us (8%)
  between operations  14.2 us (7%)
  waiting for transfers between devices  9.01 us (4%)
    all_to_all x1, starting transfers between devices, per_device(): back = lax.all_to_all(partial, 'region', 0, 0, tiled=True)  47 us
    pallas_call x1, Pallas kernels, diag(): pl.pallas_call(diag_kernel, grid=(blocks,), in_specs=[pl.BlockSpec((1, me...  41.9 us
    pallas_call x1, Pallas kernels, tiles(): pl.pallas_call(tiles_kernel, grid_spec=pltpu.PrefetchScalarGridSpec(num_s...  37 us
    pallas_call x1, Pallas kernels, apply_pairs(): pl.pallas_call(apply_kernel, grid_spec=pltpu.PrefetchScalarGridSpec(num_s...  17.4 us
    all_to_all x1, blocking collectives, per_device(): got_small = lax.all_to_all(small, 'region', 0, 0, tiled=True)  16.4 us
    unnamed x29, local copies, waits for them, and re-layouts  15.8 us
    all_to_all x1, waiting for transfers between devices, per_device(): back = lax.all_to_all(partial, 'region', 0, 0, tiled=True)  8.97 us
    all_to_all x1, starting transfers between devices, per_device(): lax.all_to_all(big.reshape(regions * groups, members * step, points), ('r...  6.81 us
  transfers between devices with their start and end apart: 3, of which 1 were waited for; matrix products, arithmetic and copies ran while one was open for 0% of the time, Pallas kernels for 46%

profile of v1, /device:TPU:0, one launch (start us, length us, event | category | flops | bytes accessed | tf_op | source)
XLA Modules:
  0.0 208.1 jit_solution(3731117638645867314)
XLA Ops:
  6.5 2.2 %copy-done = bf16[16,4,64,512]{3,2,1,0:T(8,128)(2,1)S(1)} copy-done((bf16[16,4,64,512]{3,2,1,0:T(8,128)(2,1)S(1)}, bf16[16,4,64,512]{3,2,1,0:T(8,128)(2,1)}, u32[]{:S(2)}) %copy-start) | copy-done | bytes 4194328
  8.7 1.2 copy-done.3
  10.0 0.8 copy-done.7
  10.7 0.7 copy-done.9
  11.4 1.1 pack.1
  12.5 0.0 copy-start.2
  12.5 2.0 copy-done.2
  14.4 16.4 %all_to_all.15.small_ref = bf16[16,16,512]{2,1,0:T(8,128)(2,1)S(1)} all-to-all(bf16[16,16,512]{2,1,0:T(8,128)(2,1)S(1)} %get-tuple-element.8), channel_id=1, replica_groups=mesh['region'=16,'member'=8] {'region'}, dimensions={0} | all-to-all | bytes 524288 | tf_op jit(solution)/shard_map/all_to_all | solution.py:247
  30.9 6.8 %all-to-all-start = ((bf16[128,32,512]{2,1,0:T(8,128)(2,1)}), bf16[128,32,512]{2,1,0:T(8,128)(2,1)}, u32[]{:S(2)}, u32[]{:S(2)}) async-start(bf16[128,32,512]{2,1,0:T(8,128)(2,1)} %bitcast.4), calls=%async_computation.1 | async-start | bytes 8388608 | tf_op jit(solution)/shard_map/all_to_all | solution.py:248
  37.7 0.0 reduce-scatter.2.cloned.1.call-start
  37.8 0.0 copy-done.4
  37.8 0.0 copy-done.8
  37.8 0.0 copy-start.1
  37.8 2.2 %copy-done.1 = bf16[16,4,64,512]{3,2,1,0:T(8,128)(2,1)S(1)} copy-done((bf16[16,4,64,512]{3,2,1,0:T(8,128)(2,1)S(1)}, bf16[16,4,64,512]{3,2,1,0:T(8,128)(2,1)}, u32[]{:S(2)}) %copy-start.1) | copy-done | bytes 4194328
  40.0 41.9 %diag.1 = f32[16,64,512]{2,1,0:T(8,128)} custom-call(bf16[16,4,64,512]{3,2,1,0:T(8,128)(2,1)S(1)} %copy-done.1, bf16[16,64,512]{2,1,0:T(8,128)(2,1)S(1)} %copy-done.4, bf16[16,2,512]{2,1,0:T(2,128)(2,1)S(1)} %copy-done.8), custom_call_target="tpu_custom_call" | custom-call | flops 24000000000 | bytes 8000000 | tf_op jit(solution)/shard_map/diag/pallas_call | solution.py:98
  81.9 0.0 reduce-scatter.2.cloned.1.call-update
  82.6 0.0 copy-done.13
  82.6 0.1 copy.8
  82.7 0.1 reshape.16.pairs
  82.8 0.0 copy-done.5
  82.8 0.0 copy-start.11
  82.8 37.0 %tiles.1.tiles_ref = bf16[32,512,512]{2,1,0:T(8,128)(2,1)S(1)} custom-call(s32[64]{0:T(128)S(1)} %reshape.16.pairs, s32[1]{0:T(128)S(6)} %copy.9.count, bf16[16,16,512]{2,1,0:T(8,128)(2,1)S(1)} %all_to_all.15.small_ref), custom_call_target="tpu_custom_call" | custom-call | flops 30000001024 | bytes 17000000 | tf_op jit(solution)/shard_map/tiles/pallas_call | solution.py:136
  119.8 0.0 copy-done.11
  119.8 0.0 copy-start.12
  119.9 5.7 %copy-done.12 = bf16[32,512,512]{2,1,0:T(8,128)(2,1)} copy-done((bf16[32,512,512]{2,1,0:T(8,128)(2,1)}, bf16[32,512,512]{2,1,0:T(8,128)(2,1)S(1)}, u32[]{:S(2)}) %copy-start.12) | copy-done | bytes 16777240
  125.6 0.0 all-to-all-done
  125.6 17.4 %apply.1 = f32[16,8,512]{2,1,0:T(8,128)} custom-call(s32[64]{0:T(128)} %copy-done.11, s32[1]{0:T(128)S(6)} %copy.9.count, bf16[16,256,512]{2,1,0:T(8,128)(2,1)} %bitcast.3.ens_ref, bf16[16,16,512]{2,1,0:T(8,128)(2,1)} %copy-done.5, bf16[32,512,512]{2,1,0:T(8,128)(2,1)} %copy-done.12), custom_call_target="tpu_custom_call" | custom-call | flops 8999999488 | bytes 22000000 | tf_op jit(solution)/shard_map/apply/pallas_call | solution.py:190
  143.0 47.0 %all-to-all-start.2 = ((f32[16,8,512]{2,1,0:T(8,128)}), f32[16,8,512]{2,1,0:T(8,128)S(1)}, u32[]{:S(2)}, u32[]{:S(2)}) async-start(f32[16,8,512]{2,1,0:T(8,128)} %apply.1), calls=%async_computation.3 | async-start | bytes 524288 | tf_op jit(solution)/shard_map/all_to_all | solution.py:255
  190.0 0.0 reduce-scatter.2.cloned.1.call-done.own_ref
  190.0 9.0 %all-to-all-done.2.back_ref = f32[16,8,512]{2,1,0:T(8,128)S(1)} async-done(((f32[16,8,512]{2,1,0:T(8,128)}), f32[16,8,512]{2,1,0:T(8,128)S(1)}, u32[]{:S(2)}, u32[]{:S(2)}) %all-to-all-start.2) | async-done | bytes 262176 | tf_op jit(solution)/shard_map/all_to_all | solution.py:255
  199.0 0.9 copy-done.6
  200.0 1.3 finish.1
  (11 shorter events, 0.0 us)
Async XLA Ops:
  6.5 2.2 %copy-start = (bf16[16,4,64,512]{3,2,1,0:T(8,128)(2,1)S(1)}, bf16[16,4,64,512]{3,2,1,0:T(8,128)(2,1)}, u32[]{:S(2)}) copy-start(bf16[16,4,64,512]{3,2,1,0:T(8,128)(2,1)} %ens_ref.3) | copy-start | bytes 12582916
  8.7 1.2 copy-start.3
  9.9 0.8 copy-start.7
  10.7 0.7 copy-start.9
  12.5 2.0 copy-start.2
  30.9 51.9 %copy-start.5 = (bf16[16,16,512]{2,1,0:T(8,128)(2,1)}, bf16[16,16,512]{2,1,0:T(8,128)(2,1)S(1)}, u32[]{:S(2)}) copy-start(bf16[16,16,512]{2,1,0:T(8,128)(2,1)S(1)} %all_to_all.15.small_ref) | copy-start | bytes 786436
  30.9 6.9 %copy-start.4 = (bf16[16,64,512]{2,1,0:T(8,128)(2,1)S(1)}, bf16[16,64,512]{2,1,0:T(8,128)(2,1)}, u32[]{:S(2)}) copy-start(bf16[16,64,512]{2,1,0:T(8,128)(2,1)} %inc_ref.3) | copy-start | bytes 3145732
  30.9 6.9 %copy-start.8 = (bf16[16,2,512]{2,1,0:T(2,128)(2,1)S(1)}, bf16[16,2,512]{2,1,0:T(2,128)(2,1)}, u32[]{:S(2)}) copy-start(bf16[16,2,512]{2,1,0:T(2,128)(2,1)} %coords_ref.3) | copy-start | bytes 98308
  30.9 94.7 %all-to-all-start = ((bf16[128,32,512]{2,1,0:T(8,128)(2,1)}), bf16[128,32,512]{2,1,0:T(8,128)(2,1)}, u32[]{:S(2)}, u32[]{:S(2)}) async-start(bf16[128,32,512]{2,1,0:T(8,128)(2,1)} %bitcast.4), calls=%async_computation.1 | async-start | bytes 8388608 | tf_op jit(solution)/shard_map/all_to_all | solution.py:248
  37.7 152.3 %reduce-scatter.2.cloned.1.call-start = ((), (), s32[]{:S(2)}) async-start(), calls=%async_computation.4 | async-start | bytes 2359296 | tf_op jit(solution)/shard_map/reduce_scatter | solution.py:252
  37.8 2.2 %copy-start.1 = (bf16[16,4,64,512]{3,2,1,0:T(8,128)(2,1)S(1)}, bf16[16,4,64,512]{3,2,1,0:T(8,128)(2,1)}, u32[]{:S(2)}) copy-start(bf16[16,4,64,512]{3,2,1,0:T(8,128)(2,1)} %ens_ref.3) | copy-start | bytes 12582916
  40.0 42.6 %copy-start.13 = (s32[32,2]{0,1:T(2,128)S(1)}, s32[32,2]{0,1:T(2,128)}, u32[]{:S(2)}) copy-start(s32[32,2]{0,1:T(2,128)} %param.10) | copy-start | bytes 772
  82.8 37.1 %copy-start.11 = (s32[64]{0:T(128)}, s32[64]{0:T(128)S(1)}, u32[]{:S(2)}) copy-start(s32[64]{0:T(128)S(1)} %reshape.16.pairs) | copy-start | bytes 772
  119.8 5.7 %copy-start.12 = (bf16[32,512,512]{2,1,0:T(8,128)(2,1)}, bf16[32,512,512]{2,1,0:T(8,128)(2,1)S(1)}, u32[]{:S(2)}) copy-start(bf16[32,512,512]{2,1,0:T(8,128)(2,1)S(1)} %tiles.1.tiles_ref) | copy-start | bytes 50331652
  125.6 73.4 %copy-start.10 = (s32[1,16,1]{1,2,0:T(1,128)S(1)}, s32[1,16,1]{1,2,0:T(1,128)}, u32[]{:S(2)}) copy-start(s32[1,16,1]{1,2,0:T(1,128)} %param.9) | copy-start | bytes 196
  143.0 56.0 %all-to-all-start.2 = ((f32[16,8,512]{2,1,0:T(8,128)}), f32[16,8,512]{2,1,0:T(8,128)S(1)}, u32[]{:S(2)}, u32[]{:S(2)}) async-start(f32[16,8,512]{2,1,0:T(8,128)} %apply.1), calls=%async_computation.3 | async-start | bytes 524288 | tf_op jit(solution)/shard_map/all_to_all | solution.py:255
  199.0 1.0 copy-start.6
Sparse Core Ops, SparseCore 0:
  82.0 35.1 reduce-scatter.1

commit v2 on v1

v2 whole, which is shorter than its diff:
```python
import functools

import jax
import jax.numpy as jnp
from jax import lax
from jax.experimental import pallas as pl
from jax.experimental.pallas import tpu as pltpu
from jax.sharding import PartitionSpec as P

LANES = 128
TILE_GROUP = 4
DEPTH = 4
MIB = 1024 * 1024
UNIT = 12.0**-0.2
UNIT2 = UNIT * UNIT
LEAST = UNIT2 * 2.0**-12


def select_kernel(slots, coords_ref, places_ref, sem):
    total = places_ref.shape[0]

    def copy(owner):
        return pltpu.make_async_copy(coords_ref.at[slots[owner]], places_ref.at[owner], sem.at[owner])

    for owner in range(total):
        copy(owner).start()
    for owner in range(total):
        copy(owner).wait()


def select(coords, slots):
    total = slots.shape[0]
    return pl.pallas_call(
        select_kernel,
        in_specs=[pl.BlockSpec(memory_space=pltpu.SMEM), pl.BlockSpec(memory_space=pl.ANY)],
        out_specs=pl.BlockSpec(memory_space=pl.ANY),
        out_shape=jax.ShapeDtypeStruct((total, *coords.shape[1:]), coords.dtype),
        scratch_shapes=[pltpu.SemaphoreType.DMA((total,))],
        compiler_params=pltpu.CompilerParams(vmem_limit_bytes=60 * MIB),
        name="select",
    )(slots, coords)


def pack_kernel(slots, own, ens_ref, inc_ref, big_ref, ens_buf, inc_buf, out_buf, in_sem, inc_sem, out_sem):
    total, members, levels, points = ens_buf.shape
    parts = out_buf.shape[1]
    step = levels // parts
    lane_chunks = points // LANES

    def ens_copy(owner):
        return pltpu.make_async_copy(ens_ref.at[slots[owner]], ens_buf.at[owner], in_sem.at[owner])

    def inc_copy(owner):
        return pltpu.make_async_copy(inc_ref.at[slots[owner]], inc_buf.at[owner], inc_sem.at[owner])

    def out_copy(owner):
        return pltpu.make_async_copy(out_buf.at[owner], big_ref.at[owner], out_sem.at[owner])

    for owner in range(total):
        ens_copy(owner).start()
        inc_copy(owner).start()
    chunk = pl.multiple_of(lax.rem(own[0], lane_chunks) * LANES, LANES)
    for owner in range(total):
        ens_copy(owner).wait()
        inc_copy(owner).wait()
        for part in range(parts):
            here = slice(part * step, (part + 1) * step)
            for lane in range(lane_chunks):
                out_buf[owner, part, lane * members * step : (lane + 1) * members * step, :] = ens_buf[
                    owner, :, here, lane * LANES : (lane + 1) * LANES
                ].reshape(members * step, LANES)
            out_buf[owner, part, members * step * lane_chunks :, :] = inc_buf[owner, here, pl.ds(chunk, LANES)]
        out_copy(owner).start()
    for owner in range(total):
        out_copy(owner).wait()


def pack(ensemble, increment, slots, own, parts):
    blocks, members, levels, points = ensemble.shape
    total = slots.shape[0]
    step = levels // parts
    rows = members * step * (points // LANES) + step
    return pl.pallas_call(
        pack_kernel,
        in_specs=[
            pl.BlockSpec(memory_space=pltpu.SMEM),
            pl.BlockSpec(memory_space=pltpu.SMEM),
            pl.BlockSpec(memory_space=pl.ANY),
            pl.BlockSpec(memory_space=pl.ANY),
        ],
        out_specs=pl.BlockSpec(memory_space=pl.ANY),
        out_shape=jax.ShapeDtypeStruct((total, parts, rows, LANES), ensemble.dtype),
        scratch_shapes=[
            pltpu.VMEM((total, members, levels, points), ensemble.dtype),
            pltpu.VMEM((total, levels, points), increment.dtype),
            pltpu.VMEM((total, parts, rows, LANES), ensemble.dtype),
            pltpu.SemaphoreType.DMA((total,)),
            pltpu.SemaphoreType.DMA((total,)),
            pltpu.SemaphoreType.DMA((total,)),
        ],
        compiler_params=pltpu.CompilerParams(vmem_limit_bytes=60 * MIB),
        name="pack",
    )(slots, own, ensemble, increment)


def three_parts(value):
    first = value.astype(jnp.bfloat16).astype(jnp.float32)
    rest = value - first
    second = rest.astype(jnp.bfloat16).astype(jnp.float32)
    return [first, second, rest - second]


def left_rows(places):
    east, north = places[0:1], places[1:2]
    one = jnp.ones_like(east)
    norm = UNIT2 * (east * east + north * north)
    rows = three_parts((-2.0 * UNIT2) * east) + three_parts((-2.0 * UNIT2) * north) + three_parts(norm)
    rows = rows + [one] * 3 + [jnp.zeros_like(east)] * 4
    return jnp.concatenate(rows, axis=0).astype(jnp.bfloat16)


def right_rows(places):
    east, north = places[0:1], places[1:2]
    one = jnp.ones_like(east)
    norm = UNIT2 * (east * east + north * north)
    rows = [east] * 3 + [north] * 3 + [one] * 3 + three_parts(norm) + [jnp.zeros_like(east)] * 4
    return jnp.concatenate(rows, axis=0).astype(jnp.bfloat16)


def tile_of(left, right):
    squared = lax.dot_general(left, right, (((0,), (0,)), ((), ())), preferred_element_type=jnp.float32)
    squared = jnp.maximum(squared, LEAST)
    inverse = lax.rsqrt(squared)
    z = squared * inverse
    outer = jnp.maximum(2.0 * UNIT - z, 0.0)
    inner = jnp.maximum(UNIT - z, 0.0)
    outer2 = outer * outer
    inner2 = inner * inner
    shifted = z + 2.0 * UNIT
    first = (outer2 * outer2) * (z * shifted - 0.5 * UNIT2)
    second = (inner2 * inner2) * (inner * shifted)
    return ((first + 4.0 * second) * inverse).astype(jnp.bfloat16)


def diag_kernel(ens_ref, inc_ref, coords_ref, out_ref):
    members, levels, points = ens_ref.shape[1:]
    rows = members * levels
    half = points // 2
    places = coords_ref[0].astype(jnp.float32)
    left, right = left_rows(places), right_rows(places)
    upper = tile_of(left[:, :half], right)
    lower = tile_of(left[:, half:], right[:, half:])
    weighted = (ens_ref[0] * inc_ref[0][None]).reshape(rows, points)
    near, far = weighted[:, :half], weighted[:, half:]
    field_near = jnp.dot(near, upper[:, :half], preferred_element_type=jnp.float32) + lax.dot_general(
        far, upper[:, half:], (((1,), (1,)), ((), ())), preferred_element_type=jnp.float32
    )
    field_far = jnp.dot(near, upper[:, half:], preferred_element_type=jnp.float32) + jnp.dot(
        far, lower, preferred_element_type=jnp.float32
    )
    block = ens_ref[0].astype(jnp.float32)
    out_ref[0, :, :half] = jnp.sum(block[:, :, :half] * field_near.reshape(members, levels, half), axis=0)
    out_ref[0, :, half:] = jnp.sum(block[:, :, half:] * field_far.reshape(members, levels, half), axis=0)


def diag(ensemble, increment, coords):
    blocks, members, levels, points = ensemble.shape
    return pl.pallas_call(
        diag_kernel,
        grid=(blocks,),
        in_specs=[
            pl.BlockSpec((1, members, levels, points), lambda b: (b, 0, 0, 0)),
            pl.BlockSpec((1, levels, points), lambda b: (b, 0, 0)),
            pl.BlockSpec((1, 2, points), lambda b: (b, 0, 0)),
        ],
        out_specs=pl.BlockSpec((1, levels, points), lambda b: (b, 0, 0)),
        out_shape=jax.ShapeDtypeStruct((blocks, levels, points), jnp.float32),
        compiler_params=pltpu.CompilerParams(vmem_limit_bytes=16 * MIB),
        cost_estimate=pl.CostEstimate(flops=20_000_000_000, bytes_accessed=8_000_000, transcendentals=0),
        name="diag",
    )(ensemble, increment, coords)


def tiles_kernel(pairs, count, places_ref, out_ref):
    group = out_ref.shape[0]
    base = pl.program_id(0) * group

    def one(within, carry):
        pair = 2 * (base + within)
        left = left_rows(places_ref[pairs[pair]].astype(jnp.float32))
        right = right_rows(places_ref[pairs[pair + 1]].astype(jnp.float32))
        out_ref[within] = tile_of(left, right)
        return carry

    lax.fori_loop(0, jnp.clip(count[0] - base, 0, group), one, 0)


def tiles(places, pairs, count):
    slot_total, _, points = places.shape
    cap = pairs.shape[0] // 2
    return pl.pallas_call(
        tiles_kernel,
        grid_spec=pltpu.PrefetchScalarGridSpec(
            num_scalar_prefetch=2,
            grid=(cap // TILE_GROUP,),
            in_specs=[pl.BlockSpec((slot_total, 2, points), lambda i, p, c: (0, 0, 0))],
            out_specs=pl.BlockSpec((TILE_GROUP, points, points), lambda i, p, c: (i, 0, 0)),
        ),
        out_shape=jax.ShapeDtypeStruct((cap, points, points), jnp.bfloat16),
        compiler_params=pltpu.CompilerParams(vmem_limit_bytes=60 * MIB),
        cost_estimate=pl.CostEstimate(flops=30_000_000_000, bytes_accessed=17_000_000, transcendentals=0),
        name="tiles",
    )(pairs, count, places)


def apply_kernel(
    pairs, count, got_ref, tiles_ref, out_ref, ens_ref, inc_ref, weighted_ref, field_ref, ring_ref, ens_sem, inc_sem, ring_sem
):
    slot_total, sources, rows, points = ens_ref.shape
    step = inc_ref.shape[2]
    lane_chunks = points // LANES
    every = sources * rows

    def ens_copies(slot):
        return [
            pltpu.make_async_copy(
                got_ref.at[slot, :, lane * rows : (lane + 1) * rows, :],
                ens_ref.at[slot, :, :, lane * LANES : (lane + 1) * LANES],
                ens_sem.at[slot, lane],
            )
            for lane in range(lane_chunks)
        ]

    inc_copy = pltpu.make_async_copy(got_ref.at[:, :lane_chunks, rows * lane_chunks :, :], inc_ref, inc_sem)
    inc_copy.start()
    for slot in range(slot_total):
        for copy in ens_copies(slot):
            copy.start()
    def ring_copy(index):
        place = lax.rem(index, DEPTH)
        return pltpu.make_async_copy(tiles_ref.at[index], ring_ref.at[place], ring_sem.at[place])

    for index in range(DEPTH):

        @pl.when(index < count[0])
        def _():
            ring_copy(index).start()

    inc_copy.wait()
    for slot in range(slot_total):
        field_ref[slot] = jnp.zeros((every, points), jnp.float32)
        for copy in ens_copies(slot):
            copy.wait()
        for lane in range(lane_chunks):
            here = slice(lane * LANES, (lane + 1) * LANES)
            gain = inc_ref[slot, lane]
            block = ens_ref[slot, :, :, here].reshape(every // step, step, LANES)
            weighted_ref[slot, :, here] = (block * gain[None]).reshape(every, LANES)

    def one(index, carry):
        first = pairs[2 * index]
        second = pairs[2 * index + 1]
        ring_copy(index).wait()
        tile = ring_ref[lax.rem(index, DEPTH)]
        field_ref[first] += lax.dot_general(
            weighted_ref[second], tile, (((1,), (1,)), ((), ())), preferred_element_type=jnp.float32
        )
        field_ref[second] += jnp.dot(weighted_ref[first], tile, preferred_element_type=jnp.float32)

        @pl.when(index + DEPTH < count[0])
        def _():
            ring_copy(index + DEPTH).start()

        return carry

    lax.fori_loop(0, count[0], one, 0)

    for slot in range(slot_total):
        product = ens_ref[slot].reshape(every, points).astype(jnp.float32) * field_ref[slot]
        out_ref[slot] = jnp.sum(product.reshape(every // step, step, points), axis=0)


def apply_pairs(got, tile_stack, pairs, count, members, step):
    slot_total, sources, rows, _ = got.shape
    cap, points, _ = tile_stack.shape
    lane_chunks = points // LANES
    every = sources * members * step
    return pl.pallas_call(
        apply_kernel,
        in_specs=[
            pl.BlockSpec(memory_space=pltpu.SMEM),
            pl.BlockSpec(memory_space=pltpu.SMEM),
            pl.BlockSpec(memory_space=pl.ANY),
            pl.BlockSpec(memory_space=pl.ANY),
        ],
        out_specs=pl.BlockSpec(memory_space=pltpu.VMEM),
        scratch_shapes=[
            pltpu.VMEM((slot_total, sources, members * step, points), jnp.bfloat16),
            pltpu.VMEM((slot_total, lane_chunks, step, LANES), jnp.bfloat16),
            pltpu.VMEM((slot_total, every, points), jnp.bfloat16),
            pltpu.VMEM((slot_total, every, points), jnp.float32),
            pltpu.VMEM((DEPTH, points, points), jnp.bfloat16),
            pltpu.SemaphoreType.DMA((slot_total, lane_chunks)),
            pltpu.SemaphoreType.DMA,
            pltpu.SemaphoreType.DMA((DEPTH,)),
        ],
        out_shape=jax.ShapeDtypeStruct((slot_total, step, points), jnp.float32),
        compiler_params=pltpu.CompilerParams(vmem_limit_bytes=60 * MIB),
        cost_estimate=pl.CostEstimate(flops=9_000_000_000, bytes_accessed=22_000_000, transcendentals=0),
        name="apply",
    )(pairs, count, got, tile_stack)


def finish_kernel(slots, own_ref, back_ref, out_ref, *, scale):
    out_ref[...] = own_ref[...] * scale
    for owner in range(back_ref.shape[0]):
        slot = slots[owner]
        out_ref[slot] = out_ref[slot] + back_ref[owner] * scale


def finish(own, back, slots, scale):
    return pl.pallas_call(
        functools.partial(finish_kernel, scale=scale),
        in_specs=[
            pl.BlockSpec(memory_space=pltpu.SMEM),
            pl.BlockSpec(memory_space=pltpu.VMEM),
            pl.BlockSpec(memory_space=pltpu.VMEM),
        ],
        out_specs=pl.BlockSpec(memory_space=pltpu.VMEM),
        out_shape=jax.ShapeDtypeStruct(own.shape, jnp.float32),
        compiler_params=pltpu.CompilerParams(vmem_limit_bytes=16 * MIB),
        name="finish",
    )(slots, own, back)


def per_device(ensemble, increment, coords, sent_slots, pair_list, pair_count):
    blocks, members, levels, points = ensemble.shape
    regions = lax.axis_size("region")
    groups = lax.axis_size("member")
    step = levels // groups
    slots = sent_slots.reshape(-1)
    pairs = pair_list.reshape(-1)
    own = lax.axis_index("member").reshape(1).astype(jnp.int32)
    places = select(coords, slots)
    own_places = lax.all_to_all(places, "region", 0, 0, tiled=True)
    big = pack(ensemble, increment, slots, own, groups)
    got = lax.all_to_all(
        big.reshape(regions * groups, -1, LANES), ("region", "member"), 0, 0, tiled=True
    ).reshape(regions, groups, -1, LANES)
    diagonal = diag(ensemble, increment, coords)
    diagonal = lax.psum_scatter(diagonal, "member", scatter_dimension=1, tiled=True)
    tile_stack = tiles(own_places, pairs, pair_count)
    partial = apply_pairs(got, tile_stack, pairs, pair_count, members, step)
    back = lax.all_to_all(partial, "region", 0, 0, tiled=True)
    return finish(diagonal, back, slots, 1.0 / (members * groups - 1))


def solution(mesh):
    in_specs = (
        P("region", "member", None, None),
        P("region", None, None),
        P("region", None, None),
        P("region", None, None),
        P("region", None),
        P("region"),
    )
    out_specs = P("region", "member", None)
    return jax.shard_map(
        per_device, mesh=mesh, in_specs=in_specs, out_specs=out_specs, check_vma=False
    )
```

time: 209 us -> 134 us (0.64)
  starting transfers between devices: 53.9 us -> 25.2 us
  Pallas kernels: 98.8 us -> 75 us
  blocking collectives: 16.4 us -> 0 us
  local copies, waits for them, and re-layouts: 15.9 us -> 4.49 us
  waiting for transfers between devices: 9.01 us -> 15.8 us
    all_to_all x1, starting transfers between devices: 47 us -> 8.46 us  [per_device(): back = lax.all_to_all(partial, 'region', 0, 0, tiled=True)]
    pallas_call x1, Pallas kernels: 41.9 us -> 17.2 us  [diag(): pl.pallas_call(diag_kernel, grid=(blocks,), in_specs=[pl.BlockSpec((1, me...]
    all_to_all x1 -> x0, blocking collectives: 16.4 us -> none  [per_device(): got_small = lax.all_to_all(small, 'region', 0, 0, tiled=True)]
    unnamed x29 -> x15, local copies, waits for them, and re-layouts: 15.8 us -> 3.85 us
    all_to_all x1 -> x2, starting transfers between devices: 6.81 us -> 16.7 us  [the longest x1 8.73 us: per_device(): lax.all_to_all(big.reshape(regions * groups, -1, LANES), ('region', 'memb...]
    pallas_call x3 -> x4, Pallas kernels: 19.8 us -> 28 us  [the longest x1 18.2 us: apply_pairs(): pl.pallas_call(apply_kernel, in_specs=[pl.BlockSpec(memory_space=pltpu.SM...]
    pallas_call x1, Pallas kernels: 37 us -> 29.8 us  [tiles(): pl.pallas_call(tiles_kernel, grid_spec=pltpu.PrefetchScalarGridSpec(num_s...]
    all_to_all x1 -> x2, waiting for transfers between devices: 0.01 us -> 6.78 us  [the longest x1 4.77 us: per_device(): lax.all_to_all(big.reshape(regions * groups, -1, LANES), ('region', 'memb...]
  transfers between devices with their start and end apart: 3 -> 4, of which waited for: 1 -> 3; matrix products, arithmetic and copies ran while one was open for 0% -> 1% of each run, Pallas kernels for 46% -> 53%
where the time goes in v2:
time: 134 us; the launch traced here: 135 us
  Pallas kernels  75 us (56%)
  starting transfers between devices  25.2 us (19%)
  waiting for transfers between devices  15.8 us (12%)
  between operations  14.1 us (11%)
  local copies, waits for them, and re-layouts  4.49 us (3%)
    pallas_call x1, Pallas kernels, tiles(): pl.pallas_call(tiles_kernel, grid_spec=pltpu.PrefetchScalarGridSpec(num_s...  29.8 us
    pallas_call x1, Pallas kernels, apply_pairs(): pl.pallas_call(apply_kernel, in_specs=[pl.BlockSpec(memory_space=pltpu.SM...  18.2 us
    pallas_call x1, Pallas kernels, diag(): pl.pallas_call(diag_kernel, grid=(blocks,), in_specs=[pl.BlockSpec((1, me...  17.2 us
    all_to_all x1, waiting for transfers between devices, per_device(): back = lax.all_to_all(partial, 'region', 0, 0, tiled=True)  8.96 us
    all_to_all x1, starting transfers between devices, per_device(): lax.all_to_all(big.reshape(regions * groups, -1, LANES), ('region', 'memb...  8.73 us
    all_to_all x1, starting transfers between devices, per_device(): back = lax.all_to_all(partial, 'region', 0, 0, tiled=True)  8.46 us
    all_to_all x1, starting transfers between devices, per_device(): own_places = lax.all_to_all(places, 'region', 0, 0, tiled=True)  7.97 us
    pallas_call x1, Pallas kernels, pack(): pl.pallas_call(pack_kernel, in_specs=[pl.BlockSpec(memory_space=pltpu.SME...  5.58 us
  transfers between devices with their start and end apart: 4, of which 3 were waited for; matrix products, arithmetic and copies ran while one was open for 1% of the time, Pallas kernels for 53%

profile of v2, /device:TPU:0, one launch (start us, length us, event | category | flops | bytes accessed | tf_op | source)
XLA Modules:
  0.0 134.6 jit_solution(17551918308733034309)
XLA Ops:
  6.5 2.9 %select.1 = bf16[16,2,512]{2,1,0:T(2,128)(2,1)} custom-call(s32[16]{0:T(128)} %bitcast.4, bf16[16,2,512]{2,1,0:T(2,128)(2,1)} %coords_ref.3), custom_call_target="tpu_custom_call" | custom-call | tf_op jit(solution)/shard_map/select/pallas_call | solution.py:33
  9.4 8.0 %all-to-all-start.1 = ((bf16[16,2,512]{2,1,0:T(2,128)(2,1)}), bf16[16,2,512]{2,1,0:T(2,128)(2,1)S(1)}, u32[]{:S(2)}, u32[]{:S(2)}) async-start(bf16[16,2,512]{2,1,0:T(2,128)(2,1)} %select.1), calls=%async_computation.2 | async-start | bytes 65536 | tf_op jit(solution)/shard_map/all_to_all | solution.py:345
  17.4 5.6 %pack.1 = bf16[16,8,136,128]{3,2,1,0:T(8,128)(2,1)} custom-call(s32[16]{0:T(128)} %bitcast.5, s32[1]{0:T(128)} %bitcast.1.own, bf16[16,4,64,512]{3,2,1,0:T(8,128)(2,1)} %ens_ref.3, bf16[16,64,512]{2,1,0:T(8,128)(2,1)} %inc_ref.3), custom_call_target="tpu_custom_call" | custom-call | tf_op jit(solution)/shard_map/pack/pallas_call | solution.py:83
  23.0 2.0 %all-to-all-done.1.places_ref = bf16[16,2,512]{2,1,0:T(2,128)(2,1)S(1)} async-done(((bf16[16,2,512]{2,1,0:T(2,128)(2,1)}), bf16[16,2,512]{2,1,0:T(2,128)(2,1)S(1)}, u32[]{:S(2)}, u32[]{:S(2)}) %all-to-all-start.1) | async-done | bytes 32800 | tf_op jit(solution)/shard_map/all_to_all | solution.py:345
  25.0 0.0 copy-start.5
  25.0 0.0 copy-start.1
  25.0 0.0 copy-start.3
  25.0 0.6 copy-done.5
  25.6 8.7 %all-to-all-start = ((bf16[128,136,128]{2,1,0:T(8,128)(2,1)}), bf16[128,136,128]{2,1,0:T(8,128)(2,1)}, u32[]{:S(2)}, u32[]{:S(2)}) async-start(bf16[128,136,128]{2,1,0:T(8,128)(2,1)} %bitcast.7), calls=%async_computation.1 | async-start | bytes 8912896 | tf_op jit(solution)/shard_map/all_to_all | solution.py:347
  34.4 0.0 reduce-scatter.2.cloned.1.call-start
  34.4 0.0 copy-done.1
  34.4 0.0 copy-done.3
  34.4 0.0 copy-start
  34.5 2.2 %copy-done = bf16[16,4,64,512]{3,2,1,0:T(8,128)(2,1)S(1)} copy-done((bf16[16,4,64,512]{3,2,1,0:T(8,128)(2,1)S(1)}, bf16[16,4,64,512]{3,2,1,0:T(8,128)(2,1)}, u32[]{:S(2)}) %copy-start) | copy-done | bytes 4194328
  36.6 0.0 copy-start.6
  36.6 17.2 %diag.1 = f32[16,64,512]{2,1,0:T(8,128)} custom-call(bf16[16,4,64,512]{3,2,1,0:T(8,128)(2,1)S(1)} %copy-done, bf16[16,64,512]{2,1,0:T(8,128)(2,1)S(1)} %copy-done.1, bf16[16,2,512]{2,1,0:T(2,128)(2,1)S(1)} %copy-done.3), custom_call_target="tpu_custom_call" | custom-call | flops 20000000000 | bytes 8000000 | tf_op jit(solution)/shard_map/diag/pallas_call | solution.py:168
  53.9 0.0 reduce-scatter.2.cloned.1.call-update
  54.5 0.0 copy-done.6
  54.5 0.1 copy.8
  54.6 0.6 reshape.16.pairs
  55.3 29.8 %tiles.1.tiles_ref = bf16[32,512,512]{2,1,0:T(8,128)(2,1)} custom-call(s32[64]{0:T(128)} %reshape.16.pairs, s32[1]{0:T(128)S(6)} %copy.9.count, bf16[16,2,512]{2,1,0:T(2,128)(2,1)} %copy-done.5), custom_call_target="tpu_custom_call" | custom-call | flops 30000001024 | bytes 17000000 | tf_op jit(solution)/shard_map/tiles/pallas_call | solution.py:201
  85.0 4.8 %all-to-all-done = bf16[128,136,128]{2,1,0:T(8,128)(2,1)} async-done(((bf16[128,136,128]{2,1,0:T(8,128)(2,1)}), bf16[128,136,128]{2,1,0:T(8,128)(2,1)}, u32[]{:S(2)}, u32[]{:S(2)}) %all-to-all-start) | async-done | bytes 4456480 | tf_op jit(solution)/shard_map/all_to_all | solution.py:347
  89.8 0.0 copy-start.4
  89.8 18.2 %apply.1 = f32[16,8,512]{2,1,0:T(8,128)} custom-call(s32[64]{0:T(128)} %reshape.16.pairs, s32[1]{0:T(128)S(6)} %copy.9.count, bf16[16,8,136,128]{3,2,1,0:T(8,128)(2,1)} %bitcast.3.got_ref, bf16[32,512,512]{2,1,0:T(8,128)(2,1)} %tiles.1.tiles_ref), custom_call_target="tpu_custom_call" | custom-call | flops 8999999488 | bytes 22000000 | tf_op jit(solution)/shard_map/apply/pallas_call | solution.py:288
  108.0 8.5 %all-to-all-start.2 = ((f32[16,8,512]{2,1,0:T(8,128)}), f32[16,8,512]{2,1,0:T(8,128)S(1)}, u32[]{:S(2)}, u32[]{:S(2)}) async-start(f32[16,8,512]{2,1,0:T(8,128)} %apply.1), calls=%async_computation.3 | async-start | bytes 524288 | tf_op jit(solution)/shard_map/all_to_all | solution.py:354
  116.5 0.0 reduce-scatter.2.cloned.1.call-done.own_ref
  116.5 9.0 %all-to-all-done.2.back_ref = f32[16,8,512]{2,1,0:T(8,128)S(1)} async-done(((f32[16,8,512]{2,1,0:T(8,128)}), f32[16,8,512]{2,1,0:T(8,128)S(1)}, u32[]{:S(2)}, u32[]{:S(2)}) %all-to-all-start.2) | async-done | bytes 262176 | tf_op jit(solution)/shard_map/all_to_all | solution.py:354
  125.5 0.0 copy-done.4
  125.5 0.0 copy-start.2
  125.5 0.9 copy-done.2
  126.5 1.3 finish.1
Async XLA Ops:
  9.4 15.6 %all-to-all-start.1 = ((bf16[16,2,512]{2,1,0:T(2,128)(2,1)}), bf16[16,2,512]{2,1,0:T(2,128)(2,1)S(1)}, u32[]{:S(2)}, u32[]{:S(2)}) async-start(bf16[16,2,512]{2,1,0:T(2,128)(2,1)} %select.1), calls=%async_computation.2 | async-start | bytes 65536 | tf_op jit(solution)/shard_map/all_to_all | solution.py:345
  25.0 0.6 copy-start.5
  25.0 9.4 %copy-start.1 = (bf16[16,64,512]{2,1,0:T(8,128)(2,1)S(1)}, bf16[16,64,512]{2,1,0:T(8,128)(2,1)}, u32[]{:S(2)}) copy-start(bf16[16,64,512]{2,1,0:T(8,128)(2,1)} %inc_ref.3) | copy-start | bytes 3145732
  25.0 9.4 %copy-start.3 = (bf16[16,2,512]{2,1,0:T(2,128)(2,1)S(1)}, bf16[16,2,512]{2,1,0:T(2,128)(2,1)}, u32[]{:S(2)}) copy-start(bf16[16,2,512]{2,1,0:T(2,128)(2,1)} %coords_ref.3) | copy-start | bytes 98308
  25.6 64.2 %all-to-all-start = ((bf16[128,136,128]{2,1,0:T(8,128)(2,1)}), bf16[128,136,128]{2,1,0:T(8,128)(2,1)}, u32[]{:S(2)}, u32[]{:S(2)}) async-start(bf16[128,136,128]{2,1,0:T(8,128)(2,1)} %bitcast.7), calls=%async_computation.1 | async-start | bytes 8912896 | tf_op jit(solution)/shard_map/all_to_all | solution.py:347
  34.4 82.1 %reduce-scatter.2.cloned.1.call-start = ((), (), s32[]{:S(2)}) async-start(), calls=%async_computation.4 | async-start | bytes 2359296 | tf_op jit(solution)/shard_map/reduce_scatter | solution.py:351
  34.4 2.2 %copy-start = (bf16[16,4,64,512]{3,2,1,0:T(8,128)(2,1)S(1)}, bf16[16,4,64,512]{3,2,1,0:T(8,128)(2,1)}, u32[]{:S(2)}) copy-start(bf16[16,4,64,512]{3,2,1,0:T(8,128)(2,1)} %ens_ref.3) | copy-start | bytes 12582916
  36.6 17.9 %copy-start.6 = (s32[32,2]{0,1:T(2,128)S(1)}, s32[32,2]{0,1:T(2,128)}, u32[]{:S(2)}) copy-start(s32[32,2]{0,1:T(2,128)} %param.10) | copy-start | bytes 772
  89.8 35.7 %copy-start.4 = (s32[1,16,1]{1,2,0:T(1,128)S(1)}, s32[1,16,1]{1,2,0:T(1,128)}, u32[]{:S(2)}) copy-start(s32[1,16,1]{1,2,0:T(1,128)} %param.9) | copy-start | bytes 196
  108.0 17.5 %all-to-all-start.2 = ((f32[16,8,512]{2,1,0:T(8,128)}), f32[16,8,512]{2,1,0:T(8,128)S(1)}, u32[]{:S(2)}, u32[]{:S(2)}) async-start(f32[16,8,512]{2,1,0:T(8,128)} %apply.1), calls=%async_computation.3 | async-start | bytes 524288 | tf_op jit(solution)/shard_map/all_to_all | solution.py:354
  125.5 1.0 copy-start.2
Sparse Core Ops, SparseCore 0:
  54.0 48.8 reduce-scatter.1

commit v3 on v2

--- a/solution.py
+++ b/solution.py
@@ -9,7 +9,6 @@
 
 LANES = 128
 TILE_GROUP = 4
-DEPTH = 4
 MIB = 1024 * 1024
 UNIT = 12.0**-0.2
 UNIT2 = UNIT * UNIT
@@ -144,6 +143,7 @@
 
 def diag_kernel(ens_ref, inc_ref, coords_ref, out_ref):
     members, levels, points = ens_ref.shape[1:]
+    parts, _, step, _ = out_ref.shape
     rows = members * levels
     half = points // 2
     places = coords_ref[0].astype(jnp.float32)
@@ -159,12 +159,15 @@
         far, lower, preferred_element_type=jnp.float32
     )
     block = ens_ref[0].astype(jnp.float32)
-    out_ref[0, :, :half] = jnp.sum(block[:, :, :half] * field_near.reshape(members, levels, half), axis=0)
-    out_ref[0, :, half:] = jnp.sum(block[:, :, half:] * field_far.reshape(members, levels, half), axis=0)
-
-
-def diag(ensemble, increment, coords):
+    sum_near = jnp.sum(block[:, :, :half] * field_near.reshape(members, levels, half), axis=0)
+    sum_far = jnp.sum(block[:, :, half:] * field_far.reshape(members, levels, half), axis=0)
+    out_ref[:, 0, :, :half] = sum_near.reshape(parts, step, half).astype(out_ref.dtype)
+    out_ref[:, 0, :, half:] = sum_far.reshape(parts, step, half).astype(out_ref.dtype)
+
+
+def diag(ensemble, increment, coords, parts):
     blocks, members, levels, points = ensemble.shape
+    step = levels // parts
     return pl.pallas_call(
         diag_kernel,
         grid=(blocks,),
@@ -173,48 +176,44 @@
             pl.BlockSpec((1, levels, points), lambda b: (b, 0, 0)),
             pl.BlockSpec((1, 2, points), lambda b: (b, 0, 0)),
         ],
-        out_specs=pl.BlockSpec((1, levels, points), lambda b: (b, 0, 0)),
-        out_shape=jax.ShapeDtypeStruct((blocks, levels, points), jnp.float32),
-        compiler_params=pltpu.CompilerParams(vmem_limit_bytes=16 * MIB),
+        out_specs=pl.BlockSpec((parts, 1, step, points), lambda b: (0, b, 0, 0)),
+        out_shape=jax.ShapeDtypeStruct((parts, blocks, step, points), jnp.bfloat16),
+        compiler_params=pltpu.CompilerParams(vmem_limit_bytes=24 * MIB),
         cost_estimate=pl.CostEstimate(flops=20_000_000_000, bytes_accessed=8_000_000, transcendentals=0),
         name="diag",
     )(ensemble, increment, coords)
 
 
-def tiles_kernel(pairs, count, places_ref, out_ref):
-    group = out_ref.shape[0]
-    base = pl.program_id(0) * group
-
-    def one(within, carry):
-        pair = 2 * (base + within)
+def tiles_kernel(pairs, places_ref, out_ref):
+    first = pl.program_id(0) * TILE_GROUP
+    for within in range(TILE_GROUP):
+        pair = 2 * (first + within)
         left = left_rows(places_ref[pairs[pair]].astype(jnp.float32))
         right = right_rows(places_ref[pairs[pair + 1]].astype(jnp.float32))
         out_ref[within] = tile_of(left, right)
-        return carry
-
-    lax.fori_loop(0, jnp.clip(count[0] - base, 0, group), one, 0)
-
-
-def tiles(places, pairs, count):
+
+
+def tiles(places, pairs):
     slot_total, _, points = places.shape
     cap = pairs.shape[0] // 2
     return pl.pallas_call(
         tiles_kernel,
         grid_spec=pltpu.PrefetchScalarGridSpec(
-            num_scalar_prefetch=2,
+            num_scalar_prefetch=1,
             grid=(cap // TILE_GROUP,),
-            in_specs=[pl.BlockSpec((slot_total, 2, points), lambda i, p, c: (0, 0, 0))],
-            out_specs=pl.BlockSpec((TILE_GROUP, points, points), lambda i, p, c: (i, 0, 0)),
+            in_specs=[pl.BlockSpec((slot_total, 2, points), lambda i, p: (0, 0, 0))],
+            out_specs=pl.BlockSpec((TILE_GROUP, points, points), lambda i, p: (i, 0, 0)),
         ),
         out_shape=jax.ShapeDtypeStruct((cap, points, points), jnp.bfloat16),
         compiler_params=pltpu.CompilerParams(vmem_limit_bytes=60 * MIB),
         cost_estimate=pl.CostEstimate(flops=30_000_000_000, bytes_accessed=17_000_000, transcendentals=0),
         name="tiles",
-    )(pairs, count, places)
+    )(pairs, places)
 
 
 def apply_kernel(
-    pairs, count, got_ref, tiles_ref, out_ref, ens_ref, inc_ref, weighted_ref, field_ref, ring_ref, ens_sem, inc_sem, ring_sem
+    pairs, count, got_ref, stack_ref, out_ref,
+    ens_ref, inc_ref, weighted_ref, field_ref, tiles_ref, ens_sem, inc_sem, tiles_sem,
 ):
     slot_total, sources, rows, points = ens_ref.shape
     step = inc_ref.shape[2]
@@ -232,20 +231,16 @@
         ]
 
     inc_copy = pltpu.make_async_copy(got_ref.at[:, :lane_chunks, rows * lane_chunks :, :], inc_ref, inc_sem)
+
+    def tile_copy(index):
+        return pltpu.make_async_copy(stack_ref.at[index], tiles_ref.at[index], tiles_sem.at[index])
+
     inc_copy.start()
     for slot in range(slot_total):
         for copy in ens_copies(slot):
             copy.start()
-    def ring_copy(index):
-        place = lax.rem(index, DEPTH)
-        return pltpu.make_async_copy(tiles_ref.at[index], ring_ref.at[place], ring_sem.at[place])
-
-    for index in range(DEPTH):
-
-        @pl.when(index < count[0])
-        def _():
-            ring_copy(index).start()
-
+    for index in range(tiles_ref.shape[0]):
+        tile_copy(index).start()
     inc_copy.wait()
     for slot in range(slot_total):
         field_ref[slot] = jnp.zeros((every, points), jnp.float32)
@@ -260,20 +255,22 @@
     def one(index, carry):
         first = pairs[2 * index]
         second = pairs[2 * index + 1]
-        ring_copy(index).wait()
-        tile = ring_ref[lax.rem(index, DEPTH)]
-        field_ref[first] += lax.dot_general(
+        tile_copy(index).wait()
+        tile = tiles_ref[index]
+        to_first = lax.dot_general(
             weighted_ref[second], tile, (((1,), (1,)), ((), ())), preferred_element_type=jnp.float32
         )
-        field_ref[second] += jnp.dot(weighted_ref[first], tile, preferred_element_type=jnp.float32)
-
-        @pl.when(index + DEPTH < count[0])
-        def _():
-            ring_copy(index + DEPTH).start()
-
+        to_second = jnp.dot(weighted_ref[first], tile, preferred_element_type=jnp.float32)
+        field_ref[first] += to_first
+        field_ref[second] += to_second
         return carry
 
+    def skip(index, carry):
+        tile_copy(index).wait()
+        return carry
+
     lax.fori_loop(0, count[0], one, 0)
+    lax.fori_loop(count[0], tiles_ref.shape[0], skip, 0)
 
     for slot in range(slot_total):
         product = ens_ref[slot].reshape(every, points).astype(jnp.float32) * field_ref[slot]
@@ -282,7 +279,7 @@
 
 def apply_pairs(got, tile_stack, pairs, count, members, step):
     slot_total, sources, rows, _ = got.shape
-    cap, points, _ = tile_stack.shape
+    points = tile_stack.shape[2]
     lane_chunks = points // LANES
     every = sources * members * step
     return pl.pallas_call(
@@ -299,10 +296,10 @@
             pltpu.VMEM((slot_total, lane_chunks, step, LANES), jnp.bfloat16),
             pltpu.VMEM((slot_total, every, points), jnp.bfloat16),
             pltpu.VMEM((slot_total, every, points), jnp.float32),
-            pltpu.VMEM((DEPTH, points, points), jnp.bfloat16),
+            pltpu.VMEM(tile_stack.shape, jnp.bfloat16),
             pltpu.SemaphoreType.DMA((slot_total, lane_chunks)),
             pltpu.SemaphoreType.DMA,
-            pltpu.SemaphoreType.DMA((DEPTH,)),
+            pltpu.SemaphoreType.DMA((tile_stack.shape[0],)),
         ],
         out_shape=jax.ShapeDtypeStruct((slot_total, step, points), jnp.float32),
         compiler_params=pltpu.CompilerParams(vmem_limit_bytes=60 * MIB),
@@ -311,14 +308,14 @@
     )(pairs, count, got, tile_stack)
 
 
-def finish_kernel(slots, own_ref, back_ref, out_ref, *, scale):
-    out_ref[...] = own_ref[...] * scale
+def finish_kernel(slots, parts_ref, back_ref, out_ref, *, scale):
+    out_ref[...] = jnp.sum(parts_ref[...].astype(jnp.float32), axis=0) * scale
     for owner in range(back_ref.shape[0]):
         slot = slots[owner]
         out_ref[slot] = out_ref[slot] + back_ref[owner] * scale
 
 
-def finish(own, back, slots, scale):
+def finish(parts, back, slots, scale):
     return pl.pallas_call(
         functools.partial(finish_kernel, scale=scale),
         in_specs=[
@@ -327,10 +324,10 @@
             pl.BlockSpec(memory_space=pltpu.VMEM),
         ],
         out_specs=pl.BlockSpec(memory_space=pltpu.VMEM),
-        out_shape=jax.ShapeDtypeStruct(own.shape, jnp.float32),
+        out_shape=jax.ShapeDtypeStruct(parts.shape[1:], jnp.float32),
         compiler_params=pltpu.CompilerParams(vmem_limit_bytes=16 * MIB),
         name="finish",
-    )(slots, own, back)
+    )(slots, parts, back)
 
 
 def per_device(ensemble, increment, coords, sent_slots, pair_list, pair_count):
@@ -344,15 +341,18 @@
     places = select(coords, slots)
     own_places = lax.all_to_all(places, "region", 0, 0, tiled=True)
     big = pack(ensemble, increment, slots, own, groups)
+    big, own_places = lax.optimization_barrier((big, own_places))
     got = lax.all_to_all(
         big.reshape(regions * groups, -1, LANES), ("region", "member"), 0, 0, tiled=True
     ).reshape(regions, groups, -1, LANES)
-    diagonal = diag(ensemble, increment, coords)
-    diagonal = lax.psum_scatter(diagonal, "member", scatter_dimension=1, tiled=True)
-    tile_stack = tiles(own_places, pairs, pair_count)
+    diagonal = diag(ensemble, increment, coords, groups)
+    tile_stack = tiles(own_places, pairs)
+    got, diagonal, tile_stack = lax.optimization_barrier((got, diagonal, tile_stack))
+    parts = lax.all_to_all(diagonal, "member", 0, 0, tiled=True)
     partial = apply_pairs(got, tile_stack, pairs, pair_count, members, step)
+    partial, parts = lax.optimization_barrier((partial, parts))
     back = lax.all_to_all(partial, "region", 0, 0, tiled=True)
-    return finish(diagonal, back, slots, 1.0 / (members * groups - 1))
+    return finish(parts, back, slots, 1.0 / (members * groups - 1))
 
 
 def solution(mesh):

time: 134 us -> 125 us (0.933); the launches traced: 135 us -> 123 us
  blocking collectives: 0 us -> 14.8 us
  between operations: 14.1 us -> 0.75 us
  waiting for transfers between devices: 15.8 us -> 6.94 us
  starting transfers between devices: 25.2 us -> 21.9 us
    all_to_all x0 -> x1, blocking collectives: none -> 14.8 us  [per_device(): back = lax.all_to_all(partial, 'region', 0, 0, tiled=True)]
    all_to_all x1, waiting for transfers between devices: 8.96 us -> 0.01 us  [per_device(): parts = lax.all_to_all(diagonal, 'member', 0, 0, tiled=True)]
    all_to_all x1, starting transfers between devices: 8.46 us -> 3.56 us  [per_device(): parts = lax.all_to_all(diagonal, 'member', 0, 0, tiled=True)]
    all_to_all x1, waiting for transfers between devices: 4.77 us -> 6.65 us  [per_device(): lax.all_to_all(big.reshape(regions * groups, -1, LANES), ('region', 'memb...]
    all_to_all x1, waiting for transfers between devices: 2.01 us -> 0.3 us  [per_device(): own_places = lax.all_to_all(places, 'region', 0, 0, tiled=True)]
    all_to_all x1, starting transfers between devices: 8.73 us -> 10.4 us  [per_device(): lax.all_to_all(big.reshape(regions * groups, -1, LANES), ('region', 'memb...]
    unnamed x15 -> x11, local copies, waits for them, and re-layouts: 3.85 us -> 3.57 us
  transfers between devices with their start and end apart: 4 -> 3, of which waited for: 3 -> 2; matrix products, arithmetic and copies ran while one was open for 1% -> 1% of each run, Pallas kernels for 53% -> 57%
where the time goes in v3:
time: 125 us; the launch traced here: 123 us
  Pallas kernels  74.4 us (60%)
  starting transfers between devices  21.9 us (18%)
  blocking collectives  14.8 us (12%)
  waiting for transfers between devices  6.94 us (6%)
  local copies, waits for them, and re-layouts  4.2 us (3%)
    pallas_call x1, Pallas kernels, tiles(): pl.pallas_call(tiles_kernel, grid_spec=pltpu.PrefetchScalarGridSpec(num_s...  29.3 us
    pallas_call x1, Pallas kernels, apply_pairs(): pl.pallas_call(apply_kernel, in_specs=[pl.BlockSpec(memory_space=pltpu.SM...  17.6 us
    pallas_call x1, Pallas kernels, diag(): pl.pallas_call(diag_kernel, grid=(blocks,), in_specs=[pl.BlockSpec((1, me...  17.2 us
    all_to_all x1, blocking collectives, per_device(): back = lax.all_to_all(partial, 'region', 0, 0, tiled=True)  14.8 us
    all_to_all x1, starting transfers between devices, per_device(): lax.all_to_all(big.reshape(regions * groups, -1, LANES), ('region', 'memb...  10.4 us
    all_to_all x1, starting transfers between devices, per_device(): own_places = lax.all_to_all(places, 'region', 0, 0, tiled=True)  7.96 us
    all_to_all x1, waiting for transfers between devices, per_device(): lax.all_to_all(big.reshape(regions * groups, -1, LANES), ('region', 'memb...  6.65 us
    pallas_call x1, Pallas kernels, pack(): pl.pallas_call(pack_kernel, in_specs=[pl.BlockSpec(memory_space=pltpu.SME...  5.9 us
  transfers between devices with their start and end apart: 3, of which 2 were waited for; matrix products, arithmetic and copies ran while one was open for 1% of the time, Pallas kernels for 57%

profile of v3, /device:TPU:0, one launch (start us, length us, event | category | flops | bytes accessed | tf_op | source)
XLA Modules:
  0.0 123.0 jit_solution(8172020412403359873)
XLA Ops:
  0.0 2.9 %select.1 = bf16[16,2,512]{2,1,0:T(2,128)(2,1)} custom-call(s32[16]{0:T(128)} %bitcast.4, bf16[16,2,512]{2,1,0:T(2,128)(2,1)} %coords_ref.3), custom_call_target="tpu_custom_call" | custom-call | tf_op jit(solution)/shard_map/select/pallas_call | solution.py:32
  2.9 8.0 %all-to-all-start = ((bf16[16,2,512]{2,1,0:T(2,128)(2,1)}), bf16[16,2,512]{2,1,0:T(2,128)(2,1)S(1)}, u32[]{:S(2)}, u32[]{:S(2)}) async-start(bf16[16,2,512]{2,1,0:T(2,128)(2,1)} %select.1), calls=%async_computation | async-start | bytes 65536 | tf_op jit(solution)/shard_map/all_to_all | solution.py:342
  10.9 0.8 copy.8
  11.7 0.6 reshape.16.pairs
  12.3 5.9 %pack.1 = bf16[16,8,136,128]{3,2,1,0:T(8,128)(2,1)} custom-call(s32[16]{0:T(128)} %bitcast.5, s32[1]{0:T(128)} %bitcast.1.own, bf16[16,4,64,512]{3,2,1,0:T(8,128)(2,1)} %ens_ref.3, bf16[16,64,512]{2,1,0:T(8,128)(2,1)} %inc_ref.3), custom_call_target="tpu_custom_call" | custom-call | tf_op jit(solution)/shard_map/pack/pallas_call | solution.py:82
  18.2 0.3 all-to-all-done.places_ref
  18.5 0.0 copy-start.4
  18.5 0.0 copy-start.1
  18.5 0.0 copy-start.2
  18.5 0.6 copy-done.4
  19.1 10.4 %all-to-all-start.1 = ((bf16[128,136,128]{2,1,0:T(8,128)(2,1)}), bf16[128,136,128]{2,1,0:T(8,128)(2,1)}, u32[]{:S(2)}, u32[]{:S(2)}) async-start(bf16[128,136,128]{2,1,0:T(8,128)(2,1)} %bitcast.7), calls=%async_computation.1 | async-start | bytes 8912896 | tf_op jit(solution)/shard_map/all_to_all | solution.py:345
  29.5 0.0 copy-done.1
  29.5 0.0 copy-done.2
  29.5 0.0 copy-start
  29.5 2.2 %copy-done = bf16[16,4,64,512]{3,2,1,0:T(8,128)(2,1)S(1)} copy-done((bf16[16,4,64,512]{3,2,1,0:T(8,128)(2,1)S(1)}, bf16[16,4,64,512]{3,2,1,0:T(8,128)(2,1)}, u32[]{:S(2)}) %copy-start) | copy-done | bytes 4194328
  31.7 17.2 %diag.1 = bf16[8,16,8,512]{3,2,1,0:T(8,128)(2,1)} custom-call(bf16[16,4,64,512]{3,2,1,0:T(8,128)(2,1)S(1)} %copy-done, bf16[16,64,512]{2,1,0:T(8,128)(2,1)S(1)} %copy-done.1, bf16[16,2,512]{2,1,0:T(2,128)(2,1)S(1)} %copy-done.2), custom_call_target="tpu_custom_call" | custom-call | flops 20000000000 | bytes 8000000 | tf_op jit(solution)/shard_map/diag/pallas_call | solution.py:171
  48.9 29.3 %tiles.1.stack_ref = bf16[32,512,512]{2,1,0:T(8,128)(2,1)} custom-call(s32[64]{0:T(128)} %reshape.16.pairs, bf16[16,2,512]{2,1,0:T(2,128)(2,1)} %copy-done.4), custom_call_target="tpu_custom_call" | custom-call | flops 30000001024 | bytes 17000000 | tf_op jit(solution)/shard_map/tiles/pallas_call | solution.py:199
  78.2 6.6 %all-to-all-done.1 = bf16[128,136,128]{2,1,0:T(8,128)(2,1)} async-done(((bf16[128,136,128]{2,1,0:T(8,128)(2,1)}), bf16[128,136,128]{2,1,0:T(8,128)(2,1)}, u32[]{:S(2)}, u32[]{:S(2)}) %all-to-all-start.1) | async-done | bytes 4456480 | tf_op jit(solution)/shard_map/all_to_all | solution.py:345
  84.9 3.6 %all-to-all-start.2 = ((bf16[8,16,8,512]{3,2,1,0:T(8,128)(2,1)}), bf16[8,16,8,512]{3,2,1,0:T(8,128)(2,1)S(1)}, u32[]{:S(2)}, u32[]{:S(2)}) async-start(bf16[8,16,8,512]{3,2,1,0:T(8,128)(2,1)} %diag.1), calls=%async_computation.2 | async-start | bytes 2097152 | tf_op jit(solution)/shard_map/all_to_all | solution.py:351
  89.1 0.0 copy-start.3
  89.1 17.6 %apply.1 = f32[16,8,512]{2,1,0:T(8,128)} custom-call(s32[64]{0:T(128)} %reshape.16.pairs, s32[1]{0:T(128)S(6)} %copy.9.count, bf16[16,8,136,128]{3,2,1,0:T(8,128)(2,1)} %bitcast.3.got_ref, bf16[32,512,512]{2,1,0:T(8,128)(2,1)} %tiles.1.stack_ref), custom_call_target="tpu_custom_call" | custom-call | flops 8999999488 | bytes 22000000 | tf_op jit(solution)/shard_map/apply/pallas_call | solution.py:285
  106.7 0.0 all-to-all-done.2.parts_ref
  106.7 14.8 %all_to_all.20.back_ref = f32[16,8,512]{2,1,0:T(8,128)S(1)} all-to-all(f32[16,8,512]{2,1,0:T(8,128)} %apply.1), channel_id=1, replica_groups=mesh['region'=16,'member'=8] {'region'}, dimensions={0} | all-to-all | bytes 524288 | tf_op jit(solution)/shard_map/all_to_all | solution.py:354
  121.5 0.0 copy-done.3
  121.5 1.5 %finish.1 = f32[16,8,512]{2,1,0:T(8,128)} custom-call(s32[16]{0:T(128)S(1)} %bitcast.6, bf16[8,16,8,512]{3,2,1,0:T(8,128)(2,1)S(1)} %all-to-all-done.2.parts_ref, f32[16,8,512]{2,1,0:T(8,128)S(1)} %all_to_all.20.back_ref), custom_call_target="tpu_custom_call" | custom-call | tf_op jit(solution)/shard_map/finish/pallas_call | solution.py:319
Async XLA Ops:
  2.9 15.6 %all-to-all-start = ((bf16[16,2,512]{2,1,0:T(2,128)(2,1)}), bf16[16,2,512]{2,1,0:T(2,128)(2,1)S(1)}, u32[]{:S(2)}, u32[]{:S(2)}) async-start(bf16[16,2,512]{2,1,0:T(2,128)(2,1)} %select.1), calls=%async_computation | async-start | bytes 65536 | tf_op jit(solution)/shard_map/all_to_all | solution.py:342
  18.5 0.6 copy-start.4
  18.5 11.0 %copy-start.1 = (bf16[16,64,512]{2,1,0:T(8,128)(2,1)S(1)}, bf16[16,64,512]{2,1,0:T(8,128)(2,1)}, u32[]{:S(2)}) copy-start(bf16[16,64,512]{2,1,0:T(8,128)(2,1)} %inc_ref.3) | copy-start | bytes 3145732
  18.5 11.0 %copy-start.2 = (bf16[16,2,512]{2,1,0:T(2,128)(2,1)S(1)}, bf16[16,2,512]{2,1,0:T(2,128)(2,1)}, u32[]{:S(2)}) copy-start(bf16[16,2,512]{2,1,0:T(2,128)(2,1)} %coords_ref.3) | copy-start | bytes 98308
  19.1 65.8 %all-to-all-start.1 = ((bf16[128,136,128]{2,1,0:T(8,128)(2,1)}), bf16[128,136,128]{2,1,0:T(8,128)(2,1)}, u32[]{:S(2)}, u32[]{:S(2)}) async-start(bf16[128,136,128]{2,1,0:T(8,128)(2,1)} %bitcast.7), calls=%async_computation.1 | async-start | bytes 8912896 | tf_op jit(solution)/shard_map/all_to_all | solution.py:345
  29.5 2.2 %copy-start = (bf16[16,4,64,512]{3,2,1,0:T(8,128)(2,1)S(1)}, bf16[16,4,64,512]{3,2,1,0:T(8,128)(2,1)}, u32[]{:S(2)}) copy-start(bf16[16,4,64,512]{3,2,1,0:T(8,128)(2,1)} %ens_ref.3) | copy-start | bytes 12582916
  84.9 21.8 %all-to-all-start.2 = ((bf16[8,16,8,512]{3,2,1,0:T(8,128)(2,1)}), bf16[8,16,8,512]{3,2,1,0:T(8,128)(2,1)S(1)}, u32[]{:S(2)}, u32[]{:S(2)}) async-start(bf16[8,16,8,512]{3,2,1,0:T(8,128)(2,1)} %diag.1), calls=%async_computation.2 | async-start | bytes 2097152 | tf_op jit(solution)/shard_map/all_to_all | solution.py:351
  89.1 32.4 %copy-start.3 = (s32[1,16,1]{1,2,0:T(1,128)S(1)}, s32[1,16,1]{1,2,0:T(1,128)}, u32[]{:S(2)}) copy-start(s32[1,16,1]{1,2,0:T(1,128)} %param.9) | copy-start | bytes 196

commit v4 on v3

--- a/solution.py
+++ b/solution.py
@@ -9,6 +9,7 @@
 
 LANES = 128
 TILE_GROUP = 4
+PAIR_GROUP = 4
 MIB = 1024 * 1024
 UNIT = 12.0**-0.2
 UNIT2 = UNIT * UNIT
@@ -178,7 +179,7 @@
         ],
         out_specs=pl.BlockSpec((parts, 1, step, points), lambda b: (0, b, 0, 0)),
         out_shape=jax.ShapeDtypeStruct((parts, blocks, step, points), jnp.bfloat16),
-        compiler_params=pltpu.CompilerParams(vmem_limit_bytes=24 * MIB),
+        compiler_params=pltpu.CompilerParams(vmem_limit_bytes=60 * MIB),
         cost_estimate=pl.CostEstimate(flops=20_000_000_000, bytes_accessed=8_000_000, transcendentals=0),
         name="diag",
     )(ensemble, increment, coords)
@@ -187,15 +188,14 @@
 def tiles_kernel(pairs, places_ref, out_ref):
     first = pl.program_id(0) * TILE_GROUP
     for within in range(TILE_GROUP):
-        pair = 2 * (first + within)
-        left = left_rows(places_ref[pairs[pair]].astype(jnp.float32))
-        right = right_rows(places_ref[pairs[pair + 1]].astype(jnp.float32))
+        left = left_rows(places_ref[pairs[0, first + within]].astype(jnp.float32))
+        right = right_rows(places_ref[pairs[1, first + within]].astype(jnp.float32))
         out_ref[within] = tile_of(left, right)
 
 
 def tiles(places, pairs):
     slot_total, _, points = places.shape
-    cap = pairs.shape[0] // 2
+    cap = pairs.shape[1]
     return pl.pallas_call(
         tiles_kernel,
         grid_spec=pltpu.PrefetchScalarGridSpec(
@@ -252,24 +252,37 @@
             block = ens_ref[slot, :, :, here].reshape(every // step, step, LANES)
             weighted_ref[slot, :, here] = (block * gain[None]).reshape(every, LANES)
 
+    def some(start, number):
+        products = []
+        for within in range(number):
+            tile_copy(start + within).wait()
+        for within in range(number):
+            index = start + within
+            first, second = pairs[0, index], pairs[1, index]
+            tile = tiles_ref[index]
+            to_first = lax.dot_general(
+                weighted_ref[second], tile, (((1,), (1,)), ((), ())), preferred_element_type=jnp.float32
+            )
+            to_second = jnp.dot(weighted_ref[first], tile, preferred_element_type=jnp.float32)
+            products += [(first, to_first), (second, to_second)]
+        for slot, product in products:
+            field_ref[slot] += product
+
+    def group(turn, carry):
+        some(turn * PAIR_GROUP, PAIR_GROUP)
+        return carry
+
     def one(index, carry):
-        first = pairs[2 * index]
-        second = pairs[2 * index + 1]
-        tile_copy(index).wait()
-        tile = tiles_ref[index]
-        to_first = lax.dot_general(
-            weighted_ref[second], tile, (((1,), (1,)), ((), ())), preferred_element_type=jnp.float32
-        )
-        to_second = jnp.dot(weighted_ref[first], tile, preferred_element_type=jnp.float32)
-        field_ref[first] += to_first
-        field_ref[second] += to_second
+        some(index, 1)
         return carry
 
     def skip(index, carry):
         tile_copy(index).wait()
         return carry
 
-    lax.fori_loop(0, count[0], one, 0)
+    groups = count[0] // PAIR_GROUP
+    lax.fori_loop(0, groups, group, 0)
+    lax.fori_loop(groups * PAIR_GROUP, count[0], one, 0)
     lax.fori_loop(count[0], tiles_ref.shape[0], skip, 0)
 
     for slot in range(slot_total):
@@ -336,7 +349,7 @@
     groups = lax.axis_size("member")
     step = levels // groups
     slots = sent_slots.reshape(-1)
-    pairs = pair_list.reshape(-1)
+    pairs = pair_list.T
     own = lax.axis_index("member").reshape(1).astype(jnp.int32)
     places = select(coords, slots)
     own_places = lax.all_to_all(places, "region", 0, 0, tiled=True)

time: 125 us -> 119 us (0.952)
  waiting for transfers between devices: 6.94 us -> 10.9 us
  local copies, waits for them, and re-layouts: 4.2 us -> 0.62 us
  Pallas kernels: 74.4 us -> 71.7 us
  starting transfers between devices: 21.9 us -> 20.3 us
  blocking collectives: 14.8 us -> 13.3 us
    pallas_call x1, Pallas kernels: 17.6 us -> 14.2 us  [apply_pairs(): pl.pallas_call(apply_kernel, in_specs=[pl.BlockSpec(memory_space=pltpu.SM...]
    unnamed x11 -> x4, local copies, waits for them, and re-layouts: 3.57 us -> 0.62 us
    all_to_all x1, waiting for transfers between devices: 0.3 us -> 2.03 us  [per_device(): own_places = lax.all_to_all(places, 'region', 0, 0, tiled=True)]
    all_to_all x1, starting transfers between devices: 10.4 us -> 8.8 us  [per_device(): lax.all_to_all(big.reshape(regions * groups, -1, LANES), ('region', 'memb...]
    all_to_all x1, blocking collectives: 14.8 us -> 13.3 us  [per_device(): back = lax.all_to_all(partial, 'region', 0, 0, tiled=True)]
  transfers between devices with their start and end apart: 3 -> 3, of which waited for: 2 -> 3; matrix products, arithmetic and copies ran while one was open for 1% -> 0% of each run, Pallas kernels for 57% -> 57%
where the time goes in v4:
time: 119 us; the launch traced here: 118 us
  Pallas kernels  71.7 us (60%)
  starting transfers between devices  20.3 us (17%)
  blocking collectives  13.3 us (11%)
  waiting for transfers between devices  10.9 us (9%)
    pallas_call x1, Pallas kernels, tiles(): pl.pallas_call(tiles_kernel, grid_spec=pltpu.PrefetchScalarGridSpec(num_s...  29.1 us
    pallas_call x1, Pallas kernels, diag(): pl.pallas_call(diag_kernel, grid=(blocks,), in_specs=[pl.BlockSpec((1, me...  18.5 us
    pallas_call x1, Pallas kernels, apply_pairs(): pl.pallas_call(apply_kernel, in_specs=[pl.BlockSpec(memory_space=pltpu.SM...  14.2 us
    all_to_all x1, blocking collectives, per_device(): back = lax.all_to_all(partial, 'region', 0, 0, tiled=True)  13.3 us
    all_to_all x1, starting transfers between devices, per_device(): lax.all_to_all(big.reshape(regions * groups, -1, LANES), ('region', 'memb...  8.8 us
    all_to_all x1, starting transfers between devices, per_device(): own_places = lax.all_to_all(places, 'region', 0, 0, tiled=True)  7.97 us
    all_to_all x1, waiting for transfers between devices, per_device(): lax.all_to_all(big.reshape(regions * groups, -1, LANES), ('region', 'memb...  7.8 us
    pallas_call x1, Pallas kernels, pack(): pl.pallas_call(pack_kernel, in_specs=[pl.BlockSpec(memory_space=pltpu.SME...  5.55 us
  transfers between devices with their start and end apart: 3, of which 3 were waited for; matrix products, arithmetic and copies ran while one was open for 0% of the time, Pallas kernels for 57%

profile of v4, /device:TPU:0, one launch (start us, length us, event | category | flops | bytes accessed | tf_op | source)
XLA Modules:
  0.0 117.5 jit_solution(13130636571107250100)
XLA Ops:
  0.0 2.9 %select.1 = bf16[16,2,512]{2,1,0:T(2,128)(2,1)} custom-call(s32[16]{0:T(128)} %bitcast.5, bf16[16,2,512]{2,1,0:T(2,128)(2,1)} %coords_ref.3), custom_call_target="tpu_custom_call" | custom-call | tf_op jit(solution)/shard_map/select/pallas_call | solution.py:33
  2.9 8.0 %all-to-all-start = ((bf16[16,2,512]{2,1,0:T(2,128)(2,1)}), bf16[16,2,512]{2,1,0:T(2,128)(2,1)S(1)}, u32[]{:S(2)}, u32[]{:S(2)}) async-start(bf16[16,2,512]{2,1,0:T(2,128)(2,1)} %select.1), calls=%async_computation | async-start | bytes 65536 | tf_op jit(solution)/shard_map/all_to_all | solution.py:355
  10.9 5.6 %pack.1 = bf16[16,8,136,128]{3,2,1,0:T(8,128)(2,1)} custom-call(s32[16]{0:T(128)} %bitcast.6, s32[1]{0:T(128)} %bitcast.2.own, bf16[16,4,64,512]{3,2,1,0:T(8,128)(2,1)} %ens_ref.3, bf16[16,64,512]{2,1,0:T(8,128)(2,1)} %inc_ref.3), custom_call_target="tpu_custom_call" | custom-call | tf_op jit(solution)/shard_map/pack/pallas_call | solution.py:83
  16.5 2.0 %all-to-all-done.places_ref = bf16[16,2,512]{2,1,0:T(2,128)(2,1)S(1)} async-done(((bf16[16,2,512]{2,1,0:T(2,128)(2,1)}), bf16[16,2,512]{2,1,0:T(2,128)(2,1)S(1)}, u32[]{:S(2)}, u32[]{:S(2)}) %all-to-all-start) | async-done | bytes 32800 | tf_op jit(solution)/shard_map/all_to_all | solution.py:355
  18.5 0.0 copy-start.1
  18.5 0.6 copy-done.1
  19.1 8.8 %all-to-all-start.1 = ((bf16[128,136,128]{2,1,0:T(8,128)(2,1)}), bf16[128,136,128]{2,1,0:T(8,128)(2,1)}, u32[]{:S(2)}, u32[]{:S(2)}) async-start(bf16[128,136,128]{2,1,0:T(8,128)(2,1)} %bitcast.8), calls=%async_computation.1 | async-start | bytes 8912896 | tf_op jit(solution)/shard_map/all_to_all | solution.py:358
  27.9 18.5 %diag.1 = bf16[8,16,8,512]{3,2,1,0:T(8,128)(2,1)} custom-call(bf16[16,4,64,512]{3,2,1,0:T(8,128)(2,1)} %ens_ref.3, bf16[16,64,512]{2,1,0:T(8,128)(2,1)} %inc_ref.3, bf16[16,2,512]{2,1,0:T(2,128)(2,1)} %coords_ref.3), custom_call_target="tpu_custom_call" | custom-call | flops 20000000000 | bytes 8000000 | tf_op jit(solution)/shard_map/diag/pallas_call | solution.py:172
  46.4 29.1 %tiles.1.stack_ref = bf16[32,512,512]{2,1,0:T(8,128)(2,1)} custom-call(s32[2,32]{1,0:T(2,128)} %bitcast.9, bf16[16,2,512]{2,1,0:T(2,128)(2,1)} %copy-done.1), custom_call_target="tpu_custom_call" | custom-call | flops 30000001024 | bytes 17000000 | tf_op jit(solution)/shard_map/tiles/pallas_call | solution.py:199
  75.5 7.8 %all-to-all-done.1 = bf16[128,136,128]{2,1,0:T(8,128)(2,1)} async-done(((bf16[128,136,128]{2,1,0:T(8,128)(2,1)}), bf16[128,136,128]{2,1,0:T(8,128)(2,1)}, u32[]{:S(2)}, u32[]{:S(2)}) %all-to-all-start.1) | async-done | bytes 4456480 | tf_op jit(solution)/shard_map/all_to_all | solution.py:358
  83.3 3.6 %all-to-all-start.2 = ((bf16[8,16,8,512]{3,2,1,0:T(8,128)(2,1)}), bf16[8,16,8,512]{3,2,1,0:T(8,128)(2,1)S(1)}, u32[]{:S(2)}, u32[]{:S(2)}) async-start(bf16[8,16,8,512]{3,2,1,0:T(8,128)(2,1)} %diag.1), calls=%async_computation.2 | async-start | bytes 2097152 | tf_op jit(solution)/shard_map/all_to_all | solution.py:364
  87.5 0.0 copy-start
  87.5 14.2 %apply.1 = f32[16,8,512]{2,1,0:T(8,128)} custom-call(s32[2,32]{1,0:T(2,128)} %bitcast.10, s32[1]{0:T(128)S(6)} %copy.7.count, bf16[16,8,136,128]{3,2,1,0:T(8,128)(2,1)} %bitcast.4.got_ref, bf16[32,512,512]{2,1,0:T(8,128)(2,1)} %tiles.1.stack_ref), custom_call_target="tpu_custom_call" | custom-call | flops 8999999488 | bytes 22000000 | tf_op jit(solution)/shard_map/apply/pallas_call | solution.py:298
  101.7 1.1 all-to-all-done.2.parts_ref
  102.7 13.3 %all_to_all.20.back_ref = f32[16,8,512]{2,1,0:T(8,128)S(1)} all-to-all(f32[16,8,512]{2,1,0:T(8,128)} %apply.1), channel_id=1, replica_groups=mesh['region'=16,'member'=8] {'region'}, dimensions={0} | all-to-all | bytes 524288 | tf_op jit(solution)/shard_map/all_to_all | solution.py:367
  116.0 0.0 copy-done
  116.0 1.5 %finish.1 = f32[16,8,512]{2,1,0:T(8,128)} custom-call(s32[16]{0:T(128)S(1)} %bitcast.7, bf16[8,16,8,512]{3,2,1,0:T(8,128)(2,1)S(1)} %all-to-all-done.2.parts_ref, f32[16,8,512]{2,1,0:T(8,128)S(1)} %all_to_all.20.back_ref), custom_call_target="tpu_custom_call" | custom-call | tf_op jit(solution)/shard_map/finish/pallas_call | solution.py:332
Async XLA Ops:
  2.9 15.6 %all-to-all-start = ((bf16[16,2,512]{2,1,0:T(2,128)(2,1)}), bf16[16,2,512]{2,1,0:T(2,128)(2,1)S(1)}, u32[]{:S(2)}, u32[]{:S(2)}) async-start(bf16[16,2,512]{2,1,0:T(2,128)(2,1)} %select.1), calls=%async_computation | async-start | bytes 65536 | tf_op jit(solution)/shard_map/all_to_all | solution.py:355
  18.5 0.6 copy-start.1
  19.1 64.2 %all-to-all-start.1 = ((bf16[128,136,128]{2,1,0:T(8,128)(2,1)}), bf16[128,136,128]{2,1,0:T(8,128)(2,1)}, u32[]{:S(2)}, u32[]{:S(2)}) async-start(bf16[128,136,128]{2,1,0:T(8,128)(2,1)} %bitcast.8), calls=%async_computation.1 | async-start | bytes 8912896 | tf_op jit(solution)/shard_map/all_to_all | solution.py:358
  83.3 19.4 %all-to-all-start.2 = ((bf16[8,16,8,512]{3,2,1,0:T(8,128)(2,1)}), bf16[8,16,8,512]{3,2,1,0:T(8,128)(2,1)S(1)}, u32[]{:S(2)}, u32[]{:S(2)}) async-start(bf16[8,16,8,512]{3,2,1,0:T(8,128)(2,1)} %diag.1), calls=%async_computation.2 | async-start | bytes 2097152 | tf_op jit(solution)/shard_map/all_to_all | solution.py:364
  87.5 28.5 %copy-start = (s32[1,16,1]{1,2,0:T(1,128)S(1)}, s32[1,16,1]{1,2,0:T(1,128)}, u32[]{:S(2)}) copy-start(s32[1,16,1]{1,2,0:T(1,128)} %param.9) | copy-start | bytes 196

commit v5 on v4

--- a/solution.py
+++ b/solution.py
@@ -8,7 +8,6 @@
 from jax.sharding import PartitionSpec as P
 
 LANES = 128
-TILE_GROUP = 4
 PAIR_GROUP = 4
 MIB = 1024 * 1024
 UNIT = 12.0**-0.2
@@ -142,9 +141,9 @@
     return ((first + 4.0 * second) * inverse).astype(jnp.bfloat16)
 
 
-def diag_kernel(ens_ref, inc_ref, coords_ref, out_ref):
+def diag_kernel(core, ens_ref, inc_ref, coords_ref, keep_ref, send_ref, sum_ref):
     members, levels, points = ens_ref.shape[1:]
-    parts, _, step, _ = out_ref.shape
+    parts, _, step, _ = keep_ref.shape
     rows = members * levels
     half = points // 2
     places = coords_ref[0].astype(jnp.float32)
@@ -160,63 +159,93 @@
         far, lower, preferred_element_type=jnp.float32
     )
     block = ens_ref[0].astype(jnp.float32)
-    sum_near = jnp.sum(block[:, :, :half] * field_near.reshape(members, levels, half), axis=0)
-    sum_far = jnp.sum(block[:, :, half:] * field_far.reshape(members, levels, half), axis=0)
-    out_ref[:, 0, :, :half] = sum_near.reshape(parts, step, half).astype(out_ref.dtype)
-    out_ref[:, 0, :, half:] = sum_far.reshape(parts, step, half).astype(out_ref.dtype)
-
-
-def diag(ensemble, increment, coords, parts):
+    sum_ref[:, :half] = jnp.sum(block[:, :, :half] * field_near.reshape(members, levels, half), axis=0)
+    sum_ref[:, half:] = jnp.sum(block[:, :, half:] * field_far.reshape(members, levels, half), axis=0)
+    for part in range(parts):
+        mine = pl.multiple_of((2 * part + core[0]) * step, step)
+        other = pl.multiple_of((2 * part + 1 - core[0]) * step, step)
+        keep_ref[part, 0] = sum_ref[pl.ds(mine, step), :]
+        send_ref[part, 0] = sum_ref[pl.ds(other, step), :]
+
+
+def diag(ensemble, increment, coords, core, parts):
     blocks, members, levels, points = ensemble.shape
-    step = levels // parts
+    step = levels // (2 * parts)
+    out = jax.ShapeDtypeStruct((parts, blocks, step, points), jnp.float32)
     return pl.pallas_call(
         diag_kernel,
-        grid=(blocks,),
-        in_specs=[
-            pl.BlockSpec((1, members, levels, points), lambda b: (b, 0, 0, 0)),
-            pl.BlockSpec((1, levels, points), lambda b: (b, 0, 0)),
-            pl.BlockSpec((1, 2, points), lambda b: (b, 0, 0)),
-        ],
-        out_specs=pl.BlockSpec((parts, 1, step, points), lambda b: (0, b, 0, 0)),
-        out_shape=jax.ShapeDtypeStruct((parts, blocks, step, points), jnp.bfloat16),
+        grid_spec=pltpu.PrefetchScalarGridSpec(
+            num_scalar_prefetch=1,
+            grid=(blocks,),
+            in_specs=[
+                pl.BlockSpec((1, members, levels, points), lambda b, c: (b, 0, 0, 0)),
+                pl.BlockSpec((1, levels, points), lambda b, c: (b, 0, 0)),
+                pl.BlockSpec((1, 2, points), lambda b, c: (b, 0, 0)),
+            ],
+            out_specs=[pl.BlockSpec((parts, 1, step, points), lambda b, c: (0, b, 0, 0))] * 2,
+            scratch_shapes=[pltpu.VMEM((levels, points), jnp.float32)],
+        ),
+        out_shape=[out, out],
         compiler_params=pltpu.CompilerParams(vmem_limit_bytes=60 * MIB),
         cost_estimate=pl.CostEstimate(flops=20_000_000_000, bytes_accessed=8_000_000, transcendentals=0),
         name="diag",
-    )(ensemble, increment, coords)
-
-
-def tiles_kernel(pairs, places_ref, out_ref):
-    first = pl.program_id(0) * TILE_GROUP
-    for within in range(TILE_GROUP):
-        left = left_rows(places_ref[pairs[0, first + within]].astype(jnp.float32))
-        right = right_rows(places_ref[pairs[1, first + within]].astype(jnp.float32))
+    )(core, ensemble, increment, coords)
+
+
+def merge_kernel(row, keep_ref, got_ref, own_ref, *send_refs):
+    parts = keep_ref.shape[0]
+    own_ref[...] = keep_ref[row[0]] + got_ref[row[0]]
+    for shift, send_ref in enumerate(send_refs, 1):
+        there = lax.rem(row[0] + shift, parts)
+        send_ref[...] = (keep_ref[there] + got_ref[there]).astype(send_ref.dtype)
+
+
+def merge(keep, got, row):
+    parts = keep.shape[0]
+    out = [jax.ShapeDtypeStruct(keep.shape[1:], jnp.float32)]
+    out += [jax.ShapeDtypeStruct(keep.shape[1:], jnp.bfloat16)] * (parts - 1)
+    return pl.pallas_call(
+        merge_kernel,
+        in_specs=[pl.BlockSpec(memory_space=pltpu.SMEM)] + [pl.BlockSpec(memory_space=pltpu.VMEM)] * 2,
+        out_specs=[pl.BlockSpec(memory_space=pltpu.VMEM)] * parts,
+        out_shape=out,
+        compiler_params=pltpu.CompilerParams(vmem_limit_bytes=16 * MIB),
+        name="merge",
+    )(row, keep, got)
+
+
+def tiles_kernel(pairs, first, places_ref, out_ref):
+    for within in range(out_ref.shape[0]):
+        index = first[0] + within
+        left = left_rows(places_ref[pairs[0, index]].astype(jnp.float32))
+        right = right_rows(places_ref[pairs[1, index]].astype(jnp.float32))
         out_ref[within] = tile_of(left, right)
 
 
-def tiles(places, pairs):
-    slot_total, _, points = places.shape
-    cap = pairs.shape[1]
+def tiles(places, pairs, first):
+    points = places.shape[2]
     return pl.pallas_call(
         tiles_kernel,
-        grid_spec=pltpu.PrefetchScalarGridSpec(
-            num_scalar_prefetch=1,
-            grid=(cap // TILE_GROUP,),
-            in_specs=[pl.BlockSpec((slot_total, 2, points), lambda i, p: (0, 0, 0))],
-            out_specs=pl.BlockSpec((TILE_GROUP, points, points), lambda i, p: (i, 0, 0)),
-        ),
-        out_shape=jax.ShapeDtypeStruct((cap, points, points), jnp.bfloat16),
+        in_specs=[
+            pl.BlockSpec(memory_space=pltpu.SMEM),
+            pl.BlockSpec(memory_space=pltpu.SMEM),
+            pl.BlockSpec(memory_space=pltpu.VMEM),
+        ],
+        out_specs=pl.BlockSpec(memory_space=pltpu.VMEM),
+        out_shape=jax.ShapeDtypeStruct((PAIR_GROUP, points, points), jnp.bfloat16),
         compiler_params=pltpu.CompilerParams(vmem_limit_bytes=60 * MIB),
-        cost_estimate=pl.CostEstimate(flops=30_000_000_000, bytes_accessed=17_000_000, transcendentals=0),
+        cost_estimate=pl.CostEstimate(flops=4_000_000_000, bytes_accessed=2_000_000, transcendentals=0),
         name="tiles",
-    )(pairs, places)
+    )(pairs, first, places)
 
 
 def apply_kernel(
-    pairs, count, got_ref, stack_ref, out_ref,
-    ens_ref, inc_ref, weighted_ref, field_ref, tiles_ref, ens_sem, inc_sem, tiles_sem,
+    pairs, count, core, got_ref, *refs,
 ):
+    *stacks, out_ref, ens_ref, inc_ref, weighted_ref, field_ref, tiles_ref, ens_sem, inc_sem, tiles_sem = refs
     slot_total, sources, rows, points = ens_ref.shape
     step = inc_ref.shape[2]
+    groups = len(stacks)
     lane_chunks = points // LANES
     every = sources * rows
 
@@ -232,15 +261,15 @@
 
     inc_copy = pltpu.make_async_copy(got_ref.at[:, :lane_chunks, rows * lane_chunks :, :], inc_ref, inc_sem)
 
-    def tile_copy(index):
-        return pltpu.make_async_copy(stack_ref.at[index], tiles_ref.at[index], tiles_sem.at[index])
+    def tile_copy(group):
+        return pltpu.make_async_copy(stacks[group], tiles_ref.at[group], tiles_sem.at[group])
 
     inc_copy.start()
     for slot in range(slot_total):
         for copy in ens_copies(slot):
             copy.start()
-    for index in range(tiles_ref.shape[0]):
-        tile_copy(index).start()
+    for group in range(groups):
+        tile_copy(group).start()
     inc_copy.wait()
     for slot in range(slot_total):
         field_ref[slot] = jnp.zeros((every, points), jnp.float32)
@@ -252,14 +281,11 @@
             block = ens_ref[slot, :, :, here].reshape(every // step, step, LANES)
             weighted_ref[slot, :, here] = (block * gain[None]).reshape(every, LANES)
 
-    def some(start, number):
+    def some(group, row, within, number):
         products = []
-        for within in range(number):
-            tile_copy(start + within).wait()
-        for within in range(number):
-            index = start + within
-            first, second = pairs[0, index], pairs[1, index]
-            tile = tiles_ref[index]
+        for each in range(number):
+            first, second = pairs[0, row + each], pairs[1, row + each]
+            tile = tiles_ref[group, within + each]
             to_first = lax.dot_general(
                 weighted_ref[second], tile, (((1,), (1,)), ((), ())), preferred_element_type=jnp.float32
             )
@@ -268,31 +294,36 @@
         for slot, product in products:
             field_ref[slot] += product
 
-    def group(turn, carry):
-        some(turn * PAIR_GROUP, PAIR_GROUP)
+    def turn(group, carry):
+        away = core[0] * (groups // 2)
+        row = PAIR_GROUP * jnp.where(group < groups // 2, group + away, group - away)
+        live = count[0] - row
+        pltpu.make_async_copy(stacks[0], tiles_ref.at[group], tiles_sem.at[group]).wait()
+
+        @pl.when(live >= PAIR_GROUP)
+        def _():
+            some(group, row, 0, PAIR_GROUP)
+
+        @pl.when(live < PAIR_GROUP)
+        def _():
+            def one(within, inner):
+                some(group, row + within, within, 1)
+                return inner
+
+            lax.fori_loop(0, jnp.maximum(live, 0), one, 0)
+
         return carry
 
-    def one(index, carry):
-        some(index, 1)
-        return carry
-
-    def skip(index, carry):
-        tile_copy(index).wait()
-        return carry
-
-    groups = count[0] // PAIR_GROUP
-    lax.fori_loop(0, groups, group, 0)
-    lax.fori_loop(groups * PAIR_GROUP, count[0], one, 0)
-    lax.fori_loop(count[0], tiles_ref.shape[0], skip, 0)
+    lax.fori_loop(0, groups, turn, 0)
 
     for slot in range(slot_total):
         product = ens_ref[slot].reshape(every, points).astype(jnp.float32) * field_ref[slot]
         out_ref[slot] = jnp.sum(product.reshape(every // step, step, points), axis=0)
 
 
-def apply_pairs(got, tile_stack, pairs, count, members, step):
+def apply_pairs(got, stacks, pairs, count, core, members, step):
     slot_total, sources, rows, _ = got.shape
-    points = tile_stack.shape[2]
+    points = stacks[0].shape[2]
     lane_chunks = points // LANES
     every = sources * members * step
     return pl.pallas_call(
@@ -300,8 +331,9 @@
         in_specs=[
             pl.BlockSpec(memory_space=pltpu.SMEM),
             pl.BlockSpec(memory_space=pltpu.SMEM),
+            pl.BlockSpec(memory_space=pltpu.SMEM),
             pl.BlockSpec(memory_space=pl.ANY),
-            pl.BlockSpec(memory_space=pl.ANY),
+            *[pl.BlockSpec(memory_space=pl.ANY)] * len(stacks),
         ],
         out_specs=pl.BlockSpec(memory_space=pltpu.VMEM),
         scratch_shapes=[
@@ -309,38 +341,38 @@
             pltpu.VMEM((slot_total, lane_chunks, step, LANES), jnp.bfloat16),
             pltpu.VMEM((slot_total, every, points), jnp.bfloat16),
             pltpu.VMEM((slot_total, every, points), jnp.float32),
-            pltpu.VMEM(tile_stack.shape, jnp.bfloat16),
+            pltpu.VMEM((len(stacks), *stacks[0].shape), jnp.bfloat16),
             pltpu.SemaphoreType.DMA((slot_total, lane_chunks)),
             pltpu.SemaphoreType.DMA,
-            pltpu.SemaphoreType.DMA((tile_stack.shape[0],)),
+            pltpu.SemaphoreType.DMA((len(stacks),)),
         ],
         out_shape=jax.ShapeDtypeStruct((slot_total, step, points), jnp.float32),
         compiler_params=pltpu.CompilerParams(vmem_limit_bytes=60 * MIB),
         cost_estimate=pl.CostEstimate(flops=9_000_000_000, bytes_accessed=22_000_000, transcendentals=0),
         name="apply",
-    )(pairs, count, got, tile_stack)
-
-
-def finish_kernel(slots, parts_ref, back_ref, out_ref, *, scale):
-    out_ref[...] = jnp.sum(parts_ref[...].astype(jnp.float32), axis=0) * scale
+    )(pairs, count, core, got, *stacks)
+
+
+def finish_kernel(slots, own_ref, *refs, scale):
+    *part_refs, back_ref, out_ref = refs
+    total = own_ref[...]
+    for part_ref in part_refs:
+        total = total + part_ref[...].astype(jnp.float32)
+    out_ref[...] = total * scale
     for owner in range(back_ref.shape[0]):
         slot = slots[owner]
         out_ref[slot] = out_ref[slot] + back_ref[owner] * scale
 
 
-def finish(parts, back, slots, scale):
+def finish(own, parts, back, slots, scale):
     return pl.pallas_call(
         functools.partial(finish_kernel, scale=scale),
-        in_specs=[
-            pl.BlockSpec(memory_space=pltpu.SMEM),
-            pl.BlockSpec(memory_space=pltpu.VMEM),
-            pl.BlockSpec(memory_space=pltpu.VMEM),
-        ],
+        in_specs=[pl.BlockSpec(memory_space=pltpu.SMEM)] + [pl.BlockSpec(memory_space=pltpu.VMEM)] * (len(parts) + 2),
         out_specs=pl.BlockSpec(memory_space=pltpu.VMEM),
-        out_shape=jax.ShapeDtypeStruct(parts.shape[1:], jnp.float32),
+        out_shape=jax.ShapeDtypeStruct(own.shape, jnp.float32),
         compiler_params=pltpu.CompilerParams(vmem_limit_bytes=16 * MIB),
         name="finish",
-    )(slots, parts, back)
+    )(slots, own, *parts, back)
 
 
 def per_device(ensemble, increment, coords, sent_slots, pair_list, pair_count):
@@ -358,14 +390,22 @@
     got = lax.all_to_all(
         big.reshape(regions * groups, -1, LANES), ("region", "member"), 0, 0, tiled=True
     ).reshape(regions, groups, -1, LANES)
-    diagonal = diag(ensemble, increment, coords, groups)
-    tile_stack = tiles(own_places, pairs)
-    got, diagonal, tile_stack = lax.optimization_barrier((got, diagonal, tile_stack))
-    parts = lax.all_to_all(diagonal, "member", 0, 0, tiled=True)
-    partial = apply_pairs(got, tile_stack, pairs, pair_count, members, step)
-    partial, parts = lax.optimization_barrier((partial, parts))
+    swap = [(i, i ^ 1) for i in range(groups)]
+    core, row = own & 1, own >> 1
+    rows = groups // 2
+    share = pairs.shape[1] // 2
+    mine = [tiles(own_places, pairs, core * share + start) for start in range(0, share, PAIR_GROUP)]
+    theirs = [lax.ppermute(stack, "member", swap) for stack in mine]
+    keep, send = diag(ensemble, increment, coords, core, rows)
+    merged = merge(keep, lax.ppermute(send, "member", swap), row)
+    parts = [
+        lax.ppermute(part, "member", [(i, (i + 2 * shift) % groups) for i in range(groups)])
+        for shift, part in enumerate(merged[1:], 1)
+    ]
+    got, parts = lax.optimization_barrier((got, parts))
+    partial = apply_pairs(got, mine + theirs, pairs, pair_count, core, members, step)
     back = lax.all_to_all(partial, "region", 0, 0, tiled=True)
-    return finish(parts, back, slots, 1.0 / (members * groups - 1))
+    return finish(merged[0], parts, back, slots, 1.0 / (members * groups - 1))
 
 
 def solution(mesh):

time: 119 us -> 129 us (1.084)
  waiting for transfers between devices: 10.9 us -> 22.9 us
  Pallas kernels: 71.7 us -> 61.9 us
  blocking collectives: 13.3 us -> 20.3 us
  local copies, waits for them, and re-layouts: 0.62 us -> 3.18 us
    ppermute x0 -> x8, waiting for transfers between devices: none -> 20.9 us  [the longest x3 18 us: per_device(): lax.ppermute(part, 'member', [(i, (i + 2 * shift) % groups) for i in rang...]
    all_to_all x1, waiting for transfers between devices: 7.8 us -> 0.01 us  [per_device(): lax.all_to_all(big.reshape(regions * groups, -1, LANES), ('region', 'memb...]
    pallas_call x2 -> x6, Pallas kernels: 47.6 us -> 40.3 us  [the longest x4 21.5 us: tiles(): pl.pallas_call(tiles_kernel, in_specs=[pl.BlockSpec(memory_space=pltpu.SM...]
    all_to_all x1, blocking collectives: 13.3 us -> 20.3 us  [per_device(): back = lax.all_to_all(partial, 'region', 0, 0, tiled=True)]
    all_to_all x1 -> x0, starting transfers between devices: 3.56 us -> none  [per_device(): parts = lax.all_to_all(diagonal, 'member', 0, 0, tiled=True)]
    unnamed x4 -> x8, local copies, waits for them, and re-layouts: 0.62 us -> 3.18 us
    ppermute x0 -> x8, starting transfers between devices: none -> 2.56 us  [the longest x3 1.53 us: per_device(): lax.ppermute(part, 'member', [(i, (i + 2 * shift) % groups) for i in rang...]
    pallas_call x1, Pallas kernels: 14.2 us -> 11.7 us  [apply_pairs(): pl.pallas_call(apply_kernel, in_specs=[pl.BlockSpec(memory_space=pltpu.SM...]
  transfers between devices with their start and end apart: 3 -> 10, of which waited for: 3 -> 5; matrix products, arithmetic and copies ran while one was open for 0% -> 0% of each run, Pallas kernels for 57% -> 36%
where the time goes in v5:
time: 129 us
  Pallas kernels  61.9 us (48%)
  waiting for transfers between devices  22.9 us (18%)
  blocking collectives  20.3 us (16%)
  starting transfers between devices  19.5 us (15%)
  local copies, waits for them, and re-layouts  3.18 us (2%)
    pallas_call x4, Pallas kernels, tiles(): pl.pallas_call(tiles_kernel, in_specs=[pl.BlockSpec(memory_space=pltpu.SM...  21.5 us
    all_to_all x1, blocking collectives, per_device(): back = lax.all_to_all(partial, 'region', 0, 0, tiled=True)  20.3 us
    pallas_call x1, Pallas kernels, diag(): pl.pallas_call(diag_kernel, grid_spec=pltpu.PrefetchScalarGridSpec(num_sc...  18.6 us
    ppermute x3, waiting for transfers between devices, per_device(): lax.ppermute(part, 'member', [(i, (i + 2 * shift) % groups) for i in rang...  18 us
    pallas_call x1, Pallas kernels, apply_pairs(): pl.pallas_call(apply_kernel, in_specs=[pl.BlockSpec(memory_space=pltpu.SM...  11.7 us
    all_to_all x1, starting transfers between devices, per_device(): lax.all_to_all(big.reshape(regions * groups, -1, LANES), ('region', 'memb...  9 us
    all_to_all x1, starting transfers between devices, per_device(): own_places = lax.all_to_all(places, 'region', 0, 0, tiled=True)  7.97 us
    pallas_call x1, Pallas kernels, pack(): pl.pallas_call(pack_kernel, in_specs=[pl.BlockSpec(memory_space=pltpu.SME...  5.57 us
  transfers between devices with their start and end apart: 10, of which 5 were waited for; matrix products, arithmetic and copies ran while one was open for 0% of the time, Pallas kernels for 36%

profile of v5, /device:TPU:0, one launch (start us, length us, event | category | flops | bytes accessed | tf_op | source)
XLA Modules:
  0.0 128.5 jit_solution(13391928551593065718)
XLA Ops:
  0.0 2.9 %select.1 = bf16[16,2,512]{2,1,0:T(2,128)(2,1)} custom-call(s32[16]{0:T(128)} %bitcast.5, bf16[16,2,512]{2,1,0:T(2,128)(2,1)} %coords_ref.3), custom_call_target="tpu_custom_call" | custom-call | tf_op jit(solution)/shard_map/select/pallas_call | solution.py:32
  2.9 8.0 %all-to-all-start = ((bf16[16,2,512]{2,1,0:T(2,128)(2,1)}), bf16[16,2,512]{2,1,0:T(2,128)(2,1)S(1)}, u32[]{:S(2)}, u32[]{:S(2)}) async-start(bf16[16,2,512]{2,1,0:T(2,128)(2,1)} %select.1), calls=%async_computation | async-start | bytes 65536 | tf_op jit(solution)/shard_map/all_to_all | solution.py:387
  10.9 5.6 %pack.1 = bf16[16,8,136,128]{3,2,1,0:T(8,128)(2,1)} custom-call(s32[16]{0:T(128)} %bitcast.6, s32[1]{0:T(128)} %bitcast.1.own, bf16[16,4,64,512]{3,2,1,0:T(8,128)(2,1)} %ens_ref.3, bf16[16,64,512]{2,1,0:T(8,128)(2,1)} %inc_ref.3), custom_call_target="tpu_custom_call" | custom-call | tf_op jit(solution)/shard_map/pack/pallas_call | solution.py:82
  16.5 2.0 %all-to-all-done.places_ref = bf16[16,2,512]{2,1,0:T(2,128)(2,1)S(1)} async-done(((bf16[16,2,512]{2,1,0:T(2,128)(2,1)}), bf16[16,2,512]{2,1,0:T(2,128)(2,1)S(1)}, u32[]{:S(2)}, u32[]{:S(2)}) %all-to-all-start) | async-done | bytes 32800 | tf_op jit(solution)/shard_map/all_to_all | solution.py:387
  18.5 0.6 copy-done.2
  19.1 9.0 %all-to-all-start.1 = ((bf16[128,136,128]{2,1,0:T(8,128)(2,1)}), bf16[128,136,128]{2,1,0:T(8,128)(2,1)}, u32[]{:S(2)}, u32[]{:S(2)}) async-start(bf16[128,136,128]{2,1,0:T(8,128)(2,1)} %bitcast.8), calls=%async_computation.1 | async-start | bytes 8912896 | tf_op jit(solution)/shard_map/all_to_all | solution.py:390
  28.1 5.4 %tiles.4.refs_0_ = bf16[4,512,512]{2,1,0:T(8,128)(2,1)} custom-call(s32[2,32]{1,0:T(2,128)} %bitcast.9, s32[1]{0:T(128)S(6)} %mul.2.first, bf16[16,2,512]{2,1,0:T(2,128)(2,1)} %copy-done.2), custom_call_target="tpu_custom_call" | custom-call | flops 4000000000 | bytes 2000000 | tf_op jit(solution)/shard_map/tiles/pallas_call | solution.py:227
  33.5 0.0 collective-permute-start.4
  33.5 5.5 %tiles.5.refs_1_ = bf16[4,512,512]{2,1,0:T(8,128)(2,1)} custom-call(s32[2,32]{1,0:T(2,128)} %bitcast.10, s32[1]{0:T(128)S(6)} %add.9.first, bf16[16,2,512]{2,1,0:T(2,128)(2,1)} %copy-done.2), custom_call_target="tpu_custom_call" | custom-call | flops 4000000000 | bytes 2000000 | tf_op jit(solution)/shard_map/tiles/pallas_call | solution.py:227
  39.0 0.5 collective-permute-start.5
  39.5 5.4 %tiles.6.refs_2_ = bf16[4,512,512]{2,1,0:T(8,128)(2,1)} custom-call(s32[2,32]{1,0:T(2,128)} %bitcast.11, s32[1]{0:T(128)S(6)} %add.10.first, bf16[16,2,512]{2,1,0:T(2,128)(2,1)} %copy-done.2), custom_call_target="tpu_custom_call" | custom-call | flops 4000000000 | bytes 2000000 | tf_op jit(solution)/shard_map/tiles/pallas_call | solution.py:227
  44.8 0.0 collective-permute-start.6
  44.8 5.3 %tiles.7.refs_3_ = bf16[4,512,512]{2,1,0:T(8,128)(2,1)} custom-call(s32[2,32]{1,0:T(2,128)} %bitcast.12, s32[1]{0:T(128)S(6)} %add.11.first, bf16[16,2,512]{2,1,0:T(2,128)(2,1)} %copy-done.2), custom_call_target="tpu_custom_call" | custom-call | flops 4000000000 | bytes 2000000 | tf_op jit(solution)/shard_map/tiles/pallas_call | solution.py:227
  50.2 0.5 collective-permute-start.7
  50.7 18.6 %diag.1 = (f32[4,16,8,512]{3,2,1,0:T(8,128)}, f32[4,16,8,512]{3,2,1,0:T(8,128)}) custom-call(s32[1]{0:T(128)S(6)} %and.4.core, bf16[16,4,64,512]{3,2,1,0:T(8,128)(2,1)} %ens_ref.3, bf16[16,64,512]{2,1,0:T(8,128)(2,1)} %inc_ref.3, bf16[16,2,512]{2,1,0:T(2,128)(2,1)} %coords_ref.3), custom_call_target="tpu_custom_call" | custom-call | flops 20000000000 | bytes 8000000 | tf_op jit(solution)/shard_map/diag/pallas_call | solution.py:175
  69.3 0.0 collective-permute-start
  69.3 2.9 %collective-permute-done.got_ref = f32[4,16,8,512]{3,2,1,0:T(8,128)S(1)} collective-permute-done((f32[4,16,8,512]{3,2,1,0:T(8,128)}, f32[4,16,8,512]{3,2,1,0:T(8,128)S(1)}, u32[]{:S(2)}, u32[]{:S(2)}) %collective-permute-start) | collective-permute-done | bytes 1048608 | tf_op jit(solution)/shard_map/ppermute | solution.py:400
  72.2 1.2 copy-done
  73.4 0.1 merge.1
  73.5 1.0 collective-permute-start.1
  74.5 7.7 %collective-permute-done.1.refs_0_ = bf16[16,8,512]{2,1,0:T(8,128)(2,1)S(1)} collective-permute-done((bf16[16,8,512]{2,1,0:T(8,128)(2,1)S(1)}, bf16[16,8,512]{2,1,0:T(8,128)(2,1)S(1)}, u32[]{:S(2)}, u32[]{:S(2)}) %collective-permute-start.1) | collective-permute-done | bytes 131104 | tf_op jit(solution)/shard_map/ppermute | solution.py:402
  82.2 0.1 collective-permute-start.2
  82.3 6.5 %collective-permute-done.2.refs_1_ = bf16[16,8,512]{2,1,0:T(8,128)(2,1)S(1)} collective-permute-done((bf16[16,8,512]{2,1,0:T(8,128)(2,1)S(1)}, bf16[16,8,512]{2,1,0:T(8,128)(2,1)S(1)}, u32[]{:S(2)}, u32[]{:S(2)}) %collective-permute-start.2) | collective-permute-done | bytes 131104 | tf_op jit(solution)/shard_map/ppermute | solution.py:402
  88.7 0.4 collective-permute-start.3
  89.8 3.9 %collective-permute-done.3.refs_2_ = bf16[16,8,512]{2,1,0:T(8,128)(2,1)S(1)} collective-permute-done((bf16[16,8,512]{2,1,0:T(8,128)(2,1)S(1)}, bf16[16,8,512]{2,1,0:T(8,128)(2,1)S(1)}, u32[]{:S(2)}, u32[]{:S(2)}) %collective-permute-start.3) | collective-permute-done | bytes 131104 | tf_op jit(solution)/shard_map/ppermute | solution.py:402
  93.7 0.0 all-to-all-done.1
  93.7 0.0 collective-permute-done.4.refs_4_
  93.7 0.0 collective-permute-done.5.refs_5_
  93.7 1.3 %copy-done.3 = bf16[4,512,512]{2,1,0:T(8,128)(2,1)} copy-done((bf16[4,512,512]{2,1,0:T(8,128)(2,1)}, bf16[4,512,512]{2,1,0:T(8,128)(2,1)S(1)}, u32[]{:S(2)}) %copy-start.3) | copy-done | bytes 2097176
  95.1 11.7 %apply.1 = f32[16,8,512]{2,1,0:T(8,128)} custom-call(s32[2,32]{1,0:T(2,128)} %bitcast.13, s32[1]{0:T(128)S(6)} %copy.7.count, s32[1]{0:T(128)S(6)} %and.4.core, bf16[16,8,136,128]{3,2,1,0:T(8,128)(2,1)} %bitcast.3.got_ref, bf16[4,512,512]{2,1,0:T(8,128)(2,1)} %tiles.4.refs_0_, bf16[4,512,512]{2,1,0:T(8,128)(2,1)} %tiles.5.refs_1_, ...), custom_call_target="tpu_custom_call" | custom-call | flops 8999999488 | bytes 22000000 | tf_op jit(solution)/shard_map/apply/pallas_call | solution.py:329
  106.8 20.3 %all_to_all.15.refs_3_ = f32[16,8,512]{2,1,0:T(8,128)S(1)} all-to-all(f32[16,8,512]{2,1,0:T(8,128)} %apply.1), channel_id=1, replica_groups=mesh['region'=16,'member'=8] {'region'}, dimensions={0} | all-to-all | bytes 524288 | tf_op jit(solution)/shard_map/all_to_all | solution.py:407
  127.1 1.4 %finish.1 = f32[16,8,512]{2,1,0:T(8,128)} custom-call(s32[16]{0:T(128)S(1)} %bitcast.7, f32[16,8,512]{2,1,0:T(8,128)S(1)} %get-tuple-element.19.own_ref, bf16[16,8,512]{2,1,0:T(8,128)(2,1)S(1)} %collective-permute-done.1.refs_0_, bf16[16,8,512]{2,1,0:T(8,128)(2,1)S(1)} %collective-permute-done.2.refs_1_, ...), custom_call_target="tpu_custom_call" | custom-call | tf_op jit(solution)/shard_map/finish/pallas_call | solution.py:368
  (7 shorter events, 0.0 us)
Async XLA Ops:
  2.9 15.6 %all-to-all-start = ((bf16[16,2,512]{2,1,0:T(2,128)(2,1)}), bf16[16,2,512]{2,1,0:T(2,128)(2,1)S(1)}, u32[]{:S(2)}, u32[]{:S(2)}) async-start(bf16[16,2,512]{2,1,0:T(2,128)(2,1)} %select.1), calls=%async_computation | async-start | bytes 65536 | tf_op jit(solution)/shard_map/all_to_all | solution.py:387
  18.5 0.6 copy-start.2
  19.1 74.6 %all-to-all-start.1 = ((bf16[128,136,128]{2,1,0:T(8,128)(2,1)}), bf16[128,136,128]{2,1,0:T(8,128)(2,1)}, u32[]{:S(2)}, u32[]{:S(2)}) async-start(bf16[128,136,128]{2,1,0:T(8,128)(2,1)} %bitcast.8), calls=%async_computation.1 | async-start | bytes 8912896 | tf_op jit(solution)/shard_map/all_to_all | solution.py:390
  33.5 60.2 %collective-permute-start.4 = (bf16[4,512,512]{2,1,0:T(8,128)(2,1)}, bf16[4,512,512]{2,1,0:T(8,128)(2,1)S(1)}, u32[]{:S(2)}, u32[]{:S(2)}) collective-permute-start(bf16[4,512,512]{2,1,0:T(8,128)(2,1)} %tiles.4.refs_0_), channel_id=1, source_target_pairs={{0,1},{1,0},{2,3},{3,2},{4,5},{5,4},{6,7},{7,6},{8,9},{9,8},{10,11... | collective-permute-start | bytes 6291464 | tf_op jit(solution)/shard_map/ppermute | solution.py:398
  39.0 54.8 %collective-permute-start.5 = (bf16[4,512,512]{2,1,0:T(8,128)(2,1)}, bf16[4,512,512]{2,1,0:T(8,128)(2,1)}, u32[]{:S(2)}, u32[]{:S(2)}) collective-permute-start(bf16[4,512,512]{2,1,0:T(8,128)(2,1)} %tiles.5.refs_1_), channel_id=1, source_target_pairs={{0,1},{1,0},{2,3},{3,2},{4,5},{5,4},{6,7},{7,6},{8,9},{9,8},{10,11... | collective-permute-start | bytes 6291464 | tf_op jit(solution)/shard_map/ppermute | solution.py:398
  44.8 48.9 %collective-permute-start.6 = (bf16[4,512,512]{2,1,0:T(8,128)(2,1)}, bf16[4,512,512]{2,1,0:T(8,128)(2,1)}, u32[]{:S(2)}, u32[]{:S(2)}) collective-permute-start(bf16[4,512,512]{2,1,0:T(8,128)(2,1)} %tiles.6.refs_2_), channel_id=1, source_target_pairs={{0,1},{1,0},{2,3},{3,2},{4,5},{5,4},{6,7},{7,6},{8,9},{9,8},{10,11... | collective-permute-start | bytes 6291464 | tf_op jit(solution)/shard_map/ppermute | solution.py:398
  50.2 43.6 %collective-permute-start.7 = (bf16[4,512,512]{2,1,0:T(8,128)(2,1)}, bf16[4,512,512]{2,1,0:T(8,128)(2,1)}, u32[]{:S(2)}, u32[]{:S(2)}) collective-permute-start(bf16[4,512,512]{2,1,0:T(8,128)(2,1)} %tiles.7.refs_3_), channel_id=1, source_target_pairs={{0,1},{1,0},{2,3},{3,2},{4,5},{5,4},{6,7},{7,6},{8,9},{9,8},{10,11... | collective-permute-start | bytes 6291464 | tf_op jit(solution)/shard_map/ppermute | solution.py:398
  69.3 2.9 %collective-permute-start = (f32[4,16,8,512]{3,2,1,0:T(8,128)}, f32[4,16,8,512]{3,2,1,0:T(8,128)S(1)}, u32[]{:S(2)}, u32[]{:S(2)}) collective-permute-start(f32[4,16,8,512]{3,2,1,0:T(8,128)} %get-tuple-element.18), channel_id=1, source_target_pairs={{0,1},{1,0},{2,3},{3,2},{4,5},{5,4},{6,7},{7,6},{8,9},{9,8},{10,11... | collective-permute-start | bytes 3145736 | tf_op jit(solution)/shard_map/ppermute | solution.py:400
  72.2 1.2 copy-start
  73.5 8.7 %collective-permute-start.1 = (bf16[16,8,512]{2,1,0:T(8,128)(2,1)S(1)}, bf16[16,8,512]{2,1,0:T(8,128)(2,1)S(1)}, u32[]{:S(2)}, u32[]{:S(2)}) collective-permute-start(bf16[16,8,512]{2,1,0:T(8,128)(2,1)S(1)} %get-tuple-element.21), channel_id=1, source_target_pairs={{0,2},{1,3},{2,4},{3,5},{4,6},{5,7},{6,0},{7,1},{8,10},{9,11},{10,... | collective-permute-start | bytes 393224 | tf_op jit(solution)/shard_map/ppermute | solution.py:402
  82.2 6.6 %collective-permute-start.2 = (bf16[16,8,512]{2,1,0:T(8,128)(2,1)S(1)}, bf16[16,8,512]{2,1,0:T(8,128)(2,1)S(1)}, u32[]{:S(2)}, u32[]{:S(2)}) collective-permute-start(bf16[16,8,512]{2,1,0:T(8,128)(2,1)S(1)} %get-tuple-element.22), channel_id=1, source_target_pairs={{0,4},{1,5},{2,6},{3,7},{4,0},{5,1},{6,2},{7,3},{8,12},{9,13},{10,... | collective-permute-start | bytes 393224 | tf_op jit(solution)/shard_map/ppermute | solution.py:402
  88.7 5.0 %collective-permute-start.3 = (bf16[16,8,512]{2,1,0:T(8,128)(2,1)S(1)}, bf16[16,8,512]{2,1,0:T(8,128)(2,1)S(1)}, u32[]{:S(2)}, u32[]{:S(2)}) collective-permute-start(bf16[16,8,512]{2,1,0:T(8,128)(2,1)S(1)} %get-tuple-element.23), channel_id=1, source_target_pairs={{0,6},{1,7},{2,0},{3,1},{4,2},{5,3},{6,4},{7,5},{8,14},{9,15},{10,... | collective-permute-start | bytes 393224 | tf_op jit(solution)/shard_map/ppermute | solution.py:402
  93.7 33.4 %copy-start.1 = (s32[1,16,1]{1,2,0:T(1,128)S(1)}, s32[1,16,1]{1,2,0:T(1,128)}, u32[]{:S(2)}) copy-start(s32[1,16,1]{1,2,0:T(1,128)} %param.9) | copy-start | bytes 196
  93.7 1.4 %copy-start.3 = (bf16[4,512,512]{2,1,0:T(8,128)(2,1)}, bf16[4,512,512]{2,1,0:T(8,128)(2,1)S(1)}, u32[]{:S(2)}) copy-start(bf16[4,512,512]{2,1,0:T(8,128)(2,1)S(1)} %collective-permute-done.4.refs_4_) | copy-start | bytes 6291460

commit v6 on v5

--- a/solution.py
+++ b/solution.py
@@ -1,4 +1,5 @@
 import functools
+import math
 
 import jax
 import jax.numpy as jnp
@@ -15,32 +16,9 @@
 LEAST = UNIT2 * 2.0**-12
 
 
-def select_kernel(slots, coords_ref, places_ref, sem):
-    total = places_ref.shape[0]
-
-    def copy(owner):
-        return pltpu.make_async_copy(coords_ref.at[slots[owner]], places_ref.at[owner], sem.at[owner])
-
-    for owner in range(total):
-        copy(owner).start()
-    for owner in range(total):
-        copy(owner).wait()
-
-
-def select(coords, slots):
-    total = slots.shape[0]
-    return pl.pallas_call(
-        select_kernel,
-        in_specs=[pl.BlockSpec(memory_space=pltpu.SMEM), pl.BlockSpec(memory_space=pl.ANY)],
-        out_specs=pl.BlockSpec(memory_space=pl.ANY),
-        out_shape=jax.ShapeDtypeStruct((total, *coords.shape[1:]), coords.dtype),
-        scratch_shapes=[pltpu.SemaphoreType.DMA((total,))],
-        compiler_params=pltpu.CompilerParams(vmem_limit_bytes=60 * MIB),
-        name="select",
-    )(slots, coords)
-
-
-def pack_kernel(slots, own, ens_ref, inc_ref, big_ref, ens_buf, inc_buf, out_buf, in_sem, inc_sem, out_sem):
+def pack_kernel(
+    slots, own, ens_ref, inc_ref, coords_ref, big_ref, places_ref, ens_buf, inc_buf, out_buf, in_sem, inc_sem, out_sem, places_sem
+):
     total, members, levels, points = ens_buf.shape
     parts = out_buf.shape[1]
     step = levels // parts
@@ -55,9 +33,14 @@
     def out_copy(owner):
         return pltpu.make_async_copy(out_buf.at[owner], big_ref.at[owner], out_sem.at[owner])
 
+    def places_copy(owner):
+        return pltpu.make_async_copy(coords_ref.at[slots[owner]], places_ref.at[owner], places_sem.at[owner])
+
     for owner in range(total):
         ens_copy(owner).start()
         inc_copy(owner).start()
+    for owner in range(total):
+        places_copy(owner).start()
     chunk = pl.multiple_of(lax.rem(own[0], lane_chunks) * LANES, LANES)
     for owner in range(total):
         ens_copy(owner).wait()
@@ -71,10 +54,11 @@
             out_buf[owner, part, members * step * lane_chunks :, :] = inc_buf[owner, here, pl.ds(chunk, LANES)]
         out_copy(owner).start()
     for owner in range(total):
+        places_copy(owner).wait()
         out_copy(owner).wait()
 
 
-def pack(ensemble, increment, slots, own, parts):
+def pack(ensemble, increment, coords, slots, own, parts):
     blocks, members, levels, points = ensemble.shape
     total = slots.shape[0]
     step = levels // parts
@@ -86,9 +70,13 @@
             pl.BlockSpec(memory_space=pltpu.SMEM),
             pl.BlockSpec(memory_space=pl.ANY),
             pl.BlockSpec(memory_space=pl.ANY),
+            pl.BlockSpec(memory_space=pl.ANY),
         ],
-        out_specs=pl.BlockSpec(memory_space=pl.ANY),
-        out_shape=jax.ShapeDtypeStruct((total, parts, rows, LANES), ensemble.dtype),
+        out_specs=[pl.BlockSpec(memory_space=pl.ANY)] * 2,
+        out_shape=[
+            jax.ShapeDtypeStruct((total, parts, rows, LANES), ensemble.dtype),
+            jax.ShapeDtypeStruct((total, *coords.shape[1:]), coords.dtype),
+        ],
         scratch_shapes=[
             pltpu.VMEM((total, members, levels, points), ensemble.dtype),
             pltpu.VMEM((total, levels, points), increment.dtype),
@@ -96,10 +84,15 @@
             pltpu.SemaphoreType.DMA((total,)),
             pltpu.SemaphoreType.DMA((total,)),
             pltpu.SemaphoreType.DMA((total,)),
+            pltpu.SemaphoreType.DMA((total,)),
         ],
         compiler_params=pltpu.CompilerParams(vmem_limit_bytes=60 * MIB),
         name="pack",
-    )(slots, own, ensemble, increment)
+    )(slots, own, ensemble, increment, coords)
+
+
+def in_hbm(value):
+    return pltpu.with_memory_space_constraint(value, pltpu.HBM)
 
 
 def three_parts(value):
@@ -168,8 +161,8 @@
         send_ref[part, 0] = sum_ref[pl.ds(other, step), :]
 
 
-def diag(ensemble, increment, coords, core, parts):
-    blocks, members, levels, points = ensemble.shape
+def diag(ensemble, increment, coords, core, parts, start, blocks):
+    _, members, levels, points = ensemble.shape
     step = levels // (2 * parts)
     out = jax.ShapeDtypeStruct((parts, blocks, step, points), jnp.float32)
     return pl.pallas_call(
@@ -178,65 +171,109 @@
             num_scalar_prefetch=1,
             grid=(blocks,),
             in_specs=[
-                pl.BlockSpec((1, members, levels, points), lambda b, c: (b, 0, 0, 0)),
-                pl.BlockSpec((1, levels, points), lambda b, c: (b, 0, 0)),
-                pl.BlockSpec((1, 2, points), lambda b, c: (b, 0, 0)),
+                pl.BlockSpec((1, members, levels, points), lambda b, c: (start + b, 0, 0, 0)),
+                pl.BlockSpec((1, levels, points), lambda b, c: (start + b, 0, 0)),
+                pl.BlockSpec((1, 2, points), lambda b, c: (start + b, 0, 0)),
             ],
             out_specs=[pl.BlockSpec((parts, 1, step, points), lambda b, c: (0, b, 0, 0))] * 2,
             scratch_shapes=[pltpu.VMEM((levels, points), jnp.float32)],
         ),
         out_shape=[out, out],
         compiler_params=pltpu.CompilerParams(vmem_limit_bytes=60 * MIB),
-        cost_estimate=pl.CostEstimate(flops=20_000_000_000, bytes_accessed=8_000_000, transcendentals=0),
+        cost_estimate=pl.CostEstimate(flops=10_000_000_000, bytes_accessed=8_000_000, transcendentals=0),
         name="diag",
     )(core, ensemble, increment, coords)
 
 
-def merge_kernel(row, keep_ref, got_ref, own_ref, *send_refs):
-    parts = keep_ref.shape[0]
-    own_ref[...] = keep_ref[row[0]] + got_ref[row[0]]
-    for shift, send_ref in enumerate(send_refs, 1):
-        there = lax.rem(row[0] + shift, parts)
-        send_ref[...] = (keep_ref[there] + got_ref[there]).astype(send_ref.dtype)
+def merge_kernel(row, near_keep, far_keep, near_got, far_got, own_ref, *send_refs):
+    parts, blocks = near_keep.shape[:2]
+    for half, (keep_ref, got_ref) in enumerate([(near_keep, near_got), (far_keep, far_got)]):
+        here = slice(half * blocks, (half + 1) * blocks)
+        own_ref[here] = keep_ref[row[0]] + got_ref[row[0]]
+        for shift, send_ref in enumerate(send_refs, 1):
+            there = lax.rem(row[0] + shift, parts)
+            send_ref[here] = (keep_ref[there] + got_ref[there]).astype(send_ref.dtype)
 
 
 def merge(keep, got, row):
-    parts = keep.shape[0]
-    out = [jax.ShapeDtypeStruct(keep.shape[1:], jnp.float32)]
-    out += [jax.ShapeDtypeStruct(keep.shape[1:], jnp.bfloat16)] * (parts - 1)
+    parts, blocks, step, points = keep[0].shape
+    out = [jax.ShapeDtypeStruct((2 * blocks, step, points), jnp.float32)]
+    out += [jax.ShapeDtypeStruct((2 * blocks, step, points), jnp.bfloat16)] * (parts - 1)
     return pl.pallas_call(
         merge_kernel,
-        in_specs=[pl.BlockSpec(memory_space=pltpu.SMEM)] + [pl.BlockSpec(memory_space=pltpu.VMEM)] * 2,
+        in_specs=[pl.BlockSpec(memory_space=pltpu.SMEM)] + [pl.BlockSpec(memory_space=pltpu.VMEM)] * 4,
         out_specs=[pl.BlockSpec(memory_space=pltpu.VMEM)] * parts,
         out_shape=out,
         compiler_params=pltpu.CompilerParams(vmem_limit_bytes=16 * MIB),
         name="merge",
-    )(row, keep, got)
-
-
-def tiles_kernel(pairs, first, places_ref, out_ref):
-    for within in range(out_ref.shape[0]):
-        index = first[0] + within
-        left = left_rows(places_ref[pairs[0, index]].astype(jnp.float32))
-        right = right_rows(places_ref[pairs[1, index]].astype(jnp.float32))
-        out_ref[within] = tile_of(left, right)
-
-
-def tiles(places, pairs, first):
-    points = places.shape[2]
+    )(row, *keep, *got)
+
+
+def route_kernel(slot, here_ref, *refs):
+    side = (len(refs) + 1) // 2
+    near, out_refs = (here_ref, *refs[: side - 1]), refs[side - 1 :]
+    for turn, out_ref in enumerate(out_refs):
+        owner = lax.rem(slot[0] + turn, side) * side + slot[1]
+        for back, near_ref in enumerate(near):
+            out_ref[back] = near_ref[owner]
+
+
+def route(here, near, slot):
+    side = len(near) + 1
+    out = jax.ShapeDtypeStruct((side, *here.shape[1:]), here.dtype)
+    return pl.pallas_call(
+        route_kernel,
+        in_specs=[pl.BlockSpec(memory_space=pltpu.SMEM)] + [pl.BlockSpec(memory_space=pltpu.VMEM)] * side,
+        out_specs=[pl.BlockSpec(memory_space=pltpu.VMEM)] * side,
+        out_shape=[out] * side,
+        compiler_params=pltpu.CompilerParams(vmem_limit_bytes=16 * MIB),
+        name="route",
+    )(slot, here, *near)
+
+
+def tiles_kernel(pairs, first, slot, *refs):
+    *places_refs, out_ref, tile_ref, sem = refs
+    side = len(places_refs)
+
+    def copy(within):
+        return pltpu.make_async_copy(tile_ref.at[within], out_ref.at[within], sem.at[within])
+
+    def places_of(home, stage_ref):
+        turn = lax.rem(slot[0] + side - home // side, side)
+        back = lax.rem(slot[1] + side - lax.rem(home, side), side)
+        for index, places_ref in enumerate(places_refs):
+
+            @pl.when(turn == index)
+            def _():
+                stage_ref[...] = places_ref[back].astype(jnp.float32)
+
+    def work(stage_ref):
+        for within in range(tile_ref.shape[0]):
+            places_of(pairs[0, first[0] + within], stage_ref.at[within, 0])
+            places_of(pairs[1, first[0] + within], stage_ref.at[within, 1])
+        for within in range(tile_ref.shape[0]):
+            tile_ref[within] = tile_of(left_rows(stage_ref[within, 0]), right_rows(stage_ref[within, 1]))
+            copy(within).start()
+        for within in range(tile_ref.shape[0]):
+            copy(within).wait()
+
+    pl.run_scoped(work, pltpu.VMEM((tile_ref.shape[0], 2, *places_refs[0].shape[1:]), jnp.float32))
+
+
+def tiles(places, pairs, first, slot):
+    points = places[0].shape[2]
+    shape = (PAIR_GROUP, points, points)
     return pl.pallas_call(
         tiles_kernel,
-        in_specs=[
-            pl.BlockSpec(memory_space=pltpu.SMEM),
-            pl.BlockSpec(memory_space=pltpu.SMEM),
-            pl.BlockSpec(memory_space=pltpu.VMEM),
-        ],
-        out_specs=pl.BlockSpec(memory_space=pltpu.VMEM),
-        out_shape=jax.ShapeDtypeStruct((PAIR_GROUP, points, points), jnp.bfloat16),
-        compiler_params=pltpu.CompilerParams(vmem_limit_bytes=60 * MIB),
+        in_specs=[pl.BlockSpec(memory_space=pltpu.SMEM)] * 3
+        + [pl.BlockSpec(memory_space=pltpu.VMEM)] * len(places),
+        out_specs=pl.BlockSpec(memory_space=pl.ANY),
+        out_shape=jax.ShapeDtypeStruct(shape, jnp.bfloat16),
+        scratch_shapes=[pltpu.VMEM(shape, jnp.bfloat16), pltpu.SemaphoreType.DMA((PAIR_GROUP,))],
+        compiler_params=pltpu.CompilerParams(vmem_limit_bytes=16 * MIB),
         cost_estimate=pl.CostEstimate(flops=4_000_000_000, bytes_accessed=2_000_000, transcendentals=0),
         name="tiles",
-    )(pairs, first, places)
+    )(pairs, first, slot, *places)
 
 
 def apply_kernel(
@@ -383,26 +420,49 @@
     slots = sent_slots.reshape(-1)
     pairs = pair_list.T
     own = lax.axis_index("member").reshape(1).astype(jnp.int32)
-    places = select(coords, slots)
-    own_places = lax.all_to_all(places, "region", 0, 0, tiled=True)
-    big = pack(ensemble, increment, slots, own, groups)
-    big, own_places = lax.optimization_barrier((big, own_places))
+    core, row = own & 1, own >> 1
+    rows = groups // 2
+    side = math.isqrt(regions)
+    region = lax.axis_index("region").astype(jnp.int32)
+    slot = jnp.stack([region // side, lax.rem(region, side)])
+    big, places = pack(ensemble, increment, coords, slots, own, groups)
     got = lax.all_to_all(
         big.reshape(regions * groups, -1, LANES), ("region", "member"), 0, 0, tiled=True
     ).reshape(regions, groups, -1, LANES)
+
+    near = [
+        lax.ppermute(places, "region", [(i, i - i % side + (i + hop) % side) for i in range(regions)])
+        for hop in range(1, side)
+    ]
+    halves = [diag(ensemble, increment, coords, core, rows, 0, blocks // 2)]
+    near, halves[0] = lax.optimization_barrier((near, halves[0]))
+    own_places, *sent = route(places, near, slot)
+    own_places = [own_places] + [
+        lax.ppermute(part, "region", [(i, (i + hop * side) % regions) for i in range(regions)])
+        for hop, part in enumerate(sent, 1)
+    ]
+    increment_later, _ = lax.optimization_barrier((increment, sent[0]))
+    halves.append(diag(ensemble, increment_later, coords, core, rows, blocks // 2, blocks // 2))
+    own_places, halves[1] = lax.optimization_barrier((own_places, halves[1]))
+
     swap = [(i, i ^ 1) for i in range(groups)]
-    core, row = own & 1, own >> 1
-    rows = groups // 2
+    merged = merge(
+        [keep for keep, _ in halves], [lax.ppermute(send, "member", swap) for _, send in halves], row
+    )
+    parts = [
+        lax.ppermute(part, "member", [(i, (i + 2 * hop) % groups) for i in range(groups)])
+        for hop, part in enumerate(merged[1:], 1)
+    ]
     share = pairs.shape[1] // 2
-    mine = [tiles(own_places, pairs, core * share + start) for start in range(0, share, PAIR_GROUP)]
+    mine = []
+    for start in range(0, share, PAIR_GROUP):
+        if len(mine) == 1:
+            own_places, merged = lax.optimization_barrier((own_places, merged))
+        if len(mine) == 2:
+            own_places, parts = lax.optimization_barrier((own_places, parts))
+        mine.append(tiles(own_places, pairs, core * share + start, slot))
     theirs = [lax.ppermute(stack, "member", swap) for stack in mine]
-    keep, send = diag(ensemble, increment, coords, core, rows)
-    merged = merge(keep, lax.ppermute(send, "member", swap), row)
-    parts = [
-        lax.ppermute(part, "member", [(i, (i + 2 * shift) % groups) for i in range(groups)])
-        for shift, part in enumerate(merged[1:], 1)
-    ]
-    got, parts = lax.optimization_barrier((got, parts))
+    got, mine, theirs = in_hbm(got), [in_hbm(x) for x in mine], [in_hbm(x) for x in theirs]
     partial = apply_pairs(got, mine + theirs, pairs, pair_count, core, members, step)
     back = lax.all_to_all(partial, "region", 0, 0, tiled=True)
     return finish(merged[0], parts, back, slots, 1.0 / (members * groups - 1))

time: 129 us -> 139 us (1.078)
  starting transfers between devices: 19.5 us -> 46.5 us
  waiting for transfers between devices: 22.9 us -> 5.95 us
  Pallas kernels: 61.9 us -> 64.1 us
  local copies, waits for them, and re-layouts: 3.18 us -> 1.41 us
    ppermute x4 -> x11, starting transfers between devices: 1.54 us -> 34.9 us  [the longest x3 23.9 us: per_device(): lax.ppermute(part, 'member', [(i, (i + 2 * hop) % groups) for i in range(...]
    ppermute x4 -> x11, waiting for transfers between devices: 20.9 us -> 1.02 us  [the longest x3 1 us: per_device(): lax.ppermute(part, 'member', [(i, (i + 2 * hop) % groups) for i in range(...]
    all_to_all x1 -> x0, starting transfers between devices: 7.97 us -> none  [per_device(): own_places = lax.all_to_all(places, 'region', 0, 0, tiled=True)]
    ppermute x4, waiting for transfers between devices: 0.01 us -> 4.92 us  [per_device(): theirs = [lax.ppermute(stack, 'member', swap) for stack in mine]]
    pallas_call x1, Pallas kernels: 11.7 us -> 16.1 us  [apply_pairs(): pl.pallas_call(apply_kernel, in_specs=[pl.BlockSpec(memory_space=pltpu.SM...]
    pallas_call x1, Pallas kernels: 2.9 us -> 0.56 us  [route(): pl.pallas_call(route_kernel, in_specs=[pl.BlockSpec(memory_space=pltpu.SM...]
    all_to_all x1 -> x0, waiting for transfers between devices: 2.01 us -> none  [per_device(): own_places = lax.all_to_all(places, 'region', 0, 0, tiled=True)]
    unnamed x8 -> x24, local copies, waits for them, and re-layouts: 3.18 us -> 1.41 us
  transfers between devices with their start and end apart: 10 -> 16, of which waited for: 5 -> 2; matrix products, arithmetic and copies ran while one was open for 0% -> 0% of each run, Pallas kernels for 36% -> 30%
where the time goes in v6:
time: 139 us; the launch traced here: 138 us
  Pallas kernels  64.1 us (46%)
  starting transfers between devices  46.5 us (33%)
  blocking collectives  19 us (14%)
  waiting for transfers between devices  5.95 us (4%)
  local copies, waits for them, and re-layouts  1.41 us (1%)
    ppermute x3, starting transfers between devices, per_device(): lax.ppermute(part, 'member', [(i, (i + 2 * hop) % groups) for i in range(...  23.9 us
    pallas_call x2, Pallas kernels, diag(): pl.pallas_call(diag_kernel, grid_spec=pltpu.PrefetchScalarGridSpec(num_sc...  20.3 us
    pallas_call x4, Pallas kernels, tiles(): pl.pallas_call(tiles_kernel, in_specs=[pl.BlockSpec(memory_space=pltpu.SM...  19.8 us
    all_to_all x1, blocking collectives, per_device(): back = lax.all_to_all(partial, 'region', 0, 0, tiled=True)  19 us
    pallas_call x1, Pallas kernels, apply_pairs(): pl.pallas_call(apply_kernel, in_specs=[pl.BlockSpec(memory_space=pltpu.SM...  16.1 us
    all_to_all x1, starting transfers between devices, per_device(): lax.all_to_all(big.reshape(regions * groups, -1, LANES), ('region', 'memb...  10.6 us
    pallas_call x1, Pallas kernels, pack(): pl.pallas_call(pack_kernel, in_specs=[pl.BlockSpec(memory_space=pltpu.SME...  5.76 us
    ppermute x3, starting transfers between devices, per_device(): lax.ppermute(part, 'region', [(i, (i + hop * side) % regions) for i in ra...  5.49 us
  transfers between devices with their start and end apart: 16, of which 2 were waited for; matrix products, arithmetic and copies ran while one was open for 0% of the time, Pallas kernels for 30%

profile of v6, /device:TPU:0, one launch (start us, length us, event | category | flops | bytes accessed | tf_op | source)
XLA Modules:
  0.0 137.9 jit_solution(14639009361504919136)
XLA Ops:
  0.0 5.8 %pack.1 = (bf16[16,8,136,128]{3,2,1,0:T(8,128)(2,1)}, bf16[16,2,512]{2,1,0:T(2,128)(2,1)}) custom-call(s32[16]{0:T(128)} %bitcast.7, s32[1]{0:T(128)} %bitcast.3.own, bf16[16,4,64,512]{3,2,1,0:T(8,128)(2,1)} %ens_ref.5, bf16[16,64,512]{2,1,0:T(8,128)(2,1)} %inc_ref.4, bf16[16,2,512]{2,1,0:T(2,128)(2,1)} %coords_ref.5), custom_call_target="tpu_custom_call" | custom-call | tf_op jit(solution)/shard_map/pack/pallas_call | solution.py:66
  5.8 3.1 %collective-permute-start.2 = (bf16[16,2,512]{2,1,0:T(2,128)(2,1)}, bf16[16,2,512]{2,1,0:T(2,128)(2,1)S(1)}, u32[]{:S(2)}, u32[]{:S(2)}) collective-permute-start(bf16[16,2,512]{2,1,0:T(2,128)(2,1)} %get-tuple-element.43.here_ref), channel_id=1, source_target_pairs={{0,24},{8,0},{16,8},{24,16},{32,56},{40,32},{48,40},{56,48},{64,88... | collective-permute-start | bytes 98312 | tf_op jit(solution)/shard_map/ppermute | solution.py:434
  8.8 0.6 collective-permute-start.1
  9.5 1.2 collective-permute-start
  10.6 10.6 %all-to-all-start = ((bf16[128,136,128]{2,1,0:T(8,128)(2,1)}), bf16[128,136,128]{2,1,0:T(8,128)(2,1)}, u32[]{:S(2)}, u32[]{:S(2)}) async-start(bf16[128,136,128]{2,1,0:T(8,128)(2,1)} %bitcast.14), calls=%async_computation | async-start | bytes 8912896 | tf_op jit(solution)/shard_map/all_to_all | solution.py:429
  21.3 0.0 copy-start.2
  21.3 10.2 %diag.2 = (f32[4,8,8,512]{3,2,1,0:T(8,128)}, f32[4,8,8,512]{3,2,1,0:T(8,128)}) custom-call(s32[1]{0:T(128)S(6)} %and.11.core, bf16[16,4,64,512]{3,2,1,0:T(8,128)(2,1)} %ens_ref.5, bf16[16,64,512]{2,1,0:T(8,128)(2,1)} %inc_ref.4, bf16[16,2,512]{2,1,0:T(2,128)(2,1)} %coords_ref.5), custom_call_target="tpu_custom_call" | custom-call | flops 10000000000 | bytes 8000000 | tf_op jit(solution)/shard_map/diag/pallas_call | solution.py:168
  31.5 0.1 pad_add_fusion.slot
  31.6 0.6 route.1
  32.1 1.1 collective-permute-start.3
  33.2 3.2 %collective-permute-start.4 = (bf16[4,2,512]{2,1,0:T(2,128)(2,1)S(1)}, bf16[4,2,512]{2,1,0:T(2,128)(2,1)S(1)}, u32[]{:S(2)}, u32[]{:S(2)}) collective-permute-start(bf16[4,2,512]{2,1,0:T(2,128)(2,1)S(1)} %get-tuple-element.51), channel_id=1, source_target_pairs={{0,64},{8,72},{16,80},{24,88},{32,96},{40,104},{48,112},{56,120},{... | collective-permute-start | bytes 24584 | tf_op jit(solution)/shard_map/ppermute | solution.py:441
  36.4 1.2 collective-permute-start.5
  37.6 10.2 %diag.3 = (f32[4,8,8,512]{3,2,1,0:T(8,128)}, f32[4,8,8,512]{3,2,1,0:T(8,128)}) custom-call(s32[1]{0:T(128)S(6)} %and.11.core, bf16[16,4,64,512]{3,2,1,0:T(8,128)(2,1)} %ens_ref.5, bf16[16,64,512]{2,1,0:T(8,128)(2,1)} %inc_ref.4, bf16[16,2,512]{2,1,0:T(2,128)(2,1)} %coords_ref.5), custom_call_target="tpu_custom_call" | custom-call | flops 10000000000 | bytes 8000000 | tf_op jit(solution)/shard_map/diag/pallas_call | solution.py:168
  47.8 0.6 collective-permute-start.7
  48.4 4.9 %tiles.4.refs_0_ = bf16[4,512,512]{2,1,0:T(8,128)(2,1)S(1)} custom-call(s32[2,32]{1,0:T(2,128)S(1)} %bitcast.10, s32[1]{0:T(128)S(6)} %mul.2.first, s32[2]{0:T(128)S(1)} %pad_add_fusion.slot, bf16[4,2,512]{2,1,0:T(2,128)(2,1)S(1)} %get-tuple-element.77.refs_0_, bf16[4,2,512]{2,1,0:T(2,128)(2,1)S(1)} %collective-permute-done.3.refs_1_, ...), custom_call_target="tpu_custom_call" | custom-call | flops 4000000000 | bytes 2000000 | tf_op jit(solution)/shard_map/tiles/pallas_call | solution.py:266
  53.3 0.1 collective-permute-start.11
  53.5 0.1 merge.1
  53.6 12.7 %collective-permute-start.8 = (bf16[16,8,512]{2,1,0:T(8,128)(2,1)S(1)}, bf16[16,8,512]{2,1,0:T(8,128)(2,1)S(1)}, u32[]{:S(2)}, u32[]{:S(2)}) collective-permute-start(bf16[16,8,512]{2,1,0:T(8,128)(2,1)S(1)} %get-tuple-element.65), channel_id=1, source_target_pairs={{0,2},{1,3},{2,4},{3,5},{4,6},{5,7},{6,0},{7,1},{8,10},{9,11},{10,... | collective-permute-start | bytes 393224 | tf_op jit(solution)/shard_map/ppermute | solution.py:453
  66.3 11.2 %collective-permute-start.9 = (bf16[16,8,512]{2,1,0:T(8,128)(2,1)S(1)}, bf16[16,8,512]{2,1,0:T(8,128)(2,1)S(1)}, u32[]{:S(2)}, u32[]{:S(2)}) collective-permute-start(bf16[16,8,512]{2,1,0:T(8,128)(2,1)S(1)} %get-tuple-element.66), channel_id=1, source_target_pairs={{0,4},{1,5},{2,6},{3,7},{4,0},{5,1},{6,2},{7,3},{8,12},{9,13},{10,... | collective-permute-start | bytes 393224 | tf_op jit(solution)/shard_map/ppermute | solution.py:453
  77.6 5.1 %tiles.5.refs_1_ = bf16[4,512,512]{2,1,0:T(8,128)(2,1)S(1)} custom-call(s32[2,32]{1,0:T(2,128)S(1)} %bitcast.11, s32[1]{0:T(128)S(6)} %add.10.first, s32[2]{0:T(128)S(1)} %pad_add_fusion.slot, bf16[4,2,512]{2,1,0:T(2,128)(2,1)S(1)} %get-tuple-element.77.refs_0_, bf16[4,2,512]{2,1,0:T(2,128)(2,1)S(1)} %collective-permute-done.3.refs_1_, ...), custom_call_target="tpu_custom_call" | custom-call | flops 4000000000 | bytes 2000000 | tf_op jit(solution)/shard_map/tiles/pallas_call | solution.py:266
  82.7 0.1 collective-permute-start.12
  82.8 1.0 collective-permute-done.9.refs_1_
  83.8 4.9 %tiles.7.refs_3_ = bf16[4,512,512]{2,1,0:T(8,128)(2,1)S(1)} custom-call(s32[2,32]{1,0:T(2,128)S(1)} %bitcast.12, s32[1]{0:T(128)S(6)} %add.12.first, s32[2]{0:T(128)S(1)} %pad_add_fusion.slot, bf16[4,2,512]{2,1,0:T(2,128)(2,1)S(1)} %get-tuple-element.77.refs_0_, bf16[4,2,512]{2,1,0:T(2,128)(2,1)S(1)} %collective-permute-done.3.refs_1_, ...), custom_call_target="tpu_custom_call" | custom-call | flops 4000000000 | bytes 2000000 | tf_op jit(solution)/shard_map/tiles/pallas_call | solution.py:266
  88.7 4.9 %tiles.6.refs_2_ = bf16[4,512,512]{2,1,0:T(8,128)(2,1)S(1)} custom-call(s32[2,32]{1,0:T(2,128)S(1)} %bitcast.13, s32[1]{0:T(128)S(6)} %add.11.first, s32[2]{0:T(128)S(1)} %pad_add_fusion.slot, bf16[4,2,512]{2,1,0:T(2,128)(2,1)S(1)} %get-tuple-element.77.refs_0_, bf16[4,2,512]{2,1,0:T(2,128)(2,1)S(1)} %collective-permute-done.3.refs_1_, ...), custom_call_target="tpu_custom_call" | custom-call | flops 4000000000 | bytes 2000000 | tf_op jit(solution)/shard_map/tiles/pallas_call | solution.py:266
  93.6 0.3 collective-permute-start.13
  94.0 0.5 collective-permute-start.14
  95.2 4.9 %collective-permute-done.13.refs_6_ = bf16[4,512,512]{2,1,0:T(8,128)(2,1)S(1)} collective-permute-done((bf16[4,512,512]{2,1,0:T(8,128)(2,1)S(1)}, bf16[4,512,512]{2,1,0:T(8,128)(2,1)S(1)}, u32[]{:S(2)}, u32[]{:S(2)}) %collective-permute-start.13) | collective-permute-done | bytes 2097184 | tf_op jit(solution)/shard_map/ppermute | solution.py:464
  100.1 1.4 copy-done.11
  101.5 0.0 copy-start.3
  101.5 16.1 %apply.1 = f32[16,8,512]{2,1,0:T(8,128)} custom-call(s32[2,32]{1,0:T(2,128)} %bitcast.9, s32[1]{0:T(128)S(6)} %copy.7.count, s32[1]{0:T(128)S(6)} %and.11.core, bf16[16,8,136,128]{3,2,1,0:T(8,128)(2,1)} %bitcast.6.got_ref, bf16[4,512,512]{2,1,0:T(8,128)(2,1)} %copy-done.4, bf16[4,512,512]{2,1,0:T(8,128)(2,1)} %copy-done.5, bf16[4,512,512]{2,1,0:T(8,128)(2,1)} %copy-done.7, ...), custom_call_target="tpu_custom_call" | custom-call | flops 8999999488 | bytes 22000000 | tf_op jit(solution)/shard_map/apply/pallas_call | solution.py:366
  117.5 19.0 %all_to_all.10.refs_3_ = f32[16,8,512]{2,1,0:T(8,128)S(1)} all-to-all(f32[16,8,512]{2,1,0:T(8,128)} %apply.1), channel_id=1, replica_groups=mesh['region'=16,'member'=8] {'region'}, dimensions={0} | all-to-all | bytes 524288 | tf_op jit(solution)/shard_map/all_to_all | solution.py:467
  136.5 1.4 %finish.1 = f32[16,8,512]{2,1,0:T(8,128)} custom-call(s32[16]{0:T(128)S(1)} %bitcast.8, f32[16,8,512]{2,1,0:T(8,128)S(1)} %get-tuple-element.68.own_ref, bf16[16,8,512]{2,1,0:T(8,128)(2,1)S(1)} %collective-permute-done.8.refs_0_, bf16[16,8,512]{2,1,0:T(8,128)(2,1)S(1)} %collective-permute-done.9.refs_1_, ...), custom_call_target="tpu_custom_call" | custom-call | tf_op jit(solution)/shard_map/finish/pallas_call | solution.py:405
  (37 shorter events, 0.1 us)
Async XLA Ops:
  5.8 25.8 %collective-permute-start.2 = (bf16[16,2,512]{2,1,0:T(2,128)(2,1)}, bf16[16,2,512]{2,1,0:T(2,128)(2,1)S(1)}, u32[]{:S(2)}, u32[]{:S(2)}) collective-permute-start(bf16[16,2,512]{2,1,0:T(2,128)(2,1)} %get-tuple-element.43.here_ref), channel_id=1, source_target_pairs={{0,24},{8,0},{16,8},{24,16},{32,56},{40,32},{48,40},{56,48},{64,88... | collective-permute-start | bytes 98312 | tf_op jit(solution)/shard_map/ppermute | solution.py:434
  8.8 22.7 %collective-permute-start.1 = (bf16[16,2,512]{2,1,0:T(2,128)(2,1)}, bf16[16,2,512]{2,1,0:T(2,128)(2,1)S(1)}, u32[]{:S(2)}, u32[]{:S(2)}) collective-permute-start(bf16[16,2,512]{2,1,0:T(2,128)(2,1)} %get-tuple-element.43.here_ref), channel_id=1, source_target_pairs={{0,16},{8,24},{16,0},{24,8},{32,48},{40,56},{48,32},{56,40},{64,80... | collective-permute-start | bytes 98312 | tf_op jit(solution)/shard_map/ppermute | solution.py:434
  9.5 22.1 %collective-permute-start = (bf16[16,2,512]{2,1,0:T(2,128)(2,1)}, bf16[16,2,512]{2,1,0:T(2,128)(2,1)S(1)}, u32[]{:S(2)}, u32[]{:S(2)}) collective-permute-start(bf16[16,2,512]{2,1,0:T(2,128)(2,1)} %get-tuple-element.43.here_ref), channel_id=1, source_target_pairs={{0,8},{8,16},{16,24},{24,0},{32,40},{40,48},{48,56},{56,32},{64,72... | collective-permute-start | bytes 98312 | tf_op jit(solution)/shard_map/ppermute | solution.py:434
  10.6 90.8 %all-to-all-start = ((bf16[128,136,128]{2,1,0:T(8,128)(2,1)}), bf16[128,136,128]{2,1,0:T(8,128)(2,1)}, u32[]{:S(2)}, u32[]{:S(2)}) async-start(bf16[128,136,128]{2,1,0:T(8,128)(2,1)} %bitcast.14), calls=%async_computation | async-start | bytes 8912896 | tf_op jit(solution)/shard_map/all_to_all | solution.py:429
  21.3 10.3 %copy-start.2 = (bf16[16,2,512]{2,1,0:T(2,128)(2,1)S(1)}, bf16[16,2,512]{2,1,0:T(2,128)(2,1)}, u32[]{:S(2)}) copy-start(bf16[16,2,512]{2,1,0:T(2,128)(2,1)} %get-tuple-element.43.here_ref) | copy-start | bytes 98308
  32.1 15.7 %collective-permute-start.3 = (bf16[4,2,512]{2,1,0:T(2,128)(2,1)S(1)}, bf16[4,2,512]{2,1,0:T(2,128)(2,1)S(1)}, u32[]{:S(2)}, u32[]{:S(2)}) collective-permute-start(bf16[4,2,512]{2,1,0:T(2,128)(2,1)S(1)} %get-tuple-element.50), channel_id=1, source_target_pairs={{0,32},{8,40},{16,48},{24,56},{32,64},{40,72},{48,80},{56,88},{64,... | collective-permute-start | bytes 24584 | tf_op jit(solution)/shard_map/ppermute | solution.py:441
  33.2 14.6 %collective-permute-start.4 = (bf16[4,2,512]{2,1,0:T(2,128)(2,1)S(1)}, bf16[4,2,512]{2,1,0:T(2,128)(2,1)S(1)}, u32[]{:S(2)}, u32[]{:S(2)}) collective-permute-start(bf16[4,2,512]{2,1,0:T(2,128)(2,1)S(1)} %get-tuple-element.51), channel_id=1, source_target_pairs={{0,64},{8,72},{16,80},{24,88},{32,96},{40,104},{48,112},{56,120},{... | collective-permute-start | bytes 24584 | tf_op jit(solution)/shard_map/ppermute | solution.py:441
  36.4 12.0 %copy-start.8 = (s32[32,2]{0,1:T(2,128)S(1)}, s32[32,2]{0,1:T(2,128)}, u32[]{:S(2)}) copy-start(s32[32,2]{0,1:T(2,128)} %param.10) | copy-start | bytes 772
  36.4 11.4 %collective-permute-start.5 = (bf16[4,2,512]{2,1,0:T(2,128)(2,1)S(1)}, bf16[4,2,512]{2,1,0:T(2,128)(2,1)S(1)}, u32[]{:S(2)}, u32[]{:S(2)}) collective-permute-start(bf16[4,2,512]{2,1,0:T(2,128)(2,1)S(1)} %get-tuple-element.52), channel_id=1, source_target_pairs={{0,96},{8,104},{16,112},{24,120},{32,0},{40,8},{48,16},{56,24},{64... | collective-permute-start | bytes 24584 | tf_op jit(solution)/shard_map/ppermute | solution.py:441
  37.6 15.8 %collective-permute-start.6 = (f32[4,8,8,512]{3,2,1,0:T(8,128)}, f32[4,8,8,512]{3,2,1,0:T(8,128)S(1)}, u32[]{:S(2)}, u32[]{:S(2)}) collective-permute-start(f32[4,8,8,512]{3,2,1,0:T(8,128)} %get-tuple-element.62), channel_id=1, source_target_pairs={{0,1},{1,0},{2,3},{3,2},{4,5},{5,4},{6,7},{7,6},{8,9},{9,8},{10,11... | collective-permute-start | bytes 1572872 | tf_op jit(solution)/shard_map/ppermute | solution.py:450
  47.8 5.6 %collective-permute-start.7 = (f32[4,8,8,512]{3,2,1,0:T(8,128)}, f32[4,8,8,512]{3,2,1,0:T(8,128)S(1)}, u32[]{:S(2)}, u32[]{:S(2)}) collective-permute-start(f32[4,8,8,512]{3,2,1,0:T(8,128)} %get-tuple-element.63), channel_id=1, source_target_pairs={{0,1},{1,0},{2,3},{3,2},{4,5},{5,4},{6,7},{7,6},{8,9},{9,8},{10,11... | collective-permute-start | bytes 1572872 | tf_op jit(solution)/shard_map/ppermute | solution.py:450
  48.4 5.1 %copy-start = (f32[4,8,8,512]{3,2,1,0:T(8,128)S(1)}, f32[4,8,8,512]{3,2,1,0:T(8,128)}, u32[]{:S(2)}) copy-start(f32[4,8,8,512]{3,2,1,0:T(8,128)} %get-tuple-element.60.near_keep) | copy-start | bytes 1572868
  48.4 5.1 %copy-start.1 = (f32[4,8,8,512]{3,2,1,0:T(8,128)S(1)}, f32[4,8,8,512]{3,2,1,0:T(8,128)}, u32[]{:S(2)}) copy-start(f32[4,8,8,512]{3,2,1,0:T(8,128)} %get-tuple-element.61.far_keep) | copy-start | bytes 1572868
  53.3 29.3 %copy-start.4 = (bf16[4,512,512]{2,1,0:T(8,128)(2,1)}, bf16[4,512,512]{2,1,0:T(8,128)(2,1)S(1)}, u32[]{:S(2)}) copy-start(bf16[4,512,512]{2,1,0:T(8,128)(2,1)S(1)} %tiles.4.refs_0_) | copy-start | bytes 6291460
  53.3 41.8 %collective-permute-start.11 = (bf16[4,512,512]{2,1,0:T(8,128)(2,1)S(1)}, bf16[4,512,512]{2,1,0:T(8,128)(2,1)S(1)}, u32[]{:S(2)}, u32[]{:S(2)}) collective-permute-start(bf16[4,512,512]{2,1,0:T(8,128)(2,1)S(1)} %tiles.4.refs_0_), channel_id=1, source_target_pairs={{0,1},{1,0},{2,3},{3,2},{4,5},{5,4},{6,7},{7,6},{8,9},{9,8},{10,11... | collective-permute-start | bytes 6291464 | tf_op jit(solution)/shard_map/ppermute | solution.py:464
  53.6 29.2 %collective-permute-start.8 = (bf16[16,8,512]{2,1,0:T(8,128)(2,1)S(1)}, bf16[16,8,512]{2,1,0:T(8,128)(2,1)S(1)}, u32[]{:S(2)}, u32[]{:S(2)}) collective-permute-start(bf16[16,8,512]{2,1,0:T(8,128)(2,1)S(1)} %get-tuple-element.65), channel_id=1, source_target_pairs={{0,2},{1,3},{2,4},{3,5},{4,6},{5,7},{6,0},{7,1},{8,10},{9,11},{10,... | collective-permute-start | bytes 393224 | tf_op jit(solution)/shard_map/ppermute | solution.py:453
  66.3 17.4 %collective-permute-start.9 = (bf16[16,8,512]{2,1,0:T(8,128)(2,1)S(1)}, bf16[16,8,512]{2,1,0:T(8,128)(2,1)S(1)}, u32[]{:S(2)}, u32[]{:S(2)}) collective-permute-start(bf16[16,8,512]{2,1,0:T(8,128)(2,1)S(1)} %get-tuple-element.66), channel_id=1, source_target_pairs={{0,4},{1,5},{2,6},{3,7},{4,0},{5,1},{6,2},{7,3},{8,12},{9,13},{10,... | collective-permute-start | bytes 393224 | tf_op jit(solution)/shard_map/ppermute | solution.py:453
  77.5 6.2 %collective-permute-start.10 = (bf16[16,8,512]{2,1,0:T(8,128)(2,1)S(1)}, bf16[16,8,512]{2,1,0:T(8,128)(2,1)S(1)}, u32[]{:S(2)}, u32[]{:S(2)}) collective-permute-start(bf16[16,8,512]{2,1,0:T(8,128)(2,1)S(1)} %get-tuple-element.67), channel_id=1, source_target_pairs={{0,6},{1,7},{2,0},{3,1},{4,2},{5,3},{6,4},{7,5},{8,14},{9,15},{10,... | collective-permute-start | bytes 393224 | tf_op jit(solution)/shard_map/ppermute | solution.py:453
  82.7 6.0 %copy-start.5 = (bf16[4,512,512]{2,1,0:T(8,128)(2,1)}, bf16[4,512,512]{2,1,0:T(8,128)(2,1)S(1)}, u32[]{:S(2)}) copy-start(bf16[4,512,512]{2,1,0:T(8,128)(2,1)S(1)} %tiles.5.refs_1_) | copy-start | bytes 6291460
  82.7 12.5 %collective-permute-start.12 = (bf16[4,512,512]{2,1,0:T(8,128)(2,1)S(1)}, bf16[4,512,512]{2,1,0:T(8,128)(2,1)S(1)}, u32[]{:S(2)}, u32[]{:S(2)}) collective-permute-start(bf16[4,512,512]{2,1,0:T(8,128)(2,1)S(1)} %tiles.5.refs_1_), channel_id=1, source_target_pairs={{0,1},{1,0},{2,3},{3,2},{4,5},{5,4},{6,7},{7,6},{8,9},{9,8},{10,11... | collective-permute-start | bytes 6291464 | tf_op jit(solution)/shard_map/ppermute | solution.py:464
  88.7 5.3 %copy-start.6 = (bf16[4,512,512]{2,1,0:T(8,128)(2,1)}, bf16[4,512,512]{2,1,0:T(8,128)(2,1)S(1)}, u32[]{:S(2)}) copy-start(bf16[4,512,512]{2,1,0:T(8,128)(2,1)S(1)} %tiles.7.refs_3_) | copy-start | bytes 6291460
  93.6 1.5 %copy-start.7 = (bf16[4,512,512]{2,1,0:T(8,128)(2,1)}, bf16[4,512,512]{2,1,0:T(8,128)(2,1)S(1)}, u32[]{:S(2)}) copy-start(bf16[4,512,512]{2,1,0:T(8,128)(2,1)S(1)} %tiles.6.refs_2_) | copy-start | bytes 6291460
  93.6 6.4 %collective-permute-start.13 = (bf16[4,512,512]{2,1,0:T(8,128)(2,1)S(1)}, bf16[4,512,512]{2,1,0:T(8,128)(2,1)S(1)}, u32[]{:S(2)}, u32[]{:S(2)}) collective-permute-start(bf16[4,512,512]{2,1,0:T(8,128)(2,1)S(1)} %tiles.6.refs_2_), channel_id=1, source_target_pairs={{0,1},{1,0},{2,3},{3,2},{4,5},{5,4},{6,7},{7,6},{8,9},{9,8},{10,11... | collective-permute-start | bytes 6291464 | tf_op jit(solution)/shard_map/ppermute | solution.py:464
  94.0 7.5 %collective-permute-start.14 = (bf16[4,512,512]{2,1,0:T(8,128)(2,1)S(1)}, bf16[4,512,512]{2,1,0:T(8,128)(2,1)}, u32[]{:S(2)}, u32[]{:S(2)}) collective-permute-start(bf16[4,512,512]{2,1,0:T(8,128)(2,1)S(1)} %tiles.7.refs_3_), channel_id=1, source_target_pairs={{0,1},{1,0},{2,3},{3,2},{4,5},{5,4},{6,7},{7,6},{8,9},{9,8},{10,11... | collective-permute-start | bytes 6291464 | tf_op jit(solution)/shard_map/ppermute | solution.py:464
  95.1 6.3 %copy-start.9 = (bf16[4,512,512]{2,1,0:T(8,128)(2,1)}, bf16[4,512,512]{2,1,0:T(8,128)(2,1)S(1)}, u32[]{:S(2)}) copy-start(bf16[4,512,512]{2,1,0:T(8,128)(2,1)S(1)} %collective-permute-done.11.refs_4_) | copy-start | bytes 6291460
  95.2 4.9 %copy-start.10 = (bf16[4,512,512]{2,1,0:T(8,128)(2,1)}, bf16[4,512,512]{2,1,0:T(8,128)(2,1)S(1)}, u32[]{:S(2)}) copy-start(bf16[4,512,512]{2,1,0:T(8,128)(2,1)S(1)} %collective-permute-done.12.refs_5_) | copy-start | bytes 6291460
  100.1 1.4 copy-start.11
  101.5 35.1 %copy-start.3 = (s32[1,16,1]{1,2,0:T(1,128)S(1)}, s32[1,16,1]{1,2,0:T(1,128)}, u32[]{:S(2)}) copy-start(s32[1,16,1]{1,2,0:T(1,128)} %param.9) | copy-start | bytes 196

commit v7 on v5

--- a/solution.py
+++ b/solution.py
@@ -100,6 +100,10 @@
         compiler_params=pltpu.CompilerParams(vmem_limit_bytes=60 * MIB),
         name="pack",
     )(slots, own, ensemble, increment)
+
+
+def in_hbm(value):
+    return pltpu.with_memory_space_constraint(value, pltpu.HBM)
 
 
 def three_parts(value):
@@ -214,16 +218,22 @@
     )(row, keep, got)
 
 
-def tiles_kernel(pairs, first, places_ref, out_ref):
-    for within in range(out_ref.shape[0]):
+def tiles_kernel(pairs, first, places_ref, out_ref, tile_ref, sem):
+    def copy(within):
+        return pltpu.make_async_copy(tile_ref.at[within], out_ref.at[within], sem.at[within])
+
+    for within in range(tile_ref.shape[0]):
         index = first[0] + within
         left = left_rows(places_ref[pairs[0, index]].astype(jnp.float32))
         right = right_rows(places_ref[pairs[1, index]].astype(jnp.float32))
-        out_ref[within] = tile_of(left, right)
+        tile_ref[within] = tile_of(left, right)
+        copy(within).start()
+    for within in range(tile_ref.shape[0]):
+        copy(within).wait()
 
 
 def tiles(places, pairs, first):
-    points = places.shape[2]
+    shape = (PAIR_GROUP, places.shape[2], places.shape[2])
     return pl.pallas_call(
         tiles_kernel,
         in_specs=[
@@ -231,8 +241,9 @@
             pl.BlockSpec(memory_space=pltpu.SMEM),
             pl.BlockSpec(memory_space=pltpu.VMEM),
         ],
-        out_specs=pl.BlockSpec(memory_space=pltpu.VMEM),
-        out_shape=jax.ShapeDtypeStruct((PAIR_GROUP, points, points), jnp.bfloat16),
+        out_specs=pl.BlockSpec(memory_space=pl.ANY),
+        out_shape=pltpu.HBM(shape, jnp.bfloat16),
+        scratch_shapes=[pltpu.VMEM(shape, jnp.bfloat16), pltpu.SemaphoreType.DMA((PAIR_GROUP,))],
         compiler_params=pltpu.CompilerParams(vmem_limit_bytes=60 * MIB),
         cost_estimate=pl.CostEstimate(flops=4_000_000_000, bytes_accessed=2_000_000, transcendentals=0),
         name="tiles",
@@ -394,16 +405,19 @@
     core, row = own & 1, own >> 1
     rows = groups // 2
     share = pairs.shape[1] // 2
+    keep, send = diag(ensemble, increment, coords, core, rows)
+    merged = merge(keep, lax.ppermute(send, "member", swap), row)
+    own_places, _ = lax.optimization_barrier((own_places, send))
     mine = [tiles(own_places, pairs, core * share + start) for start in range(0, share, PAIR_GROUP)]
     theirs = [lax.ppermute(stack, "member", swap) for stack in mine]
-    keep, send = diag(ensemble, increment, coords, core, rows)
-    merged = merge(keep, lax.ppermute(send, "member", swap), row)
+    got, merged = lax.optimization_barrier((got, merged))
+    stacks = [in_hbm(stack) for stack in mine + theirs]
+    partial = apply_pairs(in_hbm(got), stacks, pairs, pair_count, core, members, step)
+    partial, merged = lax.optimization_barrier((partial, merged))
     parts = [
-        lax.ppermute(part, "member", [(i, (i + 2 * shift) % groups) for i in range(groups)])
-        for shift, part in enumerate(merged[1:], 1)
+        lax.ppermute(part, "member", [(i, (i + 2 * hop) % groups) for i in range(groups)])
+        for hop, part in enumerate(merged[1:], 1)
     ]
-    got, parts = lax.optimization_barrier((got, parts))
-    partial = apply_pairs(got, mine + theirs, pairs, pair_count, core, members, step)
     back = lax.all_to_all(partial, "region", 0, 0, tiled=True)
     return finish(merged[0], parts, back, slots, 1.0 / (members * groups - 1))
 

time: 129 us -> 117 us (0.907); the launches traced: 129 us -> 115 us
  blocking collectives: 20.3 us -> 0 us
  starting transfers between devices: 19.5 us -> 28.1 us
  local copies, waits for them, and re-layouts: 3.18 us -> 0.63 us
  Pallas kernels: 61.9 us -> 64.1 us
  waiting for transfers between devices: 22.9 us -> 21.5 us
    all_to_all x1 -> x0, blocking collectives: 20.3 us -> none  [per_device(): back = lax.all_to_all(partial, 'region', 0, 0, tiled=True)]
    ppermute x3, waiting for transfers between devices: 18 us -> 4.69 us  [per_device(): lax.ppermute(part, 'member', [(i, (i + 2 * hop) % groups) for i in range(...]
    all_to_all x1, waiting for transfers between devices: 0.01 us -> 9.4 us  [per_device(): lax.all_to_all(big.reshape(regions * groups, -1, LANES), ('region', 'memb...]
    all_to_all x0 -> x1, starting transfers between devices: none -> 4.35 us  [per_device(): back = lax.all_to_all(partial, 'region', 0, 0, tiled=True)]
    ppermute x3, starting transfers between devices: 1.53 us -> 5.78 us  [per_device(): lax.ppermute(part, 'member', [(i, (i + 2 * hop) % groups) for i in range(...]
    pallas_call x1, Pallas kernels: 11.7 us -> 15.6 us  [apply_pairs(): pl.pallas_call(apply_kernel, in_specs=[pl.BlockSpec(memory_space=pltpu.SM...]
    unnamed x8, local copies, waits for them, and re-layouts: 3.18 us -> 0.63 us
    ppermute x1, waiting for transfers between devices: 2.86 us -> 5.39 us  [per_device(): merged = merge(keep, lax.ppermute(send, 'member', swap), row)]
  transfers between devices with their start and end apart: 10 -> 11, of which waited for: 5 -> 5; matrix products, arithmetic and copies ran while one was open for 0% -> 0% of each run, Pallas kernels for 36% -> 38%
where the time goes in v7:
time: 117 us; the launch traced here: 115 us
  Pallas kernels  64.1 us (55%)
  starting transfers between devices  28.1 us (24%)
  waiting for transfers between devices  21.5 us (18%)
    pallas_call x4, Pallas kernels, tiles(): pl.pallas_call(tiles_kernel, in_specs=[pl.BlockSpec(memory_space=pltpu.SM...  19.9 us
    pallas_call x1, Pallas kernels, diag(): pl.pallas_call(diag_kernel, grid_spec=pltpu.PrefetchScalarGridSpec(num_sc...  18.6 us
    pallas_call x1, Pallas kernels, apply_pairs(): pl.pallas_call(apply_kernel, in_specs=[pl.BlockSpec(memory_space=pltpu.SM...  15.6 us
    all_to_all x1, waiting for transfers between devices, per_device(): lax.all_to_all(big.reshape(regions * groups, -1, LANES), ('region', 'memb...  9.4 us
    all_to_all x1, starting transfers between devices, per_device(): lax.all_to_all(big.reshape(regions * groups, -1, LANES), ('region', 'memb...  8.82 us
    all_to_all x1, starting transfers between devices, per_device(): own_places = lax.all_to_all(places, 'region', 0, 0, tiled=True)  7.97 us
    ppermute x3, starting transfers between devices, per_device(): lax.ppermute(part, 'member', [(i, (i + 2 * hop) % groups) for i in range(...  5.78 us
    pallas_call x1, Pallas kernels, pack(): pl.pallas_call(pack_kernel, in_specs=[pl.BlockSpec(memory_space=pltpu.SME...  5.54 us
  transfers between devices with their start and end apart: 11, of which 5 were waited for; matrix products, arithmetic and copies ran while one was open for 0% of the time, Pallas kernels for 38%

profile of v7, /device:TPU:0, one launch (start us, length us, event | category | flops | bytes accessed | tf_op | source)
XLA Modules:
  0.0 115.2 jit_solution(12437485518775933861)
XLA Ops:
  0.0 2.9 %select.1 = bf16[16,2,512]{2,1,0:T(2,128)(2,1)} custom-call(s32[16]{0:T(128)} %bitcast.5, bf16[16,2,512]{2,1,0:T(2,128)(2,1)} %coords_ref.3), custom_call_target="tpu_custom_call" | custom-call | tf_op jit(solution)/shard_map/select/pallas_call | solution.py:32
  2.9 8.0 %all-to-all-start = ((bf16[16,2,512]{2,1,0:T(2,128)(2,1)}), bf16[16,2,512]{2,1,0:T(2,128)(2,1)S(1)}, u32[]{:S(2)}, u32[]{:S(2)}) async-start(bf16[16,2,512]{2,1,0:T(2,128)(2,1)} %select.1), calls=%async_computation | async-start | bytes 65536 | tf_op jit(solution)/shard_map/all_to_all | solution.py:398
  10.9 5.5 %pack.1 = bf16[16,8,136,128]{3,2,1,0:T(8,128)(2,1)} custom-call(s32[16]{0:T(128)} %bitcast.6, s32[1]{0:T(128)} %bitcast.2.own, bf16[16,4,64,512]{3,2,1,0:T(8,128)(2,1)} %ens_ref.3, bf16[16,64,512]{2,1,0:T(8,128)(2,1)} %inc_ref.3), custom_call_target="tpu_custom_call" | custom-call | tf_op jit(solution)/shard_map/pack/pallas_call | solution.py:82
  16.4 2.1 %all-to-all-done.places_ref = bf16[16,2,512]{2,1,0:T(2,128)(2,1)S(1)} async-done(((bf16[16,2,512]{2,1,0:T(2,128)(2,1)}), bf16[16,2,512]{2,1,0:T(2,128)(2,1)S(1)}, u32[]{:S(2)}, u32[]{:S(2)}) %all-to-all-start) | async-done | bytes 32800 | tf_op jit(solution)/shard_map/all_to_all | solution.py:398
  18.5 0.6 copy-done.2
  19.1 8.8 %all-to-all-start.1 = ((bf16[128,136,128]{2,1,0:T(8,128)(2,1)}), bf16[128,136,128]{2,1,0:T(8,128)(2,1)}, u32[]{:S(2)}, u32[]{:S(2)}) async-start(bf16[128,136,128]{2,1,0:T(8,128)(2,1)} %bitcast.8), calls=%async_computation.1 | async-start | bytes 8912896 | tf_op jit(solution)/shard_map/all_to_all | solution.py:401
  27.9 18.6 %diag.1 = (f32[4,16,8,512]{3,2,1,0:T(8,128)}, f32[4,16,8,512]{3,2,1,0:T(8,128)}) custom-call(s32[1]{0:T(128)S(6)} %and.4.core, bf16[16,4,64,512]{3,2,1,0:T(8,128)(2,1)} %ens_ref.3, bf16[16,64,512]{2,1,0:T(8,128)(2,1)} %inc_ref.3, bf16[16,2,512]{2,1,0:T(2,128)(2,1)} %coords_ref.3), custom_call_target="tpu_custom_call" | custom-call | flops 20000000000 | bytes 8000000 | tf_op jit(solution)/shard_map/diag/pallas_call | solution.py:179
  46.6 4.9 %tiles.4.refs_0_ = bf16[4,512,512]{2,1,0:T(8,128)(2,1)} custom-call(s32[2,32]{1,0:T(2,128)} %bitcast.9, s32[1]{0:T(128)S(6)} %mul.2.first, bf16[16,2,512]{2,1,0:T(2,128)(2,1)} %copy-done.2), custom_call_target="tpu_custom_call" | custom-call | flops 4000000000 | bytes 2000000 | tf_op jit(solution)/shard_map/tiles/pallas_call | solution.py:237
  51.5 4.9 %tiles.7.refs_3_ = bf16[4,512,512]{2,1,0:T(8,128)(2,1)} custom-call(s32[2,32]{1,0:T(2,128)} %bitcast.10, s32[1]{0:T(128)S(6)} %add.11.first, bf16[16,2,512]{2,1,0:T(2,128)(2,1)} %copy-done.2), custom_call_target="tpu_custom_call" | custom-call | flops 4000000000 | bytes 2000000 | tf_op jit(solution)/shard_map/tiles/pallas_call | solution.py:237
  56.4 4.9 %tiles.6.refs_2_ = bf16[4,512,512]{2,1,0:T(8,128)(2,1)} custom-call(s32[2,32]{1,0:T(2,128)} %bitcast.11, s32[1]{0:T(128)S(6)} %add.10.first, bf16[16,2,512]{2,1,0:T(2,128)(2,1)} %copy-done.2), custom_call_target="tpu_custom_call" | custom-call | flops 4000000000 | bytes 2000000 | tf_op jit(solution)/shard_map/tiles/pallas_call | solution.py:237
  61.3 5.3 %tiles.5.refs_1_ = bf16[4,512,512]{2,1,0:T(8,128)(2,1)} custom-call(s32[2,32]{1,0:T(2,128)} %bitcast.12, s32[1]{0:T(128)S(6)} %add.9.first, bf16[16,2,512]{2,1,0:T(2,128)(2,1)} %copy-done.2), custom_call_target="tpu_custom_call" | custom-call | flops 4000000000 | bytes 2000000 | tf_op jit(solution)/shard_map/tiles/pallas_call | solution.py:237
  66.6 0.1 collective-permute-start.1
  66.7 0.5 collective-permute-start.2
  67.2 0.1 collective-permute-start.3
  67.3 0.4 collective-permute-start.4
  67.7 0.1 collective-permute-start
  68.4 5.4 %collective-permute-done.got_ref = f32[4,16,8,512]{3,2,1,0:T(8,128)S(1)} collective-permute-done((f32[4,16,8,512]{3,2,1,0:T(8,128)S(1)}, f32[4,16,8,512]{3,2,1,0:T(8,128)S(1)}, u32[]{:S(2)}, u32[]{:S(2)}) %collective-permute-start) | collective-permute-done | bytes 1048608 | tf_op jit(solution)/shard_map/ppermute | solution.py:409
  73.8 0.1 merge.1
  73.9 9.4 %all-to-all-done.1 = bf16[128,136,128]{2,1,0:T(8,128)(2,1)} async-done(((bf16[128,136,128]{2,1,0:T(8,128)(2,1)}), bf16[128,136,128]{2,1,0:T(8,128)(2,1)}, u32[]{:S(2)}, u32[]{:S(2)}) %all-to-all-start.1) | async-done | bytes 4456480 | tf_op jit(solution)/shard_map/all_to_all | solution.py:401
  83.3 0.0 collective-permute-done.1.refs_4_
  83.3 0.0 collective-permute-done.2.refs_5_
  83.3 0.0 collective-permute-done.3.refs_6_
  83.3 0.0 collective-permute-done.4.refs_7_
  83.3 15.6 %apply.1 = f32[16,8,512]{2,1,0:T(8,128)} custom-call(s32[2,32]{1,0:T(2,128)} %bitcast.13, s32[1]{0:T(128)S(6)} %copy.7.count, s32[1]{0:T(128)S(6)} %and.4.core, bf16[16,8,136,128]{3,2,1,0:T(8,128)(2,1)} %bitcast.4.got_ref, bf16[4,512,512]{2,1,0:T(8,128)(2,1)} %tiles.4.refs_0_, bf16[4,512,512]{2,1,0:T(8,128)(2,1)} %tiles.5.refs_1_, ...), custom_call_target="tpu_custom_call" | custom-call | flops 8999999488 | bytes 22000000 | tf_op jit(solution)/shard_map/apply/pallas_call | solution.py:340
  98.9 4.4 %all-to-all-start.2 = ((f32[16,8,512]{2,1,0:T(8,128)}), f32[16,8,512]{2,1,0:T(8,128)S(1)}, u32[]{:S(2)}, u32[]{:S(2)}) async-start(f32[16,8,512]{2,1,0:T(8,128)} %apply.1), calls=%async_computation.2 | async-start | bytes 524288 | tf_op jit(solution)/shard_map/all_to_all | solution.py:421
  103.3 1.6 %collective-permute-start.5 = (bf16[16,8,512]{2,1,0:T(8,128)(2,1)S(1)}, bf16[16,8,512]{2,1,0:T(8,128)(2,1)S(1)}, u32[]{:S(2)}, u32[]{:S(2)}) collective-permute-start(bf16[16,8,512]{2,1,0:T(8,128)(2,1)S(1)} %get-tuple-element.39), channel_id=1, source_target_pairs={{0,2},{1,3},{2,4},{3,5},{4,6},{5,7},{6,0},{7,1},{8,10},{9,11},{10,... | collective-permute-start | bytes 393224 | tf_op jit(solution)/shard_map/ppermute | solution.py:418
  104.9 2.8 %collective-permute-start.6 = (bf16[16,8,512]{2,1,0:T(8,128)(2,1)S(1)}, bf16[16,8,512]{2,1,0:T(8,128)(2,1)S(1)}, u32[]{:S(2)}, u32[]{:S(2)}) collective-permute-start(bf16[16,8,512]{2,1,0:T(8,128)(2,1)S(1)} %get-tuple-element.40), channel_id=1, source_target_pairs={{0,4},{1,5},{2,6},{3,7},{4,0},{5,1},{6,2},{7,3},{8,12},{9,13},{10,... | collective-permute-start | bytes 393224 | tf_op jit(solution)/shard_map/ppermute | solution.py:418
  107.7 1.4 %collective-permute-start.7 = (bf16[16,8,512]{2,1,0:T(8,128)(2,1)S(1)}, bf16[16,8,512]{2,1,0:T(8,128)(2,1)S(1)}, u32[]{:S(2)}, u32[]{:S(2)}) collective-permute-start(bf16[16,8,512]{2,1,0:T(8,128)(2,1)S(1)} %get-tuple-element.41), channel_id=1, source_target_pairs={{0,6},{1,7},{2,0},{3,1},{4,2},{5,3},{6,4},{7,5},{8,14},{9,15},{10,... | collective-permute-start | bytes 393224 | tf_op jit(solution)/shard_map/ppermute | solution.py:418
  109.1 0.8 collective-permute-done.5.refs_0_
  109.9 3.9 %collective-permute-done.6.refs_1_ = bf16[16,8,512]{2,1,0:T(8,128)(2,1)S(1)} collective-permute-done((bf16[16,8,512]{2,1,0:T(8,128)(2,1)S(1)}, bf16[16,8,512]{2,1,0:T(8,128)(2,1)S(1)}, u32[]{:S(2)}, u32[]{:S(2)}) %collective-permute-start.6) | collective-permute-done | bytes 131104 | tf_op jit(solution)/shard_map/ppermute | solution.py:418
  113.8 0.0 all-to-all-done.2.refs_3_
  113.8 1.4 %finish.1 = f32[16,8,512]{2,1,0:T(8,128)} custom-call(s32[16]{0:T(128)S(1)} %bitcast.7, f32[16,8,512]{2,1,0:T(8,128)S(1)} %get-tuple-element.38.own_ref, bf16[16,8,512]{2,1,0:T(8,128)(2,1)S(1)} %collective-permute-done.5.refs_0_, bf16[16,8,512]{2,1,0:T(8,128)(2,1)S(1)} %collective-permute-done.6.refs_1_, ...), custom_call_target="tpu_custom_call" | custom-call | tf_op jit(solution)/shard_map/finish/pallas_call | solution.py:379
  (8 shorter events, 0.0 us)
Async XLA Ops:
  2.9 15.6 %all-to-all-start = ((bf16[16,2,512]{2,1,0:T(2,128)(2,1)}), bf16[16,2,512]{2,1,0:T(2,128)(2,1)S(1)}, u32[]{:S(2)}, u32[]{:S(2)}) async-start(bf16[16,2,512]{2,1,0:T(2,128)(2,1)} %select.1), calls=%async_computation | async-start | bytes 65536 | tf_op jit(solution)/shard_map/all_to_all | solution.py:398
  18.5 0.6 copy-start.2
  19.1 64.2 %all-to-all-start.1 = ((bf16[128,136,128]{2,1,0:T(8,128)(2,1)}), bf16[128,136,128]{2,1,0:T(8,128)(2,1)}, u32[]{:S(2)}, u32[]{:S(2)}) async-start(bf16[128,136,128]{2,1,0:T(8,128)(2,1)} %bitcast.8), calls=%async_computation.1 | async-start | bytes 8912896 | tf_op jit(solution)/shard_map/all_to_all | solution.py:401
  61.2 6.4 %copy-start.3 = (f32[4,16,8,512]{3,2,1,0:T(8,128)S(1)}, f32[4,16,8,512]{3,2,1,0:T(8,128)}, u32[]{:S(2)}) copy-start(f32[4,16,8,512]{3,2,1,0:T(8,128)} %get-tuple-element.26) | copy-start | bytes 3145732
  61.3 12.6 %copy-start = (f32[4,16,8,512]{3,2,1,0:T(8,128)S(1)}, f32[4,16,8,512]{3,2,1,0:T(8,128)}, u32[]{:S(2)}) copy-start(f32[4,16,8,512]{3,2,1,0:T(8,128)} %get-tuple-element.25.keep_ref) | copy-start | bytes 3145732
  66.6 16.7 %collective-permute-start.1 = (bf16[4,512,512]{2,1,0:T(8,128)(2,1)}, bf16[4,512,512]{2,1,0:T(8,128)(2,1)}, u32[]{:S(2)}, u32[]{:S(2)}) collective-permute-start(bf16[4,512,512]{2,1,0:T(8,128)(2,1)} %tiles.4.refs_0_), channel_id=1, source_target_pairs={{0,1},{1,0},{2,3},{3,2},{4,5},{5,4},{6,7},{7,6},{8,9},{9,8},{10,11... | collective-permute-start | bytes 6291464 | tf_op jit(solution)/shard_map/ppermute | solution.py:412
  66.7 16.7 %collective-permute-start.2 = (bf16[4,512,512]{2,1,0:T(8,128)(2,1)}, bf16[4,512,512]{2,1,0:T(8,128)(2,1)}, u32[]{:S(2)}, u32[]{:S(2)}) collective-permute-start(bf16[4,512,512]{2,1,0:T(8,128)(2,1)} %tiles.5.refs_1_), channel_id=1, source_target_pairs={{0,1},{1,0},{2,3},{3,2},{4,5},{5,4},{6,7},{7,6},{8,9},{9,8},{10,11... | collective-permute-start | bytes 6291464 | tf_op jit(solution)/shard_map/ppermute | solution.py:412
  67.2 16.2 %collective-permute-start.3 = (bf16[4,512,512]{2,1,0:T(8,128)(2,1)}, bf16[4,512,512]{2,1,0:T(8,128)(2,1)}, u32[]{:S(2)}, u32[]{:S(2)}) collective-permute-start(bf16[4,512,512]{2,1,0:T(8,128)(2,1)} %tiles.6.refs_2_), channel_id=1, source_target_pairs={{0,1},{1,0},{2,3},{3,2},{4,5},{5,4},{6,7},{7,6},{8,9},{9,8},{10,11... | collective-permute-start | bytes 6291464 | tf_op jit(solution)/shard_map/ppermute | solution.py:412
  67.3 16.1 %collective-permute-start.4 = (bf16[4,512,512]{2,1,0:T(8,128)(2,1)}, bf16[4,512,512]{2,1,0:T(8,128)(2,1)}, u32[]{:S(2)}, u32[]{:S(2)}) collective-permute-start(bf16[4,512,512]{2,1,0:T(8,128)(2,1)} %tiles.7.refs_3_), channel_id=1, source_target_pairs={{0,1},{1,0},{2,3},{3,2},{4,5},{5,4},{6,7},{7,6},{8,9},{9,8},{10,11... | collective-permute-start | bytes 6291464 | tf_op jit(solution)/shard_map/ppermute | solution.py:412
  67.7 6.1 %collective-permute-start = (f32[4,16,8,512]{3,2,1,0:T(8,128)S(1)}, f32[4,16,8,512]{3,2,1,0:T(8,128)S(1)}, u32[]{:S(2)}, u32[]{:S(2)}) collective-permute-start(f32[4,16,8,512]{3,2,1,0:T(8,128)S(1)} %copy-done.3), channel_id=1, source_target_pairs={{0,1},{1,0},{2,3},{3,2},{4,5},{5,4},{6,7},{7,6},{8,9},{9,8},{10,11... | collective-permute-start | bytes 3145736 | tf_op jit(solution)/shard_map/ppermute | solution.py:409
  83.3 30.5 %copy-start.1 = (s32[1,16,1]{1,2,0:T(1,128)S(1)}, s32[1,16,1]{1,2,0:T(1,128)}, u32[]{:S(2)}) copy-start(s32[1,16,1]{1,2,0:T(1,128)} %param.9) | copy-start | bytes 196
  98.9 14.8 %all-to-all-start.2 = ((f32[16,8,512]{2,1,0:T(8,128)}), f32[16,8,512]{2,1,0:T(8,128)S(1)}, u32[]{:S(2)}, u32[]{:S(2)}) async-start(f32[16,8,512]{2,1,0:T(8,128)} %apply.1), calls=%async_computation.2 | async-start | bytes 524288 | tf_op jit(solution)/shard_map/all_to_all | solution.py:421
  103.3 6.6 %collective-permute-start.5 = (bf16[16,8,512]{2,1,0:T(8,128)(2,1)S(1)}, bf16[16,8,512]{2,1,0:T(8,128)(2,1)S(1)}, u32[]{:S(2)}, u32[]{:S(2)}) collective-permute-start(bf16[16,8,512]{2,1,0:T(8,128)(2,1)S(1)} %get-tuple-element.39), channel_id=1, source_target_pairs={{0,2},{1,3},{2,4},{3,5},{4,6},{5,7},{6,0},{7,1},{8,10},{9,11},{10,... | collective-permute-start | bytes 393224 | tf_op jit(solution)/shard_map/ppermute | solution.py:418
  104.9 8.9 %collective-permute-start.6 = (bf16[16,8,512]{2,1,0:T(8,128)(2,1)S(1)}, bf16[16,8,512]{2,1,0:T(8,128)(2,1)S(1)}, u32[]{:S(2)}, u32[]{:S(2)}) collective-permute-start(bf16[16,8,512]{2,1,0:T(8,128)(2,1)S(1)} %get-tuple-element.40), channel_id=1, source_target_pairs={{0,4},{1,5},{2,6},{3,7},{4,0},{5,1},{6,2},{7,3},{8,12},{9,13},{10,... | collective-permute-start | bytes 393224 | tf_op jit(solution)/shard_map/ppermute | solution.py:418
  107.7 6.1 %collective-permute-start.7 = (bf16[16,8,512]{2,1,0:T(8,128)(2,1)S(1)}, bf16[16,8,512]{2,1,0:T(8,128)(2,1)S(1)}, u32[]{:S(2)}, u32[]{:S(2)}) collective-permute-start(bf16[16,8,512]{2,1,0:T(8,128)(2,1)S(1)} %get-tuple-element.41), channel_id=1, source_target_pairs={{0,6},{1,7},{2,0},{3,1},{4,2},{5,3},{6,4},{7,5},{8,14},{9,15},{10,... | collective-permute-start | bytes 393224 | tf_op jit(solution)/shard_map/ppermute | solution.py:418

commit v8 on v7

--- a/solution.py
+++ b/solution.py
@@ -9,6 +9,8 @@
 
 LANES = 128
 PAIR_GROUP = 4
+AFTER_MERGE = 1
+AFTER_TOTAL = 3
 MIB = 1024 * 1024
 UNIT = 12.0**-0.2
 UNIT2 = UNIT * UNIT
@@ -218,6 +220,25 @@
     )(row, keep, got)
 
 
+def total_kernel(own_ref, *refs):
+    *part_refs, out_ref = refs
+    total = own_ref[...]
+    for part_ref in part_refs:
+        total = total + part_ref[...].astype(jnp.float32)
+    out_ref[...] = total
+
+
+def total_of(own, parts):
+    return pl.pallas_call(
+        total_kernel,
+        in_specs=[pl.BlockSpec(memory_space=pltpu.VMEM)] * (len(parts) + 1),
+        out_specs=pl.BlockSpec(memory_space=pltpu.VMEM),
+        out_shape=jax.ShapeDtypeStruct(own.shape, jnp.float32),
+        compiler_params=pltpu.CompilerParams(vmem_limit_bytes=16 * MIB),
+        name="total",
+    )(own, *parts)
+
+
 def tiles_kernel(pairs, first, places_ref, out_ref, tile_ref, sem):
     def copy(within):
         return pltpu.make_async_copy(tile_ref.at[within], out_ref.at[within], sem.at[within])
@@ -364,26 +385,26 @@
     )(pairs, count, core, got, *stacks)
 
 
-def finish_kernel(slots, own_ref, *refs, scale):
-    *part_refs, back_ref, out_ref = refs
-    total = own_ref[...]
-    for part_ref in part_refs:
-        total = total + part_ref[...].astype(jnp.float32)
-    out_ref[...] = total * scale
+def finish_kernel(slots, own_ref, back_ref, out_ref, *, scale):
+    out_ref[...] = own_ref[...] * scale
     for owner in range(back_ref.shape[0]):
         slot = slots[owner]
         out_ref[slot] = out_ref[slot] + back_ref[owner] * scale
 
 
-def finish(own, parts, back, slots, scale):
+def finish(own, back, slots, scale):
     return pl.pallas_call(
         functools.partial(finish_kernel, scale=scale),
-        in_specs=[pl.BlockSpec(memory_space=pltpu.SMEM)] + [pl.BlockSpec(memory_space=pltpu.VMEM)] * (len(parts) + 2),
+        in_specs=[
+            pl.BlockSpec(memory_space=pltpu.SMEM),
+            pl.BlockSpec(memory_space=pltpu.VMEM),
+            pl.BlockSpec(memory_space=pltpu.VMEM),
+        ],
         out_specs=pl.BlockSpec(memory_space=pltpu.VMEM),
         out_shape=jax.ShapeDtypeStruct(own.shape, jnp.float32),
         compiler_params=pltpu.CompilerParams(vmem_limit_bytes=16 * MIB),
         name="finish",
-    )(slots, own, *parts, back)
+    )(slots, own, back)
 
 
 def per_device(ensemble, increment, coords, sent_slots, pair_list, pair_count):
@@ -407,19 +428,25 @@
     share = pairs.shape[1] // 2
     keep, send = diag(ensemble, increment, coords, core, rows)
     merged = merge(keep, lax.ppermute(send, "member", swap), row)
-    own_places, _ = lax.optimization_barrier((own_places, send))
-    mine = [tiles(own_places, pairs, core * share + start) for start in range(0, share, PAIR_GROUP)]
-    theirs = [lax.ppermute(stack, "member", swap) for stack in mine]
-    got, merged = lax.optimization_barrier((got, merged))
-    stacks = [in_hbm(stack) for stack in mine + theirs]
-    partial = apply_pairs(in_hbm(got), stacks, pairs, pair_count, core, members, step)
-    partial, merged = lax.optimization_barrier((partial, merged))
     parts = [
         lax.ppermute(part, "member", [(i, (i + 2 * hop) % groups) for i in range(groups)])
         for hop, part in enumerate(merged[1:], 1)
     ]
+    diagonal = total_of(merged[0], parts)
+    own_places, _ = lax.optimization_barrier((own_places, send))
+    mine = []
+    for start in range(0, share, PAIR_GROUP):
+        if start == AFTER_MERGE * PAIR_GROUP:
+            own_places, _ = lax.optimization_barrier((own_places, merged[0]))
+        if start == AFTER_TOTAL * PAIR_GROUP:
+            own_places, diagonal = lax.optimization_barrier((own_places, diagonal))
+        mine.append(tiles(own_places, pairs, core * share + start))
+    theirs = [lax.ppermute(stack, "member", swap) for stack in mine]
+    got, diagonal = lax.optimization_barrier((got, diagonal))
+    stacks = [in_hbm(stack) for stack in mine + theirs]
+    partial = apply_pairs(in_hbm(got), stacks, pairs, pair_count, core, members, step)
     back = lax.all_to_all(partial, "region", 0, 0, tiled=True)
-    return finish(merged[0], parts, back, slots, 1.0 / (members * groups - 1))
+    return finish(diagonal, back, slots, 1.0 / (members * groups - 1))
 
 
 def solution(mesh):

time: 117 us -> 129 us (1.10)
  blocking collectives: 0 us -> 20 us
  starting transfers between devices: 28.1 us -> 23 us
  Pallas kernels: 64.1 us -> 61.3 us
    all_to_all x0 -> x1, blocking collectives: none -> 20 us  [per_device(): back = lax.all_to_all(partial, 'region', 0, 0, tiled=True)]
    ppermute x3, waiting for transfers between devices: 4.69 us -> 16.5 us  [per_device(): lax.ppermute(part, 'member', [(i, (i + 2 * hop) % groups) for i in range(...]
    all_to_all x1, waiting for transfers between devices: 9.4 us -> 0.01 us  [per_device(): lax.all_to_all(big.reshape(regions * groups, -1, LANES), ('region', 'memb...]
    ppermute x1, waiting for transfers between devices: 5.39 us -> 0.01 us  [per_device(): merged = merge(keep, lax.ppermute(send, 'member', swap), row)]
    all_to_all x1 -> x0, starting transfers between devices: 4.35 us -> none  [per_device(): back = lax.all_to_all(partial, 'region', 0, 0, tiled=True)]
    ppermute x4, waiting for transfers between devices: 0.01 us -> 3.79 us  [per_device(): theirs = [lax.ppermute(stack, 'member', swap) for stack in mine]]
    pallas_call x1, Pallas kernels: 15.6 us -> 12.7 us  [apply_pairs(): pl.pallas_call(apply_kernel, in_specs=[pl.BlockSpec(memory_space=pltpu.SM...]
  transfers between devices with their start and end apart: 11 -> 10, of which waited for: 5 -> 4; matrix products, arithmetic and copies ran while one was open for 0% -> 0% of each run, Pallas kernels for 38% -> 35%
where the time goes in v8:
time: 129 us; the launch traced here: 128 us
  Pallas kernels  61.3 us (48%)
  starting transfers between devices  23 us (18%)
  waiting for transfers between devices  22 us (17%)
  blocking collectives  20 us (16%)
    all_to_all x1, blocking collectives, per_device(): back = lax.all_to_all(partial, 'region', 0, 0, tiled=True)  20 us
    pallas_call x4, Pallas kernels, tiles(): pl.pallas_call(tiles_kernel, in_specs=[pl.BlockSpec(memory_space=pltpu.SM...  19.8 us
    pallas_call x1, Pallas kernels, diag(): pl.pallas_call(diag_kernel, grid_spec=pltpu.PrefetchScalarGridSpec(num_sc...  18.6 us
    ppermute x3, waiting for transfers between devices, per_device(): lax.ppermute(part, 'member', [(i, (i + 2 * hop) % groups) for i in range(...  16.5 us
    pallas_call x1, Pallas kernels, apply_pairs(): pl.pallas_call(apply_kernel, in_specs=[pl.BlockSpec(memory_space=pltpu.SM...  12.7 us
    all_to_all x1, starting transfers between devices, per_device(): lax.all_to_all(big.reshape(regions * groups, -1, LANES), ('region', 'memb...  8.94 us
    all_to_all x1, starting transfers between devices, per_device(): own_places = lax.all_to_all(places, 'region', 0, 0, tiled=True)  7.97 us
    pallas_call x1, Pallas kernels, pack(): pl.pallas_call(pack_kernel, in_specs=[pl.BlockSpec(memory_space=pltpu.SME...  5.79 us
  transfers between devices with their start and end apart: 10, of which 4 were waited for; matrix products, arithmetic and copies ran while one was open for 0% of the time, Pallas kernels for 35%

profile of v8, /device:TPU:0, one launch (start us, length us, event | category | flops | bytes accessed | tf_op | source)
XLA Modules:
  0.0 127.8 jit_solution(13142505081527772257)
XLA Ops:
  0.0 2.9 %select.1 = bf16[16,2,512]{2,1,0:T(2,128)(2,1)} custom-call(s32[16]{0:T(128)} %bitcast.5, bf16[16,2,512]{2,1,0:T(2,128)(2,1)} %coords_ref.3), custom_call_target="tpu_custom_call" | custom-call | tf_op jit(solution)/shard_map/select/pallas_call | solution.py:34
  2.9 8.0 %all-to-all-start = ((bf16[16,2,512]{2,1,0:T(2,128)(2,1)}), bf16[16,2,512]{2,1,0:T(2,128)(2,1)S(1)}, u32[]{:S(2)}, u32[]{:S(2)}) async-start(bf16[16,2,512]{2,1,0:T(2,128)(2,1)} %select.1), calls=%async_computation | async-start | bytes 65536 | tf_op jit(solution)/shard_map/all_to_all | solution.py:419
  10.9 5.8 %pack.1 = bf16[16,8,136,128]{3,2,1,0:T(8,128)(2,1)} custom-call(s32[16]{0:T(128)} %bitcast.6, s32[1]{0:T(128)} %bitcast.1.own, bf16[16,4,64,512]{3,2,1,0:T(8,128)(2,1)} %ens_ref.3, bf16[16,64,512]{2,1,0:T(8,128)(2,1)} %inc_ref.3), custom_call_target="tpu_custom_call" | custom-call | tf_op jit(solution)/shard_map/pack/pallas_call | solution.py:84
  16.7 1.8 %all-to-all-done.places_ref = bf16[16,2,512]{2,1,0:T(2,128)(2,1)S(1)} async-done(((bf16[16,2,512]{2,1,0:T(2,128)(2,1)}), bf16[16,2,512]{2,1,0:T(2,128)(2,1)S(1)}, u32[]{:S(2)}, u32[]{:S(2)}) %all-to-all-start) | async-done | bytes 32800 | tf_op jit(solution)/shard_map/all_to_all | solution.py:419
  18.5 0.6 copy-done.2
  19.1 8.9 %all-to-all-start.1 = ((bf16[128,136,128]{2,1,0:T(8,128)(2,1)}), bf16[128,136,128]{2,1,0:T(8,128)(2,1)}, u32[]{:S(2)}, u32[]{:S(2)}) async-start(bf16[128,136,128]{2,1,0:T(8,128)(2,1)} %bitcast.8), calls=%async_computation.1 | async-start | bytes 8912896 | tf_op jit(solution)/shard_map/all_to_all | solution.py:422
  28.1 18.6 %diag.1 = (f32[4,16,8,512]{3,2,1,0:T(8,128)}, f32[4,16,8,512]{3,2,1,0:T(8,128)}) custom-call(s32[1]{0:T(128)S(6)} %and.4.core, bf16[16,4,64,512]{3,2,1,0:T(8,128)(2,1)} %ens_ref.3, bf16[16,64,512]{2,1,0:T(8,128)(2,1)} %inc_ref.3, bf16[16,2,512]{2,1,0:T(2,128)(2,1)} %coords_ref.3), custom_call_target="tpu_custom_call" | custom-call | flops 20000000000 | bytes 8000000 | tf_op jit(solution)/shard_map/diag/pallas_call | solution.py:181
  46.7 0.0 collective-permute-start
  46.7 5.0 %tiles.4.refs_0_ = bf16[4,512,512]{2,1,0:T(8,128)(2,1)} custom-call(s32[2,32]{1,0:T(2,128)} %bitcast.9, s32[1]{0:T(128)S(6)} %mul.2.first, bf16[16,2,512]{2,1,0:T(2,128)(2,1)} %copy-done.2), custom_call_target="tpu_custom_call" | custom-call | flops 4000000000 | bytes 2000000 | tf_op jit(solution)/shard_map/tiles/pallas_call | solution.py:258
  51.7 0.6 collective-permute-start.4
  52.3 0.0 collective-permute-done.got_ref
  52.3 0.1 merge.1
  52.4 1.0 collective-permute-start.1
  53.3 2.7 %collective-permute-start.2 = (bf16[16,8,512]{2,1,0:T(8,128)(2,1)S(1)}, bf16[16,8,512]{2,1,0:T(8,128)(2,1)S(1)}, u32[]{:S(2)}, u32[]{:S(2)}) collective-permute-start(bf16[16,8,512]{2,1,0:T(8,128)(2,1)S(1)} %get-tuple-element.27), channel_id=1, source_target_pairs={{0,4},{1,5},{2,6},{3,7},{4,0},{5,1},{6,2},{7,3},{8,12},{9,13},{10,... | collective-permute-start | bytes 393224 | tf_op jit(solution)/shard_map/ppermute | solution.py:432
  56.1 1.4 %collective-permute-start.3 = (bf16[16,8,512]{2,1,0:T(8,128)(2,1)S(1)}, bf16[16,8,512]{2,1,0:T(8,128)(2,1)S(1)}, u32[]{:S(2)}, u32[]{:S(2)}) collective-permute-start(bf16[16,8,512]{2,1,0:T(8,128)(2,1)S(1)} %get-tuple-element.28), channel_id=1, source_target_pairs={{0,6},{1,7},{2,0},{3,1},{4,2},{5,3},{6,4},{7,5},{8,14},{9,15},{10,... | collective-permute-start | bytes 393224 | tf_op jit(solution)/shard_map/ppermute | solution.py:432
  57.5 4.9 %tiles.6.refs_2_ = bf16[4,512,512]{2,1,0:T(8,128)(2,1)} custom-call(s32[2,32]{1,0:T(2,128)} %bitcast.10, s32[1]{0:T(128)S(6)} %add.10.first, bf16[16,2,512]{2,1,0:T(2,128)(2,1)} %copy-done.2), custom_call_target="tpu_custom_call" | custom-call | flops 4000000000 | bytes 2000000 | tf_op jit(solution)/shard_map/tiles/pallas_call | solution.py:258
  62.4 5.0 %tiles.5.refs_1_ = bf16[4,512,512]{2,1,0:T(8,128)(2,1)} custom-call(s32[2,32]{1,0:T(2,128)} %bitcast.11, s32[1]{0:T(128)S(6)} %add.9.first, bf16[16,2,512]{2,1,0:T(2,128)(2,1)} %copy-done.2), custom_call_target="tpu_custom_call" | custom-call | flops 4000000000 | bytes 2000000 | tf_op jit(solution)/shard_map/tiles/pallas_call | solution.py:258
  67.4 0.1 collective-permute-start.5
  67.5 13.2 %collective-permute-done.1.refs_0_ = bf16[16,8,512]{2,1,0:T(8,128)(2,1)S(1)} collective-permute-done((bf16[16,8,512]{2,1,0:T(8,128)(2,1)S(1)}, bf16[16,8,512]{2,1,0:T(8,128)(2,1)S(1)}, u32[]{:S(2)}, u32[]{:S(2)}) %collective-permute-start.1) | collective-permute-done | bytes 131104 | tf_op jit(solution)/shard_map/ppermute | solution.py:432
  80.8 0.0 collective-permute-start.6
  80.8 3.2 %collective-permute-done.2.refs_1_ = bf16[16,8,512]{2,1,0:T(8,128)(2,1)S(1)} collective-permute-done((bf16[16,8,512]{2,1,0:T(8,128)(2,1)S(1)}, bf16[16,8,512]{2,1,0:T(8,128)(2,1)S(1)}, u32[]{:S(2)}, u32[]{:S(2)}) %collective-permute-start.2) | collective-permute-done | bytes 131104 | tf_op jit(solution)/shard_map/ppermute | solution.py:432
  84.0 0.0 collective-permute-done.3.refs_2_
  84.0 0.1 total.1.own_ref
  84.0 4.9 %tiles.7.refs_3_ = bf16[4,512,512]{2,1,0:T(8,128)(2,1)} custom-call(s32[2,32]{1,0:T(2,128)} %bitcast.12, s32[1]{0:T(128)S(6)} %add.11.first, bf16[16,2,512]{2,1,0:T(2,128)(2,1)} %copy-done.2), custom_call_target="tpu_custom_call" | custom-call | flops 4000000000 | bytes 2000000 | tf_op jit(solution)/shard_map/tiles/pallas_call | solution.py:258
  89.0 0.3 collective-permute-start.7
  89.9 0.0 copy-start.1
  89.9 0.0 collective-permute-done.4.refs_4_
  89.9 0.0 collective-permute-done.5.refs_5_
  90.0 3.8 %collective-permute-done.7.refs_7_ = bf16[4,512,512]{2,1,0:T(8,128)(2,1)} collective-permute-done((bf16[4,512,512]{2,1,0:T(8,128)(2,1)}, bf16[4,512,512]{2,1,0:T(8,128)(2,1)}, u32[]{:S(2)}, u32[]{:S(2)}) %collective-permute-start.7) | collective-permute-done | bytes 2097184 | tf_op jit(solution)/shard_map/ppermute | solution.py:444
  93.8 12.7 %apply.1 = f32[16,8,512]{2,1,0:T(8,128)} custom-call(s32[2,32]{1,0:T(2,128)} %bitcast.13, s32[1]{0:T(128)S(6)} %copy.7.count, s32[1]{0:T(128)S(6)} %and.4.core, bf16[16,8,136,128]{3,2,1,0:T(8,128)(2,1)} %bitcast.3.got_ref, bf16[4,512,512]{2,1,0:T(8,128)(2,1)} %tiles.4.refs_0_, bf16[4,512,512]{2,1,0:T(8,128)(2,1)} %tiles.5.refs_1_, ...), custom_call_target="tpu_custom_call" | custom-call | flops 8999999488 | bytes 22000000 | tf_op jit(solution)/shard_map/apply/pallas_call | solution.py:361
  106.5 20.0 %all_to_all.15.back_ref = f32[16,8,512]{2,1,0:T(8,128)S(1)} all-to-all(f32[16,8,512]{2,1,0:T(8,128)} %apply.1), channel_id=1, replica_groups=mesh['region'=16,'member'=8] {'region'}, dimensions={0} | all-to-all | bytes 524288 | tf_op jit(solution)/shard_map/all_to_all | solution.py:448
  126.4 1.3 %finish.1 = f32[16,8,512]{2,1,0:T(8,128)} custom-call(s32[16]{0:T(128)S(1)} %bitcast.7, f32[16,8,512]{2,1,0:T(8,128)S(1)} %total.1.own_ref, f32[16,8,512]{2,1,0:T(8,128)S(1)} %all_to_all.15.back_ref), custom_call_target="tpu_custom_call" | custom-call | tf_op jit(solution)/shard_map/finish/pallas_call | solution.py:396
  (8 shorter events, 0.0 us)
Async XLA Ops:
  2.9 15.6 %all-to-all-start = ((bf16[16,2,512]{2,1,0:T(2,128)(2,1)}), bf16[16,2,512]{2,1,0:T(2,128)(2,1)S(1)}, u32[]{:S(2)}, u32[]{:S(2)}) async-start(bf16[16,2,512]{2,1,0:T(2,128)(2,1)} %select.1), calls=%async_computation | async-start | bytes 65536 | tf_op jit(solution)/shard_map/all_to_all | solution.py:419
  18.5 0.6 copy-start.2
  19.1 70.8 %all-to-all-start.1 = ((bf16[128,136,128]{2,1,0:T(8,128)(2,1)}), bf16[128,136,128]{2,1,0:T(8,128)(2,1)}, u32[]{:S(2)}, u32[]{:S(2)}) async-start(bf16[128,136,128]{2,1,0:T(8,128)(2,1)} %bitcast.8), calls=%async_computation.1 | async-start | bytes 8912896 | tf_op jit(solution)/shard_map/all_to_all | solution.py:422
  46.7 5.6 %collective-permute-start = (f32[4,16,8,512]{3,2,1,0:T(8,128)}, f32[4,16,8,512]{3,2,1,0:T(8,128)S(1)}, u32[]{:S(2)}, u32[]{:S(2)}) collective-permute-start(f32[4,16,8,512]{3,2,1,0:T(8,128)} %get-tuple-element.21), channel_id=1, source_target_pairs={{0,1},{1,0},{2,3},{3,2},{4,5},{5,4},{6,7},{7,6},{8,9},{9,8},{10,11... | collective-permute-start | bytes 3145736 | tf_op jit(solution)/shard_map/ppermute | solution.py:430
  46.7 5.6 %copy-start = (f32[4,16,8,512]{3,2,1,0:T(8,128)S(1)}, f32[4,16,8,512]{3,2,1,0:T(8,128)}, u32[]{:S(2)}) copy-start(f32[4,16,8,512]{3,2,1,0:T(8,128)} %get-tuple-element.23.keep_ref) | copy-start | bytes 3145732
  51.7 38.3 %collective-permute-start.4 = (bf16[4,512,512]{2,1,0:T(8,128)(2,1)}, bf16[4,512,512]{2,1,0:T(8,128)(2,1)}, u32[]{:S(2)}, u32[]{:S(2)}) collective-permute-start(bf16[4,512,512]{2,1,0:T(8,128)(2,1)} %tiles.4.refs_0_), channel_id=1, source_target_pairs={{0,1},{1,0},{2,3},{3,2},{4,5},{5,4},{6,7},{7,6},{8,9},{9,8},{10,11... | collective-permute-start | bytes 6291464 | tf_op jit(solution)/shard_map/ppermute | solution.py:444
  52.4 28.4 %collective-permute-start.1 = (bf16[16,8,512]{2,1,0:T(8,128)(2,1)S(1)}, bf16[16,8,512]{2,1,0:T(8,128)(2,1)S(1)}, u32[]{:S(2)}, u32[]{:S(2)}) collective-permute-start(bf16[16,8,512]{2,1,0:T(8,128)(2,1)S(1)} %get-tuple-element.26), channel_id=1, source_target_pairs={{0,2},{1,3},{2,4},{3,5},{4,6},{5,7},{6,0},{7,1},{8,10},{9,11},{10,... | collective-permute-start | bytes 393224 | tf_op jit(solution)/shard_map/ppermute | solution.py:432
  53.3 30.6 %collective-permute-start.2 = (bf16[16,8,512]{2,1,0:T(8,128)(2,1)S(1)}, bf16[16,8,512]{2,1,0:T(8,128)(2,1)S(1)}, u32[]{:S(2)}, u32[]{:S(2)}) collective-permute-start(bf16[16,8,512]{2,1,0:T(8,128)(2,1)S(1)} %get-tuple-element.27), channel_id=1, source_target_pairs={{0,4},{1,5},{2,6},{3,7},{4,0},{5,1},{6,2},{7,3},{8,12},{9,13},{10,... | collective-permute-start | bytes 393224 | tf_op jit(solution)/shard_map/ppermute | solution.py:432
  56.1 27.9 %collective-permute-start.3 = (bf16[16,8,512]{2,1,0:T(8,128)(2,1)S(1)}, bf16[16,8,512]{2,1,0:T(8,128)(2,1)S(1)}, u32[]{:S(2)}, u32[]{:S(2)}) collective-permute-start(bf16[16,8,512]{2,1,0:T(8,128)(2,1)S(1)} %get-tuple-element.28), channel_id=1, source_target_pairs={{0,6},{1,7},{2,0},{3,1},{4,2},{5,3},{6,4},{7,5},{8,14},{9,15},{10,... | collective-permute-start | bytes 393224 | tf_op jit(solution)/shard_map/ppermute | solution.py:432
  62.4 18.4 %copy-start.3 = (bf16[4,512,512]{2,1,0:T(8,128)(2,1)S(1)}, bf16[4,512,512]{2,1,0:T(8,128)(2,1)}, u32[]{:S(2)}) copy-start(bf16[4,512,512]{2,1,0:T(8,128)(2,1)} %tiles.6.refs_2_) | copy-start | bytes 6291460
  67.4 22.5 %collective-permute-start.5 = (bf16[4,512,512]{2,1,0:T(8,128)(2,1)}, bf16[4,512,512]{2,1,0:T(8,128)(2,1)}, u32[]{:S(2)}, u32[]{:S(2)}) collective-permute-start(bf16[4,512,512]{2,1,0:T(8,128)(2,1)} %tiles.5.refs_1_), channel_id=1, source_target_pairs={{0,1},{1,0},{2,3},{3,2},{4,5},{5,4},{6,7},{7,6},{8,9},{9,8},{10,11... | collective-permute-start | bytes 6291464 | tf_op jit(solution)/shard_map/ppermute | solution.py:444
  80.8 9.2 %collective-permute-start.6 = (bf16[4,512,512]{2,1,0:T(8,128)(2,1)S(1)}, bf16[4,512,512]{2,1,0:T(8,128)(2,1)}, u32[]{:S(2)}, u32[]{:S(2)}) collective-permute-start(bf16[4,512,512]{2,1,0:T(8,128)(2,1)S(1)} %copy-done.3), channel_id=1, source_target_pairs={{0,1},{1,0},{2,3},{3,2},{4,5},{5,4},{6,7},{7,6},{8,9},{9,8},{10,11... | collective-permute-start | bytes 6291464 | tf_op jit(solution)/shard_map/ppermute | solution.py:444
  89.0 4.8 %collective-permute-start.7 = (bf16[4,512,512]{2,1,0:T(8,128)(2,1)}, bf16[4,512,512]{2,1,0:T(8,128)(2,1)}, u32[]{:S(2)}, u32[]{:S(2)}) collective-permute-start(bf16[4,512,512]{2,1,0:T(8,128)(2,1)} %tiles.7.refs_3_), channel_id=1, source_target_pairs={{0,1},{1,0},{2,3},{3,2},{4,5},{5,4},{6,7},{7,6},{8,9},{9,8},{10,11... | collective-permute-start | bytes 6291464 | tf_op jit(solution)/shard_map/ppermute | solution.py:444
  89.9 36.5 %copy-start.1 = (s32[1,16,1]{1,2,0:T(1,128)S(1)}, s32[1,16,1]{1,2,0:T(1,128)}, u32[]{:S(2)}) copy-start(s32[1,16,1]{1,2,0:T(1,128)} %param.9) | copy-start | bytes 196

commit v9 on v7

--- a/solution.py
+++ b/solution.py
@@ -196,29 +196,50 @@
     )(core, ensemble, increment, coords)
 
 
-def merge_kernel(row, keep_ref, got_ref, own_ref, *send_refs):
-    parts = keep_ref.shape[0]
-    own_ref[...] = keep_ref[row[0]] + got_ref[row[0]]
-    for shift, send_ref in enumerate(send_refs, 1):
-        there = lax.rem(row[0] + shift, parts)
-        send_ref[...] = (keep_ref[there] + got_ref[there]).astype(send_ref.dtype)
+def merge_kernel(row, keep_ref, got_ref, near_ref, far_ref):
+    parts = near_ref.shape[0]
+    for part in range(parts):
+        near = 2 * part + (row[0] & 1)
+        far = 2 * part + 1 - (row[0] & 1)
+        near_ref[part] = keep_ref[near] + got_ref[near]
+        far_ref[part] = (keep_ref[far] + got_ref[far]).astype(far_ref.dtype)
 
 
 def merge(keep, got, row):
-    parts = keep.shape[0]
-    out = [jax.ShapeDtypeStruct(keep.shape[1:], jnp.float32)]
-    out += [jax.ShapeDtypeStruct(keep.shape[1:], jnp.bfloat16)] * (parts - 1)
+    shape = (keep.shape[0] // 2, *keep.shape[1:])
     return pl.pallas_call(
         merge_kernel,
         in_specs=[pl.BlockSpec(memory_space=pltpu.SMEM)] + [pl.BlockSpec(memory_space=pltpu.VMEM)] * 2,
-        out_specs=[pl.BlockSpec(memory_space=pltpu.VMEM)] * parts,
-        out_shape=out,
+        out_specs=[pl.BlockSpec(memory_space=pltpu.VMEM)] * 2,
+        out_shape=[jax.ShapeDtypeStruct(shape, jnp.float32), jax.ShapeDtypeStruct(shape, jnp.bfloat16)],
         compiler_params=pltpu.CompilerParams(vmem_limit_bytes=16 * MIB),
         name="merge",
     )(row, keep, got)
 
 
-def tiles_kernel(pairs, first, places_ref, out_ref, tile_ref, sem):
+def halve_kernel(row, near_ref, got_ref, own_ref, send_ref):
+    mine = row[0] >> 1
+    own_ref[...] = near_ref[mine] + got_ref[mine].astype(jnp.float32)
+    send_ref[...] = (near_ref[1 - mine] + got_ref[1 - mine].astype(jnp.float32)).astype(send_ref.dtype)
+
+
+def halve(near, got, row):
+    shape = near.shape[1:]
+    return pl.pallas_call(
+        halve_kernel,
+        in_specs=[pl.BlockSpec(memory_space=pltpu.SMEM)] + [pl.BlockSpec(memory_space=pltpu.VMEM)] * 2,
+        out_specs=[pl.BlockSpec(memory_space=pltpu.VMEM)] * 2,
+        out_shape=[jax.ShapeDtypeStruct(shape, jnp.float32), jax.ShapeDtypeStruct(shape, jnp.bfloat16)],
+        compiler_params=pltpu.CompilerParams(vmem_limit_bytes=16 * MIB),
+        name="halve",
+    )(row, near, got)
+
+
+def tiles_kernel(pairs, first, source_ref, out_ref, places_ref, tile_ref, sem, places_sem):
+    fetch = pltpu.make_async_copy(source_ref, places_ref, places_sem)
+    fetch.start()
+    fetch.wait()
+
     def copy(within):
         return pltpu.make_async_copy(tile_ref.at[within], out_ref.at[within], sem.at[within])
 
@@ -239,15 +260,20 @@
         in_specs=[
             pl.BlockSpec(memory_space=pltpu.SMEM),
             pl.BlockSpec(memory_space=pltpu.SMEM),
-            pl.BlockSpec(memory_space=pltpu.VMEM),
+            pl.BlockSpec(memory_space=pl.ANY),
         ],
         out_specs=pl.BlockSpec(memory_space=pl.ANY),
         out_shape=pltpu.HBM(shape, jnp.bfloat16),
-        scratch_shapes=[pltpu.VMEM(shape, jnp.bfloat16), pltpu.SemaphoreType.DMA((PAIR_GROUP,))],
+        scratch_shapes=[
+            pltpu.VMEM(places.shape, places.dtype),
+            pltpu.VMEM(shape, jnp.bfloat16),
+            pltpu.SemaphoreType.DMA((PAIR_GROUP,)),
+            pltpu.SemaphoreType.DMA,
+        ],
         compiler_params=pltpu.CompilerParams(vmem_limit_bytes=60 * MIB),
         cost_estimate=pl.CostEstimate(flops=4_000_000_000, bytes_accessed=2_000_000, transcendentals=0),
         name="tiles",
-    )(pairs, first, places)
+    )(pairs, first, in_hbm(places))
 
 
 def apply_kernel(
@@ -404,22 +430,22 @@
     swap = [(i, i ^ 1) for i in range(groups)]
     core, row = own & 1, own >> 1
     rows = groups // 2
+    assert rows == 4
     share = pairs.shape[1] // 2
     keep, send = diag(ensemble, increment, coords, core, rows)
-    merged = merge(keep, lax.ppermute(send, "member", swap), row)
+    near, far = merge(keep, lax.ppermute(send, "member", swap), row)
+    beside = lax.ppermute(far, "member", [(i, i ^ 2) for i in range(groups)])
     own_places, _ = lax.optimization_barrier((own_places, send))
     mine = [tiles(own_places, pairs, core * share + start) for start in range(0, share, PAIR_GROUP)]
     theirs = [lax.ppermute(stack, "member", swap) for stack in mine]
-    got, merged = lax.optimization_barrier((got, merged))
+    got, near, beside = lax.optimization_barrier((got, near, beside))
     stacks = [in_hbm(stack) for stack in mine + theirs]
     partial = apply_pairs(in_hbm(got), stacks, pairs, pair_count, core, members, step)
-    partial, merged = lax.optimization_barrier((partial, merged))
-    parts = [
-        lax.ppermute(part, "member", [(i, (i + 2 * hop) % groups) for i in range(groups)])
-        for hop, part in enumerate(merged[1:], 1)
-    ]
+    partial, near, beside = lax.optimization_barrier((partial, near, beside))
+    diagonal, send = halve(near, beside, row)
+    opposite = lax.ppermute(send, "member", [(i, i ^ 4) for i in range(groups)])
     back = lax.all_to_all(partial, "region", 0, 0, tiled=True)
-    return finish(merged[0], parts, back, slots, 1.0 / (members * groups - 1))
+    return finish(diagonal, [opposite], back, slots, 1.0 / (members * groups - 1))
 
 
 def solution(mesh):

time: 117 us -> 119 us (1.017)
  starting transfers between devices: 28.1 us -> 30.4 us
  Pallas kernels: 64.1 us -> 66.2 us
  waiting for transfers between devices: 21.5 us -> 20.2 us
    all_to_all x1, waiting for transfers between devices: 9.4 us -> 0.01 us  [per_device(): lax.all_to_all(big.reshape(regions * groups, -1, LANES), ('region', 'memb...]
    ppermute x4 -> x3, waiting for transfers between devices: 10.1 us -> 16.2 us  [the longest x1 6.8 us: per_device(): beside = lax.ppermute(far, 'member', [(i, i ^ 2) for i in range(groups)])]
    all_to_all x1, starting transfers between devices: 4.35 us -> 8.25 us  [per_device(): back = lax.all_to_all(partial, 'region', 0, 0, tiled=True)]
    pallas_call x4, Pallas kernels: 19.9 us -> 22.7 us  [tiles(): pl.pallas_call(tiles_kernel, in_specs=[pl.BlockSpec(memory_space=pltpu.SM...]
    all_to_all x1, waiting for transfers between devices: 0.01 us -> 2.08 us  [per_device(): back = lax.all_to_all(partial, 'region', 0, 0, tiled=True)]
    ppermute x4 -> x3, starting transfers between devices: 5.87 us -> 4.26 us  [the longest x1 3.19 us: per_device(): opposite = lax.ppermute(send, 'member', [(i, i ^ 4) for i in range(groups)])]
  transfers between devices with their start and end apart: 11 -> 10, of which waited for: 5 -> 5; matrix products, arithmetic and copies ran while one was open for 0% -> 0% of each run, Pallas kernels for 38% -> 40%
where the time goes in v9:
time: 119 us; the launch traced here: 118 us
  Pallas kernels  66.2 us (56%)
  starting transfers between devices  30.4 us (26%)
  waiting for transfers between devices  20.2 us (17%)
    pallas_call x4, Pallas kernels, tiles(): pl.pallas_call(tiles_kernel, in_specs=[pl.BlockSpec(memory_space=pltpu.SM...  22.7 us
    pallas_call x1, Pallas kernels, diag(): pl.pallas_call(diag_kernel, grid_spec=pltpu.PrefetchScalarGridSpec(num_sc...  18.7 us
    pallas_call x1, Pallas kernels, apply_pairs(): pl.pallas_call(apply_kernel, in_specs=[pl.BlockSpec(memory_space=pltpu.SM...  14.8 us
    all_to_all x1, starting transfers between devices, per_device(): lax.all_to_all(big.reshape(regions * groups, -1, LANES), ('region', 'memb...  8.88 us
    all_to_all x1, starting transfers between devices, per_device(): back = lax.all_to_all(partial, 'region', 0, 0, tiled=True)  8.25 us
    all_to_all x1, starting transfers between devices, per_device(): own_places = lax.all_to_all(places, 'region', 0, 0, tiled=True)  7.97 us
    ppermute x1, waiting for transfers between devices, per_device(): beside = lax.ppermute(far, 'member', [(i, i ^ 2) for i in range(groups)])  6.8 us
    ppermute x1, waiting for transfers between devices, per_device(): near, far = merge(keep, lax.ppermute(send, 'member', swap), row)  6.04 us
  transfers between devices with their start and end apart: 10, of which 5 were waited for; matrix products, arithmetic and copies ran while one was open for 0% of the time, Pallas kernels for 40%

profile of v9, /device:TPU:0, one launch (start us, length us, event | category | flops | bytes accessed | tf_op | source)
XLA Modules:
  0.0 118.3 jit_solution(5425806364132710845)
XLA Ops:
  0.0 2.9 %select.1 = bf16[16,2,512]{2,1,0:T(2,128)(2,1)} custom-call(s32[16]{0:T(128)} %bitcast.5, bf16[16,2,512]{2,1,0:T(2,128)(2,1)} %coords_ref.3), custom_call_target="tpu_custom_call" | custom-call | tf_op jit(solution)/shard_map/select/pallas_call | solution.py:32
  2.9 8.0 %all-to-all-start = ((bf16[16,2,512]{2,1,0:T(2,128)(2,1)}), bf16[16,2,512]{2,1,0:T(2,128)(2,1)S(1)}, u32[]{:S(2)}, u32[]{:S(2)}) async-start(bf16[16,2,512]{2,1,0:T(2,128)(2,1)} %select.1), calls=%async_computation | async-start | bytes 65536 | tf_op jit(solution)/shard_map/all_to_all | solution.py:424
  10.9 5.7 %pack.1 = bf16[16,8,136,128]{3,2,1,0:T(8,128)(2,1)} custom-call(s32[16]{0:T(128)} %bitcast.6, s32[1]{0:T(128)} %bitcast.1.own, bf16[16,4,64,512]{3,2,1,0:T(8,128)(2,1)} %ens_ref.3, bf16[16,64,512]{2,1,0:T(8,128)(2,1)} %inc_ref.3), custom_call_target="tpu_custom_call" | custom-call | tf_op jit(solution)/shard_map/pack/pallas_call | solution.py:82
  16.6 1.9 %all-to-all-done.source_ref = bf16[16,2,512]{2,1,0:T(2,128)(2,1)S(1)} async-done(((bf16[16,2,512]{2,1,0:T(2,128)(2,1)}), bf16[16,2,512]{2,1,0:T(2,128)(2,1)S(1)}, u32[]{:S(2)}, u32[]{:S(2)}) %all-to-all-start) | async-done | bytes 32800 | tf_op jit(solution)/shard_map/all_to_all | solution.py:424
  18.5 0.6 copy-done.2
  19.1 8.9 %all-to-all-start.1 = ((bf16[128,136,128]{2,1,0:T(8,128)(2,1)}), bf16[128,136,128]{2,1,0:T(8,128)(2,1)}, u32[]{:S(2)}, u32[]{:S(2)}) async-start(bf16[128,136,128]{2,1,0:T(8,128)(2,1)} %bitcast.8), calls=%async_computation.1 | async-start | bytes 8912896 | tf_op jit(solution)/shard_map/all_to_all | solution.py:427
  28.0 18.7 %diag.1 = (f32[4,16,8,512]{3,2,1,0:T(8,128)}, f32[4,16,8,512]{3,2,1,0:T(8,128)}) custom-call(s32[1]{0:T(128)S(6)} %and.4.core, bf16[16,4,64,512]{3,2,1,0:T(8,128)(2,1)} %ens_ref.3, bf16[16,64,512]{2,1,0:T(8,128)(2,1)} %inc_ref.3, bf16[16,2,512]{2,1,0:T(2,128)(2,1)} %coords_ref.3), custom_call_target="tpu_custom_call" | custom-call | flops 20000000000 | bytes 8000000 | tf_op jit(solution)/shard_map/diag/pallas_call | solution.py:179
  46.6 5.6 %tiles.4.refs_0_ = bf16[4,512,512]{2,1,0:T(8,128)(2,1)} custom-call(s32[2,32]{1,0:T(2,128)} %bitcast.9, s32[1]{0:T(128)S(6)} %mul.2.first, bf16[16,2,512]{2,1,0:T(2,128)(2,1)} %copy-done.2), custom_call_target="tpu_custom_call" | custom-call | flops 4000000000 | bytes 2000000 | tf_op jit(solution)/shard_map/tiles/pallas_call | solution.py:258
  52.2 5.6 %tiles.7.refs_3_ = bf16[4,512,512]{2,1,0:T(8,128)(2,1)} custom-call(s32[2,32]{1,0:T(2,128)} %bitcast.10, s32[1]{0:T(128)S(6)} %add.11.first, bf16[16,2,512]{2,1,0:T(2,128)(2,1)} %copy-done.2), custom_call_target="tpu_custom_call" | custom-call | flops 4000000000 | bytes 2000000 | tf_op jit(solution)/shard_map/tiles/pallas_call | solution.py:258
  57.8 5.6 %tiles.6.refs_2_ = bf16[4,512,512]{2,1,0:T(8,128)(2,1)} custom-call(s32[2,32]{1,0:T(2,128)} %bitcast.11, s32[1]{0:T(128)S(6)} %add.10.first, bf16[16,2,512]{2,1,0:T(2,128)(2,1)} %copy-done.2), custom_call_target="tpu_custom_call" | custom-call | flops 4000000000 | bytes 2000000 | tf_op jit(solution)/shard_map/tiles/pallas_call | solution.py:258
  63.4 6.0 %tiles.5.refs_1_ = bf16[4,512,512]{2,1,0:T(8,128)(2,1)} custom-call(s32[2,32]{1,0:T(2,128)} %bitcast.12, s32[1]{0:T(128)S(6)} %add.9.first, bf16[16,2,512]{2,1,0:T(2,128)(2,1)} %copy-done.2), custom_call_target="tpu_custom_call" | custom-call | flops 4000000000 | bytes 2000000 | tf_op jit(solution)/shard_map/tiles/pallas_call | solution.py:258
  69.4 0.1 collective-permute-start.2
  69.5 0.5 collective-permute-start.3
  70.0 0.1 collective-permute-start.4
  70.1 0.4 collective-permute-start.5
  70.5 0.1 collective-permute-start
  70.6 6.0 %collective-permute-done.got_ref = f32[4,16,8,512]{3,2,1,0:T(8,128)S(1)} collective-permute-done((f32[4,16,8,512]{3,2,1,0:T(8,128)S(1)}, f32[4,16,8,512]{3,2,1,0:T(8,128)S(1)}, u32[]{:S(2)}, u32[]{:S(2)}) %collective-permute-start) | collective-permute-done | bytes 1048608 | tf_op jit(solution)/shard_map/ppermute | solution.py:436
  76.6 0.1 merge.1
  76.7 1.0 collective-permute-start.1
  78.3 6.8 %collective-permute-done.1.got_ref = bf16[2,16,8,512]{3,2,1,0:T(8,128)(2,1)S(1)} collective-permute-done((bf16[2,16,8,512]{3,2,1,0:T(8,128)(2,1)S(1)}, bf16[2,16,8,512]{3,2,1,0:T(8,128)(2,1)S(1)}, u32[]{:S(2)}, u32[]{:S(2)}) %collective-permute-start.1) | collective-permute-done | bytes 262176 | tf_op jit(solution)/shard_map/ppermute | solution.py:437
  85.1 0.0 all-to-all-done.1
  85.1 0.0 collective-permute-done.2.refs_4_
  85.2 0.0 collective-permute-done.3.refs_5_
  85.2 0.0 collective-permute-done.4.refs_6_
  85.2 0.0 collective-permute-done.5.refs_7_
  85.2 14.8 %apply.1 = f32[16,8,512]{2,1,0:T(8,128)} custom-call(s32[2,32]{1,0:T(2,128)} %bitcast.13, s32[1]{0:T(128)S(6)} %copy.7.count, s32[1]{0:T(128)S(6)} %and.4.core, bf16[16,8,136,128]{3,2,1,0:T(8,128)(2,1)} %bitcast.4.got_ref, bf16[4,512,512]{2,1,0:T(8,128)(2,1)} %tiles.4.refs_0_, bf16[4,512,512]{2,1,0:T(8,128)(2,1)} %tiles.5.refs_1_, ...), custom_call_target="tpu_custom_call" | custom-call | flops 8999999488 | bytes 22000000 | tf_op jit(solution)/shard_map/apply/pallas_call | solution.py:366
  100.0 8.2 %all-to-all-start.2 = ((f32[16,8,512]{2,1,0:T(8,128)}), f32[16,8,512]{2,1,0:T(8,128)S(1)}, u32[]{:S(2)}, u32[]{:S(2)}) async-start(f32[16,8,512]{2,1,0:T(8,128)} %apply.1), calls=%async_computation.2 | async-start | bytes 524288 | tf_op jit(solution)/shard_map/all_to_all | solution.py:447
  108.2 0.1 halve.1
  108.3 3.2 %collective-permute-start.6 = (bf16[16,8,512]{2,1,0:T(8,128)(2,1)S(1)}, bf16[16,8,512]{2,1,0:T(8,128)(2,1)S(1)}, u32[]{:S(2)}, u32[]{:S(2)}) collective-permute-start(bf16[16,8,512]{2,1,0:T(8,128)(2,1)S(1)} %get-tuple-element.33), channel_id=1, source_target_pairs={{0,4},{1,5},{2,6},{3,7},{4,0},{5,1},{6,2},{7,3},{8,12},{9,13},{10,... | collective-permute-start | bytes 393224 | tf_op jit(solution)/shard_map/ppermute | solution.py:446
  111.5 3.4 %collective-permute-done.6.refs_0_ = bf16[16,8,512]{2,1,0:T(8,128)(2,1)S(1)} collective-permute-done((bf16[16,8,512]{2,1,0:T(8,128)(2,1)S(1)}, bf16[16,8,512]{2,1,0:T(8,128)(2,1)S(1)}, u32[]{:S(2)}, u32[]{:S(2)}) %collective-permute-start.6) | collective-permute-done | bytes 131104 | tf_op jit(solution)/shard_map/ppermute | solution.py:446
  114.8 2.1 %all-to-all-done.2.refs_1_ = f32[16,8,512]{2,1,0:T(8,128)S(1)} async-done(((f32[16,8,512]{2,1,0:T(8,128)}), f32[16,8,512]{2,1,0:T(8,128)S(1)}, u32[]{:S(2)}, u32[]{:S(2)}) %all-to-all-start.2) | async-done | bytes 262176 | tf_op jit(solution)/shard_map/all_to_all | solution.py:447
  116.9 1.4 %finish.1 = f32[16,8,512]{2,1,0:T(8,128)} custom-call(s32[16]{0:T(128)S(1)} %bitcast.7, f32[16,8,512]{2,1,0:T(8,128)S(1)} %get-tuple-element.32.own_ref, bf16[16,8,512]{2,1,0:T(8,128)(2,1)S(1)} %collective-permute-done.6.refs_0_, f32[16,8,512]{2,1,0:T(8,128)S(1)} %all-to-all-done.2.refs_1_), custom_call_target="tpu_custom_call" | custom-call | tf_op jit(solution)/shard_map/finish/pallas_call | solution.py:405
  (7 shorter events, 0.0 us)
Async XLA Ops:
  2.9 15.6 %all-to-all-start = ((bf16[16,2,512]{2,1,0:T(2,128)(2,1)}), bf16[16,2,512]{2,1,0:T(2,128)(2,1)S(1)}, u32[]{:S(2)}, u32[]{:S(2)}) async-start(bf16[16,2,512]{2,1,0:T(2,128)(2,1)} %select.1), calls=%async_computation | async-start | bytes 65536 | tf_op jit(solution)/shard_map/all_to_all | solution.py:424
  18.5 0.6 copy-start.2
  19.1 66.0 %all-to-all-start.1 = ((bf16[128,136,128]{2,1,0:T(8,128)(2,1)}), bf16[128,136,128]{2,1,0:T(8,128)(2,1)}, u32[]{:S(2)}, u32[]{:S(2)}) async-start(bf16[128,136,128]{2,1,0:T(8,128)(2,1)} %bitcast.8), calls=%async_computation.1 | async-start | bytes 8912896 | tf_op jit(solution)/shard_map/all_to_all | solution.py:427
  63.4 7.1 %copy-start.3 = (f32[4,16,8,512]{3,2,1,0:T(8,128)S(1)}, f32[4,16,8,512]{3,2,1,0:T(8,128)}, u32[]{:S(2)}) copy-start(f32[4,16,8,512]{3,2,1,0:T(8,128)} %get-tuple-element.22) | copy-start | bytes 3145732
  63.4 13.2 %copy-start = (f32[4,16,8,512]{3,2,1,0:T(8,128)S(1)}, f32[4,16,8,512]{3,2,1,0:T(8,128)}, u32[]{:S(2)}) copy-start(f32[4,16,8,512]{3,2,1,0:T(8,128)} %get-tuple-element.21.keep_ref) | copy-start | bytes 3145732
  69.4 15.8 %collective-permute-start.2 = (bf16[4,512,512]{2,1,0:T(8,128)(2,1)}, bf16[4,512,512]{2,1,0:T(8,128)(2,1)}, u32[]{:S(2)}, u32[]{:S(2)}) collective-permute-start(bf16[4,512,512]{2,1,0:T(8,128)(2,1)} %tiles.4.refs_0_), channel_id=1, source_target_pairs={{0,1},{1,0},{2,3},{3,2},{4,5},{5,4},{6,7},{7,6},{8,9},{9,8},{10,11... | collective-permute-start | bytes 6291464 | tf_op jit(solution)/shard_map/ppermute | solution.py:440
  69.5 15.7 %collective-permute-start.3 = (bf16[4,512,512]{2,1,0:T(8,128)(2,1)}, bf16[4,512,512]{2,1,0:T(8,128)(2,1)}, u32[]{:S(2)}, u32[]{:S(2)}) collective-permute-start(bf16[4,512,512]{2,1,0:T(8,128)(2,1)} %tiles.5.refs_1_), channel_id=1, source_target_pairs={{0,1},{1,0},{2,3},{3,2},{4,5},{5,4},{6,7},{7,6},{8,9},{9,8},{10,11... | collective-permute-start | bytes 6291464 | tf_op jit(solution)/shard_map/ppermute | solution.py:440
  70.0 15.2 %collective-permute-start.4 = (bf16[4,512,512]{2,1,0:T(8,128)(2,1)}, bf16[4,512,512]{2,1,0:T(8,128)(2,1)}, u32[]{:S(2)}, u32[]{:S(2)}) collective-permute-start(bf16[4,512,512]{2,1,0:T(8,128)(2,1)} %tiles.6.refs_2_), channel_id=1, source_target_pairs={{0,1},{1,0},{2,3},{3,2},{4,5},{5,4},{6,7},{7,6},{8,9},{9,8},{10,11... | collective-permute-start | bytes 6291464 | tf_op jit(solution)/shard_map/ppermute | solution.py:440
  70.1 15.1 %collective-permute-start.5 = (bf16[4,512,512]{2,1,0:T(8,128)(2,1)}, bf16[4,512,512]{2,1,0:T(8,128)(2,1)}, u32[]{:S(2)}, u32[]{:S(2)}) collective-permute-start(bf16[4,512,512]{2,1,0:T(8,128)(2,1)} %tiles.7.refs_3_), channel_id=1, source_target_pairs={{0,1},{1,0},{2,3},{3,2},{4,5},{5,4},{6,7},{7,6},{8,9},{9,8},{10,11... | collective-permute-start | bytes 6291464 | tf_op jit(solution)/shard_map/ppermute | solution.py:440
  70.5 6.1 %collective-permute-start = (f32[4,16,8,512]{3,2,1,0:T(8,128)S(1)}, f32[4,16,8,512]{3,2,1,0:T(8,128)S(1)}, u32[]{:S(2)}, u32[]{:S(2)}) collective-permute-start(f32[4,16,8,512]{3,2,1,0:T(8,128)S(1)} %copy-done.3), channel_id=1, source_target_pairs={{0,1},{1,0},{2,3},{3,2},{4,5},{5,4},{6,7},{7,6},{8,9},{9,8},{10,11... | collective-permute-start | bytes 3145736 | tf_op jit(solution)/shard_map/ppermute | solution.py:436
  76.7 8.4 %collective-permute-start.1 = (bf16[2,16,8,512]{3,2,1,0:T(8,128)(2,1)S(1)}, bf16[2,16,8,512]{3,2,1,0:T(8,128)(2,1)S(1)}, u32[]{:S(2)}, u32[]{:S(2)}) collective-permute-start(bf16[2,16,8,512]{3,2,1,0:T(8,128)(2,1)S(1)} %get-tuple-element.24), channel_id=1, source_target_pairs={{0,2},{1,3},{2,0},{3,1},{4,6},{5,7},{6,4},{7,5},{8,10},{9,11},{10,... | collective-permute-start | bytes 786440 | tf_op jit(solution)/shard_map/ppermute | solution.py:437
  85.1 31.8 %copy-start.1 = (s32[1,16,1]{1,2,0:T(1,128)S(1)}, s32[1,16,1]{1,2,0:T(1,128)}, u32[]{:S(2)}) copy-start(s32[1,16,1]{1,2,0:T(1,128)} %param.9) | copy-start | bytes 196
  100.0 16.9 %all-to-all-start.2 = ((f32[16,8,512]{2,1,0:T(8,128)}), f32[16,8,512]{2,1,0:T(8,128)S(1)}, u32[]{:S(2)}, u32[]{:S(2)}) async-start(f32[16,8,512]{2,1,0:T(8,128)} %apply.1), calls=%async_computation.2 | async-start | bytes 524288 | tf_op jit(solution)/shard_map/all_to_all | solution.py:447
  108.3 6.6 %collective-permute-start.6 = (bf16[16,8,512]{2,1,0:T(8,128)(2,1)S(1)}, bf16[16,8,512]{2,1,0:T(8,128)(2,1)S(1)}, u32[]{:S(2)}, u32[]{:S(2)}) collective-permute-start(bf16[16,8,512]{2,1,0:T(8,128)(2,1)S(1)} %get-tuple-element.33), channel_id=1, source_target_pairs={{0,4},{1,5},{2,6},{3,7},{4,0},{5,1},{6,2},{7,3},{8,12},{9,13},{10,... | collective-permute-start | bytes 393224 | tf_op jit(solution)/shard_map/ppermute | solution.py:446

commit v10 on v7

--- a/solution.py
+++ b/solution.py
@@ -15,32 +15,43 @@
 LEAST = UNIT2 * 2.0**-12
 
 
-def select_kernel(slots, coords_ref, places_ref, sem):
-    total = places_ref.shape[0]
+def select_kernel(slots, own, inc_ref, coords_ref, out_ref, sem):
+    total, rows, _ = out_ref.shape
+    step = rows - coords_ref.shape[1]
+    first = pl.multiple_of(own[0] * step, step)
 
     def copy(owner):
-        return pltpu.make_async_copy(coords_ref.at[slots[owner]], places_ref.at[owner], sem.at[owner])
+        return pltpu.make_async_copy(
+            inc_ref.at[slots[owner], pl.ds(first, step), :], out_ref.at[owner, :step, :], sem.at[owner]
+        )
 
     for owner in range(total):
         copy(owner).start()
     for owner in range(total):
+        out_ref[owner, step:, :] = coords_ref[slots[owner]]
+    for owner in range(total):
         copy(owner).wait()
 
 
-def select(coords, slots):
-    total = slots.shape[0]
+def select(increment, coords, slots, own, step):
+    total, points = slots.shape[0], coords.shape[2]
     return pl.pallas_call(
         select_kernel,
-        in_specs=[pl.BlockSpec(memory_space=pltpu.SMEM), pl.BlockSpec(memory_space=pl.ANY)],
-        out_specs=pl.BlockSpec(memory_space=pl.ANY),
-        out_shape=jax.ShapeDtypeStruct((total, *coords.shape[1:]), coords.dtype),
+        in_specs=[
+            pl.BlockSpec(memory_space=pltpu.SMEM),
+            pl.BlockSpec(memory_space=pltpu.SMEM),
+            pl.BlockSpec(memory_space=pl.ANY),
+            pl.BlockSpec(memory_space=pltpu.VMEM),
+        ],
+        out_specs=pl.BlockSpec(memory_space=pltpu.VMEM),
+        out_shape=jax.ShapeDtypeStruct((total, step + coords.shape[1], points), coords.dtype),
         scratch_shapes=[pltpu.SemaphoreType.DMA((total,))],
         compiler_params=pltpu.CompilerParams(vmem_limit_bytes=60 * MIB),
         name="select",
-    )(slots, coords)
-
-
-def pack_kernel(slots, own, ens_ref, inc_ref, big_ref, ens_buf, inc_buf, out_buf, in_sem, inc_sem, out_sem):
+    )(slots, own, increment, coords)
+
+
+def pack_kernel(slots, ens_ref, big_ref, ens_buf, out_buf, in_sem, out_sem):
     total, members, levels, points = ens_buf.shape
     parts = out_buf.shape[1]
     step = levels // parts
@@ -49,57 +60,42 @@
     def ens_copy(owner):
         return pltpu.make_async_copy(ens_ref.at[slots[owner]], ens_buf.at[owner], in_sem.at[owner])
 
-    def inc_copy(owner):
-        return pltpu.make_async_copy(inc_ref.at[slots[owner]], inc_buf.at[owner], inc_sem.at[owner])
-
     def out_copy(owner):
         return pltpu.make_async_copy(out_buf.at[owner], big_ref.at[owner], out_sem.at[owner])
 
     for owner in range(total):
         ens_copy(owner).start()
-        inc_copy(owner).start()
-    chunk = pl.multiple_of(lax.rem(own[0], lane_chunks) * LANES, LANES)
     for owner in range(total):
         ens_copy(owner).wait()
-        inc_copy(owner).wait()
         for part in range(parts):
             here = slice(part * step, (part + 1) * step)
             for lane in range(lane_chunks):
                 out_buf[owner, part, lane * members * step : (lane + 1) * members * step, :] = ens_buf[
                     owner, :, here, lane * LANES : (lane + 1) * LANES
                 ].reshape(members * step, LANES)
-            out_buf[owner, part, members * step * lane_chunks :, :] = inc_buf[owner, here, pl.ds(chunk, LANES)]
         out_copy(owner).start()
     for owner in range(total):
         out_copy(owner).wait()
 
 
-def pack(ensemble, increment, slots, own, parts):
+def pack(ensemble, slots, parts):
     blocks, members, levels, points = ensemble.shape
     total = slots.shape[0]
-    step = levels // parts
-    rows = members * step * (points // LANES) + step
+    rows = members * (levels // parts) * (points // LANES)
     return pl.pallas_call(
         pack_kernel,
-        in_specs=[
-            pl.BlockSpec(memory_space=pltpu.SMEM),
-            pl.BlockSpec(memory_space=pltpu.SMEM),
-            pl.BlockSpec(memory_space=pl.ANY),
-            pl.BlockSpec(memory_space=pl.ANY),
-        ],
+        in_specs=[pl.BlockSpec(memory_space=pltpu.SMEM), pl.BlockSpec(memory_space=pl.ANY)],
         out_specs=pl.BlockSpec(memory_space=pl.ANY),
         out_shape=jax.ShapeDtypeStruct((total, parts, rows, LANES), ensemble.dtype),
         scratch_shapes=[
             pltpu.VMEM((total, members, levels, points), ensemble.dtype),
-            pltpu.VMEM((total, levels, points), increment.dtype),
             pltpu.VMEM((total, parts, rows, LANES), ensemble.dtype),
-            pltpu.SemaphoreType.DMA((total,)),
             pltpu.SemaphoreType.DMA((total,)),
             pltpu.SemaphoreType.DMA((total,)),
         ],
         compiler_params=pltpu.CompilerParams(vmem_limit_bytes=60 * MIB),
         name="pack",
-    )(slots, own, ensemble, increment)
+    )(slots, ensemble)
 
 
 def in_hbm(value):
@@ -224,8 +220,8 @@
 
     for within in range(tile_ref.shape[0]):
         index = first[0] + within
-        left = left_rows(places_ref[pairs[0, index]].astype(jnp.float32))
-        right = right_rows(places_ref[pairs[1, index]].astype(jnp.float32))
+        left = left_rows(places_ref[pairs[0, index], -2:, :].astype(jnp.float32))
+        right = right_rows(places_ref[pairs[1, index], -2:, :].astype(jnp.float32))
         tile_ref[within] = tile_of(left, right)
         copy(within).start()
     for within in range(tile_ref.shape[0]):
@@ -251,11 +247,11 @@
 
 
 def apply_kernel(
-    pairs, count, core, got_ref, *refs,
+    pairs, count, core, got_ref, small_ref, *refs,
 ):
     *stacks, out_ref, ens_ref, inc_ref, weighted_ref, field_ref, tiles_ref, ens_sem, inc_sem, tiles_sem = refs
     slot_total, sources, rows, points = ens_ref.shape
-    step = inc_ref.shape[2]
+    step = inc_ref.shape[1]
     groups = len(stacks)
     lane_chunks = points // LANES
     every = sources * rows
@@ -270,7 +266,7 @@
             for lane in range(lane_chunks)
         ]
 
-    inc_copy = pltpu.make_async_copy(got_ref.at[:, :lane_chunks, rows * lane_chunks :, :], inc_ref, inc_sem)
+    inc_copy = pltpu.make_async_copy(small_ref.at[:, :step, :], inc_ref, inc_sem)
 
     def tile_copy(group):
         return pltpu.make_async_copy(stacks[group], tiles_ref.at[group], tiles_sem.at[group])
@@ -286,11 +282,8 @@
         field_ref[slot] = jnp.zeros((every, points), jnp.float32)
         for copy in ens_copies(slot):
             copy.wait()
-        for lane in range(lane_chunks):
-            here = slice(lane * LANES, (lane + 1) * LANES)
-            gain = inc_ref[slot, lane]
-            block = ens_ref[slot, :, :, here].reshape(every // step, step, LANES)
-            weighted_ref[slot, :, here] = (block * gain[None]).reshape(every, LANES)
+        block = ens_ref[slot].reshape(every // step, step, points)
+        weighted_ref[slot] = (block * inc_ref[slot][None]).reshape(every, points)
 
     def some(group, row, within, number):
         products = []
@@ -332,7 +325,7 @@
         out_ref[slot] = jnp.sum(product.reshape(every // step, step, points), axis=0)
 
 
-def apply_pairs(got, stacks, pairs, count, core, members, step):
+def apply_pairs(got, small, stacks, pairs, count, core, members, step):
     slot_total, sources, rows, _ = got.shape
     points = stacks[0].shape[2]
     lane_chunks = points // LANES
@@ -344,12 +337,12 @@
             pl.BlockSpec(memory_space=pltpu.SMEM),
             pl.BlockSpec(memory_space=pltpu.SMEM),
             pl.BlockSpec(memory_space=pl.ANY),
-            *[pl.BlockSpec(memory_space=pl.ANY)] * len(stacks),
+            *[pl.BlockSpec(memory_space=pl.ANY)] * (len(stacks) + 1),
         ],
         out_specs=pl.BlockSpec(memory_space=pltpu.VMEM),
         scratch_shapes=[
             pltpu.VMEM((slot_total, sources, members * step, points), jnp.bfloat16),
-            pltpu.VMEM((slot_total, lane_chunks, step, LANES), jnp.bfloat16),
+            pltpu.VMEM((slot_total, step, points), jnp.bfloat16),
             pltpu.VMEM((slot_total, every, points), jnp.bfloat16),
             pltpu.VMEM((slot_total, every, points), jnp.float32),
             pltpu.VMEM((len(stacks), *stacks[0].shape), jnp.bfloat16),
@@ -361,7 +354,7 @@
         compiler_params=pltpu.CompilerParams(vmem_limit_bytes=60 * MIB),
         cost_estimate=pl.CostEstimate(flops=9_000_000_000, bytes_accessed=22_000_000, transcendentals=0),
         name="apply",
-    )(pairs, count, core, got, *stacks)
+    )(pairs, count, core, got, small, *stacks)
 
 
 def finish_kernel(slots, own_ref, *refs, scale):
@@ -394,10 +387,9 @@
     slots = sent_slots.reshape(-1)
     pairs = pair_list.T
     own = lax.axis_index("member").reshape(1).astype(jnp.int32)
-    places = select(coords, slots)
-    own_places = lax.all_to_all(places, "region", 0, 0, tiled=True)
-    big = pack(ensemble, increment, slots, own, groups)
-    big, own_places = lax.optimization_barrier((big, own_places))
+    small = lax.all_to_all(select(increment, coords, slots, own, step), "region", 0, 0, tiled=True)
+    big = pack(ensemble, slots, groups)
+    big, small = lax.optimization_barrier((big, small))
     got = lax.all_to_all(
         big.reshape(regions * groups, -1, LANES), ("region", "member"), 0, 0, tiled=True
     ).reshape(regions, groups, -1, LANES)
@@ -407,12 +399,12 @@
     share = pairs.shape[1] // 2
     keep, send = diag(ensemble, increment, coords, core, rows)
     merged = merge(keep, lax.ppermute(send, "member", swap), row)
-    own_places, _ = lax.optimization_barrier((own_places, send))
-    mine = [tiles(own_places, pairs, core * share + start) for start in range(0, share, PAIR_GROUP)]
+    small, _ = lax.optimization_barrier((small, send))
+    mine = [tiles(small, pairs, core * share + start) for start in range(0, share, PAIR_GROUP)]
     theirs = [lax.ppermute(stack, "member", swap) for stack in mine]
     got, merged = lax.optimization_barrier((got, merged))
     stacks = [in_hbm(stack) for stack in mine + theirs]
-    partial = apply_pairs(in_hbm(got), stacks, pairs, pair_count, core, members, step)
+    partial = apply_pairs(in_hbm(got), in_hbm(small), stacks, pairs, pair_count, core, members, step)
     partial, merged = lax.optimization_barrier((partial, merged))
     parts = [
         lax.ppermute(part, "member", [(i, (i + 2 * hop) % groups) for i in range(groups)])

time: 117 us -> 117 us (level); the launches traced: 115 us -> 117 us
  starting transfers between devices: 28.1 us -> 31.3 us
  Pallas kernels: 64.1 us -> 62.4 us
    all_to_all x1, starting transfers between devices: 4.35 us -> 9.04 us  [per_device(): back = lax.all_to_all(partial, 'region', 0, 0, tiled=True)]
    all_to_all x1, waiting for transfers between devices: 9.4 us -> 5.81 us  [per_device(): lax.all_to_all(big.reshape(regions * groups, -1, LANES), ('region', 'memb...]
    ppermute x4, waiting for transfers between devices: 0.01 us -> 1.91 us  [per_device(): theirs = [lax.ppermute(stack, 'member', swap) for stack in mine]]
    pallas_call x1, Pallas kernels: 15.6 us -> 14 us  [apply_pairs(): pl.pallas_call(apply_kernel, in_specs=[pl.BlockSpec(memory_space=pltpu.SM...]
    all_to_all x1, starting transfers between devices: 8.82 us -> 7.33 us  [per_device(): lax.all_to_all(big.reshape(regions * groups, -1, LANES), ('region', 'memb...]
    all_to_all x1, waiting for transfers between devices: 2.05 us -> 3.51 us  [per_device(): lax.all_to_all(select(increment, coords, slots, own, step), 'region', 0,...]
  transfers between devices with their start and end apart: 11 -> 11, of which waited for: 5 -> 6; matrix products, arithmetic and copies ran while one was open for 0% -> 0% of each run, Pallas kernels for 38% -> 38%
where the time goes in v10:
time: 117 us
  Pallas kernels  62.4 us (53%)
  starting transfers between devices  31.3 us (27%)
  waiting for transfers between devices  21.3 us (18%)
    pallas_call x4, Pallas kernels, tiles(): pl.pallas_call(tiles_kernel, in_specs=[pl.BlockSpec(memory_space=pltpu.SM...  20.7 us
    pallas_call x1, Pallas kernels, diag(): pl.pallas_call(diag_kernel, grid_spec=pltpu.PrefetchScalarGridSpec(num_sc...  18.6 us
    pallas_call x1, Pallas kernels, apply_pairs(): pl.pallas_call(apply_kernel, in_specs=[pl.BlockSpec(memory_space=pltpu.SM...  14 us
    all_to_all x1, starting transfers between devices, per_device(): back = lax.all_to_all(partial, 'region', 0, 0, tiled=True)  9.04 us
    all_to_all x1, starting transfers between devices, per_device(): lax.all_to_all(select(increment, coords, slots, own, step), 'region', 0,...  7.97 us
    all_to_all x1, starting transfers between devices, per_device(): lax.all_to_all(big.reshape(regions * groups, -1, LANES), ('region', 'memb...  7.33 us
    all_to_all x1, waiting for transfers between devices, per_device(): lax.all_to_all(big.reshape(regions * groups, -1, LANES), ('region', 'memb...  5.81 us
    ppermute x3, starting transfers between devices, per_device(): lax.ppermute(part, 'member', [(i, (i + 2 * hop) % groups) for i in range(...  5.8 us
  transfers between devices with their start and end apart: 11, of which 6 were waited for; matrix products, arithmetic and copies ran while one was open for 0% of the time, Pallas kernels for 38%

profile of v10, /device:TPU:0, one launch (start us, length us, event | category | flops | bytes accessed | tf_op | source)
XLA Modules:
  0.0 116.5 jit_solution(728361264951734024)
XLA Ops:
  0.0 2.5 %select.1 = bf16[16,10,512]{2,1,0:T(8,128)(2,1)} custom-call(s32[16]{0:T(128)} %bitcast.5, s32[1]{0:T(128)} %bitcast.2.own, bf16[16,64,512]{2,1,0:T(8,128)(2,1)} %inc_ref.3, bf16[16,2,512]{2,1,0:T(2,128)(2,1)} %coords_ref.3), custom_call_target="tpu_custom_call" | custom-call | tf_op jit(solution)/shard_map/select/pallas_call | solution.py:38
  2.5 8.0 %all-to-all-start = ((bf16[16,10,512]{2,1,0:T(8,128)(2,1)}), bf16[16,10,512]{2,1,0:T(8,128)(2,1)S(1)}, u32[]{:S(2)}, u32[]{:S(2)}) async-start(bf16[16,10,512]{2,1,0:T(8,128)(2,1)} %select.1), calls=%async_computation | async-start | bytes 524288 | tf_op jit(solution)/shard_map/all_to_all | solution.py:390
  10.5 5.2 %pack.1 = bf16[16,8,128,128]{3,2,1,0:T(8,128)(2,1)} custom-call(s32[16]{0:T(128)} %bitcast.6, bf16[16,4,64,512]{3,2,1,0:T(8,128)(2,1)} %ens_ref.3), custom_call_target="tpu_custom_call" | custom-call | tf_op jit(solution)/shard_map/pack/pallas_call | solution.py:85
  15.7 3.5 %all-to-all-done.places_ref.small_ref = bf16[16,10,512]{2,1,0:T(8,128)(2,1)S(1)} async-done(((bf16[16,10,512]{2,1,0:T(8,128)(2,1)}), bf16[16,10,512]{2,1,0:T(8,128)(2,1)S(1)}, u32[]{:S(2)}, u32[]{:S(2)}) %all-to-all-start) | async-done | bytes 163872 | tf_op jit(solution)/shard_map/all_to_all | solution.py:390
  19.2 0.7 copy-done.2
  19.9 7.3 %all-to-all-start.1 = ((bf16[128,128,128]{2,1,0:T(8,128)(2,1)}), bf16[128,128,128]{2,1,0:T(8,128)(2,1)}, u32[]{:S(2)}, u32[]{:S(2)}) async-start(bf16[128,128,128]{2,1,0:T(8,128)(2,1)} %bitcast.8), calls=%async_computation.1 | async-start | bytes 8388608 | tf_op jit(solution)/shard_map/all_to_all | solution.py:393
  27.2 18.6 %diag.1 = (f32[4,16,8,512]{3,2,1,0:T(8,128)}, f32[4,16,8,512]{3,2,1,0:T(8,128)}) custom-call(s32[1]{0:T(128)S(6)} %and.4.core, bf16[16,4,64,512]{3,2,1,0:T(8,128)(2,1)} %ens_ref.3, bf16[16,64,512]{2,1,0:T(8,128)(2,1)} %inc_ref.3, bf16[16,2,512]{2,1,0:T(2,128)(2,1)} %coords_ref.3), custom_call_target="tpu_custom_call" | custom-call | flops 20000000000 | bytes 8000000 | tf_op jit(solution)/shard_map/diag/pallas_call | solution.py:175
  45.8 5.1 %tiles.4.refs_0_ = bf16[4,512,512]{2,1,0:T(8,128)(2,1)} custom-call(s32[2,32]{1,0:T(2,128)} %bitcast.9, s32[1]{0:T(128)S(6)} %mul.2.first, bf16[16,10,512]{2,1,0:T(8,128)(2,1)} %copy-done.2), custom_call_target="tpu_custom_call" | custom-call | flops 4000000000 | bytes 2000000 | tf_op jit(solution)/shard_map/tiles/pallas_call | solution.py:233
  50.9 5.1 %tiles.7.refs_3_ = bf16[4,512,512]{2,1,0:T(8,128)(2,1)} custom-call(s32[2,32]{1,0:T(2,128)} %bitcast.10, s32[1]{0:T(128)S(6)} %add.11.first, bf16[16,10,512]{2,1,0:T(8,128)(2,1)} %copy-done.2), custom_call_target="tpu_custom_call" | custom-call | flops 4000000000 | bytes 2000000 | tf_op jit(solution)/shard_map/tiles/pallas_call | solution.py:233
  56.0 5.1 %tiles.6.refs_2_ = bf16[4,512,512]{2,1,0:T(8,128)(2,1)} custom-call(s32[2,32]{1,0:T(2,128)} %bitcast.11, s32[1]{0:T(128)S(6)} %add.10.first, bf16[16,10,512]{2,1,0:T(8,128)(2,1)} %copy-done.2), custom_call_target="tpu_custom_call" | custom-call | flops 4000000000 | bytes 2000000 | tf_op jit(solution)/shard_map/tiles/pallas_call | solution.py:233
  61.1 5.4 %tiles.5.refs_1_ = bf16[4,512,512]{2,1,0:T(8,128)(2,1)} custom-call(s32[2,32]{1,0:T(2,128)} %bitcast.12, s32[1]{0:T(128)S(6)} %add.9.first, bf16[16,10,512]{2,1,0:T(8,128)(2,1)} %copy-done.2), custom_call_target="tpu_custom_call" | custom-call | flops 4000000000 | bytes 2000000 | tf_op jit(solution)/shard_map/tiles/pallas_call | solution.py:233
  66.6 0.1 collective-permute-start.1
  66.7 0.5 collective-permute-start.2
  67.2 0.1 collective-permute-start.3
  67.2 0.4 collective-permute-start.4
  67.7 0.1 collective-permute-start
  68.4 5.4 %collective-permute-done.got_ref = f32[4,16,8,512]{3,2,1,0:T(8,128)S(1)} collective-permute-done((f32[4,16,8,512]{3,2,1,0:T(8,128)S(1)}, f32[4,16,8,512]{3,2,1,0:T(8,128)S(1)}, u32[]{:S(2)}, u32[]{:S(2)}) %collective-permute-start) | collective-permute-done | bytes 1048608 | tf_op jit(solution)/shard_map/ppermute | solution.py:401
  73.8 0.1 merge.1
  73.9 5.8 %all-to-all-done.1 = bf16[128,128,128]{2,1,0:T(8,128)(2,1)} async-done(((bf16[128,128,128]{2,1,0:T(8,128)(2,1)}), bf16[128,128,128]{2,1,0:T(8,128)(2,1)}, u32[]{:S(2)}, u32[]{:S(2)}) %all-to-all-start.1) | async-done | bytes 4194336 | tf_op jit(solution)/shard_map/all_to_all | solution.py:393
  79.7 0.0 collective-permute-done.1.refs_4_
  79.7 0.0 collective-permute-done.2.refs_5_
  79.7 1.9 %collective-permute-done.4.refs_7_ = bf16[4,512,512]{2,1,0:T(8,128)(2,1)} collective-permute-done((bf16[4,512,512]{2,1,0:T(8,128)(2,1)}, bf16[4,512,512]{2,1,0:T(8,128)(2,1)}, u32[]{:S(2)}, u32[]{:S(2)}) %collective-permute-start.4) | collective-permute-done | bytes 2097184 | tf_op jit(solution)/shard_map/ppermute | solution.py:404
  81.6 14.0 %apply.1 = f32[16,8,512]{2,1,0:T(8,128)} custom-call(s32[2,32]{1,0:T(2,128)} %bitcast.13, s32[1]{0:T(128)S(6)} %copy.7.count, s32[1]{0:T(128)S(6)} %and.4.core, bf16[16,8,128,128]{3,2,1,0:T(8,128)(2,1)} %bitcast.4.got_ref, bf16[16,10,512]{2,1,0:T(8,128)(2,1)} %copy-done.2, bf16[4,512,512]{2,1,0:T(8,128)(2,1)} %tiles.4.refs_0_, ...), custom_call_target="tpu_custom_call" | custom-call | flops 8999999488 | bytes 22000000 | tf_op jit(solution)/shard_map/apply/pallas_call | solution.py:333
  95.6 9.0 %all-to-all-start.2 = ((f32[16,8,512]{2,1,0:T(8,128)}), f32[16,8,512]{2,1,0:T(8,128)S(1)}, u32[]{:S(2)}, u32[]{:S(2)}) async-start(f32[16,8,512]{2,1,0:T(8,128)} %apply.1), calls=%async_computation.2 | async-start | bytes 524288 | tf_op jit(solution)/shard_map/all_to_all | solution.py:413
  104.7 1.6 %collective-permute-start.5 = (bf16[16,8,512]{2,1,0:T(8,128)(2,1)S(1)}, bf16[16,8,512]{2,1,0:T(8,128)(2,1)S(1)}, u32[]{:S(2)}, u32[]{:S(2)}) collective-permute-start(bf16[16,8,512]{2,1,0:T(8,128)(2,1)S(1)} %get-tuple-element.39), channel_id=1, source_target_pairs={{0,2},{1,3},{2,4},{3,5},{4,6},{5,7},{6,0},{7,1},{8,10},{9,11},{10,... | collective-permute-start | bytes 393224 | tf_op jit(solution)/shard_map/ppermute | solution.py:410
  106.2 2.8 %collective-permute-start.6 = (bf16[16,8,512]{2,1,0:T(8,128)(2,1)S(1)}, bf16[16,8,512]{2,1,0:T(8,128)(2,1)S(1)}, u32[]{:S(2)}, u32[]{:S(2)}) collective-permute-start(bf16[16,8,512]{2,1,0:T(8,128)(2,1)S(1)} %get-tuple-element.40), channel_id=1, source_target_pairs={{0,4},{1,5},{2,6},{3,7},{4,0},{5,1},{6,2},{7,3},{8,12},{9,13},{10,... | collective-permute-start | bytes 393224 | tf_op jit(solution)/shard_map/ppermute | solution.py:410
  109.1 1.4 %collective-permute-start.7 = (bf16[16,8,512]{2,1,0:T(8,128)(2,1)S(1)}, bf16[16,8,512]{2,1,0:T(8,128)(2,1)S(1)}, u32[]{:S(2)}, u32[]{:S(2)}) collective-permute-start(bf16[16,8,512]{2,1,0:T(8,128)(2,1)S(1)} %get-tuple-element.41), channel_id=1, source_target_pairs={{0,6},{1,7},{2,0},{3,1},{4,2},{5,3},{6,4},{7,5},{8,14},{9,15},{10,... | collective-permute-start | bytes 393224 | tf_op jit(solution)/shard_map/ppermute | solution.py:410
  110.5 0.8 collective-permute-done.5.refs_0_
  111.2 3.9 %collective-permute-done.6.refs_1_ = bf16[16,8,512]{2,1,0:T(8,128)(2,1)S(1)} collective-permute-done((bf16[16,8,512]{2,1,0:T(8,128)(2,1)S(1)}, bf16[16,8,512]{2,1,0:T(8,128)(2,1)S(1)}, u32[]{:S(2)}, u32[]{:S(2)}) %collective-permute-start.6) | collective-permute-done | bytes 131104 | tf_op jit(solution)/shard_map/ppermute | solution.py:410
  115.1 0.0 collective-permute-done.7.refs_2_
  115.1 0.0 all-to-all-done.2.refs_3_
  115.1 1.4 %finish.1 = f32[16,8,512]{2,1,0:T(8,128)} custom-call(s32[16]{0:T(128)S(1)} %bitcast.7, f32[16,8,512]{2,1,0:T(8,128)S(1)} %get-tuple-element.38.own_ref, bf16[16,8,512]{2,1,0:T(8,128)(2,1)S(1)} %collective-permute-done.5.refs_0_, bf16[16,8,512]{2,1,0:T(8,128)(2,1)S(1)} %collective-permute-done.6.refs_1_, ...), custom_call_target="tpu_custom_call" | custom-call | tf_op jit(solution)/shard_map/finish/pallas_call | solution.py:372
  (8 shorter events, 0.0 us)
Async XLA Ops:
  2.5 16.7 %all-to-all-start = ((bf16[16,10,512]{2,1,0:T(8,128)(2,1)}), bf16[16,10,512]{2,1,0:T(8,128)(2,1)S(1)}, u32[]{:S(2)}, u32[]{:S(2)}) async-start(bf16[16,10,512]{2,1,0:T(8,128)(2,1)} %select.1), calls=%async_computation | async-start | bytes 524288 | tf_op jit(solution)/shard_map/all_to_all | solution.py:390
  19.2 0.7 copy-start.2
  19.9 59.8 %all-to-all-start.1 = ((bf16[128,128,128]{2,1,0:T(8,128)(2,1)}), bf16[128,128,128]{2,1,0:T(8,128)(2,1)}, u32[]{:S(2)}, u32[]{:S(2)}) async-start(bf16[128,128,128]{2,1,0:T(8,128)(2,1)} %bitcast.8), calls=%async_computation.1 | async-start | bytes 8388608 | tf_op jit(solution)/shard_map/all_to_all | solution.py:393
  61.1 6.6 %copy-start.3 = (f32[4,16,8,512]{3,2,1,0:T(8,128)S(1)}, f32[4,16,8,512]{3,2,1,0:T(8,128)}, u32[]{:S(2)}) copy-start(f32[4,16,8,512]{3,2,1,0:T(8,128)} %get-tuple-element.26) | copy-start | bytes 3145732
  61.1 12.7 %copy-start = (f32[4,16,8,512]{3,2,1,0:T(8,128)S(1)}, f32[4,16,8,512]{3,2,1,0:T(8,128)}, u32[]{:S(2)}) copy-start(f32[4,16,8,512]{3,2,1,0:T(8,128)} %get-tuple-element.25.keep_ref) | copy-start | bytes 3145732
  66.6 13.2 %collective-permute-start.1 = (bf16[4,512,512]{2,1,0:T(8,128)(2,1)}, bf16[4,512,512]{2,1,0:T(8,128)(2,1)}, u32[]{:S(2)}, u32[]{:S(2)}) collective-permute-start(bf16[4,512,512]{2,1,0:T(8,128)(2,1)} %tiles.4.refs_0_), channel_id=1, source_target_pairs={{0,1},{1,0},{2,3},{3,2},{4,5},{5,4},{6,7},{7,6},{8,9},{9,8},{10,11... | collective-permute-start | bytes 6291464 | tf_op jit(solution)/shard_map/ppermute | solution.py:404
  66.7 13.1 %collective-permute-start.2 = (bf16[4,512,512]{2,1,0:T(8,128)(2,1)}, bf16[4,512,512]{2,1,0:T(8,128)(2,1)}, u32[]{:S(2)}, u32[]{:S(2)}) collective-permute-start(bf16[4,512,512]{2,1,0:T(8,128)(2,1)} %tiles.5.refs_1_), channel_id=1, source_target_pairs={{0,1},{1,0},{2,3},{3,2},{4,5},{5,4},{6,7},{7,6},{8,9},{9,8},{10,11... | collective-permute-start | bytes 6291464 | tf_op jit(solution)/shard_map/ppermute | solution.py:404
  67.2 12.6 %collective-permute-start.3 = (bf16[4,512,512]{2,1,0:T(8,128)(2,1)}, bf16[4,512,512]{2,1,0:T(8,128)(2,1)}, u32[]{:S(2)}, u32[]{:S(2)}) collective-permute-start(bf16[4,512,512]{2,1,0:T(8,128)(2,1)} %tiles.6.refs_2_), channel_id=1, source_target_pairs={{0,1},{1,0},{2,3},{3,2},{4,5},{5,4},{6,7},{7,6},{8,9},{9,8},{10,11... | collective-permute-start | bytes 6291464 | tf_op jit(solution)/shard_map/ppermute | solution.py:404
  67.2 14.4 %collective-permute-start.4 = (bf16[4,512,512]{2,1,0:T(8,128)(2,1)}, bf16[4,512,512]{2,1,0:T(8,128)(2,1)}, u32[]{:S(2)}, u32[]{:S(2)}) collective-permute-start(bf16[4,512,512]{2,1,0:T(8,128)(2,1)} %tiles.7.refs_3_), channel_id=1, source_target_pairs={{0,1},{1,0},{2,3},{3,2},{4,5},{5,4},{6,7},{7,6},{8,9},{9,8},{10,11... | collective-permute-start | bytes 6291464 | tf_op jit(solution)/shard_map/ppermute | solution.py:404
  67.7 6.1 %collective-permute-start = (f32[4,16,8,512]{3,2,1,0:T(8,128)S(1)}, f32[4,16,8,512]{3,2,1,0:T(8,128)S(1)}, u32[]{:S(2)}, u32[]{:S(2)}) collective-permute-start(f32[4,16,8,512]{3,2,1,0:T(8,128)S(1)} %copy-done.3), channel_id=1, source_target_pairs={{0,1},{1,0},{2,3},{3,2},{4,5},{5,4},{6,7},{7,6},{8,9},{9,8},{10,11... | collective-permute-start | bytes 3145736 | tf_op jit(solution)/shard_map/ppermute | solution.py:401
  79.7 35.4 %copy-start.1 = (s32[1,16,1]{1,2,0:T(1,128)S(1)}, s32[1,16,1]{1,2,0:T(1,128)}, u32[]{:S(2)}) copy-start(s32[1,16,1]{1,2,0:T(1,128)} %param.9) | copy-start | bytes 196
  95.6 19.5 %all-to-all-start.2 = ((f32[16,8,512]{2,1,0:T(8,128)}), f32[16,8,512]{2,1,0:T(8,128)S(1)}, u32[]{:S(2)}, u32[]{:S(2)}) async-start(f32[16,8,512]{2,1,0:T(8,128)} %apply.1), calls=%async_computation.2 | async-start | bytes 524288 | tf_op jit(solution)/shard_map/all_to_all | solution.py:413
  104.7 6.6 %collective-permute-start.5 = (bf16[16,8,512]{2,1,0:T(8,128)(2,1)S(1)}, bf16[16,8,512]{2,1,0:T(8,128)(2,1)S(1)}, u32[]{:S(2)}, u32[]{:S(2)}) collective-permute-start(bf16[16,8,512]{2,1,0:T(8,128)(2,1)S(1)} %get-tuple-element.39), channel_id=1, source_target_pairs={{0,2},{1,3},{2,4},{3,5},{4,6},{5,7},{6,0},{7,1},{8,10},{9,11},{10,... | collective-permute-start | bytes 393224 | tf_op jit(solution)/shard_map/ppermute | solution.py:410
  106.2 8.9 %collective-permute-start.6 = (bf16[16,8,512]{2,1,0:T(8,128)(2,1)S(1)}, bf16[16,8,512]{2,1,0:T(8,128)(2,1)S(1)}, u32[]{:S(2)}, u32[]{:S(2)}) collective-permute-start(bf16[16,8,512]{2,1,0:T(8,128)(2,1)S(1)} %get-tuple-element.40), channel_id=1, source_target_pairs={{0,4},{1,5},{2,6},{3,7},{4,0},{5,1},{6,2},{7,3},{8,12},{9,13},{10,... | collective-permute-start | bytes 393224 | tf_op jit(solution)/shard_map/ppermute | solution.py:410
  109.1 6.0 %collective-permute-start.7 = (bf16[16,8,512]{2,1,0:T(8,128)(2,1)S(1)}, bf16[16,8,512]{2,1,0:T(8,128)(2,1)S(1)}, u32[]{:S(2)}, u32[]{:S(2)}) collective-permute-start(bf16[16,8,512]{2,1,0:T(8,128)(2,1)S(1)} %get-tuple-element.41), channel_id=1, source_target_pairs={{0,6},{1,7},{2,0},{3,1},{4,2},{5,3},{6,4},{7,5},{8,14},{9,15},{10,... | collective-permute-start | bytes 393224 | tf_op jit(solution)/shard_map/ppermute | solution.py:410

commit v11 on v10

--- a/solution.py
+++ b/solution.py
@@ -397,21 +397,20 @@
     core, row = own & 1, own >> 1
     rows = groups // 2
     share = pairs.shape[1] // 2
+    mine = [tiles(small, pairs, core * share + start) for start in range(0, share, PAIR_GROUP)]
+    theirs = [lax.ppermute(stack, "member", swap) for stack in mine]
     keep, send = diag(ensemble, increment, coords, core, rows)
     merged = merge(keep, lax.ppermute(send, "member", swap), row)
-    small, _ = lax.optimization_barrier((small, send))
-    mine = [tiles(small, pairs, core * share + start) for start in range(0, share, PAIR_GROUP)]
-    theirs = [lax.ppermute(stack, "member", swap) for stack in mine]
-    got, merged = lax.optimization_barrier((got, merged))
-    stacks = [in_hbm(stack) for stack in mine + theirs]
-    partial = apply_pairs(in_hbm(got), in_hbm(small), stacks, pairs, pair_count, core, members, step)
-    partial, merged = lax.optimization_barrier((partial, merged))
     parts = [
         lax.ppermute(part, "member", [(i, (i + 2 * hop) % groups) for i in range(groups)])
         for hop, part in enumerate(merged[1:], 1)
     ]
+    got, own_part = lax.optimization_barrier((got, merged[0]))
+    stacks = [in_hbm(stack) for stack in mine + theirs]
+    partial = apply_pairs(in_hbm(got), in_hbm(small), stacks, pairs, pair_count, core, members, step)
+    partial, parts = lax.optimization_barrier((partial, parts))
     back = lax.all_to_all(partial, "region", 0, 0, tiled=True)
-    return finish(merged[0], parts, back, slots, 1.0 / (members * groups - 1))
+    return finish(own_part, parts, back, slots, 1.0 / (members * groups - 1))
 
 
 def solution(mesh):

time: 117 us -> 113 us (0.966)
  blocking collectives: 0 us -> 12.2 us
  starting transfers between devices: 31.3 us -> 21 us
  waiting for transfers between devices: 21.3 us -> 12.7 us
  Pallas kernels: 62.4 us -> 64.4 us
  local copies, waits for them, and re-layouts: 0.71 us -> 1.93 us
    all_to_all x0 -> x1, blocking collectives: none -> 12.2 us  [per_device(): back = lax.all_to_all(partial, 'region', 0, 0, tiled=True)]
    all_to_all x1 -> x0, starting transfers between devices: 9.04 us -> none  [per_device(): back = lax.all_to_all(partial, 'region', 0, 0, tiled=True)]
    ppermute x3, waiting for transfers between devices: 4.65 us -> 0.01 us  [per_device(): lax.ppermute(part, 'member', [(i, (i + 2 * hop) % groups) for i in range(...]
    ppermute x1, waiting for transfers between devices: 5.39 us -> 2.21 us  [per_device(): merged = merge(keep, lax.ppermute(send, 'member', swap), row)]
    pallas_call x1, Pallas kernels: 14 us -> 16.4 us  [apply_pairs(): pl.pallas_call(apply_kernel, in_specs=[pl.BlockSpec(memory_space=pltpu.SM...]
    ppermute x4, waiting for transfers between devices: 1.91 us -> 0.01 us  [per_device(): theirs = [lax.ppermute(stack, 'member', swap) for stack in mine]]
    ppermute x3, starting transfers between devices: 5.8 us -> 4.11 us  [per_device(): lax.ppermute(part, 'member', [(i, (i + 2 * hop) % groups) for i in range(...]
    unnamed x8, local copies, waits for them, and re-layouts: 0.71 us -> 1.93 us
  transfers between devices with their start and end apart: 11 -> 10, of which waited for: 6 -> 3; matrix products, arithmetic and copies ran while one was open for 0% -> 0% of each run, Pallas kernels for 38% -> 54%
where the time goes in v11:
time: 113 us
  Pallas kernels  64.4 us (57%)
  starting transfers between devices  21 us (19%)
  waiting for transfers between devices  12.7 us (11%)
  blocking collectives  12.2 us (11%)
  local copies, waits for them, and re-layouts  1.93 us (2%)
    pallas_call x4, Pallas kernels, tiles(): pl.pallas_call(tiles_kernel, in_specs=[pl.BlockSpec(memory_space=pltpu.SM...  20.3 us
    pallas_call x1, Pallas kernels, diag(): pl.pallas_call(diag_kernel, grid_spec=pltpu.PrefetchScalarGridSpec(num_sc...  18.7 us
    pallas_call x1, Pallas kernels, apply_pairs(): pl.pallas_call(apply_kernel, in_specs=[pl.BlockSpec(memory_space=pltpu.SM...  16.4 us
    all_to_all x1, blocking collectives, per_device(): back = lax.all_to_all(partial, 'region', 0, 0, tiled=True)  12.2 us
    all_to_all x1, starting transfers between devices, per_device(): lax.all_to_all(select(increment, coords, slots, own, step), 'region', 0,...  7.97 us
    all_to_all x1, starting transfers between devices, per_device(): lax.all_to_all(big.reshape(regions * groups, -1, LANES), ('region', 'memb...  7.41 us
    all_to_all x1, waiting for transfers between devices, per_device(): lax.all_to_all(big.reshape(regions * groups, -1, LANES), ('region', 'memb...  6.85 us
    pallas_call x1, Pallas kernels, pack(): pl.pallas_call(pack_kernel, in_specs=[pl.BlockSpec(memory_space=pltpu.SME...  5.06 us
  transfers between devices with their start and end apart: 10, of which 3 were waited for; matrix products, arithmetic and copies ran while one was open for 0% of the time, Pallas kernels for 54%

profile of v11, /device:TPU:0, one launch (start us, length us, event | category | flops | bytes accessed | tf_op | source)
XLA Modules:
  0.0 113.0 jit_solution(13330118570994070169)
XLA Ops:
  0.0 2.5 %select.1 = bf16[16,10,512]{2,1,0:T(8,128)(2,1)} custom-call(s32[16]{0:T(128)} %bitcast.5, s32[1]{0:T(128)} %bitcast.1.own, bf16[16,64,512]{2,1,0:T(8,128)(2,1)} %inc_ref.3, bf16[16,2,512]{2,1,0:T(2,128)(2,1)} %coords_ref.3), custom_call_target="tpu_custom_call" | custom-call | tf_op jit(solution)/shard_map/select/pallas_call | solution.py:38
  2.5 8.0 %all-to-all-start = ((bf16[16,10,512]{2,1,0:T(8,128)(2,1)}), bf16[16,10,512]{2,1,0:T(8,128)(2,1)S(1)}, u32[]{:S(2)}, u32[]{:S(2)}) async-start(bf16[16,10,512]{2,1,0:T(8,128)(2,1)} %select.1), calls=%async_computation | async-start | bytes 524288 | tf_op jit(solution)/shard_map/all_to_all | solution.py:390
  10.5 5.1 %pack.1 = bf16[16,8,128,128]{3,2,1,0:T(8,128)(2,1)} custom-call(s32[16]{0:T(128)} %bitcast.6, bf16[16,4,64,512]{3,2,1,0:T(8,128)(2,1)} %ens_ref.3), custom_call_target="tpu_custom_call" | custom-call | tf_op jit(solution)/shard_map/pack/pallas_call | solution.py:85
  15.5 3.6 %all-to-all-done.places_ref.small_ref = bf16[16,10,512]{2,1,0:T(8,128)(2,1)S(1)} async-done(((bf16[16,10,512]{2,1,0:T(8,128)(2,1)}), bf16[16,10,512]{2,1,0:T(8,128)(2,1)S(1)}, u32[]{:S(2)}, u32[]{:S(2)}) %all-to-all-start) | async-done | bytes 163872 | tf_op jit(solution)/shard_map/all_to_all | solution.py:390
  19.2 0.7 copy-done.2
  19.9 7.4 %all-to-all-start.1 = ((bf16[128,128,128]{2,1,0:T(8,128)(2,1)}), bf16[128,128,128]{2,1,0:T(8,128)(2,1)}, u32[]{:S(2)}, u32[]{:S(2)}) async-start(bf16[128,128,128]{2,1,0:T(8,128)(2,1)} %bitcast.8), calls=%async_computation.1 | async-start | bytes 8388608 | tf_op jit(solution)/shard_map/all_to_all | solution.py:393
  27.3 5.1 %tiles.4.refs_0_ = bf16[4,512,512]{2,1,0:T(8,128)(2,1)} custom-call(s32[2,32]{1,0:T(2,128)} %bitcast.9, s32[1]{0:T(128)S(6)} %mul.2.first, bf16[16,10,512]{2,1,0:T(8,128)(2,1)} %copy-done.2), custom_call_target="tpu_custom_call" | custom-call | flops 4000000000 | bytes 2000000 | tf_op jit(solution)/shard_map/tiles/pallas_call | solution.py:233
  32.4 0.1 collective-permute-start.1
  32.5 5.1 %tiles.5.refs_1_ = bf16[4,512,512]{2,1,0:T(8,128)(2,1)} custom-call(s32[2,32]{1,0:T(2,128)} %bitcast.10, s32[1]{0:T(128)S(6)} %add.9.first, bf16[16,10,512]{2,1,0:T(8,128)(2,1)} %copy-done.2), custom_call_target="tpu_custom_call" | custom-call | flops 4000000000 | bytes 2000000 | tf_op jit(solution)/shard_map/tiles/pallas_call | solution.py:233
  37.6 0.8 collective-permute-start.2
  38.3 5.1 %tiles.6.refs_2_ = bf16[4,512,512]{2,1,0:T(8,128)(2,1)} custom-call(s32[2,32]{1,0:T(2,128)} %bitcast.11, s32[1]{0:T(128)S(6)} %add.10.first, bf16[16,10,512]{2,1,0:T(8,128)(2,1)} %copy-done.2), custom_call_target="tpu_custom_call" | custom-call | flops 4000000000 | bytes 2000000 | tf_op jit(solution)/shard_map/tiles/pallas_call | solution.py:233
  43.4 0.1 collective-permute-start.3
  43.5 5.1 %tiles.7.refs_3_ = bf16[4,512,512]{2,1,0:T(8,128)(2,1)} custom-call(s32[2,32]{1,0:T(2,128)} %bitcast.12, s32[1]{0:T(128)S(6)} %add.11.first, bf16[16,10,512]{2,1,0:T(8,128)(2,1)} %copy-done.2), custom_call_target="tpu_custom_call" | custom-call | flops 4000000000 | bytes 2000000 | tf_op jit(solution)/shard_map/tiles/pallas_call | solution.py:233
  48.6 0.6 collective-permute-start.4
  49.2 18.7 %diag.1 = (f32[4,16,8,512]{3,2,1,0:T(8,128)}, f32[4,16,8,512]{3,2,1,0:T(8,128)}) custom-call(s32[1]{0:T(128)S(6)} %and.4.core, bf16[16,4,64,512]{3,2,1,0:T(8,128)(2,1)} %ens_ref.3, bf16[16,64,512]{2,1,0:T(8,128)(2,1)} %inc_ref.3, bf16[16,2,512]{2,1,0:T(2,128)(2,1)} %coords_ref.3), custom_call_target="tpu_custom_call" | custom-call | flops 20000000000 | bytes 8000000 | tf_op jit(solution)/shard_map/diag/pallas_call | solution.py:175
  67.8 0.0 collective-permute-start
  68.5 2.2 %collective-permute-done.got_ref = f32[4,16,8,512]{3,2,1,0:T(8,128)S(1)} collective-permute-done((f32[4,16,8,512]{3,2,1,0:T(8,128)}, f32[4,16,8,512]{3,2,1,0:T(8,128)S(1)}, u32[]{:S(2)}, u32[]{:S(2)}) %collective-permute-start) | collective-permute-done | bytes 1048608 | tf_op jit(solution)/shard_map/ppermute | solution.py:403
  70.7 1.2 %copy-done = f32[4,16,8,512]{3,2,1,0:T(8,128)S(1)} copy-done((f32[4,16,8,512]{3,2,1,0:T(8,128)S(1)}, f32[4,16,8,512]{3,2,1,0:T(8,128)}, u32[]{:S(2)}) %copy-start) | copy-done | bytes 1048600
  71.9 0.1 merge.1
  72.0 1.0 collective-permute-start.5
  73.0 6.8 %all-to-all-done.1 = bf16[128,128,128]{2,1,0:T(8,128)(2,1)} async-done(((bf16[128,128,128]{2,1,0:T(8,128)(2,1)}), bf16[128,128,128]{2,1,0:T(8,128)(2,1)}, u32[]{:S(2)}, u32[]{:S(2)}) %all-to-all-start.1) | async-done | bytes 4194336 | tf_op jit(solution)/shard_map/all_to_all | solution.py:393
  79.8 0.0 collective-permute-done.1.refs_4_
  79.8 0.4 collective-permute-start.6
  80.2 0.0 collective-permute-done.2.refs_5_
  80.2 2.8 %collective-permute-start.7 = (bf16[16,8,512]{2,1,0:T(8,128)(2,1)S(1)}, bf16[16,8,512]{2,1,0:T(8,128)(2,1)S(1)}, u32[]{:S(2)}, u32[]{:S(2)}) collective-permute-start(bf16[16,8,512]{2,1,0:T(8,128)(2,1)S(1)} %get-tuple-element.28), channel_id=1, source_target_pairs={{0,6},{1,7},{2,0},{3,1},{4,2},{5,3},{6,4},{7,5},{8,14},{9,15},{10,... | collective-permute-start | bytes 393224 | tf_op jit(solution)/shard_map/ppermute | solution.py:405
  83.0 0.0 collective-permute-done.3.refs_6_
  83.0 0.0 collective-permute-done.4.refs_7_
  83.0 16.4 %apply.1 = f32[16,8,512]{2,1,0:T(8,128)} custom-call(s32[2,32]{1,0:T(2,128)} %bitcast.13, s32[1]{0:T(128)S(6)} %copy.7.count, s32[1]{0:T(128)S(6)} %and.4.core, bf16[16,8,128,128]{3,2,1,0:T(8,128)(2,1)} %bitcast.3.got_ref, bf16[16,10,512]{2,1,0:T(8,128)(2,1)} %copy-done.2, bf16[4,512,512]{2,1,0:T(8,128)(2,1)} %tiles.4.refs_0_, ...), custom_call_target="tpu_custom_call" | custom-call | flops 8999999488 | bytes 22000000 | tf_op jit(solution)/shard_map/apply/pallas_call | solution.py:333
  99.4 0.0 collective-permute-done.6.refs_1_
  99.4 0.0 collective-permute-done.7.refs_2_
  99.4 12.2 %all_to_all.15.refs_3_ = f32[16,8,512]{2,1,0:T(8,128)S(1)} all-to-all(f32[16,8,512]{2,1,0:T(8,128)} %apply.1), channel_id=1, replica_groups=mesh['region'=16,'member'=8] {'region'}, dimensions={0} | all-to-all | bytes 524288 | tf_op jit(solution)/shard_map/all_to_all | solution.py:412
  111.6 1.4 %finish.1 = f32[16,8,512]{2,1,0:T(8,128)} custom-call(s32[16]{0:T(128)S(1)} %bitcast.7, f32[16,8,512]{2,1,0:T(8,128)S(1)} %get-tuple-element.23.own_ref, bf16[16,8,512]{2,1,0:T(8,128)(2,1)S(1)} %collective-permute-done.5.refs_0_, bf16[16,8,512]{2,1,0:T(8,128)(2,1)S(1)} %collective-permute-done.6.refs_1_, ...), custom_call_target="tpu_custom_call" | custom-call | tf_op jit(solution)/shard_map/finish/pallas_call | solution.py:372
  (7 shorter events, 0.0 us)
Async XLA Ops:
  2.5 16.7 %all-to-all-start = ((bf16[16,10,512]{2,1,0:T(8,128)(2,1)}), bf16[16,10,512]{2,1,0:T(8,128)(2,1)S(1)}, u32[]{:S(2)}, u32[]{:S(2)}) async-start(bf16[16,10,512]{2,1,0:T(8,128)(2,1)} %select.1), calls=%async_computation | async-start | bytes 524288 | tf_op jit(solution)/shard_map/all_to_all | solution.py:390
  19.2 0.7 copy-start.2
  19.9 59.9 %all-to-all-start.1 = ((bf16[128,128,128]{2,1,0:T(8,128)(2,1)}), bf16[128,128,128]{2,1,0:T(8,128)(2,1)}, u32[]{:S(2)}, u32[]{:S(2)}) async-start(bf16[128,128,128]{2,1,0:T(8,128)(2,1)} %bitcast.8), calls=%async_computation.1 | async-start | bytes 8388608 | tf_op jit(solution)/shard_map/all_to_all | solution.py:393
  32.4 47.4 %collective-permute-start.1 = (bf16[4,512,512]{2,1,0:T(8,128)(2,1)}, bf16[4,512,512]{2,1,0:T(8,128)(2,1)S(1)}, u32[]{:S(2)}, u32[]{:S(2)}) collective-permute-start(bf16[4,512,512]{2,1,0:T(8,128)(2,1)} %tiles.4.refs_0_), channel_id=1, source_target_pairs={{0,1},{1,0},{2,3},{3,2},{4,5},{5,4},{6,7},{7,6},{8,9},{9,8},{10,11... | collective-permute-start | bytes 6291464 | tf_op jit(solution)/shard_map/ppermute | solution.py:401
  37.6 42.6 %collective-permute-start.2 = (bf16[4,512,512]{2,1,0:T(8,128)(2,1)}, bf16[4,512,512]{2,1,0:T(8,128)(2,1)}, u32[]{:S(2)}, u32[]{:S(2)}) collective-permute-start(bf16[4,512,512]{2,1,0:T(8,128)(2,1)} %tiles.5.refs_1_), channel_id=1, source_target_pairs={{0,1},{1,0},{2,3},{3,2},{4,5},{5,4},{6,7},{7,6},{8,9},{9,8},{10,11... | collective-permute-start | bytes 6291464 | tf_op jit(solution)/shard_map/ppermute | solution.py:401
  43.4 39.6 %collective-permute-start.3 = (bf16[4,512,512]{2,1,0:T(8,128)(2,1)}, bf16[4,512,512]{2,1,0:T(8,128)(2,1)}, u32[]{:S(2)}, u32[]{:S(2)}) collective-permute-start(bf16[4,512,512]{2,1,0:T(8,128)(2,1)} %tiles.6.refs_2_), channel_id=1, source_target_pairs={{0,1},{1,0},{2,3},{3,2},{4,5},{5,4},{6,7},{7,6},{8,9},{9,8},{10,11... | collective-permute-start | bytes 6291464 | tf_op jit(solution)/shard_map/ppermute | solution.py:401
  48.6 34.4 %collective-permute-start.4 = (bf16[4,512,512]{2,1,0:T(8,128)(2,1)}, bf16[4,512,512]{2,1,0:T(8,128)(2,1)}, u32[]{:S(2)}, u32[]{:S(2)}) collective-permute-start(bf16[4,512,512]{2,1,0:T(8,128)(2,1)} %tiles.7.refs_3_), channel_id=1, source_target_pairs={{0,1},{1,0},{2,3},{3,2},{4,5},{5,4},{6,7},{7,6},{8,9},{9,8},{10,11... | collective-permute-start | bytes 6291464 | tf_op jit(solution)/shard_map/ppermute | solution.py:401
  67.8 2.9 %collective-permute-start = (f32[4,16,8,512]{3,2,1,0:T(8,128)}, f32[4,16,8,512]{3,2,1,0:T(8,128)S(1)}, u32[]{:S(2)}, u32[]{:S(2)}) collective-permute-start(f32[4,16,8,512]{3,2,1,0:T(8,128)} %get-tuple-element.21), channel_id=1, source_target_pairs={{0,1},{1,0},{2,3},{3,2},{4,5},{5,4},{6,7},{7,6},{8,9},{9,8},{10,11... | collective-permute-start | bytes 3145736 | tf_op jit(solution)/shard_map/ppermute | solution.py:403
  70.7 1.2 %copy-start = (f32[4,16,8,512]{3,2,1,0:T(8,128)S(1)}, f32[4,16,8,512]{3,2,1,0:T(8,128)}, u32[]{:S(2)}) copy-start(f32[4,16,8,512]{3,2,1,0:T(8,128)} %get-tuple-element.20.keep_ref) | copy-start | bytes 3145732
  72.0 27.4 %collective-permute-start.5 = (bf16[16,8,512]{2,1,0:T(8,128)(2,1)S(1)}, bf16[16,8,512]{2,1,0:T(8,128)(2,1)S(1)}, u32[]{:S(2)}, u32[]{:S(2)}) collective-permute-start(bf16[16,8,512]{2,1,0:T(8,128)(2,1)S(1)} %get-tuple-element.26), channel_id=1, source_target_pairs={{0,2},{1,3},{2,4},{3,5},{4,6},{5,7},{6,0},{7,1},{8,10},{9,11},{10,... | collective-permute-start | bytes 393224 | tf_op jit(solution)/shard_map/ppermute | solution.py:405
  79.8 3.2 %copy-start.3 = (bf16[4,512,512]{2,1,0:T(8,128)(2,1)}, bf16[4,512,512]{2,1,0:T(8,128)(2,1)S(1)}, u32[]{:S(2)}) copy-start(bf16[4,512,512]{2,1,0:T(8,128)(2,1)S(1)} %collective-permute-done.1.refs_4_) | copy-start | bytes 6291460
  79.8 19.6 %collective-permute-start.6 = (bf16[16,8,512]{2,1,0:T(8,128)(2,1)S(1)}, bf16[16,8,512]{2,1,0:T(8,128)(2,1)S(1)}, u32[]{:S(2)}, u32[]{:S(2)}) collective-permute-start(bf16[16,8,512]{2,1,0:T(8,128)(2,1)S(1)} %get-tuple-element.27), channel_id=1, source_target_pairs={{0,4},{1,5},{2,6},{3,7},{4,0},{5,1},{6,2},{7,3},{8,12},{9,13},{10,... | collective-permute-start | bytes 393224 | tf_op jit(solution)/shard_map/ppermute | solution.py:405
  80.2 31.4 %copy-start.1 = (s32[1,16,1]{1,2,0:T(1,128)S(1)}, s32[1,16,1]{1,2,0:T(1,128)}, u32[]{:S(2)}) copy-start(s32[1,16,1]{1,2,0:T(1,128)} %param.9) | copy-start | bytes 196
  80.2 19.2 %collective-permute-start.7 = (bf16[16,8,512]{2,1,0:T(8,128)(2,1)S(1)}, bf16[16,8,512]{2,1,0:T(8,128)(2,1)S(1)}, u32[]{:S(2)}, u32[]{:S(2)}) collective-permute-start(bf16[16,8,512]{2,1,0:T(8,128)(2,1)S(1)} %get-tuple-element.28), channel_id=1, source_target_pairs={{0,6},{1,7},{2,0},{3,1},{4,2},{5,3},{6,4},{7,5},{8,14},{9,15},{10,... | collective-permute-start | bytes 393224 | tf_op jit(solution)/shard_map/ppermute | solution.py:405

commit v12 on v11

--- a/solution.py
+++ b/solution.py
@@ -322,7 +322,7 @@
 
     for slot in range(slot_total):
         product = ens_ref[slot].reshape(every, points).astype(jnp.float32) * field_ref[slot]
-        out_ref[slot] = jnp.sum(product.reshape(every // step, step, points), axis=0)
+        out_ref[slot] = jnp.sum(product.reshape(every // step, step, points), axis=0).astype(out_ref.dtype)
 
 
 def apply_pairs(got, small, stacks, pairs, count, core, members, step):
@@ -350,9 +350,9 @@
             pltpu.SemaphoreType.DMA,
             pltpu.SemaphoreType.DMA((len(stacks),)),
         ],
-        out_shape=jax.ShapeDtypeStruct((slot_total, step, points), jnp.float32),
+        out_shape=jax.ShapeDtypeStruct((slot_total, step, points), jnp.bfloat16),
         compiler_params=pltpu.CompilerParams(vmem_limit_bytes=60 * MIB),
-        cost_estimate=pl.CostEstimate(flops=9_000_000_000, bytes_accessed=22_000_000, transcendentals=0),
+        cost_estimate=pl.CostEstimate(flops=100_000_000, bytes_accessed=22_000_000, transcendentals=0),
         name="apply",
     )(pairs, count, core, got, small, *stacks)
 
@@ -365,7 +365,7 @@
     out_ref[...] = total * scale
     for owner in range(back_ref.shape[0]):
         slot = slots[owner]
-        out_ref[slot] = out_ref[slot] + back_ref[owner] * scale
+        out_ref[slot] = out_ref[slot] + back_ref[owner].astype(jnp.float32) * scale
 
 
 def finish(own, parts, back, slots, scale):

time: 113 us -> 111 us (0.982)
  waiting for transfers between devices: 12.7 us -> 8.5 us
    all_to_all x1, waiting for transfers between devices: 6.85 us -> 2.04 us  [per_device(): lax.all_to_all(big.reshape(regions * groups, -1, LANES), ('region', 'memb...]
where the time goes in v12:
time: 111 us
  Pallas kernels  64.1 us (58%)
  starting transfers between devices  21.9 us (20%)
  blocking collectives  13.3 us (12%)
  waiting for transfers between devices  8.5 us (8%)
  local copies, waits for them, and re-layouts  1.93 us (2%)
    pallas_call x4, Pallas kernels, tiles(): pl.pallas_call(tiles_kernel, in_specs=[pl.BlockSpec(memory_space=pltpu.SM...  20.3 us
    pallas_call x1, Pallas kernels, diag(): pl.pallas_call(diag_kernel, grid_spec=pltpu.PrefetchScalarGridSpec(num_sc...  18.7 us
    pallas_call x1, Pallas kernels, apply_pairs(): pl.pallas_call(apply_kernel, in_specs=[pl.BlockSpec(memory_space=pltpu.SM...  16 us
    all_to_all x1, blocking collectives, per_device(): back = lax.all_to_all(partial, 'region', 0, 0, tiled=True)  13.3 us
    all_to_all x1, starting transfers between devices, per_device(): lax.all_to_all(select(increment, coords, slots, own, step), 'region', 0,...  7.9 us
    all_to_all x1, starting transfers between devices, per_device(): lax.all_to_all(big.reshape(regions * groups, -1, LANES), ('region', 'memb...  7.37 us
    ppermute x3, starting transfers between devices, per_device(): lax.ppermute(part, 'member', [(i, (i + 2 * hop) % groups) for i in range(...  5.1 us
    pallas_call x1, Pallas kernels, pack(): pl.pallas_call(pack_kernel, in_specs=[pl.BlockSpec(memory_space=pltpu.SME...  5.1 us
  transfers between devices with their start and end apart: 10, of which 3 were waited for; matrix products, arithmetic and copies ran while one was open for 0% of the time, Pallas kernels for 54%

profile of v12, /device:TPU:0, one launch (start us, length us, event | category | flops | bytes accessed | tf_op | source)
XLA Modules:
  0.0 110.5 jit_solution(7776825097430704117)
XLA Ops:
  0.0 2.6 %select.1 = bf16[16,10,512]{2,1,0:T(8,128)(2,1)} custom-call(s32[16]{0:T(128)} %bitcast.5, s32[1]{0:T(128)} %bitcast.1.own, bf16[16,64,512]{2,1,0:T(8,128)(2,1)} %inc_ref.3, bf16[16,2,512]{2,1,0:T(2,128)(2,1)} %coords_ref.3), custom_call_target="tpu_custom_call" | custom-call | tf_op jit(solution)/shard_map/select/pallas_call | solution.py:38
  2.6 7.9 %all-to-all-start = ((bf16[16,10,512]{2,1,0:T(8,128)(2,1)}), bf16[16,10,512]{2,1,0:T(8,128)(2,1)S(1)}, u32[]{:S(2)}, u32[]{:S(2)}) async-start(bf16[16,10,512]{2,1,0:T(8,128)(2,1)} %select.1), calls=%async_computation | async-start | bytes 524288 | tf_op jit(solution)/shard_map/all_to_all | solution.py:390
  10.5 5.1 %pack.1 = bf16[16,8,128,128]{3,2,1,0:T(8,128)(2,1)} custom-call(s32[16]{0:T(128)} %bitcast.6, bf16[16,4,64,512]{3,2,1,0:T(8,128)(2,1)} %ens_ref.3), custom_call_target="tpu_custom_call" | custom-call | tf_op jit(solution)/shard_map/pack/pallas_call | solution.py:85
  15.6 3.6 %all-to-all-done.places_ref.small_ref = bf16[16,10,512]{2,1,0:T(8,128)(2,1)S(1)} async-done(((bf16[16,10,512]{2,1,0:T(8,128)(2,1)}), bf16[16,10,512]{2,1,0:T(8,128)(2,1)S(1)}, u32[]{:S(2)}, u32[]{:S(2)}) %all-to-all-start) | async-done | bytes 163872 | tf_op jit(solution)/shard_map/all_to_all | solution.py:390
  19.2 0.7 copy-done.3
  19.9 7.4 %all-to-all-start.1 = ((bf16[128,128,128]{2,1,0:T(8,128)(2,1)}), bf16[128,128,128]{2,1,0:T(8,128)(2,1)}, u32[]{:S(2)}, u32[]{:S(2)}) async-start(bf16[128,128,128]{2,1,0:T(8,128)(2,1)} %bitcast.8), calls=%async_computation.1 | async-start | bytes 8388608 | tf_op jit(solution)/shard_map/all_to_all | solution.py:393
  27.2 5.1 %tiles.4.refs_0_ = bf16[4,512,512]{2,1,0:T(8,128)(2,1)} custom-call(s32[2,32]{1,0:T(2,128)} %bitcast.9, s32[1]{0:T(128)S(6)} %mul.2.first, bf16[16,10,512]{2,1,0:T(8,128)(2,1)} %copy-done.3), custom_call_target="tpu_custom_call" | custom-call | flops 4000000000 | bytes 2000000 | tf_op jit(solution)/shard_map/tiles/pallas_call | solution.py:233
  32.4 0.1 collective-permute-start.1
  32.4 5.1 %tiles.5.refs_1_ = bf16[4,512,512]{2,1,0:T(8,128)(2,1)} custom-call(s32[2,32]{1,0:T(2,128)} %bitcast.10, s32[1]{0:T(128)S(6)} %add.9.first, bf16[16,10,512]{2,1,0:T(8,128)(2,1)} %copy-done.3), custom_call_target="tpu_custom_call" | custom-call | flops 4000000000 | bytes 2000000 | tf_op jit(solution)/shard_map/tiles/pallas_call | solution.py:233
  37.5 0.8 collective-permute-start.2
  38.3 5.1 %tiles.6.refs_2_ = bf16[4,512,512]{2,1,0:T(8,128)(2,1)} custom-call(s32[2,32]{1,0:T(2,128)} %bitcast.11, s32[1]{0:T(128)S(6)} %add.10.first, bf16[16,10,512]{2,1,0:T(8,128)(2,1)} %copy-done.3), custom_call_target="tpu_custom_call" | custom-call | flops 4000000000 | bytes 2000000 | tf_op jit(solution)/shard_map/tiles/pallas_call | solution.py:233
  43.4 0.1 collective-permute-start.3
  43.5 5.1 %tiles.7.refs_3_ = bf16[4,512,512]{2,1,0:T(8,128)(2,1)} custom-call(s32[2,32]{1,0:T(2,128)} %bitcast.12, s32[1]{0:T(128)S(6)} %add.11.first, bf16[16,10,512]{2,1,0:T(8,128)(2,1)} %copy-done.3), custom_call_target="tpu_custom_call" | custom-call | flops 4000000000 | bytes 2000000 | tf_op jit(solution)/shard_map/tiles/pallas_call | solution.py:233
  48.6 0.6 collective-permute-start.4
  49.1 18.7 %diag.1 = (f32[4,16,8,512]{3,2,1,0:T(8,128)}, f32[4,16,8,512]{3,2,1,0:T(8,128)}) custom-call(s32[1]{0:T(128)S(6)} %and.4.core, bf16[16,4,64,512]{3,2,1,0:T(8,128)(2,1)} %ens_ref.3, bf16[16,64,512]{2,1,0:T(8,128)(2,1)} %inc_ref.3, bf16[16,2,512]{2,1,0:T(2,128)(2,1)} %coords_ref.3), custom_call_target="tpu_custom_call" | custom-call | flops 20000000000 | bytes 8000000 | tf_op jit(solution)/shard_map/diag/pallas_call | solution.py:175
  67.8 0.0 collective-permute-start
  67.8 2.9 %collective-permute-done.got_ref = f32[4,16,8,512]{3,2,1,0:T(8,128)S(1)} collective-permute-done((f32[4,16,8,512]{3,2,1,0:T(8,128)}, f32[4,16,8,512]{3,2,1,0:T(8,128)S(1)}, u32[]{:S(2)}, u32[]{:S(2)}) %collective-permute-start) | collective-permute-done | bytes 1048608 | tf_op jit(solution)/shard_map/ppermute | solution.py:403
  70.7 1.2 %copy-done = f32[4,16,8,512]{3,2,1,0:T(8,128)S(1)} copy-done((f32[4,16,8,512]{3,2,1,0:T(8,128)S(1)}, f32[4,16,8,512]{3,2,1,0:T(8,128)}, u32[]{:S(2)}) %copy-start) | copy-done | bytes 1048600
  71.9 0.1 merge.1
  72.0 1.0 collective-permute-start.5
  72.9 0.0 collective-permute-done.1.refs_4_
  72.9 2.7 %collective-permute-start.6 = (bf16[16,8,512]{2,1,0:T(8,128)(2,1)S(1)}, bf16[16,8,512]{2,1,0:T(8,128)(2,1)S(1)}, u32[]{:S(2)}, u32[]{:S(2)}) collective-permute-start(bf16[16,8,512]{2,1,0:T(8,128)(2,1)S(1)} %get-tuple-element.27), channel_id=1, source_target_pairs={{0,4},{1,5},{2,6},{3,7},{4,0},{5,1},{6,2},{7,3},{8,12},{9,13},{10,... | collective-permute-start | bytes 393224 | tf_op jit(solution)/shard_map/ppermute | solution.py:405
  75.7 0.0 collective-permute-done.2.refs_5_
  75.7 1.4 %collective-permute-start.7 = (bf16[16,8,512]{2,1,0:T(8,128)(2,1)S(1)}, bf16[16,8,512]{2,1,0:T(8,128)(2,1)S(1)}, u32[]{:S(2)}, u32[]{:S(2)}) collective-permute-start(bf16[16,8,512]{2,1,0:T(8,128)(2,1)S(1)} %get-tuple-element.28), channel_id=1, source_target_pairs={{0,6},{1,7},{2,0},{3,1},{4,2},{5,3},{6,4},{7,5},{8,14},{9,15},{10,... | collective-permute-start | bytes 393224 | tf_op jit(solution)/shard_map/ppermute | solution.py:405
  77.7 2.0 %all-to-all-done.1 = bf16[128,128,128]{2,1,0:T(8,128)(2,1)} async-done(((bf16[128,128,128]{2,1,0:T(8,128)(2,1)}), bf16[128,128,128]{2,1,0:T(8,128)(2,1)}, u32[]{:S(2)}, u32[]{:S(2)}) %all-to-all-start.1) | async-done | bytes 4194336 | tf_op jit(solution)/shard_map/all_to_all | solution.py:393
  79.8 0.0 collective-permute-done.3.refs_6_
  79.8 0.0 collective-permute-done.4.refs_7_
  79.8 16.0 %apply.1 = bf16[16,8,512]{2,1,0:T(8,128)(2,1)} custom-call(s32[2,32]{1,0:T(2,128)} %bitcast.13, s32[1]{0:T(128)S(6)} %copy.7.count, s32[1]{0:T(128)S(6)} %and.4.core, bf16[16,8,128,128]{3,2,1,0:T(8,128)(2,1)} %bitcast.3.got_ref, bf16[16,10,512]{2,1,0:T(8,128)(2,1)} %copy-done.3, bf16[4,512,512]{2,1,0:T(8,128)(2,1)} %tiles.4.refs_0_, ...), custom_call_target="tpu_custom_call" | custom-call | flops 100000000 | bytes 22000000 | tf_op jit(solution)/shard_map/apply/pallas_call | solution.py:333
  95.8 0.0 collective-permute-done.5.refs_0_
  95.8 0.0 collective-permute-done.6.refs_1_
  95.8 13.3 %all_to_all.15.refs_3_ = bf16[16,8,512]{2,1,0:T(8,128)(2,1)S(1)} all-to-all(bf16[16,8,512]{2,1,0:T(8,128)(2,1)} %apply.1), channel_id=1, replica_groups=mesh['region'=16,'member'=8] {'region'}, dimensions={0} | all-to-all | bytes 262144 | tf_op jit(solution)/shard_map/all_to_all | solution.py:412
  109.1 1.4 %finish.1 = f32[16,8,512]{2,1,0:T(8,128)} custom-call(s32[16]{0:T(128)S(1)} %bitcast.7, f32[16,8,512]{2,1,0:T(8,128)S(1)} %get-tuple-element.23.own_ref, bf16[16,8,512]{2,1,0:T(8,128)(2,1)S(1)} %collective-permute-done.5.refs_0_, bf16[16,8,512]{2,1,0:T(8,128)(2,1)S(1)} %collective-permute-done.6.refs_1_, ...), custom_call_target="tpu_custom_call" | custom-call | tf_op jit(solution)/shard_map/finish/pallas_call | solution.py:372
  (7 shorter events, 0.0 us)
Async XLA Ops:
  2.6 16.6 %all-to-all-start = ((bf16[16,10,512]{2,1,0:T(8,128)(2,1)}), bf16[16,10,512]{2,1,0:T(8,128)(2,1)S(1)}, u32[]{:S(2)}, u32[]{:S(2)}) async-start(bf16[16,10,512]{2,1,0:T(8,128)(2,1)} %select.1), calls=%async_computation | async-start | bytes 524288 | tf_op jit(solution)/shard_map/all_to_all | solution.py:390
  19.2 0.7 copy-start.3
  19.9 59.9 %all-to-all-start.1 = ((bf16[128,128,128]{2,1,0:T(8,128)(2,1)}), bf16[128,128,128]{2,1,0:T(8,128)(2,1)}, u32[]{:S(2)}, u32[]{:S(2)}) async-start(bf16[128,128,128]{2,1,0:T(8,128)(2,1)} %bitcast.8), calls=%async_computation.1 | async-start | bytes 8388608 | tf_op jit(solution)/shard_map/all_to_all | solution.py:393
  32.4 40.6 %collective-permute-start.1 = (bf16[4,512,512]{2,1,0:T(8,128)(2,1)}, bf16[4,512,512]{2,1,0:T(8,128)(2,1)S(1)}, u32[]{:S(2)}, u32[]{:S(2)}) collective-permute-start(bf16[4,512,512]{2,1,0:T(8,128)(2,1)} %tiles.4.refs_0_), channel_id=1, source_target_pairs={{0,1},{1,0},{2,3},{3,2},{4,5},{5,4},{6,7},{7,6},{8,9},{9,8},{10,11... | collective-permute-start | bytes 6291464 | tf_op jit(solution)/shard_map/ppermute | solution.py:401
  37.5 38.1 %collective-permute-start.2 = (bf16[4,512,512]{2,1,0:T(8,128)(2,1)}, bf16[4,512,512]{2,1,0:T(8,128)(2,1)}, u32[]{:S(2)}, u32[]{:S(2)}) collective-permute-start(bf16[4,512,512]{2,1,0:T(8,128)(2,1)} %tiles.5.refs_1_), channel_id=1, source_target_pairs={{0,1},{1,0},{2,3},{3,2},{4,5},{5,4},{6,7},{7,6},{8,9},{9,8},{10,11... | collective-permute-start | bytes 6291464 | tf_op jit(solution)/shard_map/ppermute | solution.py:401
  43.4 36.4 %collective-permute-start.3 = (bf16[4,512,512]{2,1,0:T(8,128)(2,1)}, bf16[4,512,512]{2,1,0:T(8,128)(2,1)}, u32[]{:S(2)}, u32[]{:S(2)}) collective-permute-start(bf16[4,512,512]{2,1,0:T(8,128)(2,1)} %tiles.6.refs_2_), channel_id=1, source_target_pairs={{0,1},{1,0},{2,3},{3,2},{4,5},{5,4},{6,7},{7,6},{8,9},{9,8},{10,11... | collective-permute-start | bytes 6291464 | tf_op jit(solution)/shard_map/ppermute | solution.py:401
  48.6 31.2 %collective-permute-start.4 = (bf16[4,512,512]{2,1,0:T(8,128)(2,1)}, bf16[4,512,512]{2,1,0:T(8,128)(2,1)}, u32[]{:S(2)}, u32[]{:S(2)}) collective-permute-start(bf16[4,512,512]{2,1,0:T(8,128)(2,1)} %tiles.7.refs_3_), channel_id=1, source_target_pairs={{0,1},{1,0},{2,3},{3,2},{4,5},{5,4},{6,7},{7,6},{8,9},{9,8},{10,11... | collective-permute-start | bytes 6291464 | tf_op jit(solution)/shard_map/ppermute | solution.py:401
  67.8 2.9 %collective-permute-start = (f32[4,16,8,512]{3,2,1,0:T(8,128)}, f32[4,16,8,512]{3,2,1,0:T(8,128)S(1)}, u32[]{:S(2)}, u32[]{:S(2)}) collective-permute-start(f32[4,16,8,512]{3,2,1,0:T(8,128)} %get-tuple-element.21), channel_id=1, source_target_pairs={{0,1},{1,0},{2,3},{3,2},{4,5},{5,4},{6,7},{7,6},{8,9},{9,8},{10,11... | collective-permute-start | bytes 3145736 | tf_op jit(solution)/shard_map/ppermute | solution.py:403
  70.7 1.2 %copy-start = (f32[4,16,8,512]{3,2,1,0:T(8,128)S(1)}, f32[4,16,8,512]{3,2,1,0:T(8,128)}, u32[]{:S(2)}) copy-start(f32[4,16,8,512]{3,2,1,0:T(8,128)} %get-tuple-element.20.keep_ref) | copy-start | bytes 3145732
  72.0 23.8 %collective-permute-start.5 = (bf16[16,8,512]{2,1,0:T(8,128)(2,1)S(1)}, bf16[16,8,512]{2,1,0:T(8,128)(2,1)S(1)}, u32[]{:S(2)}, u32[]{:S(2)}) collective-permute-start(bf16[16,8,512]{2,1,0:T(8,128)(2,1)S(1)} %get-tuple-element.26), channel_id=1, source_target_pairs={{0,2},{1,3},{2,4},{3,5},{4,6},{5,7},{6,0},{7,1},{8,10},{9,11},{10,... | collective-permute-start | bytes 393224 | tf_op jit(solution)/shard_map/ppermute | solution.py:405
  72.9 6.9 %copy-start.2 = (bf16[4,512,512]{2,1,0:T(8,128)(2,1)}, bf16[4,512,512]{2,1,0:T(8,128)(2,1)S(1)}, u32[]{:S(2)}) copy-start(bf16[4,512,512]{2,1,0:T(8,128)(2,1)S(1)} %collective-permute-done.1.refs_4_) | copy-start | bytes 6291460
  72.9 22.9 %collective-permute-start.6 = (bf16[16,8,512]{2,1,0:T(8,128)(2,1)S(1)}, bf16[16,8,512]{2,1,0:T(8,128)(2,1)S(1)}, u32[]{:S(2)}, u32[]{:S(2)}) collective-permute-start(bf16[16,8,512]{2,1,0:T(8,128)(2,1)S(1)} %get-tuple-element.27), channel_id=1, source_target_pairs={{0,4},{1,5},{2,6},{3,7},{4,0},{5,1},{6,2},{7,3},{8,12},{9,13},{10,... | collective-permute-start | bytes 393224 | tf_op jit(solution)/shard_map/ppermute | solution.py:405
  75.7 20.2 %collective-permute-start.7 = (bf16[16,8,512]{2,1,0:T(8,128)(2,1)S(1)}, bf16[16,8,512]{2,1,0:T(8,128)(2,1)S(1)}, u32[]{:S(2)}, u32[]{:S(2)}) collective-permute-start(bf16[16,8,512]{2,1,0:T(8,128)(2,1)S(1)} %get-tuple-element.28), channel_id=1, source_target_pairs={{0,6},{1,7},{2,0},{3,1},{4,2},{5,3},{6,4},{7,5},{8,14},{9,15},{10,... | collective-permute-start | bytes 393224 | tf_op jit(solution)/shard_map/ppermute | solution.py:405
  79.8 29.4 %copy-start.1 = (s32[1,16,1]{1,2,0:T(1,128)S(1)}, s32[1,16,1]{1,2,0:T(1,128)}, u32[]{:S(2)}) copy-start(s32[1,16,1]{1,2,0:T(1,128)} %param.9) | copy-start | bytes 196

commit v13 on v12

--- a/solution.py
+++ b/solution.py
@@ -9,6 +9,7 @@
 
 LANES = 128
 PAIR_GROUP = 4
+DIAG_GROUP = 2
 MIB = 1024 * 1024
 UNIT = 12.0**-0.2
 UNIT2 = UNIT * UNIT
@@ -141,16 +142,16 @@
     return ((first + 4.0 * second) * inverse).astype(jnp.bfloat16)
 
 
-def diag_kernel(core, ens_ref, inc_ref, coords_ref, keep_ref, send_ref, sum_ref):
+def diag_block(block_index, core, ens_ref, inc_ref, coords_ref, keep_ref, send_ref, sum_ref):
     members, levels, points = ens_ref.shape[1:]
     parts, _, step, _ = keep_ref.shape
     rows = members * levels
     half = points // 2
-    places = coords_ref[0].astype(jnp.float32)
+    places = coords_ref[block_index].astype(jnp.float32)
     left, right = left_rows(places), right_rows(places)
     upper = tile_of(left[:, :half], right)
     lower = tile_of(left[:, half:], right[:, half:])
-    weighted = (ens_ref[0] * inc_ref[0][None]).reshape(rows, points)
+    weighted = (ens_ref[block_index] * inc_ref[block_index][None]).reshape(rows, points)
     near, far = weighted[:, :half], weighted[:, half:]
     field_near = jnp.dot(near, upper[:, :half], preferred_element_type=jnp.float32) + lax.dot_general(
         far, upper[:, half:], (((1,), (1,)), ((), ())), preferred_element_type=jnp.float32
@@ -158,14 +159,19 @@
     field_far = jnp.dot(near, upper[:, half:], preferred_element_type=jnp.float32) + jnp.dot(
         far, lower, preferred_element_type=jnp.float32
     )
-    block = ens_ref[0].astype(jnp.float32)
-    sum_ref[:, :half] = jnp.sum(block[:, :, :half] * field_near.reshape(members, levels, half), axis=0)
-    sum_ref[:, half:] = jnp.sum(block[:, :, half:] * field_far.reshape(members, levels, half), axis=0)
+    block = ens_ref[block_index].astype(jnp.float32)
+    sum_ref[block_index, :, :half] = jnp.sum(block[:, :, :half] * field_near.reshape(members, levels, half), axis=0)
+    sum_ref[block_index, :, half:] = jnp.sum(block[:, :, half:] * field_far.reshape(members, levels, half), axis=0)
     for part in range(parts):
         mine = pl.multiple_of((2 * part + core[0]) * step, step)
         other = pl.multiple_of((2 * part + 1 - core[0]) * step, step)
-        keep_ref[part, 0] = sum_ref[pl.ds(mine, step), :]
-        send_ref[part, 0] = sum_ref[pl.ds(other, step), :]
+        keep_ref[part, block_index] = sum_ref[block_index, pl.ds(mine, step), :]
+        send_ref[part, block_index] = sum_ref[block_index, pl.ds(other, step), :]
+
+
+def diag_kernel(core, ens_ref, *refs):
+    for block_index in range(ens_ref.shape[0]):
+        diag_block(block_index, core, ens_ref, *refs)
 
 
 def diag(ensemble, increment, coords, core, parts):
@@ -176,14 +182,14 @@
         diag_kernel,
         grid_spec=pltpu.PrefetchScalarGridSpec(
             num_scalar_prefetch=1,
-            grid=(blocks,),
+            grid=(blocks // DIAG_GROUP,),
             in_specs=[
-                pl.BlockSpec((1, members, levels, points), lambda b, c: (b, 0, 0, 0)),
-                pl.BlockSpec((1, levels, points), lambda b, c: (b, 0, 0)),
-                pl.BlockSpec((1, 2, points), lambda b, c: (b, 0, 0)),
+                pl.BlockSpec((DIAG_GROUP, members, levels, points), lambda b, c: (b, 0, 0, 0)),
+                pl.BlockSpec((DIAG_GROUP, levels, points), lambda b, c: (b, 0, 0)),
+                pl.BlockSpec((DIAG_GROUP, 2, points), lambda b, c: (b, 0, 0)),
             ],
-            out_specs=[pl.BlockSpec((parts, 1, step, points), lambda b, c: (0, b, 0, 0))] * 2,
-            scratch_shapes=[pltpu.VMEM((levels, points), jnp.float32)],
+            out_specs=[pl.BlockSpec((parts, DIAG_GROUP, step, points), lambda b, c: (0, b, 0, 0))] * 2,
+            scratch_shapes=[pltpu.VMEM((DIAG_GROUP, levels, points), jnp.float32)],
         ),
         out_shape=[out, out],
         compiler_params=pltpu.CompilerParams(vmem_limit_bytes=60 * MIB),
@@ -275,13 +281,15 @@
     for slot in range(slot_total):
         for copy in ens_copies(slot):
             copy.start()
-    for group in range(groups):
+    for group in range(2):
         tile_copy(group).start()
     inc_copy.wait()
     for slot in range(slot_total):
         field_ref[slot] = jnp.zeros((every, points), jnp.float32)
         for copy in ens_copies(slot):
             copy.wait()
+        if slot % 2 == 1 and slot // 2 + 2 < groups:
+            tile_copy(slot // 2 + 2).start()
         block = ens_ref[slot].reshape(every // step, step, points)
         weighted_ref[slot] = (block * inc_ref[slot][None]).reshape(every, points)
 

time: 111 us -> 110 us (level)
  Pallas kernels: 64.1 us -> 60.5 us
  waiting for transfers between devices: 8.5 us -> 9.94 us
    pallas_call x1, Pallas kernels: 16 us -> 13.9 us  [apply_pairs(): pl.pallas_call(apply_kernel, in_specs=[pl.BlockSpec(memory_space=pltpu.SM...]
    all_to_all x1, waiting for transfers between devices: 2.04 us -> 3.69 us  [per_device(): lax.all_to_all(big.reshape(regions * groups, -1, LANES), ('region', 'memb...]
    pallas_call x1, Pallas kernels: 18.7 us -> 17 us  [diag(): pl.pallas_call(diag_kernel, grid_spec=pltpu.PrefetchScalarGridSpec(num_sc...]
  transfers between devices with their start and end apart: 10 -> 10, of which waited for: 3 -> 3; matrix products, arithmetic and copies ran while one was open for 0% -> 0% of each run, Pallas kernels for 54% -> 52%
where the time goes in v13:
time: 110 us; the launch traced here: 109 us
  Pallas kernels  60.5 us (55%)
  starting transfers between devices  21.8 us (20%)
  blocking collectives  14.1 us (13%)
  waiting for transfers between devices  9.94 us (9%)
  local copies, waits for them, and re-layouts  1.93 us (2%)
    pallas_call x4, Pallas kernels, tiles(): pl.pallas_call(tiles_kernel, in_specs=[pl.BlockSpec(memory_space=pltpu.SM...  20.3 us
    pallas_call x1, Pallas kernels, diag(): pl.pallas_call(diag_kernel, grid_spec=pltpu.PrefetchScalarGridSpec(num_sc...  17 us
    all_to_all x1, blocking collectives, per_device(): back = lax.all_to_all(partial, 'region', 0, 0, tiled=True)  14.1 us
    pallas_call x1, Pallas kernels, apply_pairs(): pl.pallas_call(apply_kernel, in_specs=[pl.BlockSpec(memory_space=pltpu.SM...  13.9 us
    all_to_all x1, starting transfers between devices, per_device(): lax.all_to_all(select(increment, coords, slots, own, step), 'region', 0,...  7.95 us
    all_to_all x1, starting transfers between devices, per_device(): lax.all_to_all(big.reshape(regions * groups, -1, LANES), ('region', 'memb...  7.18 us
    pallas_call x1, Pallas kernels, pack(): pl.pallas_call(pack_kernel, in_specs=[pl.BlockSpec(memory_space=pltpu.SME...  5.29 us
    ppermute x3, starting transfers between devices, per_device(): lax.ppermute(part, 'member', [(i, (i + 2 * hop) % groups) for i in range(...  5.09 us
  transfers between devices with their start and end apart: 10, of which 3 were waited for; matrix products, arithmetic and copies ran while one was open for 0% of the time, Pallas kernels for 52%

profile of v13, /device:TPU:0, one launch (start us, length us, event | category | flops | bytes accessed | tf_op | source)
XLA Modules:
  0.0 109.0 jit_solution(16169885548693201035)
XLA Ops:
  0.0 2.5 %select.1 = bf16[16,10,512]{2,1,0:T(8,128)(2,1)} custom-call(s32[16]{0:T(128)} %bitcast.5, s32[1]{0:T(128)} %bitcast.1.own, bf16[16,64,512]{2,1,0:T(8,128)(2,1)} %refs_0_.1, bf16[16,2,512]{2,1,0:T(2,128)(2,1)} %refs_1_.1), custom_call_target="tpu_custom_call" | custom-call | tf_op jit(solution)/shard_map/select/pallas_call | solution.py:39
  2.5 8.0 %all-to-all-start = ((bf16[16,10,512]{2,1,0:T(8,128)(2,1)}), bf16[16,10,512]{2,1,0:T(8,128)(2,1)S(1)}, u32[]{:S(2)}, u32[]{:S(2)}) async-start(bf16[16,10,512]{2,1,0:T(8,128)(2,1)} %select.1), calls=%async_computation | async-start | bytes 524288 | tf_op jit(solution)/shard_map/all_to_all | solution.py:398
  10.5 5.3 %pack.1 = bf16[16,8,128,128]{3,2,1,0:T(8,128)(2,1)} custom-call(s32[16]{0:T(128)} %bitcast.6, bf16[16,4,64,512]{3,2,1,0:T(8,128)(2,1)} %ens_ref.3), custom_call_target="tpu_custom_call" | custom-call | tf_op jit(solution)/shard_map/pack/pallas_call | solution.py:86
  15.8 3.4 %all-to-all-done.places_ref.small_ref = bf16[16,10,512]{2,1,0:T(8,128)(2,1)S(1)} async-done(((bf16[16,10,512]{2,1,0:T(8,128)(2,1)}), bf16[16,10,512]{2,1,0:T(8,128)(2,1)S(1)}, u32[]{:S(2)}, u32[]{:S(2)}) %all-to-all-start) | async-done | bytes 163872 | tf_op jit(solution)/shard_map/all_to_all | solution.py:398
  19.2 0.7 copy-done.3
  19.9 7.2 %all-to-all-start.1 = ((bf16[128,128,128]{2,1,0:T(8,128)(2,1)}), bf16[128,128,128]{2,1,0:T(8,128)(2,1)}, u32[]{:S(2)}, u32[]{:S(2)}) async-start(bf16[128,128,128]{2,1,0:T(8,128)(2,1)} %bitcast.8), calls=%async_computation.1 | async-start | bytes 8388608 | tf_op jit(solution)/shard_map/all_to_all | solution.py:401
  27.1 5.1 %tiles.4.refs_0_ = bf16[4,512,512]{2,1,0:T(8,128)(2,1)} custom-call(s32[2,32]{1,0:T(2,128)} %bitcast.9, s32[1]{0:T(128)S(6)} %mul.2.first, bf16[16,10,512]{2,1,0:T(8,128)(2,1)} %copy-done.3), custom_call_target="tpu_custom_call" | custom-call | flops 4000000000 | bytes 2000000 | tf_op jit(solution)/shard_map/tiles/pallas_call | solution.py:239
  32.2 0.1 collective-permute-start.1
  32.3 5.1 %tiles.5.refs_1_ = bf16[4,512,512]{2,1,0:T(8,128)(2,1)} custom-call(s32[2,32]{1,0:T(2,128)} %bitcast.10, s32[1]{0:T(128)S(6)} %add.9.first, bf16[16,10,512]{2,1,0:T(8,128)(2,1)} %copy-done.3), custom_call_target="tpu_custom_call" | custom-call | flops 4000000000 | bytes 2000000 | tf_op jit(solution)/shard_map/tiles/pallas_call | solution.py:239
  37.4 0.8 collective-permute-start.2
  38.1 5.1 %tiles.6.refs_2_ = bf16[4,512,512]{2,1,0:T(8,128)(2,1)} custom-call(s32[2,32]{1,0:T(2,128)} %bitcast.11, s32[1]{0:T(128)S(6)} %add.10.first, bf16[16,10,512]{2,1,0:T(8,128)(2,1)} %copy-done.3), custom_call_target="tpu_custom_call" | custom-call | flops 4000000000 | bytes 2000000 | tf_op jit(solution)/shard_map/tiles/pallas_call | solution.py:239
  43.2 0.1 collective-permute-start.3
  43.3 5.1 %tiles.7.refs_3_ = bf16[4,512,512]{2,1,0:T(8,128)(2,1)} custom-call(s32[2,32]{1,0:T(2,128)} %bitcast.12, s32[1]{0:T(128)S(6)} %add.11.first, bf16[16,10,512]{2,1,0:T(8,128)(2,1)} %copy-done.3), custom_call_target="tpu_custom_call" | custom-call | flops 4000000000 | bytes 2000000 | tf_op jit(solution)/shard_map/tiles/pallas_call | solution.py:239
  48.4 0.6 collective-permute-start.4
  49.0 17.0 %diag.1 = (f32[4,16,8,512]{3,2,1,0:T(8,128)}, f32[4,16,8,512]{3,2,1,0:T(8,128)}) custom-call(s32[1]{0:T(128)S(6)} %and.4.core, bf16[16,4,64,512]{3,2,1,0:T(8,128)(2,1)} %ens_ref.3, bf16[16,64,512]{2,1,0:T(8,128)(2,1)} %refs_0_.1, bf16[16,2,512]{2,1,0:T(2,128)(2,1)} %refs_1_.1), custom_call_target="tpu_custom_call" | custom-call | flops 20000000000 | bytes 8000000 | tf_op jit(solution)/shard_map/diag/pallas_call | solution.py:181
  66.0 0.1 collective-permute-start
  66.0 2.8 %collective-permute-done.got_ref = f32[4,16,8,512]{3,2,1,0:T(8,128)S(1)} collective-permute-done((f32[4,16,8,512]{3,2,1,0:T(8,128)}, f32[4,16,8,512]{3,2,1,0:T(8,128)S(1)}, u32[]{:S(2)}, u32[]{:S(2)}) %collective-permute-start) | collective-permute-done | bytes 1048608 | tf_op jit(solution)/shard_map/ppermute | solution.py:411
  68.9 1.2 %copy-done = f32[4,16,8,512]{3,2,1,0:T(8,128)S(1)} copy-done((f32[4,16,8,512]{3,2,1,0:T(8,128)S(1)}, f32[4,16,8,512]{3,2,1,0:T(8,128)}, u32[]{:S(2)}) %copy-start) | copy-done | bytes 1048600
  70.1 0.1 merge.1
  70.2 1.0 collective-permute-start.5
  71.1 0.0 collective-permute-done.1.refs_4_
  71.1 2.7 %collective-permute-start.6 = (bf16[16,8,512]{2,1,0:T(8,128)(2,1)S(1)}, bf16[16,8,512]{2,1,0:T(8,128)(2,1)S(1)}, u32[]{:S(2)}, u32[]{:S(2)}) collective-permute-start(bf16[16,8,512]{2,1,0:T(8,128)(2,1)S(1)} %get-tuple-element.27), channel_id=1, source_target_pairs={{0,4},{1,5},{2,6},{3,7},{4,0},{5,1},{6,2},{7,3},{8,12},{9,13},{10,... | collective-permute-start | bytes 393224 | tf_op jit(solution)/shard_map/ppermute | solution.py:413
  73.9 0.0 collective-permute-done.2.refs_5_
  73.9 1.4 %collective-permute-start.7 = (bf16[16,8,512]{2,1,0:T(8,128)(2,1)S(1)}, bf16[16,8,512]{2,1,0:T(8,128)(2,1)S(1)}, u32[]{:S(2)}, u32[]{:S(2)}) collective-permute-start(bf16[16,8,512]{2,1,0:T(8,128)(2,1)S(1)} %get-tuple-element.28), channel_id=1, source_target_pairs={{0,6},{1,7},{2,0},{3,1},{4,2},{5,3},{6,4},{7,5},{8,14},{9,15},{10,... | collective-permute-start | bytes 393224 | tf_op jit(solution)/shard_map/ppermute | solution.py:413
  75.9 3.7 %all-to-all-done.1 = bf16[128,128,128]{2,1,0:T(8,128)(2,1)} async-done(((bf16[128,128,128]{2,1,0:T(8,128)(2,1)}), bf16[128,128,128]{2,1,0:T(8,128)(2,1)}, u32[]{:S(2)}, u32[]{:S(2)}) %all-to-all-start.1) | async-done | bytes 4194336 | tf_op jit(solution)/shard_map/all_to_all | solution.py:401
  79.6 0.0 collective-permute-done.3.refs_6_
  79.6 0.0 collective-permute-done.4.refs_7_
  79.6 13.9 %apply.1 = bf16[16,8,512]{2,1,0:T(8,128)(2,1)} custom-call(s32[2,32]{1,0:T(2,128)} %bitcast.13, s32[1]{0:T(128)S(6)} %copy.7.count, s32[1]{0:T(128)S(6)} %and.4.core, bf16[16,8,128,128]{3,2,1,0:T(8,128)(2,1)} %bitcast.3.got_ref, bf16[16,10,512]{2,1,0:T(8,128)(2,1)} %copy-done.3, bf16[4,512,512]{2,1,0:T(8,128)(2,1)} %tiles.4.refs_0_, ...), custom_call_target="tpu_custom_call" | custom-call | flops 100000000 | bytes 22000000 | tf_op jit(solution)/shard_map/apply/pallas_call | solution.py:341
  93.6 0.0 collective-permute-done.5.refs_0_
  93.6 0.0 collective-permute-done.6.refs_1_
  93.6 14.1 %all_to_all.15.refs_3_ = bf16[16,8,512]{2,1,0:T(8,128)(2,1)S(1)} all-to-all(bf16[16,8,512]{2,1,0:T(8,128)(2,1)} %apply.1), channel_id=1, replica_groups=mesh['region'=16,'member'=8] {'region'}, dimensions={0} | all-to-all | bytes 262144 | tf_op jit(solution)/shard_map/all_to_all | solution.py:420
  107.6 1.4 %finish.1 = f32[16,8,512]{2,1,0:T(8,128)} custom-call(s32[16]{0:T(128)S(1)} %bitcast.7, f32[16,8,512]{2,1,0:T(8,128)S(1)} %get-tuple-element.23.own_ref, bf16[16,8,512]{2,1,0:T(8,128)(2,1)S(1)} %collective-permute-done.5.refs_0_, bf16[16,8,512]{2,1,0:T(8,128)(2,1)S(1)} %collective-permute-done.6.refs_1_, ...), custom_call_target="tpu_custom_call" | custom-call | tf_op jit(solution)/shard_map/finish/pallas_call | solution.py:380
  (7 shorter events, 0.0 us)
Async XLA Ops:
  2.5 16.7 %all-to-all-start = ((bf16[16,10,512]{2,1,0:T(8,128)(2,1)}), bf16[16,10,512]{2,1,0:T(8,128)(2,1)S(1)}, u32[]{:S(2)}, u32[]{:S(2)}) async-start(bf16[16,10,512]{2,1,0:T(8,128)(2,1)} %select.1), calls=%async_computation | async-start | bytes 524288 | tf_op jit(solution)/shard_map/all_to_all | solution.py:398
  19.2 0.7 copy-start.3
  19.9 59.7 %all-to-all-start.1 = ((bf16[128,128,128]{2,1,0:T(8,128)(2,1)}), bf16[128,128,128]{2,1,0:T(8,128)(2,1)}, u32[]{:S(2)}, u32[]{:S(2)}) async-start(bf16[128,128,128]{2,1,0:T(8,128)(2,1)} %bitcast.8), calls=%async_computation.1 | async-start | bytes 8388608 | tf_op jit(solution)/shard_map/all_to_all | solution.py:401
  32.2 38.9 %collective-permute-start.1 = (bf16[4,512,512]{2,1,0:T(8,128)(2,1)}, bf16[4,512,512]{2,1,0:T(8,128)(2,1)S(1)}, u32[]{:S(2)}, u32[]{:S(2)}) collective-permute-start(bf16[4,512,512]{2,1,0:T(8,128)(2,1)} %tiles.4.refs_0_), channel_id=1, source_target_pairs={{0,1},{1,0},{2,3},{3,2},{4,5},{5,4},{6,7},{7,6},{8,9},{9,8},{10,11... | collective-permute-start | bytes 6291464 | tf_op jit(solution)/shard_map/ppermute | solution.py:409
  37.4 36.5 %collective-permute-start.2 = (bf16[4,512,512]{2,1,0:T(8,128)(2,1)}, bf16[4,512,512]{2,1,0:T(8,128)(2,1)}, u32[]{:S(2)}, u32[]{:S(2)}) collective-permute-start(bf16[4,512,512]{2,1,0:T(8,128)(2,1)} %tiles.5.refs_1_), channel_id=1, source_target_pairs={{0,1},{1,0},{2,3},{3,2},{4,5},{5,4},{6,7},{7,6},{8,9},{9,8},{10,11... | collective-permute-start | bytes 6291464 | tf_op jit(solution)/shard_map/ppermute | solution.py:409
  43.2 36.4 %collective-permute-start.3 = (bf16[4,512,512]{2,1,0:T(8,128)(2,1)}, bf16[4,512,512]{2,1,0:T(8,128)(2,1)}, u32[]{:S(2)}, u32[]{:S(2)}) collective-permute-start(bf16[4,512,512]{2,1,0:T(8,128)(2,1)} %tiles.6.refs_2_), channel_id=1, source_target_pairs={{0,1},{1,0},{2,3},{3,2},{4,5},{5,4},{6,7},{7,6},{8,9},{9,8},{10,11... | collective-permute-start | bytes 6291464 | tf_op jit(solution)/shard_map/ppermute | solution.py:409
  48.4 31.2 %collective-permute-start.4 = (bf16[4,512,512]{2,1,0:T(8,128)(2,1)}, bf16[4,512,512]{2,1,0:T(8,128)(2,1)}, u32[]{:S(2)}, u32[]{:S(2)}) collective-permute-start(bf16[4,512,512]{2,1,0:T(8,128)(2,1)} %tiles.7.refs_3_), channel_id=1, source_target_pairs={{0,1},{1,0},{2,3},{3,2},{4,5},{5,4},{6,7},{7,6},{8,9},{9,8},{10,11... | collective-permute-start | bytes 6291464 | tf_op jit(solution)/shard_map/ppermute | solution.py:409
  66.0 2.9 %collective-permute-start = (f32[4,16,8,512]{3,2,1,0:T(8,128)}, f32[4,16,8,512]{3,2,1,0:T(8,128)S(1)}, u32[]{:S(2)}, u32[]{:S(2)}) collective-permute-start(f32[4,16,8,512]{3,2,1,0:T(8,128)} %get-tuple-element.21), channel_id=1, source_target_pairs={{0,1},{1,0},{2,3},{3,2},{4,5},{5,4},{6,7},{7,6},{8,9},{9,8},{10,11... | collective-permute-start | bytes 3145736 | tf_op jit(solution)/shard_map/ppermute | solution.py:411
  68.9 1.2 %copy-start = (f32[4,16,8,512]{3,2,1,0:T(8,128)S(1)}, f32[4,16,8,512]{3,2,1,0:T(8,128)}, u32[]{:S(2)}) copy-start(f32[4,16,8,512]{3,2,1,0:T(8,128)} %get-tuple-element.20.keep_ref) | copy-start | bytes 3145732
  70.2 23.4 %collective-permute-start.5 = (bf16[16,8,512]{2,1,0:T(8,128)(2,1)S(1)}, bf16[16,8,512]{2,1,0:T(8,128)(2,1)S(1)}, u32[]{:S(2)}, u32[]{:S(2)}) collective-permute-start(bf16[16,8,512]{2,1,0:T(8,128)(2,1)S(1)} %get-tuple-element.26), channel_id=1, source_target_pairs={{0,2},{1,3},{2,4},{3,5},{4,6},{5,7},{6,0},{7,1},{8,10},{9,11},{10,... | collective-permute-start | bytes 393224 | tf_op jit(solution)/shard_map/ppermute | solution.py:413
  71.1 8.5 %copy-start.2 = (bf16[4,512,512]{2,1,0:T(8,128)(2,1)}, bf16[4,512,512]{2,1,0:T(8,128)(2,1)S(1)}, u32[]{:S(2)}) copy-start(bf16[4,512,512]{2,1,0:T(8,128)(2,1)S(1)} %collective-permute-done.1.refs_4_) | copy-start | bytes 6291460
  71.1 22.4 %collective-permute-start.6 = (bf16[16,8,512]{2,1,0:T(8,128)(2,1)S(1)}, bf16[16,8,512]{2,1,0:T(8,128)(2,1)S(1)}, u32[]{:S(2)}, u32[]{:S(2)}) collective-permute-start(bf16[16,8,512]{2,1,0:T(8,128)(2,1)S(1)} %get-tuple-element.27), channel_id=1, source_target_pairs={{0,4},{1,5},{2,6},{3,7},{4,0},{5,1},{6,2},{7,3},{8,12},{9,13},{10,... | collective-permute-start | bytes 393224 | tf_op jit(solution)/shard_map/ppermute | solution.py:413
  73.9 19.7 %collective-permute-start.7 = (bf16[16,8,512]{2,1,0:T(8,128)(2,1)S(1)}, bf16[16,8,512]{2,1,0:T(8,128)(2,1)S(1)}, u32[]{:S(2)}, u32[]{:S(2)}) collective-permute-start(bf16[16,8,512]{2,1,0:T(8,128)(2,1)S(1)} %get-tuple-element.28), channel_id=1, source_target_pairs={{0,6},{1,7},{2,0},{3,1},{4,2},{5,3},{6,4},{7,5},{8,14},{9,15},{10,... | collective-permute-start | bytes 393224 | tf_op jit(solution)/shard_map/ppermute | solution.py:413
  79.6 28.0 %copy-start.1 = (s32[1,16,1]{1,2,0:T(1,128)S(1)}, s32[1,16,1]{1,2,0:T(1,128)}, u32[]{:S(2)}) copy-start(s32[1,16,1]{1,2,0:T(1,128)} %param.9) | copy-start | bytes 196

commit v14 on v13

--- a/solution.py
+++ b/solution.py
@@ -9,7 +9,7 @@
 
 LANES = 128
 PAIR_GROUP = 4
-DIAG_GROUP = 2
+DIAG_GROUP = 4
 MIB = 1024 * 1024
 UNIT = 12.0**-0.2
 UNIT2 = UNIT * UNIT
@@ -297,7 +297,7 @@
         products = []
         for each in range(number):
             first, second = pairs[0, row + each], pairs[1, row + each]
-            tile = tiles_ref[group, within + each]
+            tile = tiles_ref[group + each // PAIR_GROUP, within + each % PAIR_GROUP]
             to_first = lax.dot_general(
                 weighted_ref[second], tile, (((1,), (1,)), ((), ())), preferred_element_type=jnp.float32
             )
@@ -306,27 +306,37 @@
         for slot, product in products:
             field_ref[slot] += product
 
-    def turn(group, carry):
+    def turn(couple, carry):
+        group = 2 * couple
         away = core[0] * (groups // 2)
         row = PAIR_GROUP * jnp.where(group < groups // 2, group + away, group - away)
         live = count[0] - row
-        pltpu.make_async_copy(stacks[0], tiles_ref.at[group], tiles_sem.at[group]).wait()
-
-        @pl.when(live >= PAIR_GROUP)
+        for stack in range(2):
+            pltpu.make_async_copy(stacks[0], tiles_ref.at[group + stack], tiles_sem.at[group + stack]).wait()
+
+        @pl.when(live >= 2 * PAIR_GROUP)
         def _():
-            some(group, row, 0, PAIR_GROUP)
-
-        @pl.when(live < PAIR_GROUP)
+            some(group, row, 0, 2 * PAIR_GROUP)
+
+        @pl.when(live < 2 * PAIR_GROUP)
         def _():
+            half = live >= PAIR_GROUP
+
+            @pl.when(half)
+            def _():
+                some(group, row, 0, PAIR_GROUP)
+
+            start = jnp.where(half, PAIR_GROUP, 0)
+
             def one(within, inner):
-                some(group, row + within, within, 1)
+                some(group + jnp.where(half, 1, 0), row + start + within, within, 1)
                 return inner
 
-            lax.fori_loop(0, jnp.maximum(live, 0), one, 0)
+            lax.fori_loop(0, jnp.maximum(live - start, 0), one, 0)
 
         return carry
 
-    lax.fori_loop(0, groups, turn, 0)
+    lax.fori_loop(0, groups // 2, turn, 0)
 
     for slot in range(slot_total):
         product = ens_ref[slot].reshape(every, points).astype(jnp.float32) * field_ref[slot]

time: 110 us -> 109 us (level)
  blocking collectives: 14.1 us -> 11.5 us
  Pallas kernels: 60.5 us -> 62 us
    all_to_all x1, blocking collectives: 14.1 us -> 11.5 us  [per_device(): back = lax.all_to_all(partial, 'region', 0, 0, tiled=True)]
    pallas_call x1, Pallas kernels: 13.9 us -> 16.1 us  [apply_pairs(): pl.pallas_call(apply_kernel, in_specs=[pl.BlockSpec(memory_space=pltpu.SM...]
  transfers between devices with their start and end apart: 10 -> 10, of which waited for: 3 -> 3; matrix products, arithmetic and copies ran while one was open for 0% -> 0% of each run, Pallas kernels for 52% -> 53%
where the time goes in v14:
time: 109 us
  Pallas kernels  62 us (57%)
  starting transfers between devices  22 us (20%)
  blocking collectives  11.5 us (11%)
  waiting for transfers between devices  10.6 us (10%)
  local copies, waits for them, and re-layouts  1.93 us (2%)
    pallas_call x4, Pallas kernels, tiles(): pl.pallas_call(tiles_kernel, in_specs=[pl.BlockSpec(memory_space=pltpu.SM...  20.3 us
    pallas_call x1, Pallas kernels, diag(): pl.pallas_call(diag_kernel, grid_spec=pltpu.PrefetchScalarGridSpec(num_sc...  16.3 us
    pallas_call x1, Pallas kernels, apply_pairs(): pl.pallas_call(apply_kernel, in_specs=[pl.BlockSpec(memory_space=pltpu.SM...  16.1 us
    all_to_all x1, blocking collectives, per_device(): back = lax.all_to_all(partial, 'region', 0, 0, tiled=True)  11.5 us
    all_to_all x1, starting transfers between devices, per_device(): lax.all_to_all(select(increment, coords, slots, own, step), 'region', 0,...  7.97 us
    all_to_all x1, starting transfers between devices, per_device(): lax.all_to_all(big.reshape(regions * groups, -1, LANES), ('region', 'memb...  7.43 us
    pallas_call x1, Pallas kernels, pack(): pl.pallas_call(pack_kernel, in_specs=[pl.BlockSpec(memory_space=pltpu.SME...  5.3 us
    ppermute x3, starting transfers between devices, per_device(): lax.ppermute(part, 'member', [(i, (i + 2 * hop) % groups) for i in range(...  5.1 us
  transfers between devices with their start and end apart: 10, of which 3 were waited for; matrix products, arithmetic and copies ran while one was open for 0% of the time, Pallas kernels for 53%

profile of v14, /device:TPU:0, one launch (start us, length us, event | category | flops | bytes accessed | tf_op | source)
XLA Modules:
  0.0 108.8 jit_solution(7831350752928855142)
XLA Ops:
  0.0 2.5 %select.1 = bf16[16,10,512]{2,1,0:T(8,128)(2,1)} custom-call(s32[16]{0:T(128)} %bitcast.5, s32[1]{0:T(128)} %bitcast.1.own, bf16[16,64,512]{2,1,0:T(8,128)(2,1)} %refs_0_.1, bf16[16,2,512]{2,1,0:T(2,128)(2,1)} %refs_1_.1), custom_call_target="tpu_custom_call" | custom-call | tf_op jit(solution)/shard_map/select/pallas_call | solution.py:39
  2.5 8.0 %all-to-all-start = ((bf16[16,10,512]{2,1,0:T(8,128)(2,1)}), bf16[16,10,512]{2,1,0:T(8,128)(2,1)S(1)}, u32[]{:S(2)}, u32[]{:S(2)}) async-start(bf16[16,10,512]{2,1,0:T(8,128)(2,1)} %select.1), calls=%async_computation | async-start | bytes 524288 | tf_op jit(solution)/shard_map/all_to_all | solution.py:408
  10.5 5.3 %pack.1 = bf16[16,8,128,128]{3,2,1,0:T(8,128)(2,1)} custom-call(s32[16]{0:T(128)} %bitcast.6, bf16[16,4,64,512]{3,2,1,0:T(8,128)(2,1)} %ens_ref.3), custom_call_target="tpu_custom_call" | custom-call | tf_op jit(solution)/shard_map/pack/pallas_call | solution.py:86
  15.8 3.4 %all-to-all-done.places_ref.small_ref = bf16[16,10,512]{2,1,0:T(8,128)(2,1)S(1)} async-done(((bf16[16,10,512]{2,1,0:T(8,128)(2,1)}), bf16[16,10,512]{2,1,0:T(8,128)(2,1)S(1)}, u32[]{:S(2)}, u32[]{:S(2)}) %all-to-all-start) | async-done | bytes 163872 | tf_op jit(solution)/shard_map/all_to_all | solution.py:408
  19.2 0.7 copy-done.3
  19.9 7.4 %all-to-all-start.1 = ((bf16[128,128,128]{2,1,0:T(8,128)(2,1)}), bf16[128,128,128]{2,1,0:T(8,128)(2,1)}, u32[]{:S(2)}, u32[]{:S(2)}) async-start(bf16[128,128,128]{2,1,0:T(8,128)(2,1)} %bitcast.8), calls=%async_computation.1 | async-start | bytes 8388608 | tf_op jit(solution)/shard_map/all_to_all | solution.py:411
  27.3 5.1 %tiles.4.refs_0_ = bf16[4,512,512]{2,1,0:T(8,128)(2,1)} custom-call(s32[2,32]{1,0:T(2,128)} %bitcast.9, s32[1]{0:T(128)S(6)} %mul.2.first, bf16[16,10,512]{2,1,0:T(8,128)(2,1)} %copy-done.3), custom_call_target="tpu_custom_call" | custom-call | flops 4000000000 | bytes 2000000 | tf_op jit(solution)/shard_map/tiles/pallas_call | solution.py:239
  32.4 0.1 collective-permute-start.1
  32.5 5.1 %tiles.5.refs_1_ = bf16[4,512,512]{2,1,0:T(8,128)(2,1)} custom-call(s32[2,32]{1,0:T(2,128)} %bitcast.10, s32[1]{0:T(128)S(6)} %add.9.first, bf16[16,10,512]{2,1,0:T(8,128)(2,1)} %copy-done.3), custom_call_target="tpu_custom_call" | custom-call | flops 4000000000 | bytes 2000000 | tf_op jit(solution)/shard_map/tiles/pallas_call | solution.py:239
  37.6 0.8 collective-permute-start.2
  38.3 5.1 %tiles.6.refs_2_ = bf16[4,512,512]{2,1,0:T(8,128)(2,1)} custom-call(s32[2,32]{1,0:T(2,128)} %bitcast.11, s32[1]{0:T(128)S(6)} %add.10.first, bf16[16,10,512]{2,1,0:T(8,128)(2,1)} %copy-done.3), custom_call_target="tpu_custom_call" | custom-call | flops 4000000000 | bytes 2000000 | tf_op jit(solution)/shard_map/tiles/pallas_call | solution.py:239
  43.4 0.1 collective-permute-start.3
  43.5 5.1 %tiles.7.refs_3_ = bf16[4,512,512]{2,1,0:T(8,128)(2,1)} custom-call(s32[2,32]{1,0:T(2,128)} %bitcast.12, s32[1]{0:T(128)S(6)} %add.11.first, bf16[16,10,512]{2,1,0:T(8,128)(2,1)} %copy-done.3), custom_call_target="tpu_custom_call" | custom-call | flops 4000000000 | bytes 2000000 | tf_op jit(solution)/shard_map/tiles/pallas_call | solution.py:239
  48.6 0.6 collective-permute-start.4
  49.2 16.3 %diag.1 = (f32[4,16,8,512]{3,2,1,0:T(8,128)}, f32[4,16,8,512]{3,2,1,0:T(8,128)}) custom-call(s32[1]{0:T(128)S(6)} %and.4.core, bf16[16,4,64,512]{3,2,1,0:T(8,128)(2,1)} %ens_ref.3, bf16[16,64,512]{2,1,0:T(8,128)(2,1)} %refs_0_.1, bf16[16,2,512]{2,1,0:T(2,128)(2,1)} %refs_1_.1), custom_call_target="tpu_custom_call" | custom-call | flops 20000000000 | bytes 8000000 | tf_op jit(solution)/shard_map/diag/pallas_call | solution.py:181
  65.5 0.0 collective-permute-start
  65.5 2.8 %collective-permute-done.got_ref = f32[4,16,8,512]{3,2,1,0:T(8,128)S(1)} collective-permute-done((f32[4,16,8,512]{3,2,1,0:T(8,128)}, f32[4,16,8,512]{3,2,1,0:T(8,128)S(1)}, u32[]{:S(2)}, u32[]{:S(2)}) %collective-permute-start) | collective-permute-done | bytes 1048608 | tf_op jit(solution)/shard_map/ppermute | solution.py:421
  68.3 1.2 %copy-done = f32[4,16,8,512]{3,2,1,0:T(8,128)S(1)} copy-done((f32[4,16,8,512]{3,2,1,0:T(8,128)S(1)}, f32[4,16,8,512]{3,2,1,0:T(8,128)}, u32[]{:S(2)}) %copy-start) | copy-done | bytes 1048600
  69.6 0.1 merge.1
  69.7 1.0 collective-permute-start.5
  70.6 0.0 collective-permute-done.1.refs_4_
  70.6 2.7 %collective-permute-start.6 = (bf16[16,8,512]{2,1,0:T(8,128)(2,1)S(1)}, bf16[16,8,512]{2,1,0:T(8,128)(2,1)S(1)}, u32[]{:S(2)}, u32[]{:S(2)}) collective-permute-start(bf16[16,8,512]{2,1,0:T(8,128)(2,1)S(1)} %get-tuple-element.27), channel_id=1, source_target_pairs={{0,4},{1,5},{2,6},{3,7},{4,0},{5,1},{6,2},{7,3},{8,12},{9,13},{10,... | collective-permute-start | bytes 393224 | tf_op jit(solution)/shard_map/ppermute | solution.py:423
  73.4 0.0 collective-permute-done.2.refs_5_
  73.4 1.4 %collective-permute-start.7 = (bf16[16,8,512]{2,1,0:T(8,128)(2,1)S(1)}, bf16[16,8,512]{2,1,0:T(8,128)(2,1)S(1)}, u32[]{:S(2)}, u32[]{:S(2)}) collective-permute-start(bf16[16,8,512]{2,1,0:T(8,128)(2,1)S(1)} %get-tuple-element.28), channel_id=1, source_target_pairs={{0,6},{1,7},{2,0},{3,1},{4,2},{5,3},{6,4},{7,5},{8,14},{9,15},{10,... | collective-permute-start | bytes 393224 | tf_op jit(solution)/shard_map/ppermute | solution.py:423
  75.4 4.4 %all-to-all-done.1 = bf16[128,128,128]{2,1,0:T(8,128)(2,1)} async-done(((bf16[128,128,128]{2,1,0:T(8,128)(2,1)}), bf16[128,128,128]{2,1,0:T(8,128)(2,1)}, u32[]{:S(2)}, u32[]{:S(2)}) %all-to-all-start.1) | async-done | bytes 4194336 | tf_op jit(solution)/shard_map/all_to_all | solution.py:411
  79.8 0.0 collective-permute-done.3.refs_6_
  79.8 0.0 collective-permute-done.4.refs_7_
  79.9 16.1 %apply.1 = bf16[16,8,512]{2,1,0:T(8,128)(2,1)} custom-call(s32[2,32]{1,0:T(2,128)} %bitcast.13, s32[1]{0:T(128)S(6)} %copy.7.count, s32[1]{0:T(128)S(6)} %and.4.core, bf16[16,8,128,128]{3,2,1,0:T(8,128)(2,1)} %bitcast.3.got_ref, bf16[16,10,512]{2,1,0:T(8,128)(2,1)} %copy-done.3, bf16[4,512,512]{2,1,0:T(8,128)(2,1)} %tiles.4.refs_0_, ...), custom_call_target="tpu_custom_call" | custom-call | flops 100000000 | bytes 22000000 | tf_op jit(solution)/shard_map/apply/pallas_call | solution.py:351
  96.0 0.0 collective-permute-done.5.refs_0_
  96.0 0.0 collective-permute-done.7.refs_2_
  96.0 11.5 %all_to_all.15.refs_3_ = bf16[16,8,512]{2,1,0:T(8,128)(2,1)S(1)} all-to-all(bf16[16,8,512]{2,1,0:T(8,128)(2,1)} %apply.1), channel_id=1, replica_groups=mesh['region'=16,'member'=8] {'region'}, dimensions={0} | all-to-all | bytes 262144 | tf_op jit(solution)/shard_map/all_to_all | solution.py:430
  107.5 1.4 %finish.1 = f32[16,8,512]{2,1,0:T(8,128)} custom-call(s32[16]{0:T(128)S(1)} %bitcast.7, f32[16,8,512]{2,1,0:T(8,128)S(1)} %get-tuple-element.23.own_ref, bf16[16,8,512]{2,1,0:T(8,128)(2,1)S(1)} %collective-permute-done.5.refs_0_, bf16[16,8,512]{2,1,0:T(8,128)(2,1)S(1)} %collective-permute-done.6.refs_1_, ...), custom_call_target="tpu_custom_call" | custom-call | tf_op jit(solution)/shard_map/finish/pallas_call | solution.py:390
  (7 shorter events, 0.0 us)
Async XLA Ops:
  2.5 16.7 %all-to-all-start = ((bf16[16,10,512]{2,1,0:T(8,128)(2,1)}), bf16[16,10,512]{2,1,0:T(8,128)(2,1)S(1)}, u32[]{:S(2)}, u32[]{:S(2)}) async-start(bf16[16,10,512]{2,1,0:T(8,128)(2,1)} %select.1), calls=%async_computation | async-start | bytes 524288 | tf_op jit(solution)/shard_map/all_to_all | solution.py:408
  19.2 0.7 copy-start.3
  19.9 60.0 %all-to-all-start.1 = ((bf16[128,128,128]{2,1,0:T(8,128)(2,1)}), bf16[128,128,128]{2,1,0:T(8,128)(2,1)}, u32[]{:S(2)}, u32[]{:S(2)}) async-start(bf16[128,128,128]{2,1,0:T(8,128)(2,1)} %bitcast.8), calls=%async_computation.1 | async-start | bytes 8388608 | tf_op jit(solution)/shard_map/all_to_all | solution.py:411
  32.4 38.2 %collective-permute-start.1 = (bf16[4,512,512]{2,1,0:T(8,128)(2,1)}, bf16[4,512,512]{2,1,0:T(8,128)(2,1)S(1)}, u32[]{:S(2)}, u32[]{:S(2)}) collective-permute-start(bf16[4,512,512]{2,1,0:T(8,128)(2,1)} %tiles.4.refs_0_), channel_id=1, source_target_pairs={{0,1},{1,0},{2,3},{3,2},{4,5},{5,4},{6,7},{7,6},{8,9},{9,8},{10,11... | collective-permute-start | bytes 6291464 | tf_op jit(solution)/shard_map/ppermute | solution.py:419
  37.6 35.8 %collective-permute-start.2 = (bf16[4,512,512]{2,1,0:T(8,128)(2,1)}, bf16[4,512,512]{2,1,0:T(8,128)(2,1)}, u32[]{:S(2)}, u32[]{:S(2)}) collective-permute-start(bf16[4,512,512]{2,1,0:T(8,128)(2,1)} %tiles.5.refs_1_), channel_id=1, source_target_pairs={{0,1},{1,0},{2,3},{3,2},{4,5},{5,4},{6,7},{7,6},{8,9},{9,8},{10,11... | collective-permute-start | bytes 6291464 | tf_op jit(solution)/shard_map/ppermute | solution.py:419
  43.4 36.4 %collective-permute-start.3 = (bf16[4,512,512]{2,1,0:T(8,128)(2,1)}, bf16[4,512,512]{2,1,0:T(8,128)(2,1)}, u32[]{:S(2)}, u32[]{:S(2)}) collective-permute-start(bf16[4,512,512]{2,1,0:T(8,128)(2,1)} %tiles.6.refs_2_), channel_id=1, source_target_pairs={{0,1},{1,0},{2,3},{3,2},{4,5},{5,4},{6,7},{7,6},{8,9},{9,8},{10,11... | collective-permute-start | bytes 6291464 | tf_op jit(solution)/shard_map/ppermute | solution.py:419
  48.6 31.2 %collective-permute-start.4 = (bf16[4,512,512]{2,1,0:T(8,128)(2,1)}, bf16[4,512,512]{2,1,0:T(8,128)(2,1)}, u32[]{:S(2)}, u32[]{:S(2)}) collective-permute-start(bf16[4,512,512]{2,1,0:T(8,128)(2,1)} %tiles.7.refs_3_), channel_id=1, source_target_pairs={{0,1},{1,0},{2,3},{3,2},{4,5},{5,4},{6,7},{7,6},{8,9},{9,8},{10,11... | collective-permute-start | bytes 6291464 | tf_op jit(solution)/shard_map/ppermute | solution.py:419
  65.5 2.9 %collective-permute-start = (f32[4,16,8,512]{3,2,1,0:T(8,128)}, f32[4,16,8,512]{3,2,1,0:T(8,128)S(1)}, u32[]{:S(2)}, u32[]{:S(2)}) collective-permute-start(f32[4,16,8,512]{3,2,1,0:T(8,128)} %get-tuple-element.21), channel_id=1, source_target_pairs={{0,1},{1,0},{2,3},{3,2},{4,5},{5,4},{6,7},{7,6},{8,9},{9,8},{10,11... | collective-permute-start | bytes 3145736 | tf_op jit(solution)/shard_map/ppermute | solution.py:421
  68.3 1.2 %copy-start = (f32[4,16,8,512]{3,2,1,0:T(8,128)S(1)}, f32[4,16,8,512]{3,2,1,0:T(8,128)}, u32[]{:S(2)}) copy-start(f32[4,16,8,512]{3,2,1,0:T(8,128)} %get-tuple-element.20.keep_ref) | copy-start | bytes 3145732
  69.7 26.3 %collective-permute-start.5 = (bf16[16,8,512]{2,1,0:T(8,128)(2,1)S(1)}, bf16[16,8,512]{2,1,0:T(8,128)(2,1)S(1)}, u32[]{:S(2)}, u32[]{:S(2)}) collective-permute-start(bf16[16,8,512]{2,1,0:T(8,128)(2,1)S(1)} %get-tuple-element.26), channel_id=1, source_target_pairs={{0,2},{1,3},{2,4},{3,5},{4,6},{5,7},{6,0},{7,1},{8,10},{9,11},{10,... | collective-permute-start | bytes 393224 | tf_op jit(solution)/shard_map/ppermute | solution.py:423
  70.6 9.2 %copy-start.2 = (bf16[4,512,512]{2,1,0:T(8,128)(2,1)}, bf16[4,512,512]{2,1,0:T(8,128)(2,1)S(1)}, u32[]{:S(2)}) copy-start(bf16[4,512,512]{2,1,0:T(8,128)(2,1)S(1)} %collective-permute-done.1.refs_4_) | copy-start | bytes 6291460
  70.6 25.3 %collective-permute-start.6 = (bf16[16,8,512]{2,1,0:T(8,128)(2,1)S(1)}, bf16[16,8,512]{2,1,0:T(8,128)(2,1)S(1)}, u32[]{:S(2)}, u32[]{:S(2)}) collective-permute-start(bf16[16,8,512]{2,1,0:T(8,128)(2,1)S(1)} %get-tuple-element.27), channel_id=1, source_target_pairs={{0,4},{1,5},{2,6},{3,7},{4,0},{5,1},{6,2},{7,3},{8,12},{9,13},{10,... | collective-permute-start | bytes 393224 | tf_op jit(solution)/shard_map/ppermute | solution.py:423
  73.4 22.6 %collective-permute-start.7 = (bf16[16,8,512]{2,1,0:T(8,128)(2,1)S(1)}, bf16[16,8,512]{2,1,0:T(8,128)(2,1)S(1)}, u32[]{:S(2)}, u32[]{:S(2)}) collective-permute-start(bf16[16,8,512]{2,1,0:T(8,128)(2,1)S(1)} %get-tuple-element.28), channel_id=1, source_target_pairs={{0,6},{1,7},{2,0},{3,1},{4,2},{5,3},{6,4},{7,5},{8,14},{9,15},{10,... | collective-permute-start | bytes 393224 | tf_op jit(solution)/shard_map/ppermute | solution.py:423
  79.8 27.6 %copy-start.1 = (s32[1,16,1]{1,2,0:T(1,128)S(1)}, s32[1,16,1]{1,2,0:T(1,128)}, u32[]{:S(2)}) copy-start(s32[1,16,1]{1,2,0:T(1,128)} %param.9) | copy-start | bytes 196

commit v15 on v13

--- a/solution.py
+++ b/solution.py
@@ -9,7 +9,7 @@
 
 LANES = 128
 PAIR_GROUP = 4
-DIAG_GROUP = 2
+DIAG_GROUP = 4
 MIB = 1024 * 1024
 UNIT = 12.0**-0.2
 UNIT2 = UNIT * UNIT
@@ -413,7 +413,7 @@
         lax.ppermute(part, "member", [(i, (i + 2 * hop) % groups) for i in range(groups)])
         for hop, part in enumerate(merged[1:], 1)
     ]
-    got, own_part = lax.optimization_barrier((got, merged[0]))
+    got, own_part, theirs = lax.optimization_barrier((got, merged[0], theirs))
     stacks = [in_hbm(stack) for stack in mine + theirs]
     partial = apply_pairs(in_hbm(got), in_hbm(small), stacks, pairs, pair_count, core, members, step)
     partial, parts = lax.optimization_barrier((partial, parts))

time: 110 us -> 110 us (level)
  blocking collectives: 14.1 us -> 11.5 us
  Pallas kernels: 60.5 us -> 62.1 us
    all_to_all x1, blocking collectives: 14.1 us -> 11.5 us  [per_device(): back = lax.all_to_all(partial, 'region', 0, 0, tiled=True)]
    pallas_call x1, Pallas kernels: 13.9 us -> 16.5 us  [apply_pairs(): pl.pallas_call(apply_kernel, in_specs=[pl.BlockSpec(memory_space=pltpu.SM...]
  transfers between devices with their start and end apart: 10 -> 10, of which waited for: 3 -> 3; matrix products, arithmetic and copies ran while one was open for 0% -> 0% of each run, Pallas kernels for 52% -> 53%
where the time goes in v15:
time: 110 us; the launch traced here: 109 us
  Pallas kernels  62.1 us (56%)
  starting transfers between devices  21.8 us (20%)
  blocking collectives  11.5 us (10%)
  waiting for transfers between devices  10.8 us (10%)
  local copies, waits for them, and re-layouts  1.93 us (2%)
    pallas_call x4, Pallas kernels, tiles(): pl.pallas_call(tiles_kernel, in_specs=[pl.BlockSpec(memory_space=pltpu.SM...  20.3 us
    pallas_call x1, Pallas kernels, apply_pairs(): pl.pallas_call(apply_kernel, in_specs=[pl.BlockSpec(memory_space=pltpu.SM...  16.5 us
    pallas_call x1, Pallas kernels, diag(): pl.pallas_call(diag_kernel, grid_spec=pltpu.PrefetchScalarGridSpec(num_sc...  16.3 us
    all_to_all x1, blocking collectives, per_device(): back = lax.all_to_all(partial, 'region', 0, 0, tiled=True)  11.5 us
    all_to_all x1, starting transfers between devices, per_device(): lax.all_to_all(select(increment, coords, slots, own, step), 'region', 0,...  7.97 us
    all_to_all x1, starting transfers between devices, per_device(): lax.all_to_all(big.reshape(regions * groups, -1, LANES), ('region', 'memb...  7.21 us
    ppermute x3, starting transfers between devices, per_device(): lax.ppermute(part, 'member', [(i, (i + 2 * hop) % groups) for i in range(...  5.1 us
    pallas_call x1, Pallas kernels, pack(): pl.pallas_call(pack_kernel, in_specs=[pl.BlockSpec(memory_space=pltpu.SME...  5.07 us
  transfers between devices with their start and end apart: 10, of which 3 were waited for; matrix products, arithmetic and copies ran while one was open for 0% of the time, Pallas kernels for 53%

profile of v15, /device:TPU:0, one launch (start us, length us, event | category | flops | bytes accessed | tf_op | source)
XLA Modules:
  0.0 109.0 jit_solution(7234267556513503370)
XLA Ops:
  0.0 2.5 %select.1 = bf16[16,10,512]{2,1,0:T(8,128)(2,1)} custom-call(s32[16]{0:T(128)} %bitcast.5, s32[1]{0:T(128)} %bitcast.1.own, bf16[16,64,512]{2,1,0:T(8,128)(2,1)} %refs_0_.1, bf16[16,2,512]{2,1,0:T(2,128)(2,1)} %refs_1_.1), custom_call_target="tpu_custom_call" | custom-call | tf_op jit(solution)/shard_map/select/pallas_call | solution.py:39
  2.5 8.0 %all-to-all-start = ((bf16[16,10,512]{2,1,0:T(8,128)(2,1)}), bf16[16,10,512]{2,1,0:T(8,128)(2,1)S(1)}, u32[]{:S(2)}, u32[]{:S(2)}) async-start(bf16[16,10,512]{2,1,0:T(8,128)(2,1)} %select.1), calls=%async_computation | async-start | bytes 524288 | tf_op jit(solution)/shard_map/all_to_all | solution.py:398
  10.5 5.1 %pack.1 = bf16[16,8,128,128]{3,2,1,0:T(8,128)(2,1)} custom-call(s32[16]{0:T(128)} %bitcast.6, bf16[16,4,64,512]{3,2,1,0:T(8,128)(2,1)} %ens_ref.3), custom_call_target="tpu_custom_call" | custom-call | tf_op jit(solution)/shard_map/pack/pallas_call | solution.py:86
  15.6 3.6 %all-to-all-done.places_ref.small_ref = bf16[16,10,512]{2,1,0:T(8,128)(2,1)S(1)} async-done(((bf16[16,10,512]{2,1,0:T(8,128)(2,1)}), bf16[16,10,512]{2,1,0:T(8,128)(2,1)S(1)}, u32[]{:S(2)}, u32[]{:S(2)}) %all-to-all-start) | async-done | bytes 163872 | tf_op jit(solution)/shard_map/all_to_all | solution.py:398
  19.2 0.7 copy-done.3
  19.9 7.2 %all-to-all-start.1 = ((bf16[128,128,128]{2,1,0:T(8,128)(2,1)}), bf16[128,128,128]{2,1,0:T(8,128)(2,1)}, u32[]{:S(2)}, u32[]{:S(2)}) async-start(bf16[128,128,128]{2,1,0:T(8,128)(2,1)} %bitcast.8), calls=%async_computation.1 | async-start | bytes 8388608 | tf_op jit(solution)/shard_map/all_to_all | solution.py:401
  27.1 5.1 %tiles.4.refs_0_ = bf16[4,512,512]{2,1,0:T(8,128)(2,1)} custom-call(s32[2,32]{1,0:T(2,128)} %bitcast.9, s32[1]{0:T(128)S(6)} %mul.2.first, bf16[16,10,512]{2,1,0:T(8,128)(2,1)} %copy-done.3), custom_call_target="tpu_custom_call" | custom-call | flops 4000000000 | bytes 2000000 | tf_op jit(solution)/shard_map/tiles/pallas_call | solution.py:239
  32.2 0.1 collective-permute-start.1
  32.3 5.1 %tiles.5.refs_1_ = bf16[4,512,512]{2,1,0:T(8,128)(2,1)} custom-call(s32[2,32]{1,0:T(2,128)} %bitcast.10, s32[1]{0:T(128)S(6)} %add.9.first, bf16[16,10,512]{2,1,0:T(8,128)(2,1)} %copy-done.3), custom_call_target="tpu_custom_call" | custom-call | flops 4000000000 | bytes 2000000 | tf_op jit(solution)/shard_map/tiles/pallas_call | solution.py:239
  37.4 0.8 collective-permute-start.2
  38.1 5.1 %tiles.6.refs_2_ = bf16[4,512,512]{2,1,0:T(8,128)(2,1)} custom-call(s32[2,32]{1,0:T(2,128)} %bitcast.11, s32[1]{0:T(128)S(6)} %add.10.first, bf16[16,10,512]{2,1,0:T(8,128)(2,1)} %copy-done.3), custom_call_target="tpu_custom_call" | custom-call | flops 4000000000 | bytes 2000000 | tf_op jit(solution)/shard_map/tiles/pallas_call | solution.py:239
  43.2 0.1 collective-permute-start.3
  43.3 5.1 %tiles.7.refs_3_ = bf16[4,512,512]{2,1,0:T(8,128)(2,1)} custom-call(s32[2,32]{1,0:T(2,128)} %bitcast.12, s32[1]{0:T(128)S(6)} %add.11.first, bf16[16,10,512]{2,1,0:T(8,128)(2,1)} %copy-done.3), custom_call_target="tpu_custom_call" | custom-call | flops 4000000000 | bytes 2000000 | tf_op jit(solution)/shard_map/tiles/pallas_call | solution.py:239
  48.4 0.6 collective-permute-start.4
  49.0 16.3 %diag.1 = (f32[4,16,8,512]{3,2,1,0:T(8,128)}, f32[4,16,8,512]{3,2,1,0:T(8,128)}) custom-call(s32[1]{0:T(128)S(6)} %and.4.core, bf16[16,4,64,512]{3,2,1,0:T(8,128)(2,1)} %ens_ref.3, bf16[16,64,512]{2,1,0:T(8,128)(2,1)} %refs_0_.1, bf16[16,2,512]{2,1,0:T(2,128)(2,1)} %refs_1_.1), custom_call_target="tpu_custom_call" | custom-call | flops 20000000000 | bytes 8000000 | tf_op jit(solution)/shard_map/diag/pallas_call | solution.py:181
  65.3 0.0 collective-permute-start
  65.3 2.8 %collective-permute-done.got_ref = f32[4,16,8,512]{3,2,1,0:T(8,128)S(1)} collective-permute-done((f32[4,16,8,512]{3,2,1,0:T(8,128)}, f32[4,16,8,512]{3,2,1,0:T(8,128)S(1)}, u32[]{:S(2)}, u32[]{:S(2)}) %collective-permute-start) | collective-permute-done | bytes 1048608 | tf_op jit(solution)/shard_map/ppermute | solution.py:411
  68.1 1.2 %copy-done = f32[4,16,8,512]{3,2,1,0:T(8,128)S(1)} copy-done((f32[4,16,8,512]{3,2,1,0:T(8,128)S(1)}, f32[4,16,8,512]{3,2,1,0:T(8,128)}, u32[]{:S(2)}) %copy-start) | copy-done | bytes 1048600
  69.4 0.1 merge.1
  69.5 1.0 collective-permute-start.5
  70.4 0.0 collective-permute-done.1.refs_4_
  70.4 2.7 %collective-permute-start.6 = (bf16[16,8,512]{2,1,0:T(8,128)(2,1)S(1)}, bf16[16,8,512]{2,1,0:T(8,128)(2,1)S(1)}, u32[]{:S(2)}, u32[]{:S(2)}) collective-permute-start(bf16[16,8,512]{2,1,0:T(8,128)(2,1)S(1)} %get-tuple-element.35), channel_id=1, source_target_pairs={{0,4},{1,5},{2,6},{3,7},{4,0},{5,1},{6,2},{7,3},{8,12},{9,13},{10,... | collective-permute-start | bytes 393224 | tf_op jit(solution)/shard_map/ppermute | solution.py:413
  73.1 0.0 collective-permute-done.2.refs_5_
  73.1 1.4 %collective-permute-start.7 = (bf16[16,8,512]{2,1,0:T(8,128)(2,1)S(1)}, bf16[16,8,512]{2,1,0:T(8,128)(2,1)S(1)}, u32[]{:S(2)}, u32[]{:S(2)}) collective-permute-start(bf16[16,8,512]{2,1,0:T(8,128)(2,1)S(1)} %get-tuple-element.36), channel_id=1, source_target_pairs={{0,6},{1,7},{2,0},{3,1},{4,2},{5,3},{6,4},{7,5},{8,14},{9,15},{10,... | collective-permute-start | bytes 393224 | tf_op jit(solution)/shard_map/ppermute | solution.py:413
  75.2 0.0 collective-permute-done.3.refs_6_
  75.2 0.0 collective-permute-done.4.refs_7_
  75.2 4.4 %all-to-all-done.1 = bf16[128,128,128]{2,1,0:T(8,128)(2,1)} async-done(((bf16[128,128,128]{2,1,0:T(8,128)(2,1)}), bf16[128,128,128]{2,1,0:T(8,128)(2,1)}, u32[]{:S(2)}, u32[]{:S(2)}) %all-to-all-start.1) | async-done | bytes 4194336 | tf_op jit(solution)/shard_map/all_to_all | solution.py:401
  79.6 16.5 %apply.1 = bf16[16,8,512]{2,1,0:T(8,128)(2,1)} custom-call(s32[2,32]{1,0:T(2,128)} %bitcast.13, s32[1]{0:T(128)S(6)} %copy.7.count, s32[1]{0:T(128)S(6)} %and.4.core, bf16[16,8,128,128]{3,2,1,0:T(8,128)(2,1)} %bitcast.3.got_ref, bf16[16,10,512]{2,1,0:T(8,128)(2,1)} %copy-done.3, bf16[4,512,512]{2,1,0:T(8,128)(2,1)} %tiles.4.refs_0_, ...), custom_call_target="tpu_custom_call" | custom-call | flops 100000000 | bytes 22000000 | tf_op jit(solution)/shard_map/apply/pallas_call | solution.py:341
  96.1 0.0 collective-permute-done.5.refs_0_
  96.1 0.0 collective-permute-done.6.refs_1_
  96.1 11.5 %all_to_all.15.refs_3_ = bf16[16,8,512]{2,1,0:T(8,128)(2,1)S(1)} all-to-all(bf16[16,8,512]{2,1,0:T(8,128)(2,1)} %apply.1), channel_id=1, replica_groups=mesh['region'=16,'member'=8] {'region'}, dimensions={0} | all-to-all | bytes 262144 | tf_op jit(solution)/shard_map/all_to_all | solution.py:420
  107.6 1.4 %finish.1 = f32[16,8,512]{2,1,0:T(8,128)} custom-call(s32[16]{0:T(128)S(1)} %bitcast.7, f32[16,8,512]{2,1,0:T(8,128)S(1)} %get-tuple-element.28.own_ref, bf16[16,8,512]{2,1,0:T(8,128)(2,1)S(1)} %collective-permute-done.5.refs_0_, bf16[16,8,512]{2,1,0:T(8,128)(2,1)S(1)} %collective-permute-done.6.refs_1_, ...), custom_call_target="tpu_custom_call" | custom-call | tf_op jit(solution)/shard_map/finish/pallas_call | solution.py:380
  (7 shorter events, 0.0 us)
Async XLA Ops:
  2.5 16.7 %all-to-all-start = ((bf16[16,10,512]{2,1,0:T(8,128)(2,1)}), bf16[16,10,512]{2,1,0:T(8,128)(2,1)S(1)}, u32[]{:S(2)}, u32[]{:S(2)}) async-start(bf16[16,10,512]{2,1,0:T(8,128)(2,1)} %select.1), calls=%async_computation | async-start | bytes 524288 | tf_op jit(solution)/shard_map/all_to_all | solution.py:398
  19.2 0.7 copy-start.3
  19.9 59.8 %all-to-all-start.1 = ((bf16[128,128,128]{2,1,0:T(8,128)(2,1)}), bf16[128,128,128]{2,1,0:T(8,128)(2,1)}, u32[]{:S(2)}, u32[]{:S(2)}) async-start(bf16[128,128,128]{2,1,0:T(8,128)(2,1)} %bitcast.8), calls=%async_computation.1 | async-start | bytes 8388608 | tf_op jit(solution)/shard_map/all_to_all | solution.py:401
  32.2 38.2 %collective-permute-start.1 = (bf16[4,512,512]{2,1,0:T(8,128)(2,1)}, bf16[4,512,512]{2,1,0:T(8,128)(2,1)S(1)}, u32[]{:S(2)}, u32[]{:S(2)}) collective-permute-start(bf16[4,512,512]{2,1,0:T(8,128)(2,1)} %tiles.4.refs_0_), channel_id=1, source_target_pairs={{0,1},{1,0},{2,3},{3,2},{4,5},{5,4},{6,7},{7,6},{8,9},{9,8},{10,11... | collective-permute-start | bytes 6291464 | tf_op jit(solution)/shard_map/ppermute | solution.py:409
  37.4 35.8 %collective-permute-start.2 = (bf16[4,512,512]{2,1,0:T(8,128)(2,1)}, bf16[4,512,512]{2,1,0:T(8,128)(2,1)}, u32[]{:S(2)}, u32[]{:S(2)}) collective-permute-start(bf16[4,512,512]{2,1,0:T(8,128)(2,1)} %tiles.5.refs_1_), channel_id=1, source_target_pairs={{0,1},{1,0},{2,3},{3,2},{4,5},{5,4},{6,7},{7,6},{8,9},{9,8},{10,11... | collective-permute-start | bytes 6291464 | tf_op jit(solution)/shard_map/ppermute | solution.py:409
  43.2 32.0 %collective-permute-start.3 = (bf16[4,512,512]{2,1,0:T(8,128)(2,1)}, bf16[4,512,512]{2,1,0:T(8,128)(2,1)}, u32[]{:S(2)}, u32[]{:S(2)}) collective-permute-start(bf16[4,512,512]{2,1,0:T(8,128)(2,1)} %tiles.6.refs_2_), channel_id=1, source_target_pairs={{0,1},{1,0},{2,3},{3,2},{4,5},{5,4},{6,7},{7,6},{8,9},{9,8},{10,11... | collective-permute-start | bytes 6291464 | tf_op jit(solution)/shard_map/ppermute | solution.py:409
  48.4 26.8 %collective-permute-start.4 = (bf16[4,512,512]{2,1,0:T(8,128)(2,1)}, bf16[4,512,512]{2,1,0:T(8,128)(2,1)}, u32[]{:S(2)}, u32[]{:S(2)}) collective-permute-start(bf16[4,512,512]{2,1,0:T(8,128)(2,1)} %tiles.7.refs_3_), channel_id=1, source_target_pairs={{0,1},{1,0},{2,3},{3,2},{4,5},{5,4},{6,7},{7,6},{8,9},{9,8},{10,11... | collective-permute-start | bytes 6291464 | tf_op jit(solution)/shard_map/ppermute | solution.py:409
  65.3 2.9 %collective-permute-start = (f32[4,16,8,512]{3,2,1,0:T(8,128)}, f32[4,16,8,512]{3,2,1,0:T(8,128)S(1)}, u32[]{:S(2)}, u32[]{:S(2)}) collective-permute-start(f32[4,16,8,512]{3,2,1,0:T(8,128)} %get-tuple-element.25), channel_id=1, source_target_pairs={{0,1},{1,0},{2,3},{3,2},{4,5},{5,4},{6,7},{7,6},{8,9},{9,8},{10,11... | collective-permute-start | bytes 3145736 | tf_op jit(solution)/shard_map/ppermute | solution.py:411
  68.1 1.2 %copy-start = (f32[4,16,8,512]{3,2,1,0:T(8,128)S(1)}, f32[4,16,8,512]{3,2,1,0:T(8,128)}, u32[]{:S(2)}) copy-start(f32[4,16,8,512]{3,2,1,0:T(8,128)} %get-tuple-element.24.keep_ref) | copy-start | bytes 3145732
  69.5 26.6 %collective-permute-start.5 = (bf16[16,8,512]{2,1,0:T(8,128)(2,1)S(1)}, bf16[16,8,512]{2,1,0:T(8,128)(2,1)S(1)}, u32[]{:S(2)}, u32[]{:S(2)}) collective-permute-start(bf16[16,8,512]{2,1,0:T(8,128)(2,1)S(1)} %get-tuple-element.34), channel_id=1, source_target_pairs={{0,2},{1,3},{2,4},{3,5},{4,6},{5,7},{6,0},{7,1},{8,10},{9,11},{10,... | collective-permute-start | bytes 393224 | tf_op jit(solution)/shard_map/ppermute | solution.py:413
  70.4 9.2 %copy-start.2 = (bf16[4,512,512]{2,1,0:T(8,128)(2,1)}, bf16[4,512,512]{2,1,0:T(8,128)(2,1)S(1)}, u32[]{:S(2)}) copy-start(bf16[4,512,512]{2,1,0:T(8,128)(2,1)S(1)} %collective-permute-done.1.refs_4_) | copy-start | bytes 6291460
  70.4 25.7 %collective-permute-start.6 = (bf16[16,8,512]{2,1,0:T(8,128)(2,1)S(1)}, bf16[16,8,512]{2,1,0:T(8,128)(2,1)S(1)}, u32[]{:S(2)}, u32[]{:S(2)}) collective-permute-start(bf16[16,8,512]{2,1,0:T(8,128)(2,1)S(1)} %get-tuple-element.35), channel_id=1, source_target_pairs={{0,4},{1,5},{2,6},{3,7},{4,0},{5,1},{6,2},{7,3},{8,12},{9,13},{10,... | collective-permute-start | bytes 393224 | tf_op jit(solution)/shard_map/ppermute | solution.py:413
  73.1 23.0 %collective-permute-start.7 = (bf16[16,8,512]{2,1,0:T(8,128)(2,1)S(1)}, bf16[16,8,512]{2,1,0:T(8,128)(2,1)S(1)}, u32[]{:S(2)}, u32[]{:S(2)}) collective-permute-start(bf16[16,8,512]{2,1,0:T(8,128)(2,1)S(1)} %get-tuple-element.36), channel_id=1, source_target_pairs={{0,6},{1,7},{2,0},{3,1},{4,2},{5,3},{6,4},{7,5},{8,14},{9,15},{10,... | collective-permute-start | bytes 393224 | tf_op jit(solution)/shard_map/ppermute | solution.py:413
  79.6 28.0 %copy-start.1 = (s32[1,16,1]{1,2,0:T(1,128)S(1)}, s32[1,16,1]{1,2,0:T(1,128)}, u32[]{:S(2)}) copy-start(s32[1,16,1]{1,2,0:T(1,128)} %param.9) | copy-start | bytes 196
